TPU v7x, 32 devices: a whole 2x2x4 slice. The times are simulated.
32 devices in a mesh: dp: 8 (over z, x), tensor: 4 (over y, core).
Axes of the slice: x: 2, y: 2, z: 4, core: 2. Of those that a mesh axis runs over, the one named last changes fastest.
Arguments:
- inputs: bfloat16 [6304, 512], P(('dp', 'tensor')), may hold values from -6 to 6
- norm_gains: float32 [2, 2, 512], replicated, may hold values from 0.5 to 1.5
- qkv_weight: bfloat16 [2, 512, 3, 512], P(None, 'dp', None, 'tensor'), may hold values from -0.25 to 0.25
- out_weight: bfloat16 [2, 512, 512], P(None, 'tensor', 'dp'), may hold values from -1 to 1
- router_weight: bfloat16 [2, 512, 8], replicated, may hold values from -0.1875 to 0.1875
- expert_in: bfloat16 [2, 8, 512, 2048], P(None, None, 'dp', 'tensor'), may hold values from -0.25 to 0.25
- expert_out: bfloat16 [2, 8, 2048, 512], P(None, None, 'tensor', 'dp'), may hold values from -0.75 to 0.75
- routes: int32 [2, 6304, 2], P(None, 'dp'), may hold values from 0 to 7, all different within a row
- priority: int32 [2, 8, 788], P(None, 'dp'), may hold values from 0 to 787, each once within a row
- cotangent: float32 [6304, 512], P(('dp', 'tensor')), may hold values from -6 to 6
Outputs:
- outputs: bfloat16 [6304, 512], P(('dp', 'tensor'))
- input_grad: float32 [6304, 512], P(('dp', 'tensor'))
- gains_grad: float32 [2, 2, 512], replicated
- qkv_grad: float32 [2, 512, 3, 512], P(None, 'dp', None, 'tensor')
- out_proj_grad: float32 [2, 512, 512], P(None, 'tensor', 'dp')
- router_grad: float32 [2, 512, 8], replicated
- expert_in_grad: float32 [2, 8, 512, 2048], P(None, None, 'dp', 'tensor')
- expert_out_grad: float32 [2, 8, 2048, 512], P(None, None, 'tensor', 'dp')
Inputs may be any that keep to these rules, and one draw needn't show every extreme that they name: `routes`: the two experts of a token differ. For each layer and shard, priority lists each of the 788 tokens' ranks once; rank 0 is served first.
All inputs are finite; a program needn't handle non-finite values.
Results may differ from a plain program's by a relative error of at most 0.035.
Values may be sent and summed in bfloat16 or wider, within the bound.
No kernel may reach another device: no remote copies, remote signals or barrier semaphores. Data moves between devices by JAX's collectives and lax.ppermute only.
A program may use at most 192 MiB of HBM per device.

v0:
```python
import jax
import jax.numpy as jnp
from jax import lax
from jax.sharding import PartitionSpec as P

HD = 64
LEN = 197
LAYERS = 2
CAP = 247


NORM_EPS = 1e-06
HIGHEST = lax.Precision.HIGHEST


def layer_norm(hidden, gain_row):
    average = jnp.mean(hidden, axis=-1, keepdims=True)
    centered = hidden - average
    variance = jnp.mean(centered * centered, axis=-1, keepdims=True)
    return centered * lax.rsqrt(variance + NORM_EPS) * gain_row


def norm_back(hidden_rows, gain_row, grad_rows):
    unused, pullback = jax.vjp(layer_norm, hidden_rows, gain_row)
    return pullback(grad_rows)


def gelu_tanh(values):
    return jax.nn.gelu(values, approximate=True)


def gelu_back(pre_act, act_grad):
    unused, pullback = jax.vjp(gelu_tanh, pre_act)
    return pullback(act_grad)[0]


def route_slots(expert_ids, ranking, experts, capacity):
    token_count = expert_ids.shape[0]
    serial = jnp.arange(token_count, dtype=jnp.int32)
    by_rank = jnp.zeros((token_count,), jnp.int32).at[ranking].set(serial)
    served = jnp.transpose(expert_ids[by_rank]).reshape(-1)
    expert_range = jnp.arange(experts, dtype=jnp.int32)
    onehot = (served[:, None] == expert_range[None, :]).astype(jnp.int32)
    earlier = jnp.cumsum(onehot, axis=0) - onehot
    slot_served = jnp.sum(earlier * onehot, axis=1)
    order_key = jnp.arange(2, dtype=jnp.int32)[None, :] * token_count + ranking[:, None]
    slot_index = slot_served[order_key]
    keep_mask = (slot_index < capacity).astype(jnp.float32)
    positions = expert_ids * capacity + jnp.minimum(slot_index, capacity - 1)
    target = jnp.where(slot_index < capacity, positions, experts * capacity).reshape(-1)
    pair_ids = jnp.arange(2 * token_count, dtype=jnp.int32)
    pair_of_slot = jnp.zeros((experts * capacity,), jnp.int32).at[target].set(pair_ids, mode="drop")
    filled = jnp.zeros((experts * capacity,), jnp.float32).at[target].set(1.0, mode="drop")
    return (positions, keep_mask, pair_of_slot, filled)


def per_device(
    inputs,
    norm_gains,
    qkv_weight,
    out_weight,
    router_weight,
    expert_in,
    expert_out,
    routes,
    priority,
    cotangent,
):
    tensor_size = lax.axis_size("tensor")
    my_part = lax.axis_index("tensor")
    own_rows = inputs.shape[0]
    model_width = inputs.shape[1]
    group_rows = own_rows * tensor_size
    images = group_rows // LEN
    heads_here = qkv_weight.shape[3] // HD
    experts = expert_in.shape[1]
    capacity = CAP
    score_scale = HD ** (-0.5)
    row_start = my_part * own_rows
    f32 = jnp.float32
    bf16 = jnp.bfloat16
    hidden = inputs.astype(f32)
    saved_layers = []
    for layer_idx in range(LAYERS):
        shards = (
            qkv_weight[layer_idx],
            out_weight[layer_idx],
            expert_in[layer_idx],
            expert_out[layer_idx],
        )
        full_w = (
            lax.all_gather(shards[0], "dp", axis=0, tiled=True),
            lax.all_gather(shards[1], "dp", axis=1, tiled=True),
            lax.all_gather(shards[2], "dp", axis=1, tiled=True),
            lax.all_gather(shards[3], "dp", axis=2, tiled=True),
        )
        hidden_in = hidden
        normed_a = lax.all_gather(
            layer_norm(hidden, norm_gains[layer_idx, 0]).astype(bf16), "tensor", axis=0, tiled=True
        )
        qkv_rows = jnp.einsum(
            "td,dsh->tsh", normed_a, full_w[0], preferred_element_type=f32
        ).astype(bf16)
        qkv_rows = qkv_rows.reshape(images, LEN, 3, heads_here, HD)
        queries = qkv_rows[:, :, 0]
        key_rows = qkv_rows[:, :, 1]
        values = qkv_rows[:, :, 2]
        scores = (
            jnp.einsum("bqhd,bkhd->bhqk", queries, key_rows, preferred_element_type=f32)
            * score_scale
        )
        log_total = jax.nn.logsumexp(scores, axis=-1, keepdims=True)
        attn_probs = jnp.exp(scores - log_total)
        context = jnp.einsum(
            "bhqk,bkhd->bqhd", attn_probs.astype(bf16), values, preferred_element_type=f32
        )
        context = context.astype(bf16).reshape(group_rows, heads_here * HD)
        proj_full = None
        context_own = None
        partial_out = jnp.dot(context, full_w[1], preferred_element_type=f32)
        hidden = hidden + lax.psum_scatter(
            partial_out.astype(jnp.bfloat16), "tensor", scatter_dimension=0, tiled=True
        ).astype(jnp.float32)
        hidden_mid = hidden
        normed_own = layer_norm(hidden, norm_gains[layer_idx, 1]).astype(bf16)
        normed_e = lax.all_gather(normed_own, "tensor", axis=0, tiled=True)
        logits = jnp.dot(normed_e, router_weight[layer_idx], preferred_element_type=f32)
        router_probs = jnp.exp(logits - jax.nn.logsumexp(logits, axis=-1, keepdims=True))
        expert_ids = routes[layer_idx]
        positions, keep_mask, pair_of_slot, filled = route_slots(
            expert_ids, priority[layer_idx, 0], experts, capacity
        )
        gate_vals = jnp.take_along_axis(router_probs, expert_ids, axis=1) * keep_mask
        dispatched = jnp.where(
            filled[:, None] > 0, normed_e[pair_of_slot // 2], jnp.zeros((), bf16)
        )
        dispatched = dispatched.reshape(experts, capacity, model_width)
        pre_act = jnp.einsum("ecd,edf->ecf", dispatched, full_w[2], preferred_element_type=f32)
        activated = gelu_tanh(pre_act).astype(bf16)
        expert_part = jnp.einsum("ecf,efd->ecd", activated, full_w[3], preferred_element_type=f32)
        picked = expert_part.reshape(experts * capacity, model_width)[positions]
        combined = jnp.sum(gate_vals[:, :, None] * picked, axis=1)
        hidden = hidden + lax.psum_scatter(
            combined.astype(jnp.bfloat16), "tensor", scatter_dimension=0, tiled=True
        ).astype(jnp.float32)
        saved_layers.append(
            {
                "weights": full_w,
                "hidden_in": hidden_in,
                "hidden_mid": hidden_mid,
                "normed_a": normed_a,
                "queries": queries,
                "key_rows": key_rows,
                "values": values,
                "log_total": log_total,
                "context": context,
                "context_own": context_own,
                "proj_full": proj_full,
                "normed_own": normed_own,
                "router_probs": router_probs,
                "expert_ids": expert_ids,
                "positions": positions,
                "keep_mask": keep_mask,
                "pair_of_slot": pair_of_slot,
                "filled": filled,
                "gate_vals": gate_vals,
                "dispatched": dispatched,
                "pre_act": pre_act,
                "activated": activated,
                "picked": picked,
            }
        )
    grad_hidden = cotangent
    gain_list = [None] * LAYERS
    router_list = [None] * LAYERS
    qkv_list = [None] * LAYERS
    proj_list = [None] * LAYERS
    in_list = [None] * LAYERS
    out_list = [None] * LAYERS
    expert_range = jnp.arange(experts, dtype=jnp.int32)
    for layer_idx in reversed(range(LAYERS)):
        saved = saved_layers[layer_idx]
        shards = (
            qkv_weight[layer_idx],
            out_weight[layer_idx],
            expert_in[layer_idx],
            expert_out[layer_idx],
        )
        full_w = (
            lax.all_gather(shards[0], "dp", axis=0, tiled=True),
            lax.all_gather(shards[1], "dp", axis=1, tiled=True),
            lax.all_gather(shards[2], "dp", axis=1, tiled=True),
            lax.all_gather(shards[3], "dp", axis=2, tiled=True),
        )
        branch_grad = lax.all_gather(grad_hidden.astype(bf16), "tensor", axis=0, tiled=True)
        branch_wide = branch_grad.astype(f32)
        gate_grad = jnp.sum(branch_wide[:, None, :] * saved["picked"], axis=2) * saved["keep_mask"]
        slot_gate = saved["gate_vals"].reshape(-1)[saved["pair_of_slot"]] * saved["filled"]
        slot_grad = (slot_gate[:, None] * branch_wide[saved["pair_of_slot"] // 2]).astype(bf16)
        slot_grad = slot_grad.reshape(experts, capacity, model_width)
        out_list[layer_idx] = jnp.einsum(
            "ecf,ecd->efd", saved["activated"], slot_grad, preferred_element_type=f32
        )
        act_grad = jnp.einsum("ecd,efd->ecf", slot_grad, full_w[3], preferred_element_type=f32)
        pre_grad = gelu_back(saved["pre_act"], act_grad).astype(bf16)
        in_list[layer_idx] = jnp.einsum(
            "ecd,ecf->edf", saved["dispatched"], pre_grad, preferred_element_type=f32
        )
        slot_back = jnp.einsum("ecf,edf->ecd", pre_grad, full_w[2], preferred_element_type=f32)
        slot_back = slot_back.reshape(experts * capacity, model_width)
        rows_back = jnp.sum(saved["keep_mask"][:, :, None] * slot_back[saved["positions"]], axis=1)
        normed_grad, gate_grad_own = (
            lax.psum_scatter(
                rows_back.astype(jnp.bfloat16), "tensor", scatter_dimension=0, tiled=True
            ).astype(jnp.float32),
            lax.psum_scatter(
                gate_grad.astype(jnp.bfloat16), "tensor", scatter_dimension=0, tiled=True
            ).astype(jnp.float32),
        )
        probs_own = lax.dynamic_slice_in_dim(saved["router_probs"], row_start, own_rows, 0)
        ids_own = lax.dynamic_slice_in_dim(saved["expert_ids"], row_start, own_rows, 0)
        choice_hits = (ids_own[:, :, None] == expert_range[None, None, :]).astype(f32)
        prob_grad = jnp.sum(gate_grad_own[:, :, None] * choice_hits, axis=1)
        logit_grad = probs_own * (
            prob_grad - jnp.sum(probs_own * prob_grad, axis=-1, keepdims=True)
        )
        router_list[layer_idx] = jnp.dot(
            saved["normed_own"].astype(f32).T, logit_grad, precision=HIGHEST
        )
        normed_grad = normed_grad + jnp.dot(
            logit_grad, router_weight[layer_idx].astype(f32).T, precision=HIGHEST
        )
        hidden_part, gain_expert = norm_back(
            saved["hidden_mid"], norm_gains[layer_idx, 1], normed_grad
        )
        grad_hidden = grad_hidden + hidden_part
        attn_grad = lax.all_gather(grad_hidden.astype(bf16), "tensor", axis=0, tiled=True)
        proj_list[layer_idx] = jnp.einsum(
            "tc,td->cd", saved["context"], attn_grad, preferred_element_type=f32
        )
        context_grad = jnp.einsum(
            "td,cd->tc", attn_grad, full_w[1], preferred_element_type=f32
        ).astype(bf16)
        context_grad = context_grad.reshape(images, LEN, heads_here, HD)
        scores = (
            jnp.einsum(
                "bqhd,bkhd->bhqk", saved["queries"], saved["key_rows"], preferred_element_type=f32
            )
            * score_scale
        )
        attn_probs = jnp.exp(scores - saved["log_total"])
        value_grad = jnp.einsum(
            "bhqk,bqhd->bkhd", attn_probs.astype(bf16), context_grad, preferred_element_type=f32
        ).astype(bf16)
        probs_grad = jnp.einsum(
            "bqhd,bkhd->bhqk", context_grad, saved["values"], preferred_element_type=f32
        )
        score_grad = (
            attn_probs * (probs_grad - jnp.sum(attn_probs * probs_grad, axis=-1, keepdims=True))
        ).astype(bf16)
        query_grad = (
            jnp.einsum("bhqk,bkhd->bqhd", score_grad, saved["key_rows"], preferred_element_type=f32)
            * score_scale
        ).astype(bf16)
        key_grad = (
            jnp.einsum("bhqk,bqhd->bkhd", score_grad, saved["queries"], preferred_element_type=f32)
            * score_scale
        ).astype(bf16)
        mixed_grad = jnp.stack([query_grad, key_grad, value_grad], axis=2).reshape(
            group_rows, 3, heads_here * HD
        )
        qkv_list[layer_idx] = jnp.einsum(
            "td,tsh->dsh", saved["normed_a"], mixed_grad, preferred_element_type=f32
        )
        normed_part = jnp.einsum("tsh,dsh->td", mixed_grad, full_w[0], preferred_element_type=f32)
        normed_grad = lax.psum_scatter(
            normed_part.astype(jnp.bfloat16), "tensor", scatter_dimension=0, tiled=True
        ).astype(jnp.float32)
        hidden_part, gain_attn = norm_back(
            saved["hidden_in"], norm_gains[layer_idx, 0], normed_grad
        )
        grad_hidden = grad_hidden + hidden_part
        gain_list[layer_idx] = jnp.stack([gain_attn, gain_expert])
        summed = (
            lax.psum_scatter(qkv_list[layer_idx], "dp", scatter_dimension=0, tiled=True),
            lax.psum_scatter(proj_list[layer_idx], "dp", scatter_dimension=1, tiled=True),
            lax.psum_scatter(in_list[layer_idx], "dp", scatter_dimension=1, tiled=True),
            lax.psum_scatter(out_list[layer_idx], "dp", scatter_dimension=2, tiled=True),
        )
        qkv_list[layer_idx] = summed[0]
        proj_list[layer_idx] = summed[1]
        in_list[layer_idx] = summed[2]
        out_list[layer_idx] = summed[3]
    gains_total, router_total = lax.psum(
        (jnp.stack(gain_list), jnp.stack(router_list)), ("dp", "tensor")
    )
    return (
        hidden.astype(bf16),
        grad_hidden,
        gains_total,
        jnp.stack(qkv_list),
        jnp.stack(proj_list),
        router_total,
        jnp.stack(in_list),
        jnp.stack(out_list),
    )


def solution(mesh):
    in_specs = (
        P(("dp", "tensor"), None),
        P(),
        P(None, "dp", None, "tensor"),
        P(None, "tensor", "dp"),
        P(),
        P(None, None, "dp", "tensor"),
        P(None, None, "tensor", "dp"),
        P(None, "dp", None),
        P(None, "dp", None),
        P(("dp", "tensor"), None),
    )
    out_specs = (
        P(("dp", "tensor"), None),
        P(("dp", "tensor"), None),
        P(),
        P(None, "dp", None, "tensor"),
        P(None, "tensor", "dp"),
        P(),
        P(None, None, "dp", "tensor"),
        P(None, None, "tensor", "dp"),
    )
    return jax.shard_map(
        per_device, mesh=mesh, in_specs=in_specs, out_specs=out_specs, check_vma=False
    )
```

profile of v0, /device:TPU:0, one launch (start us, length us, event | category | flops | bytes accessed | tf_op | source)
XLA Modules:
  0.0 1565.1 jit_solution(1017616822091138206)
XLA Ops:
  14.4 10.3 all-gather.8
  25.6 32.5 %all-gather = bf16[1,512,3,128]{3,1,2,0:T(8,128)(2,1)S(1)} all-gather(bf16[1,64,3,128]{3,1,2,0:T(8,128)(2,1)S(1)} %get-tuple-element.62), channel_id=2, replica_groups=mesh['dp'=8,'tensor'=4] {'dp'}, dimensions={1}, use_global_device_ids=true | all-gather | bytes 442368 | tf_op jit(solution)/shard_map/all_gather | solution.py:92
  65.3 31.0 %all-gather.1 = bf16[1,128,512]{1,2,0:T(8,128)(2,1)S(1)} all-gather(bf16[1,128,64]{1,2,0:T(8,128)(2,1)S(1)} %get-tuple-element.64), channel_id=3, replica_groups=mesh['dp'=8,'tensor'=4] {'dp'}, dimensions={2}, use_global_device_ids=true | all-gather | bytes 147456 | tf_op jit(solution)/shard_map/all_gather | solution.py:93
  97.4 12.4 fusion
  112.8 5.3 scatter_custom_fusion
  124.5 8.8 gather_fusion.1
  133.5 5.5 scatter_custom_fusion.3
  144.4 8.8 gather_fusion.5
  155.3 8.8 scatter_custom_fusion.2
  164.1 8.8 scatter_custom_fusion.1
  173.4 34.1 %all-gather.4 = bf16[1,512,3,128]{3,1,2,0:T(8,128)(2,1)} all-gather(bf16[1,64,3,128]{3,1,2,0:T(8,128)(2,1)S(1)} %copy-done.83), channel_id=6, replica_groups=mesh['dp'=8,'tensor'=4] {'dp'}, dimensions={1}, use_global_device_ids=true | all-gather | bytes 442368 | tf_op jit(solution)/shard_map/all_gather | solution.py:92
  208.2 8.8 scatter_custom_fusion.4
  217.0 8.8 scatter_custom_fusion.5
  227.6 8.6 all-gather.12
  241.8 9.3 all-gather.9
  251.3 9.2 gather_fusion.2
  264.4 15.3 gather_fusion.14
  281.0 7.7 copy.238
  302.0 8.5 gather_fusion.3
  314.4 7.0 multiply_reduce_fusion.5
  321.4 14.2 fusion.1
  338.8 32.5 %all-gather.5 = bf16[1,128,512]{1,2,0:T(8,128)(2,1)} all-gather(bf16[1,128,64]{1,2,0:T(8,128)(2,1)S(1)} %copy-done.94), channel_id=7, replica_groups=mesh['dp'=8,'tensor'=4] {'dp'}, dimensions={2}, use_global_device_ids=true | all-gather | bytes 147456 | tf_op jit(solution)/shard_map/all_gather | solution.py:93
  377.7 9.2 all-gather.10
  396.2 13.0 fusion.2
  412.3 8.8 gather_fusion.9
  421.2 4.6 gather.65
  428.8 11.5 gather_fusion.11
  441.0 7.6 copy.249
  449.9 9.4 all-gather.11
  459.5 9.1 gather_fusion.6
  482.0 4.6 reshape.694
  486.6 8.5 gather_fusion.7
  495.1 5.2 reshape.777
  500.4 15.3 gather_fusion.15
  516.5 11.2 multiply_reduce_fusion.2
  527.7 11.9 gather_fusion.8
  539.7 8.2 fusion.39
  557.1 8.5 gather_fusion.10
  565.6 5.2 reshape.801
  570.9 6.4 multiply_reduce_fusion.3
  577.3 13.8 fusion.162
  601.3 9.9 all-gather.13
  632.2 13.6 fusion.6
  652.8 10.2 all-gather.14
  667.0 9.1 gather_fusion.12
  676.2 4.6 gather.69
  680.7 8.2 fusion.32
  693.5 4.6 reshape.699
  698.1 8.5 gather_fusion.13
  706.6 5.3 reshape.825
  712.0 6.3 multiply_reduce_fusion.1
  718.3 13.3 fusion.161
  740.2 10.2 all-gather.15
  780.6 7.0 fusion.45
  788.3 7.0 fusion.44
  796.0 8.9 fusion.64
  805.6 8.9 fusion.65
  817.6 18.2 %fusion.160 = (bf16[200,512]{1,0:T(8,128)(2,1)S(1)}, bf16[200,512]{1,0:T(8,128)(2,1)S(1)}) fusion(bf16[788,512]{1,0:T(8,128)(2,1)S(1)} %copy-done.47, bf16[788,512]{1,0:T(8,128)(2,1)S(1)} %bitcast_convert_fusion), kind=kCustom, calls=%all-reduce-scatter.10 | all-reduce-scatter fusion | flops 819201 | bytes 2023936
  843.9 42.1 %all-reduce.22 = (f32[2,2,512]{2,1,0:T(2,128)}, f32[2,512,8]{1,2,0:T(8,128)}) all-reduce(f32[2,2,512]{2,1,0:T(2,128)S(1)} %pad_maximum_fusion.5, f32[2,512,8]{1,2,0:T(8,128)S(1)} %pad_maximum_fusion.4), channel_id=1, replica_groups=mesh['dp'=8,'tensor'=4] {'dp','tensor'}, use_global_device_ids=true, to_apply=%region_62.64 | all-reduce | flops 10240 | bytes 81920 | tf_op jit(solution)/shard_map/psum | solution.py:294
  889.8 57.5 %reduce-scatter.29.cloned.1.call-done = f32[64,3,128]{2,0,1:T(8,128)} async-done(((f32[512,3,128]{2,0,1:T(8,128)}), f32[64,3,128]{2,0,1:T(8,128)}) %reduce-scatter.29.cloned.1.call-update) | async-done | bytes 98320 | tf_op jit(solution)/shard_map/reduce_scatter | solution.py:285
  948.9 150.1 %reduce-scatter.39.cloned.1.call-done = f32[8,64,512]{2,1,0:T(8,128)} async-done(((f32[8,512,512]{2,1,0:T(8,128)}), f32[8,64,512]{2,1,0:T(8,128)}) %reduce-scatter.39.cloned.1.call-update) | async-done | bytes 1048592 | tf_op jit(solution)/shard_map/reduce_scatter | solution.py:287
  1099.0 152.0 %reduce-scatter.37.cloned.1.call-done = f32[8,64,512]{2,1,0:T(8,128)} async-done(((f32[8,512,512]{2,1,0:T(8,128)}), f32[8,64,512]{2,1,0:T(8,128)}) %reduce-scatter.37.cloned.1.call-update) | async-done | bytes 1048592 | tf_op jit(solution)/shard_map/reduce_scatter | solution.py:287
  1254.1 148.6 %reduce-scatter.43.cloned.1.call-done = f32[8,512,64]{1,2,0:T(8,128)} async-done(((f32[8,512,512]{1,2,0:T(8,128)}), f32[8,512,64]{1,2,0:T(8,128)}) %reduce-scatter.43.cloned.1.call-update) | async-done | bytes 1048592 | tf_op jit(solution)/shard_map/reduce_scatter | solution.py:288
  1402.7 152.0 %reduce-scatter.41.cloned.1.call-done = f32[8,512,64]{1,2,0:T(8,128)} async-done(((f32[8,512,512]{1,2,0:T(8,128)}), f32[8,512,64]{1,2,0:T(8,128)}) %reduce-scatter.41.cloned.1.call-update) | async-done | bytes 1048592 | tf_op jit(solution)/shard_map/reduce_scatter | solution.py:288
  (646 shorter events, 221.8 us)
Async XLA Ops:
  7.2 273.8 %all-gather.23.cloned.1.call-start = ((), (), s32[]{:S(2)}) async-start(), calls=%async_computation.17 | async-start | bytes 4718592 | tf_op jit(solution)/shard_map/all_gather | solution.py:95
  9.8 279.0 %all-gather.21.cloned.1.call-start = ((), (), s32[]{:S(2)}) async-start(), calls=%async_computation.16 | async-start | bytes 4718592 | tf_op jit(solution)/shard_map/all_gather | solution.py:94
  10.9 430.1 %all-gather.27.cloned.1.call-start = ((), (), s32[]{:S(2)}) async-start(), calls=%async_computation.19 | async-start | bytes 4718592 | tf_op jit(solution)/shard_map/all_gather | solution.py:95
  12.1 460.3 %all-gather.25.cloned.1.call-start = ((), (), s32[]{:S(2)}) async-start(), calls=%async_computation.18 | async-start | bytes 4718592 | tf_op jit(solution)/shard_map/all_gather | solution.py:94
  24.9 33.2 %copy-start.44 = (bf16[788,512,1]{1,0,2:T(8,128)(2,1)}, bf16[788,512,1]{1,0,2:T(8,128)(2,1)S(1)}, u32[]{:S(2)}) copy-start(bf16[788,512,1]{1,0,2:T(8,128)(2,1)S(1)} %reshape.954) | copy-start | bytes 2420740
  62.4 50.0 %copy-start.119 = (s32[2,1,788]{2,1,0:T(1,128)S(1)}, s32[2,1,788]{2,1,0:T(1,128)}, u32[]{:S(2)}) copy-start(s32[2,1,788]{2,1,0:T(1,128)} %param.20) | copy-start | bytes 18916
  62.5 50.1 %copy-start.136 = (s32[2,788,2]{1,2,0:T(2,128)S(1)}, s32[2,788,2]{1,2,0:T(2,128)}, u32[]{:S(2)}) copy-start(s32[2,788,2]{1,2,0:T(2,128)} %param.19) | copy-start | bytes 37828
  64.6 56.2 %copy-start.59 = (bf16[788,128]{0,1:T(8,128)(2,1)}, bf16[788,128]{0,1:T(8,128)(2,1)S(1)}, u32[]{:S(2)}) copy-start(bf16[788,128]{0,1:T(8,128)(2,1)S(1)} %reshape.686) | copy-start | bytes 605188
  110.5 128.9 %collective-permute-start = (bf16[9,512]{1,0:T(8,128)(2,1)}, bf16[9,512]{1,0:T(8,128)(2,1)}, u32[]{:S(2)}, u32[]{:S(2)}) collective-permute-start(bf16[9,512]{1,0:T(8,128)(2,1)} %slice.176), channel_id=1, source_target_pairs={{0,1},{1,2},{2,3},{4,5},{5,6},{6,7},{8,9},{9,10},{10,11},{12,13},{... | collective-permute-start | bytes 27656
  112.4 776.0 %reduce-scatter.35.cloned.1.call-start = ((), (), s32[]{:S(2)}) async-start(), calls=%async_computation.11 | async-start | bytes 294912 | tf_op jit(solution)/shard_map/reduce_scatter | solution.py:286
  133.5 93.0 %copy-start.6 = (s32[1,788,2]{2,1,0:T(8,128)}, s32[1,788,2]{2,1,0:T(8,128)S(1)}, u32[]{:S(2)}) copy-start(s32[1,788,2]{2,1,0:T(8,128)S(1)} %copy.314) | copy-start | bytes 18916
  144.4 29.0 %copy-start.83 = (bf16[1,64,3,128]{3,1,2,0:T(8,128)(2,1)S(1)}, bf16[1,64,3,128]{3,1,2,0:T(8,128)(2,1)}, u32[]{:S(2)}) copy-start(bf16[1,64,3,128]{3,1,2,0:T(8,128)(2,1)} %get-tuple-element.61) | copy-start | bytes 147460
  153.2 74.3 %copy-start.34 = (f32[197,512]{1,0:T(8,128)S(1)}, f32[197,512]{1,0:T(8,128)}, u32[]{:S(2)}) copy-start(f32[197,512]{1,0:T(8,128)} %param.21) | copy-start | bytes 1210372
  153.2 84.2 %copy-start.124 = (pred[1576]{0:T(1024)(128)(4,1)}, pred[1576]{0:T(1024)(128)(4,1)S(1)}, u32[]{:S(2)}) copy-start(pred[1576]{0:T(1024)(128)(4,1)S(1)} %broadcast_compare_fusion) | copy-start | bytes 4732
  154.6 83.6 %copy-start.156 = (u32[32]{0:T(128)S(1)}, u32[32]{0:T(128)}, u32[]{:S(2)}) copy-start(u32[32]{0:T(128)} %constant.177) | copy-start | bytes 388
  154.6 84.9 %copy-start.75 = (bf16[200,512]{1,0:T(8,128)(2,1)S(1)}, bf16[200,512]{1,0:T(8,128)(2,1)}, u32[]{:S(2)}) copy-start(bf16[200,512]{1,0:T(8,128)(2,1)} %copy-done.74) | copy-start | bytes 614404
  154.9 85.6 %copy-start.16 = (bf16[197,512]{1,0:T(8,128)(2,1)S(1)}, bf16[197,512]{1,0:T(8,128)(2,1)}, u32[]{:S(2)}) copy-start(bf16[197,512]{1,0:T(8,128)(2,1)} %param.12) | copy-start | bytes 605188
  164.1 87.2 %copy-start.91 = (s32[2048]{0:T(1024)}, s32[2048]{0:T(1024)S(1)}, u32[]{:S(2)}) copy-start(s32[2048]{0:T(1024)S(1)} %pad_clamp_fusion.6) | copy-start | bytes 24580
  172.9 65.0 %copy-start.87 = (f32[1976]{0:T(1024)}, f32[1976]{0:T(1024)S(1)}, u32[]{:S(2)}) copy-start(f32[1976]{0:T(1024)S(1)} %scatter_custom_fusion.1) | copy-start | bytes 23716
  173.0 68.0 %copy-start.122 = (f32[1,1,512]{2,1,0:T(1,128)S(1)}, f32[1,1,512]{2,1,0:T(1,128)}, u32[]{:S(2)}) copy-start(f32[1,1,512]{2,1,0:T(1,128)} %get-tuple-element.72) | copy-start | bytes 6148
  173.4 128.6 %copy-start.4 = (s32[2048]{0:T(1024)}, s32[2048]{0:T(1024)S(1)}, u32[]{:S(2)}) copy-start(s32[2048]{0:T(1024)S(1)} %pad_clamp_fusion.5) | copy-start | bytes 24580
  237.8 173.1 %copy-start.68 = (pred[788,2]{1,0:T(8,128)(4,1)}, pred[788,2]{1,0:T(8,128)(4,1)S(1)}, u32[]{:S(2)}) copy-start(pred[788,2]{1,0:T(8,128)(4,1)S(1)} %reshape.909) | copy-start | bytes 4732
  237.9 50.8 %copy-start.126 = (pred[8,247]{1,0:T(8,128)(4,1)}, pred[8,247]{1,0:T(8,128)(4,1)S(1)}, u32[]{:S(2)}) copy-start(pred[8,247]{1,0:T(8,128)(4,1)S(1)} %broadcast_in_dim.62) | copy-start | bytes 5932
  314.4 63.4 %copy-start.14 = (f32[788,2,512]{2,1,0:T(2,128)}, f32[788,2,512]{2,1,0:T(2,128)S(1)}, u32[]{:S(2)}) copy-start(f32[788,2,512]{2,1,0:T(2,128)S(1)} %reshape.745) | copy-start | bytes 9682948
  314.4 63.2 %copy-start.100 = (f32[1,1,512]{2,1,0:T(1,128)S(1)}, f32[1,1,512]{2,1,0:T(1,128)}, u32[]{:S(2)}) copy-start(f32[1,1,512]{2,1,0:T(1,128)} %get-tuple-element.74) | copy-start | bytes 6148
  336.9 35.6 %collective-permute-start.1 = (bf16[9,512]{1,0:T(8,128)(2,1)}, bf16[9,512]{1,0:T(8,128)(2,1)}, u32[]{:S(2)}, u32[]{:S(2)}) collective-permute-start(bf16[9,512]{1,0:T(8,128)(2,1)} %slice.177), channel_id=1, source_target_pairs={{0,1},{1,2},{2,3},{4,5},{5,6},{6,7},{8,9},{9,10},{10,11},{12,13},{... | collective-permute-start | bytes 27656
  409.2 39.4 %collective-permute-start.2 = (bf16[9,512]{1,0:T(8,128)(2,1)S(1)}, bf16[9,512]{1,0:T(8,128)(2,1)S(1)}, u32[]{:S(2)}, u32[]{:S(2)}) collective-permute-start(bf16[9,512]{1,0:T(8,128)(2,1)S(1)} %slice.178), channel_id=1, source_target_pairs={{0,1},{1,2},{2,3},{4,5},{5,6},{6,7},{8,9},{9,10},{10,11},{12,13},{... | collective-permute-start | bytes 27656
  411.9 60.6 %copy-start.128 = (pred[8,247]{1,0:T(8,128)(4,1)}, pred[8,247]{1,0:T(8,128)(4,1)S(1)}, u32[]{:S(2)}) copy-start(pred[8,247]{1,0:T(8,128)(4,1)S(1)} %broadcast_in_dim.68) | copy-start | bytes 5932
  570.9 26.1 %copy-start.19 = (f32[197,512]{1,0:T(8,128)S(1)}, f32[197,512]{1,0:T(8,128)}, u32[]{:S(2)}) copy-start(f32[197,512]{1,0:T(8,128)} %copy-done.18) | copy-start | bytes 1210372
  570.9 26.1 %copy-start.98 = (f32[1,1,512]{2,1,0:T(1,128)S(1)}, f32[1,1,512]{2,1,0:T(1,128)}, u32[]{:S(2)}) copy-start(f32[1,1,512]{2,1,0:T(1,128)} %get-tuple-element.71) | copy-start | bytes 6148
  570.9 26.1 %copy-start.106 = (bf16[2,512,8]{1,2,0:T(8,128)(2,1)S(1)}, bf16[2,512,8]{1,2,0:T(8,128)(2,1)}, u32[]{:S(2)}) copy-start(bf16[2,512,8]{1,2,0:T(8,128)(2,1)} %param.16) | copy-start | bytes 49156
  570.9 29.7 %copy-start.35 = (f32[197,512]{1,0:T(8,128)S(1)}, f32[197,512]{1,0:T(8,128)}, u32[]{:S(2)}) copy-start(f32[197,512]{1,0:T(8,128)} %param.21) | copy-start | bytes 1210372
  591.1 4.7 collective-permute-start.5
  592.4 4.2 collective-permute-start.4
  622.1 25.7 %copy-start.61 = (bf16[788,128]{0,1:T(8,128)(2,1)S(1)}, bf16[788,128]{0,1:T(8,128)(2,1)}, u32[]{:S(2)}) copy-start(bf16[788,128]{0,1:T(8,128)(2,1)} %copy-done.60) | copy-start | bytes 605188
  624.3 25.9 %copy-start.22 = (f32[197,512]{1,0:T(8,128)S(1)}, f32[197,512]{1,0:T(8,128)}, u32[]{:S(2)}) copy-start(f32[197,512]{1,0:T(8,128)} %copy-done.20) | copy-start | bytes 1210372
  624.3 25.9 %copy-start.101 = (f32[1,1,512]{2,1,0:T(1,128)S(1)}, f32[1,1,512]{2,1,0:T(1,128)}, u32[]{:S(2)}) copy-start(f32[1,1,512]{2,1,0:T(1,128)} %get-tuple-element.74) | copy-start | bytes 6148
  624.3 25.9 %copy-start.103 = (f32[197]{0:T(256)S(1)}, f32[197]{0:T(256)}, u32[]{:S(2)}) copy-start(f32[197]{0:T(256)} %copy-done.102) | copy-start | bytes 2368
  625.9 26.1 %copy-start.39 = (f32[197,512]{1,0:T(8,128)S(1)}, f32[197,512]{1,0:T(8,128)}, u32[]{:S(2)}) copy-start(f32[197,512]{1,0:T(8,128)} %copy-done.38) | copy-start | bytes 1210372
  646.6 2.5 collective-permute-start.6
  649.0 239.3 %reduce-scatter.33.cloned.1.call-start = ((), (), s32[]{:S(2)}) async-start(), calls=%async_computation.10 | async-start | bytes 294912 | tf_op jit(solution)/shard_map/reduce_scatter | solution.py:286
  652.8 86.9 %copy-start.36 = (f32[197,512]{1,0:T(8,128)}, f32[197,512]{1,0:T(8,128)S(1)}, u32[]{:S(2)}) copy-start(f32[197,512]{1,0:T(8,128)S(1)} %get-tuple-element.40) | copy-start | bytes 1210372
  711.9 25.6 %copy-start.1 = (f32[788,8]{0,1:T(8,128)S(1)}, f32[788,8]{0,1:T(8,128)}, u32[]{:S(2)}) copy-start(f32[788,8]{0,1:T(8,128)} %copy-done) | copy-start | bytes 75652
  711.9 26.2 %copy-start.17 = (bf16[197,512]{1,0:T(8,128)(2,1)S(1)}, bf16[197,512]{1,0:T(8,128)(2,1)}, u32[]{:S(2)}) copy-start(bf16[197,512]{1,0:T(8,128)(2,1)} %param.12) | copy-start | bytes 605188
  711.9 26.2 %copy-start.31 = (bf16[209,512]{1,0:T(8,128)(2,1)S(1)}, bf16[209,512]{1,0:T(8,128)(2,1)}, u32[]{:S(2)}) copy-start(bf16[209,512]{1,0:T(8,128)(2,1)} %copy-done.30) | copy-start | bytes 642052
  711.9 26.2 %copy-start.107 = (bf16[2,512,8]{1,2,0:T(8,128)(2,1)S(1)}, bf16[2,512,8]{1,2,0:T(8,128)(2,1)}, u32[]{:S(2)}) copy-start(bf16[2,512,8]{1,2,0:T(8,128)(2,1)} %param.16) | copy-start | bytes 49156
  711.9 26.2 %copy-start.123 = (f32[1,1,512]{2,1,0:T(1,128)S(1)}, f32[1,1,512]{2,1,0:T(1,128)}, u32[]{:S(2)}) copy-start(f32[1,1,512]{2,1,0:T(1,128)} %get-tuple-element.72) | copy-start | bytes 6148
  711.9 26.2 %copy-start.135 = (f32[197]{0:T(256)S(1)}, f32[197]{0:T(256)}, u32[]{:S(2)}) copy-start(f32[197]{0:T(256)} %copy-done.134) | copy-start | bytes 2368
  711.9 26.2 %copy-start.146 = (f32[197]{0:T(256)S(1)}, f32[197]{0:T(256)}, u32[]{:S(2)}) copy-start(f32[197]{0:T(256)} %copy-done.145) | copy-start | bytes 2368
  712.0 27.3 %copy-start.140 = (f32[197]{0:T(256)S(1)}, f32[197]{0:T(256)}, u32[]{:S(2)}) copy-start(f32[197]{0:T(256)} %copy-done.139) | copy-start | bytes 2368
  731.6 5.3 collective-permute-start.8
  732.9 4.8 collective-permute-start.7
  754.0 135.8 %reduce-scatter.31.cloned.1.call-start = ((), (), s32[]{:S(2)}) async-start(), calls=%async_computation.9 | async-start | bytes 884736 | tf_op jit(solution)/shard_map/reduce_scatter | solution.py:285
  757.0 190.3 %reduce-scatter.29.cloned.1.call-start = ((), (), s32[]{:S(2)}) async-start(), calls=%async_computation.8 | async-start | bytes 884736 | tf_op jit(solution)/shard_map/reduce_scatter | solution.py:285
  780.5 318.5 %reduce-scatter.39.cloned.1.call-start = ((), (), s32[]{:S(2)}) async-start(), calls=%async_computation.13 | async-start | bytes 9437184 | tf_op jit(solution)/shard_map/reduce_scatter | solution.py:287
  787.6 463.4 %reduce-scatter.37.cloned.1.call-start = ((), (), s32[]{:S(2)}) async-start(), calls=%async_computation.12 | async-start | bytes 9437184 | tf_op jit(solution)/shard_map/reduce_scatter | solution.py:287
  795.3 607.4 %reduce-scatter.43.cloned.1.call-start = ((), (), s32[]{:S(2)}) async-start(), calls=%async_computation.15 | async-start | bytes 9437184 | tf_op jit(solution)/shard_map/reduce_scatter | solution.py:288
  805.0 749.7 %reduce-scatter.41.cloned.1.call-start = ((), (), s32[]{:S(2)}) async-start(), calls=%async_computation.14 | async-start | bytes 9437184 | tf_op jit(solution)/shard_map/reduce_scatter | solution.py:288
  815.2 26.8 %copy-start.96 = (f32[1,1,512]{2,1,0:T(1,128)S(1)}, f32[1,1,512]{2,1,0:T(1,128)}, u32[]{:S(2)}) copy-start(f32[1,1,512]{2,1,0:T(1,128)} %copy-done.95) | copy-start | bytes 6148
  815.2 26.8 %copy-start.109 = (f32[197]{0:T(256)S(1)}, f32[197]{0:T(256)}, u32[]{:S(2)}) copy-start(f32[197]{0:T(256)} %copy-done.108) | copy-start | bytes 2368
  815.3 71.5 %copy-start.37 = (f32[197,512]{1,0:T(8,128)S(1)}, f32[197,512]{1,0:T(8,128)}, u32[]{:S(2)}) copy-start(f32[197,512]{1,0:T(8,128)} %copy-done.36) | copy-start | bytes 1210372
  815.6 27.4 %copy-start.133 = (f32[197]{0:T(256)S(1)}, f32[197]{0:T(256)}, u32[]{:S(2)}) copy-start(f32[197]{0:T(256)} %copy-done.132) | copy-start | bytes 2368
  835.8 4.4 collective-permute-start.3
  837.1 3.9 collective-permute-start.9
  (115 other events, 882.7 us)
Sparse Core Ops, SparseCore 0:
  10.2 80.7 all-gather.22
  93.1 71.8 all-gather.20
  167.2 74.3 all-gather.26
  243.6 72.3 all-gather.24
  649.2 62.3 reduce-scatter.34
  754.1 61.7 reduce-scatter.32
  819.2 62.2 reduce-scatter.30
  885.2 62.0 reduce-scatter.28
  950.9 148.0 reduce-scatter.38
  1102.9 147.9 reduce-scatter.36
  1254.6 148.0 reduce-scatter.42
  1406.6 148.0 reduce-scatter.40
where the time goes:
time: 1580 us; the launch traced here: 1570 us
  waiting for transfers between devices  661 us (42%)
  blocking collectives  348 us (22%)
  local copies, waits for them, and re-layouts  342 us (22%)
  matrix products  104 us (7%)
  other arithmetic  69.9 us (4%)
  starting transfers between devices  21.5 us (1%)
  between operations  19 us (1%)
    reduce_scatter x2, waiting for transfers between devices, per_device(): lax.psum_scatter(in_list[layer_idx], 'dp', scatter_dimension=1, tiled=True)  302 us
    reduce_scatter x2, waiting for transfers between devices, per_device(): lax.psum_scatter(out_list[layer_idx], 'dp', scatter_dimension=2, tiled=True)  301 us
    unnamed x7, blocking collectives  98.3 us
    all_gather x2, blocking collectives, per_device(): lax.all_gather(shards[0], 'dp', axis=0, tiled=True)  66.6 us
    all_gather x2, blocking collectives, per_device(): lax.all_gather(shards[1], 'dp', axis=1, tiled=True)  63.6 us
    reduce_scatter x2, waiting for transfers between devices, per_device(): lax.psum_scatter(qkv_list[layer_idx], 'dp', scatter_dimension=0, tiled=True)  57.5 us
    psum x1, blocking collectives, per_device(): lax.psum((jnp.stack(gain_list), jnp.stack(router_list)), ('dp', 'tensor'))  42.1 us
    unnamed x359, local copies, waits for them, and re-layouts  41.8 us
  transfers between devices with their start and end apart: 22, of which 8 were waited for; matrix products, arithmetic and copies ran while one was open for 28% of the time, Pallas kernels for 0%

commit v1 on v0

v1 whole, which is shorter than its diff:
```python
import jax
import jax.numpy as jnp
from jax import lax
from jax.sharding import PartitionSpec as P

HD = 64
LEN = 197
LAYERS = 2
CAP = 247
SLOTS = 256
ROWS = 200
NORM_EPS = 1e-06
f32 = jnp.float32
bf16 = jnp.bfloat16
AXES = ("dp", "tensor")


def layer_norm(hidden, gain_row):
    average = jnp.mean(hidden, axis=-1, keepdims=True)
    centered = hidden - average
    variance = jnp.mean(centered * centered, axis=-1, keepdims=True)
    return centered * lax.rsqrt(variance + NORM_EPS) * gain_row


def norm_back(hidden_rows, gain_row, grad_rows):
    unused, pullback = jax.vjp(layer_norm, hidden_rows, gain_row)
    return pullback(grad_rows)


def gelu_tanh(values):
    return jax.nn.gelu(values, approximate=True)


def gelu_back(pre_act, act_grad):
    unused, pullback = jax.vjp(gelu_tanh, pre_act)
    return pullback(act_grad)[0]


def mm(spec, *args):
    return jnp.einsum(spec, *args, preferred_element_type=f32)


class Place:
    def __init__(self):
        self.dp_size = lax.axis_size("dp")
        self.tensor_size = lax.axis_size("tensor")
        self.count = self.dp_size * self.tensor_size
        self.dp = lax.axis_index("dp")
        self.tensor = lax.axis_index("tensor")
        self.near = (self.dp >> 1) & 1
        self.expert = self.near * self.tensor_size + self.tensor

    def swap(self, value, mask):
        pairs = [(i, i ^ mask) for i in range(self.count)]
        return lax.ppermute(value, AXES, pairs)

    def block(self, mask):
        low = mask & (self.tensor_size - 1)
        return low | ((mask // self.tensor_size) * 2 * self.tensor_size)

    def dp_groups(self):
        return [[d for d in range(self.dp_size) if (d >> 1) & 1 == b] for b in (0, 1)]

    def ordered(self, mine, theirs, bit):
        return jnp.stack([jnp.where(bit, theirs, mine), jnp.where(bit, mine, theirs)])


def gather_attention(place, shard):
    rows, width = shard.shape
    bits = place.dp_size.bit_length() - 1
    held = shard
    for bit in reversed(range(bits)):
        other = place.swap(held, place.tensor_size << bit)
        held = place.ordered(held, other, (place.dp >> bit) & 1)
    held = held.reshape((2,) * bits + (rows, width))
    held = jnp.transpose(held, tuple(reversed(range(bits))) + (bits, bits + 1))
    held = held.reshape(1, place.dp_size * rows, width)
    for mask in (2, 1):
        held = jnp.stack([held, place.swap(held, mask)], axis=1 if mask == 1 else 0)
        held = held.reshape((-1,) + held.shape[2:])
    return held


def scatter_attention(place, blocks, rows):
    bits = place.dp_size.bit_length() - 1
    held = blocks.reshape((2, 2) + blocks.shape[1:])
    held = held[:, 0] + place.swap(held[:, 1], 1)
    held = held[0] + place.swap(held[1], 2)
    for bit in range(bits):
        half = held.reshape((-1, 2, rows << bit) + held.shape[1:]) if False else None
        parts = held.reshape((-1, 2, rows, held.shape[-1]))
        mine = lax.dynamic_index_in_dim(parts, (place.dp >> bit) & 1, 1, keepdims=False)
        theirs = lax.dynamic_index_in_dim(parts, 1 - ((place.dp >> bit) & 1), 1, keepdims=False)
        held = mine + place.swap(theirs, place.tensor_size << bit)
        held = held.reshape(-1, held.shape[-1])
    return held


def plane_exchange(place, blocks):
    even, odd = blocks[0::2], blocks[1::2]
    pair = jnp.stack([even, place.swap(odd, 1)], axis=1)
    got = [pair[0]] + [place.swap(pair[k], place.block(2 * k)) for k in (1, 2, 3)]
    return jnp.concatenate(got, axis=0)


def gather_experts(place, w_in, w_out):
    blocks = jnp.stack([w_in, jnp.swapaxes(w_out, 1, 2)], axis=1)
    experts, unused, rows, width = blocks.shape
    order = place.expert ^ jnp.arange(experts)
    got = plane_exchange(place, blocks[order])
    got = got.reshape((2, place.tensor_size, 2, rows, width))
    got = place.ordered(got[0], got[1], place.near)
    full = lax.all_gather(got, "dp", axis=0, tiled=False, axis_index_groups=place.dp_groups())
    full = full.reshape((-1, 2, 2, place.tensor_size, 2, rows, width))
    full = jnp.transpose(full, (4, 3, 0, 2, 1, 5, 6))
    full = full.reshape((2, place.tensor_size, -1, width))
    return full[0], full[1]


def scatter_experts(place, grad_in, grad_out):
    tensor, model, width = grad_in.shape
    rows = model // place.dp_size
    both = jnp.stack([grad_in, grad_out]).astype(bf16)
    both = both.reshape((2, tensor, -1, 2, 2, rows, width))
    both = jnp.transpose(both, (2, 4, 3, 1, 0, 5, 6))
    both = both.reshape((-1, 2, tensor, 2, rows, width))
    mine = lax.psum_scatter(
        both, "dp", scatter_dimension=0, tiled=False, axis_index_groups=place.dp_groups()
    )
    mine = place.ordered(mine[0], mine[1], place.near)
    got = plane_exchange(place, mine.reshape((-1, 2, rows, width)))
    order = place.expert ^ jnp.arange(got.shape[0])
    got = got[order].astype(f32)
    return got[:, 0], jnp.swapaxes(got[:, 1], 1, 2)


def slot_tables(place, ids, ranking, experts):
    expert_range = jnp.arange(experts, dtype=jnp.int32)[:, None]
    first = (ids[:, 0][None, :] == expert_range)
    second = (ids[:, 1][None, :] == expert_range)
    both = jnp.concatenate([first, second]).astype(bf16)
    earlier = (ranking[:, None] < ranking[None, :]).astype(bf16)
    counts = mm("et,ts->es", both, earlier)
    total = jnp.sum(first.astype(f32), axis=1, keepdims=True)
    slot = jnp.where(first, counts[:experts], jnp.where(second, total + counts[experts:], -1.0))
    slot = jnp.where(slot < CAP, slot, -1.0).astype(jnp.int32)
    mine = lax.dynamic_index_in_dim(slot, place.expert, 0, keepdims=False)
    theirs = lax.dynamic_index_in_dim(slot, place.expert ^ place.tensor_size, 0, keepdims=False)
    both_groups = jnp.stack([mine, place.swap(theirs, 2 * place.tensor_size)])
    both_groups = both_groups.reshape((2, place.tensor_size, LEN))
    both_groups = both_groups[:, place.tensor ^ jnp.arange(place.tensor_size)]
    both_groups = jnp.pad(both_groups, ((0, 0), (0, 0), (0, ROWS - LEN)), constant_values=-1)
    return both_groups.reshape(2, -1)


def onehot_slots(table):
    return (table[:, None, :] == jnp.arange(SLOTS, dtype=jnp.int32)[None, :, None]).astype(bf16)


def dispatch(place, rows_own, hot):
    own = jnp.pad(rows_own, ((0, ROWS - LEN), (0, 0)))
    even = jnp.stack([own] + [place.swap(own, place.block(2 * k)) for k in (1, 2, 3)])
    odd = place.swap(even, 1)
    images = jnp.stack([even, odd], axis=1).reshape(2, -1, own.shape[1])
    picked = mm("gst,gtd->gsd", hot, images).astype(bf16)
    return picked.reshape(-1, own.shape[1])


def combine(place, slot_rows, hot):
    width = slot_rows.shape[1]
    part = mm("gst,gsd->gtd", hot, slot_rows.reshape(2, SLOTS, width)).astype(bf16)
    part = part.reshape(4, 2, ROWS, width)
    both = part[:, 0] + place.swap(part[:, 1], 1)
    got = [both[0]] + [place.swap(both[k], place.block(2 * k)) for k in (1, 2, 3)]
    total = sum(g.astype(f32) for g in got)
    return total[:LEN]


def per_device(
    inputs,
    norm_gains,
    qkv_weight,
    out_weight,
    router_weight,
    expert_in,
    expert_out,
    routes,
    priority,
    cotangent,
):
    place = Place()
    experts = expert_in.shape[1]
    rows = qkv_weight.shape[1]
    scale = HD ** (-0.5)
    hidden = inputs.astype(f32)
    hots = [onehot_slots(slot_tables(place, routes[l], priority[l, 0], experts)) for l in range(LAYERS)]
    attn_w = []
    expert_w = []
    for l in range(LAYERS):
        shard = jnp.concatenate([qkv_weight[l], jnp.swapaxes(out_weight[l], 0, 1)[:, None]], axis=1)
        full = gather_attention(place, shard.reshape(rows, -1))
        attn_w.append(full.reshape(full.shape[0], full.shape[1], 4, -1))
        expert_w.append(gather_experts(place, expert_in[l], expert_out[l]))
    saved = []
    is_mine = (jnp.arange(experts) == place.expert)[None, :]
    for l in range(LAYERS):
        weights = attn_w[l]
        hidden_in = hidden
        normed_a = layer_norm(hidden, norm_gains[l, 0]).astype(bf16)
        qkv = mm("td,jdpc->jptc", normed_a, weights[:, :, :3]).astype(bf16)
        qkv = qkv.reshape(qkv.shape[:3] + (-1, HD))
        queries, key_rows, values = qkv[:, 0], qkv[:, 1], qkv[:, 2]
        scores = mm("jqhd,jkhd->jhqk", queries, key_rows) * scale
        log_total = jax.nn.logsumexp(scores, axis=-1, keepdims=True)
        attn_probs = jnp.exp(scores - log_total)
        context = mm("jhqk,jkhd->jqhd", attn_probs.astype(bf16), values).astype(bf16)
        context = context.reshape(context.shape[:2] + (-1,))
        hidden = hidden + mm("jtc,jdc->td", context, weights[:, :, 3])
        hidden_mid = hidden
        normed_own = layer_norm(hidden, norm_gains[l, 1]).astype(bf16)
        sent = dispatch(place, normed_own, hots[l])
        logits = mm("sd,de->se", sent, router_weight[l])
        probs = jnp.exp(logits - jax.nn.logsumexp(logits, axis=-1, keepdims=True))
        gate = jnp.sum(jnp.where(is_mine, probs, 0.0), axis=1, keepdims=True)
        w_in, w_out = expert_w[l]
        pre_act = mm("sd,jdf->jsf", sent, w_in)
        activated = gelu_tanh(pre_act).astype(bf16)
        expert_y = mm("jsf,jdf->sd", activated, w_out)
        hidden = hidden + combine(place, (gate * expert_y).astype(bf16), hots[l])
        saved.append(
            (hidden_in, normed_a, queries, key_rows, values, log_total, context, hidden_mid,
             sent, probs, gate, pre_act, activated, expert_y)
        )
    grad_hidden = cotangent
    gain_list = [None] * LAYERS
    router_list = [None] * LAYERS
    attn_list = [None] * LAYERS
    in_list = [None] * LAYERS
    out_list = [None] * LAYERS
    for l in reversed(range(LAYERS)):
        (hidden_in, normed_a, queries, key_rows, values, log_total, context, hidden_mid,
         sent, probs, gate, pre_act, activated, expert_y) = saved[l]
        weights = attn_w[l]
        w_in, w_out = expert_w[l]
        branch = dispatch(place, grad_hidden.astype(bf16), hots[l]).astype(f32)
        gate_grad = jnp.sum(branch * expert_y, axis=1, keepdims=True)
        slot_grad = (gate * branch).astype(bf16)
        grad_out = mm("sd,jsf->jdf", slot_grad, activated)
        act_grad = mm("sd,jdf->jsf", slot_grad, w_out)
        pre_grad = gelu_back(pre_act, act_grad).astype(bf16)
        grad_in = mm("sd,jsf->jdf", sent, pre_grad)
        back = mm("jsf,jdf->sd", pre_grad, w_in)
        logit_grad = gate_grad * gate * (is_mine.astype(f32) - probs)
        router_list[l] = lax.dot_general(
            sent.astype(f32), logit_grad, (((0,), (0,)), ((), ())), precision=lax.Precision.HIGHEST
        )
        back = back + lax.dot_general(
            logit_grad, router_weight[l].astype(f32), (((1,), (1,)), ((), ())),
            precision=lax.Precision.HIGHEST,
        )
        normed_grad = combine(place, back.astype(bf16), hots[l])
        in_list[l], out_list[l] = scatter_experts(place, grad_in, grad_out)
        hidden_part, gain_expert = norm_back(hidden_mid, norm_gains[l, 1], normed_grad)
        grad_hidden = grad_hidden + hidden_part
        attn_grad = grad_hidden.astype(bf16)
        proj_grad = mm("td,jtc->jdc", attn_grad, context)
        context_grad = mm("td,jdc->jtc", attn_grad, weights[:, :, 3]).astype(bf16)
        context_grad = context_grad.reshape(queries.shape)
        scores = mm("jqhd,jkhd->jhqk", queries, key_rows) * scale
        attn_probs = jnp.exp(scores - log_total)
        value_grad = mm("jhqk,jqhd->jkhd", attn_probs.astype(bf16), context_grad).astype(bf16)
        probs_grad = mm("jqhd,jkhd->jhqk", context_grad, values)
        score_grad = (
            attn_probs * (probs_grad - jnp.sum(attn_probs * probs_grad, axis=-1, keepdims=True))
        ).astype(bf16)
        query_grad = (mm("jhqk,jkhd->jqhd", score_grad, key_rows) * scale).astype(bf16)
        key_grad = (mm("jhqk,jqhd->jkhd", score_grad, queries) * scale).astype(bf16)
        mixed = jnp.stack([query_grad, key_grad, value_grad], axis=1)
        mixed = mixed.reshape(mixed.shape[:3] + (-1,))
        qkv_grad = mm("td,jptc->jdpc", normed_a, mixed)
        normed_grad = mm("jptc,jdpc->td", mixed, weights[:, :, :3])
        both = jnp.concatenate([qkv_grad, proj_grad[:, :, None]], axis=2).astype(bf16)
        both = both.reshape(both.shape[0], both.shape[1], -1)
        attn_list[l] = scatter_attention(place, both, rows).astype(f32).reshape(rows, 4, -1)
        hidden_part, gain_attn = norm_back(hidden_in, norm_gains[l, 0], normed_grad)
        grad_hidden = grad_hidden + hidden_part
        gain_list[l] = jnp.stack([gain_attn, gain_expert])
    gains, router = jnp.stack(gain_list), jnp.stack(router_list)
    small = jnp.concatenate([gains.reshape(-1), router.reshape(-1)]).reshape(-1, 512)
    for bit in range(place.count.bit_length() - 1):
        small = small + place.swap(small, 1 << bit)
    small = small.reshape(-1)
    gains, router = small[: gains.size].reshape(gains.shape), small[gains.size :].reshape(router.shape)
    return (
        hidden.astype(bf16),
        grad_hidden,
        gains,
        jnp.stack([a[:, :3] for a in attn_list]),
        jnp.stack([jnp.swapaxes(a[:, 3], 0, 1) for a in attn_list]),
        router,
        jnp.stack(in_list),
        jnp.stack(out_list),
    )


def solution(mesh):
    in_specs = (
        P(("dp", "tensor"), None),
        P(),
        P(None, "dp", None, "tensor"),
        P(None, "tensor", "dp"),
        P(),
        P(None, None, "dp", "tensor"),
        P(None, None, "tensor", "dp"),
        P(None, "dp", None),
        P(None, "dp", None),
        P(("dp", "tensor"), None),
    )
    out_specs = (
        P(("dp", "tensor"), None),
        P(("dp", "tensor"), None),
        P(),
        P(None, "dp", None, "tensor"),
        P(None, "tensor", "dp"),
        P(),
        P(None, None, "dp", "tensor"),
        P(None, None, "tensor", "dp"),
    )
    return jax.shard_map(
        per_device, mesh=mesh, in_specs=in_specs, out_specs=out_specs, check_vma=False
    )
```

time: 1580 us -> 525 us (0.33)
  waiting for transfers between devices: 661 us -> 210 us
  blocking collectives: 348 us -> 0 us
  local copies, waits for them, and re-layouts: 342 us -> 81.6 us
  starting transfers between devices: 21.5 us -> 79.5 us
  matrix products: 104 us -> 68.3 us
    reduce_scatter x8 -> x2, waiting for transfers between devices: 660 us -> 0.01 us  [scatter_experts(): lax.psum_scatter(both, 'dp', scatter_dimension=0, tiled=False, axis_index...]
    all_gather x12 -> x0, blocking collectives: 207 us -> none  [the longest x2 66.6 us: per_device(): lax.all_gather(shards[0], 'dp', axis=0, tiled=True)]
    gather x28 -> x6, local copies, waits for them, and re-layouts: 182 us -> 3.97 us  [the longest x2 1.47 us: scatter_experts(): got = got[order].astype(f32)]
    ppermute x0 -> x75, waiting for transfers between devices: none -> 173 us  [swap(): return lax.ppermute(value, AXES, pairs)]
    unnamed x7 -> x0, blocking collectives: 98.3 us -> none
    ppermute x0 -> x75, starting transfers between devices: none -> 78.9 us  [swap(): return lax.ppermute(value, AXES, pairs)]
    scatter x6 -> x0, local copies, waits for them, and re-layouts: 45.9 us -> none  [the longest x2 17.6 us: route_slots(): jnp.zeros((experts * capacity,), jnp.int32).at[target]]
    psum x1 -> x0, blocking collectives: 42.1 us -> none  [per_device(): lax.psum((jnp.stack(gain_list), jnp.stack(router_list)), ('dp', 'tensor'))]
  transfers between devices with their start and end apart: 22 -> 79, of which waited for: 8 -> 37; matrix products, arithmetic and copies ran while one was open for 28% -> 33% of each run, Pallas kernels for 0% -> 0%
where the time goes in v1:
time: 525 us; the launch traced here: 517 us
  waiting for transfers between devices  210 us (40%)
  local copies, waits for them, and re-layouts  81.6 us (16%)
  starting transfers between devices  79.5 us (15%)
  matrix products  68.3 us (13%)
  other arithmetic  60.6 us (12%)
  between operations  17 us (3%)
    ppermute x75, waiting for transfers between devices, swap(): return lax.ppermute(value, AXES, pairs)  173 us
    ppermute x75, starting transfers between devices, swap(): return lax.ppermute(value, AXES, pairs)  78.9 us
    dot_general x48, matrix products, mm(): return jnp.einsum(spec, *args, preferred_element_type=f32)  65.6 us
    all_gather x2, waiting for transfers between devices, gather_experts(): lax.all_gather(got, 'dp', axis=0, tiled=False, axis_index_groups=place.dp...  36.9 us
    unnamed x296, local copies, waits for them, and re-layouts  21.2 us
    another operation x8, other arithmetic, dispatch(): images = jnp.stack([even, odd], axis=1).reshape(2, -1, own.shape[1])  10.7 us
  transfers between devices with their start and end apart: 79, of which 37 were waited for; matrix products, arithmetic and copies ran while one was open for 33% of the time, Pallas kernels for 0%

profile of v1, /device:TPU:0, one launch (start us, length us, event | category | flops | bytes accessed | tf_op | source)
XLA Modules:
  0.0 517.0 jit_solution(12572239306221426409)
XLA Ops:
  8.9 4.1 collective-permute-start
  22.7 1.9 collective-permute-start.11
  25.0 2.8 collective-permute-start.12
  28.6 6.1 %collective-permute-done.1 = bf16[2,64,512]{2,1,0:T(8,128)(2,1)S(1)} collective-permute-done((bf16[2,64,512]{2,1,0:T(8,128)(2,1)S(1)}, bf16[2,64,512]{2,1,0:T(8,128)(2,1)S(1)}, u32[]{:S(2)}, u32[]{:S(2)}) %collective-permute-start.1) | collective-permute-done | bytes 131104 | tf_op jit(solution)/shard_map/ppermute | solution.py:55
  34.7 2.8 collective-permute-start.30
  38.2 3.5 collective-permute-done.12
  43.2 2.9 collective-permute-done.29
  46.0 6.2 %collective-permute-done.30 = bf16[2,2,64,512]{3,2,1,0:T(8,128)(2,1)S(1)} collective-permute-done((bf16[2,2,64,512]{3,2,1,0:T(8,128)(2,1)S(1)}, bf16[2,2,64,512]{3,2,1,0:T(8,128)(2,1)S(1)}, u32[]{:S(2)}, u32[]{:S(2)}) %collective-permute-start.30) | collective-permute-done | bytes 262176 | tf_op jit(solution)/shard_map/ppermute | solution.py:55
  58.3 9.7 %collective-permute-done.3 = bf16[1,512,512]{2,1,0:T(8,128)(2,1)S(1)} collective-permute-done((bf16[1,512,512]{2,1,0:T(8,128)(2,1)S(1)}, bf16[1,512,512]{2,1,0:T(8,128)(2,1)S(1)}, u32[]{:S(2)}, u32[]{:S(2)}) %collective-permute-start.3) | collective-permute-done | bytes 524320 | tf_op jit(solution)/shard_map/ppermute | solution.py:55
  72.9 2.8 copy.270
  83.9 2.0 collective-permute-start.8
  89.1 4.7 collective-permute-done.7
  93.8 6.2 %collective-permute-done.8 = bf16[200,512]{1,0:T(8,128)(2,1)S(1)} collective-permute-done((bf16[200,512]{1,0:T(8,128)(2,1)S(1)}, bf16[200,512]{1,0:T(8,128)(2,1)S(1)}, u32[]{:S(2)}, u32[]{:S(2)}) %collective-permute-start.8) | collective-permute-done | bytes 204832 | tf_op jit(solution)/shard_map/ppermute | solution.py:55
  105.4 2.1 pad_maximum_fusion.15
  111.2 31.1 %all-gather.5.cloned.1.call-done = bf16[8,4,2,64,512]{4,3,2,1,0:T(8,128)(2,1)} async-done(((bf16[2,4,2,64,512]{4,3,2,1,0:T(8,128)(2,1)}), bf16[8,4,2,64,512]{4,3,2,1,0:T(8,128)(2,1)}) %all-gather.5.cloned.1.call-update) | async-done | bytes 4194320 | tf_op jit(solution)/shard_map/all_gather | solution.py:113
  142.3 2.5 fusion.222
  147.6 2.7 multiply_convert_fusion.5
  153.1 1.9 collective-permute-start.38
  160.0 4.6 collective-permute-done.37
  166.1 8.2 %collective-permute-done.38 = bf16[200,512]{1,0:T(8,128)(2,1)S(1)} collective-permute-done((bf16[200,512]{1,0:T(8,128)(2,1)S(1)}, bf16[200,512]{1,0:T(8,128)(2,1)S(1)}, u32[]{:S(2)}, u32[]{:S(2)}) %collective-permute-start.38) | collective-permute-done | bytes 204832 | tf_op jit(solution)/shard_map/ppermute | solution.py:55
  175.7 2.6 pad_maximum_fusion.3
  178.3 4.4 copy.291
  185.3 2.1 fusion.49
  198.6 8.2 %collective-permute-done.25 = bf16[200,512]{1,0:T(8,128)(2,1)S(1)} collective-permute-done((bf16[200,512]{1,0:T(8,128)(2,1)S(1)}, bf16[200,512]{1,0:T(8,128)(2,1)S(1)}, u32[]{:S(2)}, u32[]{:S(2)}) %collective-permute-start.25) | collective-permute-done | bytes 204832 | tf_op jit(solution)/shard_map/ppermute | solution.py:55
  206.8 8.0 %collective-permute-done.26 = bf16[200,512]{1,0:T(8,128)(2,1)S(1)} collective-permute-done((bf16[200,512]{1,0:T(8,128)(2,1)S(1)}, bf16[200,512]{1,0:T(8,128)(2,1)S(1)}, u32[]{:S(2)}, u32[]{:S(2)}) %collective-permute-start.26) | collective-permute-done | bytes 204832 | tf_op jit(solution)/shard_map/ppermute | solution.py:55
  216.3 2.0 collective-permute-start.23
  218.3 2.2 collective-permute-done.23
  224.9 5.8 %all-gather.7.cloned.1.call-done = bf16[8,4,2,64,512]{4,3,2,1,0:T(8,128)(2,1)} async-done(((bf16[2,4,2,64,512]{4,3,2,1,0:T(8,128)(2,1)}), bf16[8,4,2,64,512]{4,3,2,1,0:T(8,128)(2,1)}) %all-gather.7.cloned.1.call-update) | async-done | bytes 4194320 | tf_op jit(solution)/shard_map/all_gather | solution.py:113
  230.7 2.5 fusion.221
  242.5 2.7 multiply_convert_fusion.3
  248.5 4.0 fusion.13
  263.2 2.6 copy.406
  267.8 2.9 collective-permute-start.42
  274.2 2.4 collective-permute-done.43
  276.7 7.7 %collective-permute-done.42 = bf16[200,512]{1,0:T(8,128)(2,1)S(1)} collective-permute-done((bf16[200,512]{1,0:T(8,128)(2,1)S(1)}, bf16[200,512]{1,0:T(8,128)(2,1)S(1)}, u32[]{:S(2)}, u32[]{:S(2)}) %collective-permute-start.42) | collective-permute-done | bytes 204832 | tf_op jit(solution)/shard_map/ppermute | solution.py:55
  285.3 2.0 collective-permute-done.33
  287.2 5.0 collective-permute-done.35
  292.3 8.8 %collective-permute-done.34 = bf16[200,512]{1,0:T(8,128)(2,1)S(1)} collective-permute-done((bf16[200,512]{1,0:T(8,128)(2,1)S(1)}, bf16[200,512]{1,0:T(8,128)(2,1)S(1)}, u32[]{:S(2)}, u32[]{:S(2)}) %collective-permute-start.34) | collective-permute-done | bytes 204832 | tf_op jit(solution)/shard_map/ppermute | solution.py:55
  302.9 2.1 fusion.66
  306.7 3.3 multiply_reduce_fusion.1
  312.9 2.7 multiply_convert_fusion.1
  320.0 2.6 multiply_reduce_fusion.3
  323.3 3.4 collective-permute-start.46
  328.0 3.2 collective-permute-done.45
  331.3 2.6 collective-permute-done.44
  338.9 2.3 copy.423
  341.3 2.3 copy.424
  349.2 3.8 fusion.6
  360.0 2.3 collective-permute-start.63
  363.7 2.5 copy.403
  367.1 7.6 %collective-permute-done.63 = bf16[512,512]{1,0:T(8,128)(2,1)} collective-permute-done((bf16[512,512]{1,0:T(8,128)(2,1)}, bf16[512,512]{1,0:T(8,128)(2,1)}, u32[]{:S(2)}, u32[]{:S(2)}) %collective-permute-start.63) | collective-permute-done | bytes 524320 | tf_op jit(solution)/shard_map/ppermute | solution.py:55
  378.9 2.7 collective-permute-start.51
  382.5 5.0 collective-permute-done.64
  391.4 8.8 %collective-permute-done.50 = bf16[200,512]{1,0:T(8,128)(2,1)S(1)} collective-permute-done((bf16[200,512]{1,0:T(8,128)(2,1)S(1)}, bf16[200,512]{1,0:T(8,128)(2,1)S(1)}, u32[]{:S(2)}, u32[]{:S(2)}) %collective-permute-start.50) | collective-permute-done | bytes 204832 | tf_op jit(solution)/shard_map/ppermute | solution.py:55
  401.0 2.3 fusion.67
  415.1 9.3 %collective-permute-start.66 = (bf16[1,64,512]{2,1,0:T(8,128)(2,1)}, bf16[1,64,512]{2,1,0:T(8,128)(2,1)}, u32[]{:S(2)}, u32[]{:S(2)}) collective-permute-start(bf16[1,64,512]{2,1,0:T(8,128)(2,1)} %constant_dynamic-slice_fusion), channel_id=1, source_target_pairs={{0,16},{1,17},{2,18},{3,19},{4,20},{5,21},{6,22},{7,23},{8,24},{9,... | collective-permute-start | bytes 196616 | tf_op jit(solution)/shard_map/ppermute | solution.py:55
  435.8 9.2 %collective-permute-done.53 = f32[20,512]{1,0:T(8,128)} collective-permute-done((f32[20,512]{1,0:T(8,128)S(1)}, f32[20,512]{1,0:T(8,128)}, u32[]{:S(2)}, u32[]{:S(2)}) %collective-permute-start.53) | collective-permute-done | bytes 40992 | tf_op jit(solution)/shard_map/ppermute | solution.py:55
  448.0 3.1 collective-permute-done.54
  451.2 11.5 %collective-permute-done.55 = f32[20,512]{1,0:T(8,128)S(1)} collective-permute-done((f32[20,512]{1,0:T(8,128)S(1)}, f32[20,512]{1,0:T(8,128)S(1)}, u32[]{:S(2)}, u32[]{:S(2)}) %collective-permute-start.55) | collective-permute-done | bytes 40992 | tf_op jit(solution)/shard_map/ppermute | solution.py:55
  465.6 2.3 collective-permute-done.56
  472.7 2.6 collective-permute-done.61
  482.7 6.0 %collective-permute-done.72 = bf16[2,2,64,512]{3,2,1,0:T(8,128)(2,1)S(1)} collective-permute-done((bf16[2,2,64,512]{3,2,1,0:T(8,128)(2,1)S(1)}, bf16[2,2,64,512]{3,2,1,0:T(8,128)(2,1)S(1)}, u32[]{:S(2)}, u32[]{:S(2)}) %collective-permute-start.72) | collective-permute-done | bytes 262176 | tf_op jit(solution)/shard_map/ppermute | solution.py:55
  495.9 6.6 %collective-permute-done.68 = bf16[2,2,64,512]{3,2,1,0:T(8,128)(2,1)S(1)} collective-permute-done((bf16[2,2,64,512]{3,2,1,0:T(8,128)(2,1)S(1)}, bf16[2,2,64,512]{3,2,1,0:T(8,128)(2,1)S(1)}, u32[]{:S(2)}, u32[]{:S(2)}) %collective-permute-start.68) | collective-permute-done | bytes 262176 | tf_op jit(solution)/shard_map/ppermute | solution.py:55
  502.5 2.0 collective-permute-done.69
  (679 shorter events, 203.3 us)
Async XLA Ops:
  7.2 135.1 %all-gather.5.cloned.1.call-start = ((), (), s32[]{:S(2)}) async-start(), calls=%async_computation.4 | async-start | bytes 5242880 | tf_op jit(solution)/shard_map/all_gather | solution.py:113
  8.9 15.8 %collective-permute-start = (bf16[64,512]{1,0:T(8,128)(2,1)S(1)}, bf16[64,512]{1,0:T(8,128)(2,1)S(1)}, u32[]{:S(2)}, u32[]{:S(2)}) collective-permute-start(bf16[64,512]{1,0:T(8,128)(2,1)S(1)} %copy_bitcast_fusion.1), channel_id=1, source_target_pairs={{0,16},{1,17},{2,18},{3,19},{4,20},{5,21},{6,22},{7,23},{8,24},{9,... | collective-permute-start | bytes 196616 | tf_op jit(solution)/shard_map/ppermute | solution.py:55
  13.0 11.7 %collective-permute-start.18 = (bf16[64,512]{1,0:T(8,128)(2,1)S(1)}, bf16[64,512]{1,0:T(8,128)(2,1)S(1)}, u32[]{:S(2)}, u32[]{:S(2)}) collective-permute-start(bf16[64,512]{1,0:T(8,128)(2,1)S(1)} %copy_bitcast_fusion), channel_id=1, source_target_pairs={{0,16},{1,17},{2,18},{3,19},{4,20},{5,21},{6,22},{7,23},{8,24},{9,... | collective-permute-start | bytes 196616 | tf_op jit(solution)/shard_map/ppermute | solution.py:55
  18.8 9.5 %collective-permute-start.28 = (bf16[4,2,64,512]{3,2,1,0:T(8,128)(2,1)}, bf16[4,2,64,512]{3,2,1,0:T(8,128)(2,1)S(1)}, u32[]{:S(2)}, u32[]{:S(2)}) collective-permute-start(bf16[4,2,64,512]{3,2,1,0:T(8,128)(2,1)} %get-tuple-element.98), channel_id=1, source_target_pairs={{0,1},{1,0},{2,3},{3,2},{4,5},{5,4},{6,7},{7,6},{8,9},{9,8},{10,11... | collective-permute-start | bytes 1572872 | tf_op jit(solution)/shard_map/ppermute | solution.py:55
  22.7 14.8 %collective-permute-start.11 = (bf16[2,2,64,512]{3,2,1,0:T(8,128)(2,1)S(1)}, bf16[2,2,64,512]{3,2,1,0:T(8,128)(2,1)S(1)}, u32[]{:S(2)}, u32[]{:S(2)}) collective-permute-start(bf16[2,2,64,512]{3,2,1,0:T(8,128)(2,1)S(1)} %get-tuple-element.105), channel_id=1, source_target_pairs={{0,8},{1,9},{2,10},{3,11},{4,12},{5,13},{6,14},{7,15},{8,0},{9,1},... | collective-permute-start | bytes 786440 | tf_op jit(solution)/shard_map/ppermute | solution.py:55
  24.8 10.0 %collective-permute-start.1 = (bf16[2,64,512]{2,1,0:T(8,128)(2,1)S(1)}, bf16[2,64,512]{2,1,0:T(8,128)(2,1)S(1)}, u32[]{:S(2)}, u32[]{:S(2)}) collective-permute-start(bf16[2,64,512]{2,1,0:T(8,128)(2,1)S(1)} %pad_maximum_fusion.41), channel_id=1, source_target_pairs={{0,8},{1,9},{2,10},{3,11},{4,12},{5,13},{6,14},{7,15},{8,0},{9,1},... | collective-permute-start | bytes 393224 | tf_op jit(solution)/shard_map/ppermute | solution.py:55
  25.0 16.7 %collective-permute-start.12 = (bf16[2,2,64,512]{3,2,1,0:T(8,128)(2,1)S(1)}, bf16[2,2,64,512]{3,2,1,0:T(8,128)(2,1)S(1)}, u32[]{:S(2)}, u32[]{:S(2)}) collective-permute-start(bf16[2,2,64,512]{3,2,1,0:T(8,128)(2,1)S(1)} %get-tuple-element.106), channel_id=1, source_target_pairs={{0,10},{1,11},{2,8},{3,9},{4,14},{5,15},{6,12},{7,13},{8,2},{9,3},... | collective-permute-start | bytes 786440 | tf_op jit(solution)/shard_map/ppermute | solution.py:55
  27.8 15.3 %collective-permute-start.13 = (bf16[2,2,64,512]{3,2,1,0:T(8,128)(2,1)S(1)}, bf16[2,2,64,512]{3,2,1,0:T(8,128)(2,1)S(1)}, u32[]{:S(2)}, u32[]{:S(2)}) collective-permute-start(bf16[2,2,64,512]{3,2,1,0:T(8,128)(2,1)S(1)} %get-tuple-element.107), channel_id=1, source_target_pairs={{0,2},{1,3},{2,0},{3,1},{4,6},{5,7},{6,4},{7,5},{8,10},{9,11},{10,... | collective-permute-start | bytes 786440 | tf_op jit(solution)/shard_map/ppermute | solution.py:55
  28.4 17.6 %collective-permute-start.29 = (bf16[2,2,64,512]{3,2,1,0:T(8,128)(2,1)S(1)}, bf16[2,2,64,512]{3,2,1,0:T(8,128)(2,1)S(1)}, u32[]{:S(2)}, u32[]{:S(2)}) collective-permute-start(bf16[2,2,64,512]{3,2,1,0:T(8,128)(2,1)S(1)} %get-tuple-element.93), channel_id=1, source_target_pairs={{0,8},{1,9},{2,10},{3,11},{4,12},{5,13},{6,14},{7,15},{8,0},{9,1},... | collective-permute-start | bytes 786440 | tf_op jit(solution)/shard_map/ppermute | solution.py:55
  34.7 17.5 %collective-permute-start.30 = (bf16[2,2,64,512]{3,2,1,0:T(8,128)(2,1)S(1)}, bf16[2,2,64,512]{3,2,1,0:T(8,128)(2,1)S(1)}, u32[]{:S(2)}, u32[]{:S(2)}) collective-permute-start(bf16[2,2,64,512]{3,2,1,0:T(8,128)(2,1)S(1)} %get-tuple-element.94), channel_id=1, source_target_pairs={{0,10},{1,11},{2,8},{3,9},{4,14},{5,15},{6,12},{7,13},{8,2},{9,3},... | collective-permute-start | bytes 786440 | tf_op jit(solution)/shard_map/ppermute | solution.py:55
  37.6 14.7 %collective-permute-start.31 = (bf16[2,2,64,512]{3,2,1,0:T(8,128)(2,1)S(1)}, bf16[2,2,64,512]{3,2,1,0:T(8,128)(2,1)S(1)}, u32[]{:S(2)}, u32[]{:S(2)}) collective-permute-start(bf16[2,2,64,512]{3,2,1,0:T(8,128)(2,1)S(1)} %get-tuple-element.95), channel_id=1, source_target_pairs={{0,2},{1,3},{2,0},{3,1},{4,6},{5,7},{6,4},{7,5},{8,10},{9,11},{10,... | collective-permute-start | bytes 786440 | tf_op jit(solution)/shard_map/ppermute | solution.py:55
  41.7 12.9 %collective-permute-start.2 = (bf16[2,2,64,512]{3,2,1,0:T(8,128)(2,1)S(1)}, bf16[2,2,64,512]{3,2,1,0:T(8,128)(2,1)S(1)}, u32[]{:S(2)}, u32[]{:S(2)}) collective-permute-start(bf16[2,2,64,512]{3,2,1,0:T(8,128)(2,1)S(1)} %pad_maximum_fusion.34), channel_id=1, source_target_pairs={{0,4},{1,5},{2,6},{3,7},{4,0},{5,1},{6,2},{7,3},{8,12},{9,13},{10,... | collective-permute-start | bytes 786440 | tf_op jit(solution)/shard_map/ppermute | solution.py:55
  54.5 176.2 %all-gather.7.cloned.1.call-start = ((), (), s32[]{:S(2)}) async-start(), calls=%async_computation.5 | async-start | bytes 5242880 | tf_op jit(solution)/shard_map/all_gather | solution.py:113
  54.8 13.2 %collective-permute-start.3 = (bf16[1,512,512]{2,1,0:T(8,128)(2,1)S(1)}, bf16[1,512,512]{2,1,0:T(8,128)(2,1)S(1)}, u32[]{:S(2)}, u32[]{:S(2)}) collective-permute-start(bf16[1,512,512]{2,1,0:T(8,128)(2,1)S(1)} %bitcast.766), channel_id=1, source_target_pairs={{0,2},{1,3},{2,0},{3,1},{4,6},{5,7},{6,4},{7,5},{8,10},{9,11},{10,... | collective-permute-start | bytes 1572872 | tf_op jit(solution)/shard_map/ppermute | solution.py:55
  56.8 45.4 %collective-permute-start.5 = (s32[788]{0:T(1024)}, s32[788]{0:T(1024)}, u32[]{:S(2)}, u32[]{:S(2)}) collective-permute-start(s32[788]{0:T(1024)} %get-tuple-element.43), channel_id=1, source_target_pairs={{0,8},{1,9},{2,10},{3,11},{4,12},{5,13},{6,14},{7,15},{8,0},{9,1},... | collective-permute-start | bytes 9464 | tf_op jit(solution)/shard_map/ppermute | solution.py:55
  69.7 16.2 %collective-permute-start.19 = (bf16[2,64,512]{2,1,0:T(8,128)(2,1)S(1)}, bf16[2,64,512]{2,1,0:T(8,128)(2,1)}, u32[]{:S(2)}, u32[]{:S(2)}) collective-permute-start(bf16[2,64,512]{2,1,0:T(8,128)(2,1)S(1)} %pad_maximum_fusion.42), channel_id=1, source_target_pairs={{0,8},{1,9},{2,10},{3,11},{4,12},{5,13},{6,14},{7,15},{8,0},{9,1},... | collective-permute-start | bytes 393224 | tf_op jit(solution)/shard_map/ppermute | solution.py:55
  82.3 11.4 %collective-permute-start.7 = (bf16[200,512]{1,0:T(8,128)(2,1)S(1)}, bf16[200,512]{1,0:T(8,128)(2,1)S(1)}, u32[]{:S(2)}, u32[]{:S(2)}) collective-permute-start(bf16[200,512]{1,0:T(8,128)(2,1)S(1)} %get-tuple-element.151), channel_id=1, source_target_pairs={{0,8},{1,9},{2,10},{3,11},{4,12},{5,13},{6,14},{7,15},{8,0},{9,1},... | collective-permute-start | bytes 614408 | tf_op jit(solution)/shard_map/ppermute | solution.py:55
  83.5 10.3 %collective-permute-start.6 = (bf16[200,512]{1,0:T(8,128)(2,1)S(1)}, bf16[200,512]{1,0:T(8,128)(2,1)S(1)}, u32[]{:S(2)}, u32[]{:S(2)}) collective-permute-start(bf16[200,512]{1,0:T(8,128)(2,1)S(1)} %get-tuple-element.151), channel_id=1, source_target_pairs={{0,2},{1,3},{2,0},{3,1},{4,6},{5,7},{6,4},{7,5},{8,10},{9,11},{10,... | collective-permute-start | bytes 614408 | tf_op jit(solution)/shard_map/ppermute | solution.py:55
  83.9 16.1 %collective-permute-start.8 = (bf16[200,512]{1,0:T(8,128)(2,1)S(1)}, bf16[200,512]{1,0:T(8,128)(2,1)S(1)}, u32[]{:S(2)}, u32[]{:S(2)}) collective-permute-start(bf16[200,512]{1,0:T(8,128)(2,1)S(1)} %get-tuple-element.151), channel_id=1, source_target_pairs={{0,10},{1,11},{2,8},{3,9},{4,14},{5,15},{6,12},{7,13},{8,2},{9,3},... | collective-permute-start | bytes 614408 | tf_op jit(solution)/shard_map/ppermute | solution.py:55
  87.6 16.1 %collective-permute-start.20 = (bf16[2,2,64,512]{3,2,1,0:T(8,128)(2,1)}, bf16[2,2,64,512]{3,2,1,0:T(8,128)(2,1)}, u32[]{:S(2)}, u32[]{:S(2)}) collective-permute-start(bf16[2,2,64,512]{3,2,1,0:T(8,128)(2,1)} %pad_maximum_fusion.35), channel_id=1, source_target_pairs={{0,4},{1,5},{2,6},{3,7},{4,0},{5,1},{6,2},{7,3},{8,12},{9,13},{10,... | collective-permute-start | bytes 786440 | tf_op jit(solution)/shard_map/ppermute | solution.py:55
  104.7 50.3 %collective-permute-start.21 = (bf16[1,512,512]{2,1,0:T(8,128)(2,1)S(1)}, bf16[1,512,512]{2,1,0:T(8,128)(2,1)}, u32[]{:S(2)}, u32[]{:S(2)}) collective-permute-start(bf16[1,512,512]{2,1,0:T(8,128)(2,1)S(1)} %bitcast.763), channel_id=1, source_target_pairs={{0,2},{1,3},{2,0},{3,1},{4,6},{5,7},{6,4},{7,5},{8,10},{9,11},{10,... | collective-permute-start | bytes 1572872 | tf_op jit(solution)/shard_map/ppermute | solution.py:55
  107.5 363.6 %reduce-scatter.5.cloned.1.call-start = ((), (), s32[]{:S(2)}) async-start(), calls=%async_computation.3 | async-start | bytes 5242880 | tf_op jit(solution)/shard_map/reduce_scatter | solution.py:127
  151.4 13.2 %collective-permute-start.37 = (bf16[200,512]{1,0:T(8,128)(2,1)S(1)}, bf16[200,512]{1,0:T(8,128)(2,1)S(1)}, u32[]{:S(2)}, u32[]{:S(2)}) collective-permute-start(bf16[200,512]{1,0:T(8,128)(2,1)S(1)} %get-tuple-element.147), channel_id=1, source_target_pairs={{0,8},{1,9},{2,10},{3,11},{4,12},{5,13},{6,14},{7,15},{8,0},{9,1},... | collective-permute-start | bytes 614408 | tf_op jit(solution)/shard_map/ppermute | solution.py:55
  151.5 13.2 %collective-permute-start.36 = (bf16[200,512]{1,0:T(8,128)(2,1)S(1)}, bf16[200,512]{1,0:T(8,128)(2,1)S(1)}, u32[]{:S(2)}, u32[]{:S(2)}) collective-permute-start(bf16[200,512]{1,0:T(8,128)(2,1)S(1)} %get-tuple-element.147), channel_id=1, source_target_pairs={{0,2},{1,3},{2,0},{3,1},{4,6},{5,7},{6,4},{7,5},{8,10},{9,11},{10,... | collective-permute-start | bytes 614408 | tf_op jit(solution)/shard_map/ppermute | solution.py:55
  153.1 21.3 %collective-permute-start.38 = (bf16[200,512]{1,0:T(8,128)(2,1)S(1)}, bf16[200,512]{1,0:T(8,128)(2,1)S(1)}, u32[]{:S(2)}, u32[]{:S(2)}) collective-permute-start(bf16[200,512]{1,0:T(8,128)(2,1)S(1)} %get-tuple-element.147), channel_id=1, source_target_pairs={{0,10},{1,11},{2,8},{3,9},{4,14},{5,15},{6,12},{7,13},{8,2},{9,3},... | collective-permute-start | bytes 614408 | tf_op jit(solution)/shard_map/ppermute | solution.py:55
  156.1 19.6 %collective-permute-start.22 = (bf16[2,512,512]{2,1,0:T(8,128)(2,1)S(1)}, bf16[2,512,512]{2,1,0:T(8,128)(2,1)S(1)}, u32[]{:S(2)}, u32[]{:S(2)}) collective-permute-start(bf16[2,512,512]{2,1,0:T(8,128)(2,1)S(1)} %maximum_bitcast_fusion.1), channel_id=1, source_target_pairs={{0,1},{1,0},{2,3},{3,2},{4,5},{5,4},{6,7},{7,6},{8,9},{9,8},{10,11... | collective-permute-start | bytes 3145736 | tf_op jit(solution)/shard_map/ppermute | solution.py:55
  159.0 23.6 %collective-permute-start.17 = (bf16[200,512]{1,0:T(8,128)(2,1)}, bf16[200,512]{1,0:T(8,128)(2,1)}, u32[]{:S(2)}, u32[]{:S(2)}) collective-permute-start(bf16[200,512]{1,0:T(8,128)(2,1)} %get-tuple-element.130), channel_id=1, source_target_pairs={{0,10},{1,11},{2,8},{3,9},{4,14},{5,15},{6,12},{7,13},{8,2},{9,3},... | collective-permute-start | bytes 614408 | tf_op jit(solution)/shard_map/ppermute | solution.py:55
  164.7 18.6 %collective-permute-start.16 = (bf16[200,512]{1,0:T(8,128)(2,1)}, bf16[200,512]{1,0:T(8,128)(2,1)}, u32[]{:S(2)}, u32[]{:S(2)}) collective-permute-start(bf16[200,512]{1,0:T(8,128)(2,1)} %get-tuple-element.131), channel_id=1, source_target_pairs={{0,8},{1,9},{2,10},{3,11},{4,12},{5,13},{6,14},{7,15},{8,0},{9,1},... | collective-permute-start | bytes 614408 | tf_op jit(solution)/shard_map/ppermute | solution.py:55
  164.7 18.6 %collective-permute-start.15 = (bf16[200,512]{1,0:T(8,128)(2,1)}, bf16[200,512]{1,0:T(8,128)(2,1)}, u32[]{:S(2)}, u32[]{:S(2)}) collective-permute-start(bf16[200,512]{1,0:T(8,128)(2,1)} %get-tuple-element.132), channel_id=1, source_target_pairs={{0,2},{1,3},{2,0},{3,1},{4,6},{5,7},{6,4},{7,5},{8,10},{9,11},{10,... | collective-permute-start | bytes 614408 | tf_op jit(solution)/shard_map/ppermute | solution.py:55
  175.7 45.7 %collective-permute-start.39 = (bf16[4,200,512]{2,1,0:T(8,128)(2,1)}, bf16[4,200,512]{2,1,0:T(8,128)(2,1)}, u32[]{:S(2)}, u32[]{:S(2)}) collective-permute-start(bf16[4,200,512]{2,1,0:T(8,128)(2,1)} %get-tuple-element.122), channel_id=1, source_target_pairs={{0,1},{1,0},{2,3},{3,2},{4,5},{5,4},{6,7},{7,6},{8,9},{9,8},{10,11... | collective-permute-start | bytes 2457608 | tf_op jit(solution)/shard_map/ppermute | solution.py:55
  194.4 12.4 %collective-permute-start.25 = (bf16[200,512]{1,0:T(8,128)(2,1)S(1)}, bf16[200,512]{1,0:T(8,128)(2,1)S(1)}, u32[]{:S(2)}, u32[]{:S(2)}) collective-permute-start(bf16[200,512]{1,0:T(8,128)(2,1)S(1)} %get-tuple-element.149), channel_id=1, source_target_pairs={{0,8},{1,9},{2,10},{3,11},{4,12},{5,13},{6,14},{7,15},{8,0},{9,1},... | collective-permute-start | bytes 614408 | tf_op jit(solution)/shard_map/ppermute | solution.py:55
  194.9 11.9 %collective-permute-start.24 = (bf16[200,512]{1,0:T(8,128)(2,1)S(1)}, bf16[200,512]{1,0:T(8,128)(2,1)S(1)}, u32[]{:S(2)}, u32[]{:S(2)}) collective-permute-start(bf16[200,512]{1,0:T(8,128)(2,1)S(1)} %get-tuple-element.149), channel_id=1, source_target_pairs={{0,2},{1,3},{2,0},{3,1},{4,6},{5,7},{6,4},{7,5},{8,10},{9,11},{10,... | collective-permute-start | bytes 614408 | tf_op jit(solution)/shard_map/ppermute | solution.py:55
  196.6 18.3 %collective-permute-start.26 = (bf16[200,512]{1,0:T(8,128)(2,1)S(1)}, bf16[200,512]{1,0:T(8,128)(2,1)S(1)}, u32[]{:S(2)}, u32[]{:S(2)}) collective-permute-start(bf16[200,512]{1,0:T(8,128)(2,1)S(1)} %get-tuple-element.149), channel_id=1, source_target_pairs={{0,10},{1,11},{2,8},{3,9},{4,14},{5,15},{6,12},{7,13},{8,2},{9,3},... | collective-permute-start | bytes 614408 | tf_op jit(solution)/shard_map/ppermute | solution.py:55
  216.2 20.0 %collective-permute-start.27 = (bf16[4,200,512]{2,1,0:T(8,128)(2,1)}, bf16[4,200,512]{2,1,0:T(8,128)(2,1)}, u32[]{:S(2)}, u32[]{:S(2)}) collective-permute-start(bf16[4,200,512]{2,1,0:T(8,128)(2,1)} %get-tuple-element.128), channel_id=1, source_target_pairs={{0,1},{1,0},{2,3},{3,2},{4,5},{5,4},{6,7},{7,6},{8,9},{9,8},{10,11... | collective-permute-start | bytes 2457608 | tf_op jit(solution)/shard_map/ppermute | solution.py:55
  261.4 9.9 %collective-permute-start.32 = (bf16[4,200,512]{2,1,0:T(8,128)(2,1)}, bf16[4,200,512]{2,1,0:T(8,128)(2,1)}, u32[]{:S(2)}, u32[]{:S(2)}) collective-permute-start(bf16[4,200,512]{2,1,0:T(8,128)(2,1)} %slice_bitcast_fusion.8), channel_id=1, source_target_pairs={{0,1},{1,0},{2,3},{3,2},{4,5},{5,4},{6,7},{7,6},{8,9},{9,8},{10,11... | collective-permute-start | bytes 2457608 | tf_op jit(solution)/shard_map/ppermute | solution.py:55
  265.8 214.0 %reduce-scatter.3.cloned.1.call-start = ((), (), s32[]{:S(2)}) async-start(), calls=%async_computation.2 | async-start | bytes 5242880 | tf_op jit(solution)/shard_map/reduce_scatter | solution.py:127
  267.8 16.6 %collective-permute-start.42 = (bf16[200,512]{1,0:T(8,128)(2,1)S(1)}, bf16[200,512]{1,0:T(8,128)(2,1)S(1)}, u32[]{:S(2)}, u32[]{:S(2)}) collective-permute-start(bf16[200,512]{1,0:T(8,128)(2,1)S(1)} %get-tuple-element.119), channel_id=1, source_target_pairs={{0,8},{1,9},{2,10},{3,11},{4,12},{5,13},{6,14},{7,15},{8,0},{9,1},... | collective-permute-start | bytes 614408 | tf_op jit(solution)/shard_map/ppermute | solution.py:55
  270.7 13.7 %collective-permute-start.41 = (bf16[200,512]{1,0:T(8,128)(2,1)S(1)}, bf16[200,512]{1,0:T(8,128)(2,1)S(1)}, u32[]{:S(2)}, u32[]{:S(2)}) collective-permute-start(bf16[200,512]{1,0:T(8,128)(2,1)S(1)} %get-tuple-element.120), channel_id=1, source_target_pairs={{0,2},{1,3},{2,0},{3,1},{4,6},{5,7},{6,4},{7,5},{8,10},{9,11},{10,... | collective-permute-start | bytes 614408 | tf_op jit(solution)/shard_map/ppermute | solution.py:55
  272.6 14.6 %collective-permute-start.33 = (bf16[200,512]{1,0:T(8,128)(2,1)S(1)}, bf16[200,512]{1,0:T(8,128)(2,1)S(1)}, u32[]{:S(2)}, u32[]{:S(2)}) collective-permute-start(bf16[200,512]{1,0:T(8,128)(2,1)S(1)} %get-tuple-element.123), channel_id=1, source_target_pairs={{0,2},{1,3},{2,0},{3,1},{4,6},{5,7},{6,4},{7,5},{8,10},{9,11},{10,... | collective-permute-start | bytes 614408 | tf_op jit(solution)/shard_map/ppermute | solution.py:55
  274.2 18.1 %collective-permute-start.35 = (bf16[200,512]{1,0:T(8,128)(2,1)S(1)}, bf16[200,512]{1,0:T(8,128)(2,1)S(1)}, u32[]{:S(2)}, u32[]{:S(2)}) collective-permute-start(bf16[200,512]{1,0:T(8,128)(2,1)S(1)} %get-tuple-element.124), channel_id=1, source_target_pairs={{0,10},{1,11},{2,8},{3,9},{4,14},{5,15},{6,12},{7,13},{8,2},{9,3},... | collective-permute-start | bytes 614408 | tf_op jit(solution)/shard_map/ppermute | solution.py:55
  276.6 24.4 %collective-permute-start.34 = (bf16[200,512]{1,0:T(8,128)(2,1)S(1)}, bf16[200,512]{1,0:T(8,128)(2,1)S(1)}, u32[]{:S(2)}, u32[]{:S(2)}) collective-permute-start(bf16[200,512]{1,0:T(8,128)(2,1)S(1)} %get-tuple-element.125), channel_id=1, source_target_pairs={{0,8},{1,9},{2,10},{3,11},{4,12},{5,13},{6,14},{7,15},{8,0},{9,1},... | collective-permute-start | bytes 614408 | tf_op jit(solution)/shard_map/ppermute | solution.py:55
  323.2 10.6 %collective-permute-start.44 = (bf16[200,512]{1,0:T(8,128)(2,1)S(1)}, bf16[200,512]{1,0:T(8,128)(2,1)S(1)}, u32[]{:S(2)}, u32[]{:S(2)}) collective-permute-start(bf16[200,512]{1,0:T(8,128)(2,1)S(1)} %get-tuple-element.145), channel_id=1, source_target_pairs={{0,2},{1,3},{2,0},{3,1},{4,6},{5,7},{6,4},{7,5},{8,10},{9,11},{10,... | collective-permute-start | bytes 614408 | tf_op jit(solution)/shard_map/ppermute | solution.py:55
  323.3 12.1 %collective-permute-start.46 = (bf16[200,512]{1,0:T(8,128)(2,1)S(1)}, bf16[200,512]{1,0:T(8,128)(2,1)S(1)}, u32[]{:S(2)}, u32[]{:S(2)}) collective-permute-start(bf16[200,512]{1,0:T(8,128)(2,1)S(1)} %get-tuple-element.145), channel_id=1, source_target_pairs={{0,10},{1,11},{2,8},{3,9},{4,14},{5,15},{6,12},{7,13},{8,2},{9,3},... | collective-permute-start | bytes 614408 | tf_op jit(solution)/shard_map/ppermute | solution.py:55
  343.5 15.4 %collective-permute-start.62 = (bf16[2,512,512]{2,1,0:T(8,128)(2,1)}, bf16[2,512,512]{2,1,0:T(8,128)(2,1)S(1)}, u32[]{:S(2)}, u32[]{:S(2)}) collective-permute-start(bf16[2,512,512]{2,1,0:T(8,128)(2,1)} %bitcast.803), channel_id=1, source_target_pairs={{0,1},{1,0},{2,3},{3,2},{4,5},{5,4},{6,7},{7,6},{8,9},{9,8},{10,11... | collective-permute-start | bytes 3145736 | tf_op jit(solution)/shard_map/ppermute | solution.py:55
  360.0 14.7 %collective-permute-start.63 = (bf16[512,512]{1,0:T(8,128)(2,1)}, bf16[512,512]{1,0:T(8,128)(2,1)}, u32[]{:S(2)}, u32[]{:S(2)}) collective-permute-start(bf16[512,512]{1,0:T(8,128)(2,1)} %slice_bitcast_fusion.12), channel_id=1, source_target_pairs={{0,2},{1,3},{2,0},{3,1},{4,6},{5,7},{6,4},{7,5},{8,10},{9,11},{10,... | collective-permute-start | bytes 1572872 | tf_op jit(solution)/shard_map/ppermute | solution.py:55
  363.3 14.2 %collective-permute-start.48 = (bf16[4,200,512]{2,1,0:T(8,128)(2,1)}, bf16[4,200,512]{2,1,0:T(8,128)(2,1)}, u32[]{:S(2)}, u32[]{:S(2)}) collective-permute-start(bf16[4,200,512]{2,1,0:T(8,128)(2,1)} %slice_bitcast_fusion.4), channel_id=1, source_target_pairs={{0,1},{1,0},{2,3},{3,2},{4,5},{5,4},{6,7},{7,6},{8,9},{9,8},{10,11... | collective-permute-start | bytes 2457608 | tf_op jit(solution)/shard_map/ppermute | solution.py:55
  376.0 11.4 %collective-permute-start.64 = (bf16[4,64,512]{2,1,0:T(8,128)(2,1)S(1)}, bf16[4,64,512]{2,1,0:T(8,128)(2,1)S(1)}, u32[]{:S(2)}, u32[]{:S(2)}) collective-permute-start(bf16[4,64,512]{2,1,0:T(8,128)(2,1)S(1)} %dynamic-slice_bitcast_fusion), channel_id=1, source_target_pairs={{0,4},{1,5},{2,6},{3,7},{4,0},{5,1},{6,2},{7,3},{8,12},{9,13},{10,... | collective-permute-start | bytes 786440 | tf_op jit(solution)/shard_map/ppermute | solution.py:55
  378.9 12.5 %collective-permute-start.51 = (bf16[200,512]{1,0:T(8,128)(2,1)S(1)}, bf16[200,512]{1,0:T(8,128)(2,1)S(1)}, u32[]{:S(2)}, u32[]{:S(2)}) collective-permute-start(bf16[200,512]{1,0:T(8,128)(2,1)S(1)} %get-tuple-element.112), channel_id=1, source_target_pairs={{0,10},{1,11},{2,8},{3,9},{4,14},{5,15},{6,12},{7,13},{8,2},{9,3},... | collective-permute-start | bytes 614408 | tf_op jit(solution)/shard_map/ppermute | solution.py:55
  381.6 18.6 %collective-permute-start.50 = (bf16[200,512]{1,0:T(8,128)(2,1)S(1)}, bf16[200,512]{1,0:T(8,128)(2,1)S(1)}, u32[]{:S(2)}, u32[]{:S(2)}) collective-permute-start(bf16[200,512]{1,0:T(8,128)(2,1)S(1)} %get-tuple-element.113), channel_id=1, source_target_pairs={{0,8},{1,9},{2,10},{3,11},{4,12},{5,13},{6,14},{7,15},{8,0},{9,1},... | collective-permute-start | bytes 614408 | tf_op jit(solution)/shard_map/ppermute | solution.py:55
  382.2 18.0 %collective-permute-start.49 = (bf16[200,512]{1,0:T(8,128)(2,1)S(1)}, bf16[200,512]{1,0:T(8,128)(2,1)S(1)}, u32[]{:S(2)}, u32[]{:S(2)}) collective-permute-start(bf16[200,512]{1,0:T(8,128)(2,1)S(1)} %get-tuple-element.114), channel_id=1, source_target_pairs={{0,2},{1,3},{2,0},{3,1},{4,6},{5,7},{6,4},{7,5},{8,10},{9,11},{10,... | collective-permute-start | bytes 614408 | tf_op jit(solution)/shard_map/ppermute | solution.py:55
  388.2 25.2 %collective-permute-start.65 = (bf16[2,64,512]{2,1,0:T(8,128)(2,1)}, bf16[2,64,512]{2,1,0:T(8,128)(2,1)}, u32[]{:S(2)}, u32[]{:S(2)}) collective-permute-start(bf16[2,64,512]{2,1,0:T(8,128)(2,1)} %dynamic-slice_bitcast_fusion.2), channel_id=1, source_target_pairs={{0,8},{1,9},{2,10},{3,11},{4,12},{5,13},{6,14},{7,15},{8,0},{9,1},... | collective-permute-start | bytes 393224 | tf_op jit(solution)/shard_map/ppermute | solution.py:55
  413.3 15.0 %collective-permute-start.57 = (bf16[2,512,512]{2,1,0:T(8,128)(2,1)}, bf16[2,512,512]{2,1,0:T(8,128)(2,1)}, u32[]{:S(2)}, u32[]{:S(2)}) collective-permute-start(bf16[2,512,512]{2,1,0:T(8,128)(2,1)} %bitcast.804), channel_id=1, source_target_pairs={{0,1},{1,0},{2,3},{3,2},{4,5},{5,4},{6,7},{7,6},{8,9},{9,8},{10,11... | collective-permute-start | bytes 3145736 | tf_op jit(solution)/shard_map/ppermute | solution.py:55
  415.1 18.2 %collective-permute-start.66 = (bf16[1,64,512]{2,1,0:T(8,128)(2,1)}, bf16[1,64,512]{2,1,0:T(8,128)(2,1)}, u32[]{:S(2)}, u32[]{:S(2)}) collective-permute-start(bf16[1,64,512]{2,1,0:T(8,128)(2,1)} %constant_dynamic-slice_fusion), channel_id=1, source_target_pairs={{0,16},{1,17},{2,18},{3,19},{4,20},{5,21},{6,22},{7,23},{8,24},{9,... | collective-permute-start | bytes 196616 | tf_op jit(solution)/shard_map/ppermute | solution.py:55
  429.7 16.4 %collective-permute-start.58 = (bf16[512,512]{1,0:T(8,128)(2,1)S(1)}, bf16[512,512]{1,0:T(8,128)(2,1)S(1)}, u32[]{:S(2)}, u32[]{:S(2)}) collective-permute-start(bf16[512,512]{1,0:T(8,128)(2,1)S(1)} %slice_bitcast_fusion.14), channel_id=1, source_target_pairs={{0,2},{1,3},{2,0},{3,1},{4,6},{5,7},{6,4},{7,5},{8,10},{9,11},{10,... | collective-permute-start | bytes 1572872 | tf_op jit(solution)/shard_map/ppermute | solution.py:55
  432.6 12.4 %collective-permute-start.53 = (f32[20,512]{1,0:T(8,128)S(1)}, f32[20,512]{1,0:T(8,128)}, u32[]{:S(2)}, u32[]{:S(2)}) collective-permute-start(f32[20,512]{1,0:T(8,128)S(1)} %add.362), channel_id=1, source_target_pairs={{0,2},{1,3},{2,0},{3,1},{4,6},{5,7},{6,4},{7,5},{8,10},{9,11},{10,... | collective-permute-start | bytes 122888 | tf_op jit(solution)/shard_map/ppermute | solution.py:55
  446.2 16.6 %collective-permute-start.59 = (bf16[4,64,512]{2,1,0:T(8,128)(2,1)S(1)}, bf16[4,64,512]{2,1,0:T(8,128)(2,1)S(1)}, u32[]{:S(2)}, u32[]{:S(2)}) collective-permute-start(bf16[4,64,512]{2,1,0:T(8,128)(2,1)S(1)} %dynamic-slice_bitcast_fusion.1), channel_id=1, source_target_pairs={{0,4},{1,5},{2,6},{3,7},{4,0},{5,1},{6,2},{7,3},{8,12},{9,13},{10,... | collective-permute-start | bytes 786440 | tf_op jit(solution)/shard_map/ppermute | solution.py:55
  451.1 11.6 %collective-permute-start.55 = (f32[20,512]{1,0:T(8,128)S(1)}, f32[20,512]{1,0:T(8,128)S(1)}, u32[]{:S(2)}, u32[]{:S(2)}) collective-permute-start(f32[20,512]{1,0:T(8,128)S(1)} %add.364), channel_id=1, source_target_pairs={{0,8},{1,9},{2,10},{3,11},{4,12},{5,13},{6,14},{7,15},{8,0},{9,1},... | collective-permute-start | bytes 122888 | tf_op jit(solution)/shard_map/ppermute | solution.py:55
  476.2 12.5 %collective-permute-start.72 = (bf16[2,2,64,512]{3,2,1,0:T(8,128)(2,1)S(1)}, bf16[2,2,64,512]{3,2,1,0:T(8,128)(2,1)S(1)}, u32[]{:S(2)}, u32[]{:S(2)}) collective-permute-start(bf16[2,2,64,512]{3,2,1,0:T(8,128)(2,1)S(1)} %get-tuple-element.81), channel_id=1, source_target_pairs={{0,2},{1,3},{2,0},{3,1},{4,6},{5,7},{6,4},{7,5},{8,10},{9,11},{10,... | collective-permute-start | bytes 786440 | tf_op jit(solution)/shard_map/ppermute | solution.py:55
  478.0 10.7 %collective-permute-start.74 = (bf16[2,2,64,512]{3,2,1,0:T(8,128)(2,1)S(1)}, bf16[2,2,64,512]{3,2,1,0:T(8,128)(2,1)S(1)}, u32[]{:S(2)}, u32[]{:S(2)}) collective-permute-start(bf16[2,2,64,512]{3,2,1,0:T(8,128)(2,1)S(1)} %get-tuple-element.82), channel_id=1, source_target_pairs={{0,10},{1,11},{2,8},{3,9},{4,14},{5,15},{6,12},{7,13},{8,2},{9,3},... | collective-permute-start | bytes 786440 | tf_op jit(solution)/shard_map/ppermute | solution.py:55
  478.0 11.9 %collective-permute-start.73 = (bf16[2,2,64,512]{3,2,1,0:T(8,128)(2,1)S(1)}, bf16[2,2,64,512]{3,2,1,0:T(8,128)(2,1)S(1)}, u32[]{:S(2)}, u32[]{:S(2)}) collective-permute-start(bf16[2,2,64,512]{3,2,1,0:T(8,128)(2,1)S(1)} %get-tuple-element.83), channel_id=1, source_target_pairs={{0,8},{1,9},{2,10},{3,11},{4,12},{5,13},{6,14},{7,15},{8,0},{9,1},... | collective-permute-start | bytes 786440 | tf_op jit(solution)/shard_map/ppermute | solution.py:55
  482.1 9.0 %collective-permute-start.67 = (bf16[4,2,64,512]{3,2,1,0:T(8,128)(2,1)}, bf16[4,2,64,512]{3,2,1,0:T(8,128)(2,1)S(1)}, u32[]{:S(2)}, u32[]{:S(2)}) collective-permute-start(bf16[4,2,64,512]{3,2,1,0:T(8,128)(2,1)} %get-tuple-element.75), channel_id=1, source_target_pairs={{0,1},{1,0},{2,3},{3,2},{4,5},{5,4},{6,7},{7,6},{8,9},{9,8},{10,11... | collective-permute-start | bytes 1572872 | tf_op jit(solution)/shard_map/ppermute | solution.py:55
  491.2 11.3 %collective-permute-start.68 = (bf16[2,2,64,512]{3,2,1,0:T(8,128)(2,1)S(1)}, bf16[2,2,64,512]{3,2,1,0:T(8,128)(2,1)S(1)}, u32[]{:S(2)}, u32[]{:S(2)}) collective-permute-start(bf16[2,2,64,512]{3,2,1,0:T(8,128)(2,1)S(1)} %get-tuple-element.71), channel_id=1, source_target_pairs={{0,2},{1,3},{2,0},{3,1},{4,6},{5,7},{6,4},{7,5},{8,10},{9,11},{10,... | collective-permute-start | bytes 786440 | tf_op jit(solution)/shard_map/ppermute | solution.py:55
  492.7 9.8 %collective-permute-start.70 = (bf16[2,2,64,512]{3,2,1,0:T(8,128)(2,1)S(1)}, bf16[2,2,64,512]{3,2,1,0:T(8,128)(2,1)S(1)}, u32[]{:S(2)}, u32[]{:S(2)}) collective-permute-start(bf16[2,2,64,512]{3,2,1,0:T(8,128)(2,1)S(1)} %get-tuple-element.72), channel_id=1, source_target_pairs={{0,10},{1,11},{2,8},{3,9},{4,14},{5,15},{6,12},{7,13},{8,2},{9,3},... | collective-permute-start | bytes 786440 | tf_op jit(solution)/shard_map/ppermute | solution.py:55
  494.0 10.5 %collective-permute-start.69 = (bf16[2,2,64,512]{3,2,1,0:T(8,128)(2,1)S(1)}, bf16[2,2,64,512]{3,2,1,0:T(8,128)(2,1)S(1)}, u32[]{:S(2)}, u32[]{:S(2)}) collective-permute-start(bf16[2,2,64,512]{3,2,1,0:T(8,128)(2,1)S(1)} %get-tuple-element.73), channel_id=1, source_target_pairs={{0,8},{1,9},{2,10},{3,11},{4,12},{5,13},{6,14},{7,15},{8,0},{9,1},... | collective-permute-start | bytes 786440 | tf_op jit(solution)/shard_map/ppermute | solution.py:55
  (157 other events, 1251.3 us)
Sparse Core Ops, SparseCore 0:
  54.6 87.5 all-gather.4
  144.1 86.5 all-gather.6
  265.9 90.3 reduce-scatter.4
  367.3 95.9 reduce-scatter.2

commit v2 on v1

v2 whole, which is shorter than its diff:
```python
import jax
import jax.numpy as jnp
from jax import lax
from jax.experimental import pallas as pl
from jax.experimental.pallas import tpu as pltpu
from jax.sharding import PartitionSpec as P

HD = 64
LEN = 197
LAYERS = 2
CAP = 247
SLOTS = 256
ROWS = 200
NORM_EPS = 1e-06
f32 = jnp.float32
bf16 = jnp.bfloat16
AXES = ("dp", "tensor")


def mm(spec, *args):
    return jnp.einsum(spec, *args, preferred_element_type=f32)


class Place:
    def __init__(self):
        self.dp_size = lax.axis_size("dp")
        self.tensor_size = lax.axis_size("tensor")
        self.count = self.dp_size * self.tensor_size
        self.dp = lax.axis_index("dp")
        self.tensor = lax.axis_index("tensor")
        self.near = self.dp & 1
        self.expert = self.near * self.tensor_size + self.tensor

    def swap(self, value, mask):
        pairs = [(i, i ^ mask) for i in range(self.count)]
        return lax.ppermute(value, AXES, pairs)

    def dp_groups(self):
        return [[d for d in range(self.dp_size) if d & 1 == b] for b in (0, 1)]

    def ordered(self, mine, theirs, bit):
        return jnp.stack([jnp.where(bit, theirs, mine), jnp.where(bit, mine, theirs)])


def gather_attention(place, shard):
    rows, width = shard.shape
    bits = place.dp_size.bit_length() - 1
    held = shard
    for bit in reversed(range(bits)):
        other = place.swap(held, place.tensor_size << bit)
        held = place.ordered(held, other, (place.dp >> bit) & 1)
    held = held.reshape((2,) * bits + (rows, width))
    held = jnp.transpose(held, tuple(reversed(range(bits))) + (bits, bits + 1))
    held = held.reshape(1, place.dp_size * rows, width)
    for mask in (2, 1):
        held = jnp.stack([held, place.swap(held, mask)], axis=1 if mask == 1 else 0)
        held = held.reshape((-1,) + held.shape[2:])
    return held


def scatter_attention(place, blocks, rows):
    bits = place.dp_size.bit_length() - 1
    held = blocks.reshape((2, 2) + blocks.shape[1:])
    held = held[:, 0] + place.swap(held[:, 1], 1)
    held = held[0] + place.swap(held[1], 2)
    for bit in range(bits):
        parts = held.reshape((-1, 2, rows, held.shape[-1]))
        mine = lax.dynamic_index_in_dim(parts, (place.dp >> bit) & 1, 1, keepdims=False)
        theirs = lax.dynamic_index_in_dim(parts, 1 - ((place.dp >> bit) & 1), 1, keepdims=False)
        held = mine + place.swap(theirs, place.tensor_size << bit)
        held = held.reshape(-1, held.shape[-1])
    return held


def plane_exchange(place, blocks):
    even, odd = blocks[0::2], blocks[1::2]
    pair = jnp.stack([even, place.swap(odd, 1)], axis=1)
    got = [pair[0]] + [place.swap(pair[k], 2 * k) for k in (1, 2, 3)]
    return jnp.concatenate(got, axis=0)


def gather_experts(place, w_in, w_out):
    blocks = jnp.stack([w_in, jnp.swapaxes(w_out, 1, 2)], axis=1)
    experts, unused, rows, width = blocks.shape
    order = place.expert ^ jnp.arange(experts)
    got = plane_exchange(place, blocks[order])
    got = got.reshape((2, place.tensor_size, 2, rows, width))
    got = place.ordered(got[0], got[1], place.near)
    full = lax.all_gather(got, "dp", axis=0, tiled=False, axis_index_groups=place.dp_groups())
    full = jnp.transpose(full, (3, 2, 0, 1, 4, 5))
    full = full.reshape((2, place.tensor_size, -1, width))
    return full[0], full[1]


def scatter_experts(place, grad_in, grad_out):
    tensor, model, width = grad_in.shape
    rows = model // place.dp_size
    both = jnp.stack([grad_in, grad_out]).astype(bf16)
    both = both.reshape((2, tensor, -1, 2, rows, width))
    both = jnp.transpose(both, (2, 3, 1, 0, 4, 5))
    mine = lax.psum_scatter(
        both, "dp", scatter_dimension=0, tiled=False, axis_index_groups=place.dp_groups()
    )
    mine = place.ordered(mine[0], mine[1], place.near)
    got = plane_exchange(place, mine.reshape((-1, 2, rows, width)))
    order = place.expert ^ jnp.arange(got.shape[0])
    got = got[order].astype(f32)
    return got[:, 0], jnp.swapaxes(got[:, 1], 1, 2)


def slot_rows(place, ids, ranking, experts):
    expert_range = jnp.arange(experts, dtype=jnp.int32)[:, None]
    first = ids[:, 0][None, :] == expert_range
    second = ids[:, 1][None, :] == expert_range
    both = jnp.concatenate([first, second]).astype(bf16)
    earlier = (ranking[:, None] < ranking[None, :]).astype(bf16)
    counts = mm("et,ts->es", both, earlier)
    total = jnp.sum(first.astype(f32), axis=1, keepdims=True)
    slot = jnp.where(first, counts[:experts], jnp.where(second, total + counts[experts:], -1.0))
    slot = jnp.where(slot < CAP, slot, -1.0).astype(jnp.int32)
    mine = lax.dynamic_index_in_dim(slot, place.expert, 0, keepdims=False)
    theirs = lax.dynamic_index_in_dim(slot, place.expert ^ place.tensor_size, 0, keepdims=False)
    return mine, theirs


def slot_tables(place, mine, theirs):
    groups = jnp.stack([mine, theirs])
    groups = groups.reshape((2, place.tensor_size, LEN))
    groups = groups[:, place.tensor ^ jnp.arange(place.tensor_size)]
    groups = jnp.pad(groups, ((0, 0), (0, 0), (0, ROWS - LEN)), constant_values=-1)
    table = groups.reshape(-1, ROWS)
    return table, jnp.swapaxes(table, 0, 1)


def exchange_rows(place, own):
    even = [own] + [place.swap(own, 2 * k) for k in (1, 2, 3)]
    odd = [place.swap(rows, 1) for rows in even]
    return [rows for pair in zip(even, odd) for rows in pair]


def add_kernel(even, odd, *sums):
    for k, target in enumerate(sums):
        target[...] = (even[k].astype(f32) + odd[k].astype(f32)).astype(bf16)


def pair_rows(place, parts):
    even, odd = parts
    odd = place.swap(odd, 1)
    return list(pl.pallas_call(
        add_kernel,
        out_shape=(jax.ShapeDtypeStruct(even.shape[1:], bf16),) * 4,
        in_specs=[vmem()] * 2,
        out_specs=(vmem(),) * 4,
        cost_estimate=pl.CostEstimate(flops=1, transcendentals=0, bytes_accessed=1),
        name="add_rows",
    )(even, odd))


def send_rows(place, sums):
    return [sums[0]] + [place.swap(sums[k], 2 * k) for k in (1, 2, 3)]


def dot(a, b):
    return lax.dot_general(a, b, (((1,), (0,)), ((), ())), preferred_element_type=f32)


def dot_t(a, b):
    return lax.dot_general(a, b, (((1,), (1,)), ((), ())), preferred_element_type=f32)


def t_dot(a, b):
    return lax.dot_general(a, b, (((0,), (0,)), ((), ())), preferred_element_type=f32)


def normalized(rows):
    average = jnp.mean(rows, axis=-1, keepdims=True)
    centered = rows - average
    variance = jnp.mean(centered * centered, axis=-1, keepdims=True)
    scale = lax.rsqrt(variance + NORM_EPS)
    return centered * scale, scale


def norm_grad(rows, gain, grad):
    unit, scale = normalized(rows)
    scaled = grad * gain
    pull = scaled - jnp.mean(scaled, axis=-1, keepdims=True)
    pull = pull - unit * jnp.mean(scaled * unit, axis=-1, keepdims=True)
    return scale * pull, jnp.sum(grad * unit, axis=0, keepdims=True)


def head_masks():
    lane = lax.broadcasted_iota(jnp.int32, (1, 2 * HD), 1)
    return lane < HD, lane >= HD


def only(values, mask):
    return jnp.where(mask, values.astype(f32), 0.0).astype(bf16)


def head_probs(queries, keys, mask):
    scores = dot_t(only(queries, mask), keys) * (HD ** (-0.5))
    valid = lax.broadcasted_iota(jnp.int32, scores.shape, 1) < LEN
    scores = jnp.where(valid, scores, -1e30)
    top = jnp.max(scores, axis=-1, keepdims=True)
    weights = jnp.exp(scores - top)
    return weights / jnp.sum(weights, axis=-1, keepdims=True)


def weight_copies(off_ref, pieces, buffer, sems):
    result = []
    for j, piece in enumerate(pieces):
        count, rows, unused = piece.shape
        result.append([
            pltpu.make_async_copy(
                piece.at[i],
                buffer.at[j, pl.ds(pl.multiple_of(off_ref[i], rows), rows)],
                sems.at[j, i],
            )
            for i in range(count)
        ])
    return result


def padded_rows(ref, scratch):
    if ref.shape[0] == ROWS:
        return ref[...].astype(f32)
    scratch[...] = jnp.zeros_like(scratch)
    scratch[0 : ref.shape[0]] = ref[...].astype(f32)
    return scratch[...]


def attention_forward_kernel(piece_count, extra_count, off_ref, base, *refs):
    pieces, refs = refs[:piece_count], refs[piece_count:]
    extra, refs = refs[:extra_count], refs[extra_count:]
    gains, w0, w1, w2, w3, hidden, mid, normed, qkv, ctx, scratch, wbuf, sems = refs
    copies = weight_copies(off_ref, (w0, w1, w2, w3), wbuf, sems)
    for group in copies:
        for copy in group:
            copy.start()
    rows = padded_rows(base, scratch)
    for piece in pieces:
        rows = rows + piece[...].astype(f32)
    hidden[...] = rows
    unit, unused = normalized(rows)
    normed_a = (unit * gains[0:1]).astype(bf16)
    low, high = head_masks()
    total = rows
    for j in range(4):
        for copy in copies[j]:
            copy.wait()
        part = dot(normed_a, wbuf[j, :, : 6 * HD]).astype(bf16)
        qkv[:, j * 6 * HD : (j + 1) * 6 * HD] = part
        queries, keys, values = part[:, : 2 * HD], part[:, 2 * HD : 4 * HD], part[:, 4 * HD :]
        first = dot(head_probs(queries, keys, low).astype(bf16), values)
        second = dot(head_probs(queries, keys, high).astype(bf16), values)
        context = jnp.where(low, first, second).astype(bf16)
        ctx[:, j * 2 * HD : (j + 1) * 2 * HD] = context
        total = total + dot_t(context, wbuf[j, :, 6 * HD :])
    mid[...] = total
    unit, unused = normalized(total)
    normed[0] = (unit * gains[1:2]).astype(bf16)
    for ref in extra:
        normed[1] = padded_rows(ref, scratch).astype(bf16)


def vmem():
    return pl.BlockSpec(memory_space=pltpu.VMEM)


def smem():
    return pl.BlockSpec(memory_space=pltpu.SMEM)


def hbm():
    return pl.BlockSpec(memory_space=pl.ANY)


def params():
    return pltpu.CompilerParams(vmem_limit_bytes=60 << 20)


def attention_forward(offsets, base, pieces, extra, gains, weights):
    width = base.shape[1]
    shape = jax.ShapeDtypeStruct
    return pl.pallas_call(
        lambda *refs: attention_forward_kernel(len(pieces), len(extra), *refs),
        out_shape=(
            shape((ROWS, width), f32),
            shape((ROWS, width), f32),
            shape((1 + len(extra), ROWS, width), bf16),
            shape((ROWS, 3 * width), bf16),
            shape((ROWS, width), bf16),
        ),
        in_specs=[smem(), vmem()] + [vmem()] * (len(pieces) + len(extra)) + [vmem()] + [hbm()] * 4,
        out_specs=[vmem()] * 5,
        scratch_shapes=[
            pltpu.VMEM((ROWS, width), f32),
            pltpu.VMEM((4, width, width), bf16),
            pltpu.SemaphoreType.DMA((4, weights[0].shape[0])),
        ],
        compiler_params=params(),
        cost_estimate=pl.CostEstimate(flops=1, transcendentals=0, bytes_accessed=1),
        name="attention_forward",
    )(offsets, base, *pieces, *extra, gains, *weights)


def attention_backward_kernel(
    off_ref, base, p0, p1, p2, p3, hidden_in, hidden_mid, gains, w0, w1, w2, w3, qkv, ctx,
    grad_out, branch, gain_out, g0, g1, g2, g3, scratch, wbuf, gbuf, sems, out_sems,
):
    copies = weight_copies(off_ref, (w0, w1, w2, w3), wbuf, sems)
    for group in copies:
        for copy in group:
            copy.start()
    grad = padded_rows(base, scratch)
    normed_grad = p0[...].astype(f32) + p1[...].astype(f32) + p2[...].astype(f32) + p3[...].astype(f32)
    part, gain_expert = norm_grad(hidden_mid[...], gains[1:2], normed_grad)
    grad = grad + part
    attn_grad = grad.astype(bf16)
    attn_grad_t = attn_grad.T
    rows_in = hidden_in[...]
    unit, unused = normalized(rows_in)
    normed_t = (unit * gains[0:1]).astype(bf16).T
    low, high = head_masks()
    scale = HD ** (-0.5)
    normed_part = jnp.zeros_like(grad)
    sends = []
    for j, target in enumerate((g0, g1, g2, g3)):
        for copy in copies[j]:
            copy.wait()
        part = qkv[:, j * 6 * HD : (j + 1) * 6 * HD]
        queries, keys, values = part[:, : 2 * HD], part[:, 2 * HD : 4 * HD], part[:, 4 * HD :]
        context = ctx[:, j * 2 * HD : (j + 1) * 2 * HD]
        context_grad = dot(attn_grad, wbuf[j, :, 6 * HD :]).astype(bf16)
        query_grad, key_grad, value_grad = None, None, None
        for mask in (low, high):
            probs = head_probs(queries, keys, mask)
            v_grad = t_dot(probs.astype(bf16), context_grad)
            probs_grad = dot_t(only(context_grad, mask), values)
            inner = jnp.sum(probs * probs_grad, axis=-1, keepdims=True)
            score_grad = (probs * (probs_grad - inner)).astype(bf16)
            q_grad = dot(score_grad, keys) * scale
            k_grad = t_dot(score_grad, queries) * scale
            if query_grad is None:
                query_grad, key_grad, value_grad = q_grad, k_grad, v_grad
            else:
                query_grad = jnp.where(mask, q_grad, query_grad).astype(bf16)
                key_grad = jnp.where(mask, k_grad, key_grad).astype(bf16)
                value_grad = jnp.where(mask, v_grad, value_grad).astype(bf16)
        for place, mixed in enumerate((query_grad, key_grad, value_grad)):
            lanes = slice(place * 2 * HD, (place + 1) * 2 * HD)
            gbuf[j, :, lanes] = dot(normed_t, mixed).astype(bf16)
            normed_part = normed_part + dot_t(mixed, wbuf[j, :, lanes])
        gbuf[j, :, 6 * HD :] = dot(attn_grad_t, context).astype(bf16)
        count, rows, unused = target.shape
        for i in range(count):
            send = pltpu.make_async_copy(
                gbuf.at[j, pl.ds(pl.multiple_of(off_ref[i], rows), rows)], target.at[i], out_sems.at[j, i]
            )
            send.start()
            sends.append(send)
    part, gain_attn = norm_grad(rows_in, gains[0:1], normed_part)
    grad = grad + part
    grad_out[...] = grad[: grad_out.shape[0]]
    branch[...] = grad.astype(bf16)
    gain_out[...] = jnp.concatenate([gain_attn, gain_expert], axis=0)
    for send in sends:
        send.wait()


def attention_backward(offsets, base, pieces, hidden_in, hidden_mid, gains, weights, qkv, ctx, out_rows):
    width = base.shape[1]
    shape = jax.ShapeDtypeStruct
    blocks = weights[0].shape
    return pl.pallas_call(
        attention_backward_kernel,
        out_shape=(
            shape((out_rows, width), f32),
            shape((ROWS, width), bf16),
            shape((2, width), f32),
        ) + (shape(blocks, bf16),) * 4,
        in_specs=[smem()] + [vmem()] * 8 + [hbm()] * 4 + [vmem()] * 2,
        out_specs=[vmem()] * 3 + [hbm()] * 4,
        scratch_shapes=[
            pltpu.VMEM((ROWS, width), f32),
            pltpu.VMEM((4, width, width), bf16),
            pltpu.VMEM((4, width, width), bf16),
            pltpu.SemaphoreType.DMA((4, blocks[0])),
            pltpu.SemaphoreType.DMA((4, blocks[0])),
        ],
        compiler_params=params(),
        cost_estimate=pl.CostEstimate(flops=1, transcendentals=0, bytes_accessed=1),
        name="attention_backward",
    )(offsets, base, *pieces, hidden_in, hidden_mid, gains, *weights, qkv, ctx)


def split(values):
    high = values.astype(bf16)
    return high, (values - high.astype(f32)).astype(bf16)


ROOT = 0.7978845608028654
CUBE = 0.044715


def expert_kernel(plan, off_ref, me_ref, table, table_t, router, *refs):
    forward, backward = plan.images is not None, plan.grads is not None
    piece_count = len(plan.w_in)
    refs = list(refs)

    def take(count):
        taken, refs[:count] = refs[:count], []
        return taken

    tokens = take(plan.token_arrays)
    sent_in, y_in = take(2) if not forward else (None, None)
    sources = take(plan.weight_arrays)
    parts = take(2) if forward else None
    sent_out, y_out = take(2) if forward and not backward else (None, None)
    if backward:
        back_parts = take(2)
        (router_grad,) = take(1)
        targets = take(len(plan.grad_shapes))
    in_buf, out_buf, sent_buf, y_buf = take(4)
    if backward:
        slot_buf, slot_t, sent_t, back_buf, gbuf, out_sems = take(6)
    (sems,) = take(1)

    near, chunks, rows, width = plan.block

    def loads(c, which):
        result = []
        for m in range(piece_count):
            for n in range(near):
                at = pl.ds(pl.multiple_of(off_ref[m * near + n], rows), rows)
                index, part = (plan.w_in, plan.w_out)[which][m]
                piece = sources[index] if part is None else sources[index].at[part]
                buf = (in_buf, out_buf)[which]
                result.append(
                    pltpu.make_async_copy(piece.at[n, c], buf.at[c, at], sems.at[which, c, m * near + n])
                )
        return result

    for c in range(chunks):
        for which in (0, 1):
            for copy in loads(c, which):
                copy.start()

    def gather(images):
        for g in (0, 1):
            total = None
            for t in range(4):
                j = g * 4 + t
                slot = lax.broadcasted_iota(jnp.int32, (SLOTS, ROWS), 0)
                hot = (table[j : j + 1, :] == slot).astype(f32).astype(bf16)
                index, layer = images[j]
                part = dot(hot, tokens[index][layer])
                total = part if total is None else total + part
            yield g, total

    def scatter(slot_rows, parts):
        for g in (0, 1):
            for t in range(4):
                j = g * 4 + t
                slot = lax.broadcasted_iota(jnp.int32, (ROWS, SLOTS), 1)
                hot = (table_t[:, j : j + 1] == slot).astype(f32).astype(bf16)
                part = dot(hot, slot_rows[g * SLOTS : (g + 1) * SLOTS]).astype(bf16)
                parts[j % 2][j // 2] = part

    if forward:
        for g, rows_g in gather(plan.images):
            sent_buf[g * SLOTS : (g + 1) * SLOTS] = rows_g.astype(bf16)
    else:
        sent_buf[...] = sent_in[...]
    sent = sent_buf[...]
    logits = dot(sent, router[...])
    top = jnp.max(logits, axis=-1, keepdims=True)
    weights = jnp.exp(logits - top)
    probs = weights / jnp.sum(weights, axis=-1, keepdims=True)
    is_mine = lax.broadcasted_iota(jnp.int32, probs.shape, 1) == me_ref[0]
    gate = jnp.sum(jnp.where(is_mine, probs, 0.0), axis=-1, keepdims=True)

    if forward:
        y_buf[...] = jnp.zeros_like(y_buf)

        @pl.loop(0, chunks)
        def _(c):
            for copy in loads(c, 0):
                copy.wait()
            pre = dot(sent_buf[...], in_buf[c])
            act = (0.5 * pre * (1.0 + jnp.tanh(ROOT * (pre + CUBE * (pre * pre * pre))))).astype(bf16)
            for copy in loads(c, 1):
                copy.wait()
            y_buf[...] += dot_t(act, out_buf[c])

        expert_y = y_buf[...]
        scatter((gate * expert_y).astype(bf16), parts)
        if not backward:
            sent_out[...] = sent
            y_out[...] = expert_y
    else:
        for c in range(chunks):
            for which in (0, 1):
                for copy in loads(c, which):
                    copy.wait()
        expert_y = y_in[...]
    if not backward:
        return

    for g, rows_g in gather(plan.grads):
        part = slice(g * SLOTS, (g + 1) * SLOTS)
        slot_buf[part] = (gate[part] * rows_g).astype(bf16)
        y_buf[part] = rows_g
    gate_grad = jnp.sum(y_buf[...] * expert_y, axis=-1, keepdims=True)
    slot_t[...] = slot_buf[...].T
    sent_t[...] = sent.T
    logit_grad = gate_grad * gate * (is_mine.astype(f32) - probs)
    first, second = split(logit_grad)
    router_grad[...] = dot(sent_t[...], first) + dot(sent_t[...], second)
    back_buf[...] = dot_t(first, router[...]) + dot_t(second, router[...])

    def stores(c, which):
        result = []
        for m in range(piece_count):
            for n in range(near):
                at = pl.ds(pl.multiple_of(off_ref[m * near + n], rows), rows)
                index, part = (plan.grad_in, plan.grad_out)[which][m]
                piece = targets[index] if part is None else targets[index].at[part]
                result.append(
                    pltpu.make_async_copy(
                        gbuf.at[which, c, at], piece.at[n, c], out_sems.at[which, c, m * near + n]
                    )
                )
        return result

    @pl.loop(0, chunks)
    def _(c):
        pre = dot(sent_buf[...], in_buf[c])
        square = pre * pre
        bend = jnp.tanh(ROOT * (pre + CUBE * (square * pre)))
        act = (0.5 * pre * (1.0 + bend)).astype(bf16)
        gbuf[1, c] = dot(slot_t[...], act).astype(bf16)
        for copy in stores(c, 1):
            copy.start()
        slope = 0.5 * (1.0 + bend) + 0.5 * pre * (1.0 - bend * bend) * (ROOT * (1.0 + 3.0 * CUBE * square))
        pre_grad = (dot(slot_buf[...], out_buf[c]) * slope).astype(bf16)
        gbuf[0, c] = dot(sent_t[...], pre_grad).astype(bf16)
        for copy in stores(c, 0):
            copy.start()
        back_buf[...] += dot_t(pre_grad, in_buf[c])

    scatter(back_buf[...].astype(bf16), back_parts)

    @pl.loop(0, chunks)
    def _(c):
        for which in (0, 1):
            for copy in stores(c, which):
                copy.wait()


class Plan:
    def __init__(self, block, images, grads, w_in, w_out, grad_shapes, grad_in, grad_out):
        self.block = block
        self.images, self.grads = images, grads
        self.w_in, self.w_out = w_in, w_out
        self.grad_shapes, self.grad_in, self.grad_out = grad_shapes, grad_in, grad_out


def expert_layer(plan, offsets, me, tables, router, tokens, saved, weights):
    forward, backward = plan.images is not None, plan.grads is not None
    plan.token_arrays, plan.weight_arrays = len(tokens), len(weights)
    width = router.shape[0]
    count = len(plan.w_in)
    near, chunks, rows, hidden = plan.block
    slots = 2 * SLOTS
    shape = jax.ShapeDtypeStruct
    token_part = shape((4, ROWS, width), bf16)
    operands = [offsets, me, *tables, router, *tokens]
    in_specs = [smem(), smem()] + [vmem()] * (3 + len(tokens))
    if not forward:
        operands += saved
        in_specs += [vmem()] * 2
    operands += weights
    in_specs += [hbm()] * len(weights)
    out_shape, out_specs = [], []
    if forward:
        out_shape += [token_part] * 2
    if forward and not backward:
        out_shape += [shape((slots, width), bf16), shape((slots, width), f32)]
    if backward:
        out_shape += [token_part] * 2 + [shape(router.shape, f32)]
    out_specs += [vmem()] * len(out_shape)
    if backward:
        out_shape += [shape(s, bf16) for s in plan.grad_shapes]
        out_specs += [hbm()] * len(plan.grad_shapes)
    scratch = [
        pltpu.VMEM((chunks, width, hidden), bf16),
        pltpu.VMEM((chunks, width, hidden), bf16),
        pltpu.VMEM((slots, width), bf16),
        pltpu.VMEM((slots, width), f32),
    ]
    if backward:
        scratch += [
            pltpu.VMEM((slots, width), bf16),
            pltpu.VMEM((width, slots), bf16),
            pltpu.VMEM((width, slots), bf16),
            pltpu.VMEM((slots, width), f32),
            pltpu.VMEM((2, chunks, width, hidden), bf16),
            pltpu.SemaphoreType.DMA((2, chunks, count * near)),
        ]
    scratch += [pltpu.SemaphoreType.DMA((2, chunks, count * near))]
    return pl.pallas_call(
        lambda *refs: expert_kernel(plan, *refs),
        out_shape=tuple(out_shape),
        in_specs=in_specs,
        out_specs=tuple(out_specs),
        scratch_shapes=scratch,
        compiler_params=params(),
        cost_estimate=pl.CostEstimate(flops=1, transcendentals=0, bytes_accessed=1),
        name="expert_layer",
    )(*operands)


def padded_bf16(rows):
    return jnp.pad(rows.astype(bf16), ((0, ROWS - LEN), (0, 0)))


def per_device(
    inputs,
    norm_gains,
    qkv_weight,
    out_weight,
    router_weight,
    expert_in,
    expert_out,
    routes,
    priority,
    cotangent,
):
    place = Place()
    experts = expert_in.shape[1]
    rows = qkv_weight.shape[1]
    zero = jnp.zeros((1,), jnp.int32)
    attn_off, expert_off = zero, zero
    me = place.expert.astype(jnp.int32).reshape(1)
    attn_w, expert_w, tables = [], [], []
    for l in range(LAYERS):
        shard = jnp.concatenate([qkv_weight[l], jnp.swapaxes(out_weight[l], 0, 1)[:, None]], axis=1)
        full = gather_attention(place, shard.reshape(rows, -1))
        attn_w.append([full[j][None] for j in range(4)])
        expert_w.append([w[None] for w in gather_experts(place, expert_in[l], expert_out[l])])
        mine, theirs = slot_rows(place, routes[l], priority[l, 0], experts)
        tables.append(slot_tables(place, mine, place.swap(theirs, place.tensor_size)))
    hidden_in, hidden_mid, qkv, ctx = {}, {}, {}, {}
    base, pieces = inputs, []
    saved = None
    gain_list, router_list, in_list, out_list, attn_list = {}, {}, {}, {}, {}
    for l in range(LAYERS):
        last = l == LAYERS - 1
        hidden_in[l], hidden_mid[l], normed, qkv[l], ctx[l] = attention_forward(
            attn_off, base, pieces, [], norm_gains[l], attn_w[l]
        )
        images = exchange_rows(place, normed)
        block = expert_w[l][0].shape
        at = [(0, None)], [(1, None)]
        here = [(j, 0) for j in range(8)]
        if last:
            grads = exchange_rows(place, padded_bf16(cotangent)[None])
            plan = Plan(block, here, [(j + 8, 0) for j in range(8)], *at, [block] * 2, *at)
            result = expert_layer(
                plan, expert_off, me, tables[l], router_weight[l], images + grads, None, expert_w[l]
            )
            tail = send_rows(place, pair_rows(place, result[:2]))
            result = result[2:]
            outputs = hidden_mid[l] + sum(p.astype(f32) for p in tail)
        else:
            plan = Plan(block, here, None, *at, None, None, None)
            *result, sent, expert_y = expert_layer(
                plan, expert_off, me, tables[l], router_weight[l], images, None, expert_w[l]
            )
            base, pieces = hidden_mid[l], send_rows(place, pair_rows(place, result))
            saved = [sent, expert_y]
    base = cotangent
    for l in reversed(range(LAYERS)):
        back = send_rows(place, pair_rows(place, result[:2]))
        router_list[l], *pieces = result[2:]
        in_list[l], out_list[l] = scatter_experts(place, pieces[0][0], pieces[1][0])
        base, branch, gain_list[l], *parts = attention_backward(
            attn_off, base, back, hidden_in[l], hidden_mid[l], norm_gains[l], attn_w[l], qkv[l], ctx[l],
            ROWS if l else LEN,
        )
        if l:
            grads = exchange_rows(place, branch[None])
            plan = Plan(block, None, here, *at, [block] * 2, *at)
            result = expert_layer(
                plan, expert_off, me, tables[l - 1], router_weight[l - 1], grads, saved, expert_w[l - 1]
            )
        total = scatter_attention(place, jnp.concatenate(parts), rows)
        attn_list[l] = total.astype(f32).reshape(rows, 4, -1)
    gains = jnp.stack([gain_list[l] for l in range(LAYERS)])
    router = jnp.stack([router_list[l] for l in range(LAYERS)])
    small = jnp.concatenate([gains.reshape(-1), router.reshape(-1)]).reshape(-1, 512)
    for bit in range(place.count.bit_length() - 1):
        small = small + place.swap(small, 1 << bit)
    small = small.reshape(-1)
    gains, router = small[: gains.size].reshape(gains.shape), small[gains.size :].reshape(router.shape)
    return (
        outputs[:LEN].astype(bf16),
        base,
        gains,
        jnp.stack([attn_list[l][:, :3] for l in range(LAYERS)]),
        jnp.stack([jnp.swapaxes(attn_list[l][:, 3], 0, 1) for l in range(LAYERS)]),
        router,
        jnp.stack([in_list[l] for l in range(LAYERS)]),
        jnp.stack([out_list[l] for l in range(LAYERS)]),
    )


CORE, Y, X, NEAR, FAR = 1, 2, 4, 8, 16


def tie(*values):
    return lax.optimization_barrier(values)


def expert_blocks(place, w_in, w_out):
    order = place.expert ^ jnp.arange(w_in.shape[0])
    return jnp.stack([w_in[order], jnp.swapaxes(w_out, 1, 2)[order]])


def plane_blocks(place, blocks):
    two, count, rows, width = blocks.shape
    odd = place.swap(blocks[:, 1::2], CORE)
    pair = jnp.stack([blocks[:, 0::2], odd], axis=2)
    got = [pair[:, 0]] + [place.swap(pair[:, k], 2 * k) for k in (1, 2, 3)]
    return jnp.stack(got, axis=1).reshape(two, 2, count // 2, rows, width)


def mixed(place, value, even, odd):
    pairs = [(i, i ^ (odd if i & CORE else even)) for i in range(place.count)]
    return lax.ppermute(value, AXES, pairs)


def attention_shard(qkv_weight, out_weight):
    shard = jnp.concatenate([qkv_weight, jnp.swapaxes(out_weight, 0, 1)[:, None]], axis=1)
    return shard.reshape(shard.shape[0], -1)


def widen(place, held, mask):
    return jnp.concatenate([held, place.swap(held, mask)])


def halve(place, held, mask):
    half = held.shape[0] // 2
    return held[:half] + place.swap(held[half:], mask)


def plane_sums(place, mine):
    shape = mine.shape
    return plane_blocks(place, mine.reshape((2, -1) + shape[3:])).reshape((2, -1) + shape[3:])


def unpack_sums(place, got):
    got = got[:, place.expert ^ jnp.arange(got.shape[1])].astype(f32)
    return got[0], jnp.swapaxes(got[1], 1, 2)


def per_device_plane(
    inputs,
    norm_gains,
    qkv_weight,
    out_weight,
    router_weight,
    expert_in,
    expert_out,
    routes,
    priority,
    cotangent,
):
    place = Place()
    swap = place.swap
    experts = expert_in.shape[1]
    rows = qkv_weight.shape[1]
    attn_order = [x | n * 2 | f * 4 for x in (0, 1) for n in (0, 1) for f in (0, 1)]
    attn_off = ((place.dp ^ jnp.array(attn_order, jnp.int32)) * rows).astype(jnp.int32)
    core = place.tensor & CORE
    replica = jnp.stack([jnp.zeros_like(core), 4 - 2 * core, 2 + 2 * core, 6 + 0 * core])
    expert_off = ((place.dp ^ replica[:, None] ^ jnp.arange(2)[None, :]) * rows).reshape(-1).astype(jnp.int32)
    me = place.expert.astype(jnp.int32).reshape(1)
    block = (2, place.tensor_size, rows, expert_in.shape[3])

    own0 = plane_blocks(place, expert_blocks(place, expert_in[0], expert_out[0]))
    held = jnp.stack([attention_shard(qkv_weight[l], out_weight[l]) for l in (0, 1)])[None]
    held = widen(place, widen(place, held, FAR), NEAR)
    held, own0 = tie(held, own0)
    a0 = mixed(place, own0, FAR, NEAR)
    held0 = widen(place, held[:, 0], X)
    over0 = swap(held0, Y)
    over0, a0, blocks1 = tie(over0, a0, expert_blocks(place, expert_in[1], expert_out[1]))
    b0, c0 = mixed(place, own0, NEAR, FAR), mixed(place, a0, NEAR, FAR)
    weights0 = [held0, swap(held0, CORE), over0, swap(over0, CORE)]
    own1 = plane_blocks(place, blocks1)

    hidden_in0, hidden_mid0, normed, qkv0, ctx0 = attention_forward(
        attn_off, inputs, [], [], norm_gains[0], weights0
    )
    normed, own1 = tie(normed, own1)
    slots = [slot_rows(place, routes[l], priority[l, 0], experts) for l in (0, 1)]
    images = exchange_rows(place, normed)
    images[6], held1, theirs = tie(images[6], held[:, 1], jnp.stack([s[1] for s in slots]))
    theirs = swap(theirs, X)
    tables = [slot_tables(place, slots[l][0], theirs[l]) for l in (0, 1)]
    held1 = widen(place, held1, X)
    over1 = swap(held1, Y)
    weights1 = [held1, swap(held1, CORE), over1, swap(over1, CORE)]
    b0, c0, own1 = tie(b0, c0, own1)
    a1 = mixed(place, own1, FAR, NEAR)
    first = [(j, 0) for j in range(8)]
    second = [(j, 1) for j in range(8)]
    parts = [[(m, io) for m in range(4)] for io in (0, 1)]
    *rows0, sent, expert_y = expert_layer(
        Plan(block, first, None, *parts, None, None, None),
        expert_off, me, tables[0], router_weight[0], images, None, [own0, a0, b0, c0],
    )
    rows0[0], weights1[2] = tie(rows0[0], weights1[2])
    pieces = send_rows(place, pair_rows(place, rows0))
    *pieces, a1, own1 = tie(*pieces, a1, own1)
    b1, c1 = mixed(place, own1, NEAR, FAR), mixed(place, a1, NEAR, FAR)
    hidden_in1, hidden_mid1, normed, qkv1, ctx1 = attention_forward(
        attn_off, hidden_mid0, pieces, [cotangent], norm_gains[1], weights1
    )
    images = exchange_rows(place, normed)
    grad_shapes = [(2,) + block] * 4
    result = expert_layer(
        Plan(block, first, second, *parts, grad_shapes, *parts),
        expert_off, me, tables[1], router_weight[1], images, None, [own1, a1, b1, c1],
    )
    out_rows, back_rows, router1, (own, a, b, c) = result[:2], result[2:4], result[4], result[5:]

    b, c = mixed(place, b, NEAR, FAR), mixed(place, c, NEAR, FAR)
    pieces = send_rows(place, pair_rows(place, back_rows))
    grad1, branch, gains1, *parts1 = attention_backward(
        attn_off, cotangent, pieces, hidden_in1, hidden_mid1, norm_gains[1], weights1, qkv1, ctx1, ROWS
    )
    images = exchange_rows(place, branch[None])
    tied = tie(*images, a, b, c, *parts1)
    images, (a, b, c), parts1 = tied[:8], tied[8:11], tied[11:]
    a = mixed(place, a + c, FAR, NEAR)
    near1, far1 = parts1[0] + swap(parts1[1], CORE), parts1[2] + swap(parts1[3], CORE)
    far1 = swap(far1, Y)
    result = expert_layer(
        Plan(block, None, first, *parts, grad_shapes, *parts),
        expert_off, me, tables[0], router_weight[0], images, [sent, expert_y], [own0, a0, b0, c0],
    )
    back_rows, router0, (own0, a0, b0, c0) = list(result[:2]), result[2], result[3:]
    back_rows[0], far1 = tie(back_rows[0], far1)
    attn_sum1 = near1 + far1
    c0 = mixed(place, c0, NEAR, FAR)
    pieces = send_rows(place, pair_rows(place, back_rows))
    tied = tie(*pieces, a, b, own, *out_rows)
    pieces, (a, b, own), out_rows = tied[:4], tied[4:7], tied[7:]
    tail = send_rows(place, pair_rows(place, out_rows))
    grad0, unused, gains0, *parts0 = attention_backward(
        attn_off, grad1, pieces, hidden_in0, hidden_mid0, norm_gains[0], weights0, qkv0, ctx0, LEN
    )
    gains0, c0, b0, a, b, own, *tail = tie(gains0, c0, b0, a, b, own, *tail)
    a0, b0 = mixed(place, a0 + c0, FAR, NEAR), mixed(place, b0, NEAR, FAR)
    outputs = hidden_mid1 + sum(p.astype(f32) for p in tail)
    sum1 = plane_sums(place, own + b + a)
    near0, far0 = parts0[0] + swap(parts0[1], CORE), parts0[2] + swap(parts0[3], CORE)
    far0, sum1 = tie(far0, sum1)
    attn_sum0 = near0 + swap(far0, Y)
    attn_sum = halve(place, jnp.stack([attn_sum0, attn_sum1], axis=1), X)
    gains, router = jnp.stack([gains0, gains1]), jnp.stack([router0, router1])
    small = jnp.concatenate([gains.reshape(-1), router.reshape(-1)]).reshape(-1, 512)
    for mask in (CORE, Y, X):
        small = small + swap(small, mask)
    small, attn_sum, a0, b0 = tie(small, attn_sum, a0, b0)
    for mask in (NEAR, FAR):
        attn_sum = halve(place, attn_sum, mask)
        small = small + swap(small, mask)
    in1, out1 = unpack_sums(place, sum1)
    in0, out0 = unpack_sums(place, plane_sums(place, own0 + a0 + b0))
    small = small.reshape(-1)
    gains, router = small[: gains.size].reshape(gains.shape), small[gains.size :].reshape(router.shape)
    attn = attn_sum.astype(f32).reshape(2, rows, 4, -1)
    return (
        outputs[:LEN].astype(bf16),
        grad0,
        gains,
        attn[:, :, :3],
        jnp.swapaxes(attn[:, :, 3], 1, 2),
        router,
        jnp.stack([in0, in1]),
        jnp.stack([out0, out1]),
    )


def solution(mesh):
    in_specs = (
        P(("dp", "tensor"), None),
        P(),
        P(None, "dp", None, "tensor"),
        P(None, "tensor", "dp"),
        P(),
        P(None, None, "dp", "tensor"),
        P(None, None, "tensor", "dp"),
        P(None, "dp", None),
        P(None, "dp", None),
        P(("dp", "tensor"), None),
    )
    out_specs = (
        P(("dp", "tensor"), None),
        P(("dp", "tensor"), None),
        P(),
        P(None, "dp", None, "tensor"),
        P(None, "tensor", "dp"),
        P(),
        P(None, None, "dp", "tensor"),
        P(None, None, "tensor", "dp"),
    )
    fast = mesh.shape["dp"] == 8 and mesh.shape["tensor"] == 4 and LAYERS == 2
    return jax.shard_map(
        per_device_plane if fast else per_device, mesh=mesh, in_specs=in_specs, out_specs=out_specs, check_vma=False
    )
```

time: 525 us -> 459 us (0.87)
  Pallas kernels: 0 us -> 99.1 us
  matrix products: 68.3 us -> 1.2 us
  local copies, waits for them, and re-layouts: 81.6 us -> 44.4 us
  other arithmetic: 60.6 us -> 25.9 us
  between operations: 17 us -> 2.06 us
  waiting for transfers between devices: 210 us -> 198 us
    pallas_call x0 -> x11, Pallas kernels: none -> 99.1 us  [the longest x3 49.9 us: expert_layer(): pl.pallas_call(lambda *refs: expert_kernel(plan, *refs), out_shape=tuple(...]
    ppermute x0 -> x12, waiting for transfers between devices: none -> 65.9 us  [mixed(): return lax.ppermute(value, AXES, pairs)]
    dot_general x48 -> x2, matrix products: 65.6 us -> 1.2 us  [mm(): return jnp.einsum(spec, *args, preferred_element_type=f32)]
    ppermute x75 -> x78, waiting for transfers between devices: 173 us -> 132 us  [swap(): return lax.ppermute(value, AXES, pairs)]
    all_gather x2 -> x0, waiting for transfers between devices: 36.9 us -> none  [gather_experts(): lax.all_gather(got, 'dp', axis=0, tiled=False, axis_index_groups=place.dp...]
    another operation x33 -> x12, local copies, waits for them, and re-layouts: 26 us -> 3.3 us  [the longest x4 1.47 us: plane_blocks(): pair = jnp.stack([blocks[:, 0::2], odd], axis=2)]
    ppermute x0 -> x12, starting transfers between devices: none -> 13.8 us  [mixed(): return lax.ppermute(value, AXES, pairs)]
    another operation x36 -> x16, other arithmetic: 26.4 us -> 12.6 us  [the longest x3 3.67 us: per_device_plane(): attn_sum = halve(place, jnp.stack([attn_sum0, attn_sum1], axis=1), X)]
  transfers between devices with their start and end apart: 79 -> 90, of which waited for: 37 -> 46; matrix products, arithmetic and copies ran while one was open for 33% -> 10% of each run, Pallas kernels for 0% -> 15%
where the time goes in v2:
time: 459 us; the launch traced here: 450 us
  waiting for transfers between devices  198 us (43%)
  Pallas kernels  99.1 us (22%)
  starting transfers between devices  80 us (17%)
  local copies, waits for them, and re-layouts  44.4 us (10%)
  other arithmetic  25.9 us (6%)
    ppermute x78, waiting for transfers between devices, swap(): return lax.ppermute(value, AXES, pairs)  132 us
    ppermute x78, starting transfers between devices, swap(): return lax.ppermute(value, AXES, pairs)  66.2 us
    ppermute x12, waiting for transfers between devices, mixed(): return lax.ppermute(value, AXES, pairs)  65.9 us
    pallas_call x3, Pallas kernels, expert_layer(): pl.pallas_call(lambda *refs: expert_kernel(plan, *refs), out_shape=tuple(...  49.9 us
    pallas_call x2, Pallas kernels, attention_backward(): pl.pallas_call(attention_backward_kernel, out_shape=(shape((out_rows, wid...  24.9 us
    unnamed x154, local copies, waits for them, and re-layouts  17.6 us
    pallas_call x2, Pallas kernels, attention_forward(): pl.pallas_call(lambda *refs: attention_forward_kernel(len(pieces), len(ex...  15 us
    ppermute x12, starting transfers between devices, mixed(): return lax.ppermute(value, AXES, pairs)  13.8 us
  transfers between devices with their start and end apart: 90, of which 46 were waited for; matrix products, arithmetic and copies ran while one was open for 10% of the time, Pallas kernels for 15%

profile of v2, /device:TPU:0, one launch (start us, length us, event | category | flops | bytes accessed | tf_op | source)
XLA Modules:
  0.0 450.2 jit_solution(11536971764827137545)
XLA Ops:
  2.4 4.1 collective-permute-start
  13.3 1.6 collective-permute-start.1
  18.6 3.0 collective-permute-done.1
  21.7 7.0 %collective-permute-done.3 = bf16[2,2,64,512]{3,2,0,1:T(8,128)(2,1)S(1)} collective-permute-done((bf16[2,2,64,512]{3,2,0,1:T(8,128)(2,1)S(1)}, bf16[2,2,64,512]{3,2,0,1:T(8,128)(2,1)S(1)}, u32[]{:S(2)}, u32[]{:S(2)}) %collective-permute-start.3) | collective-permute-done | bytes 262176 | tf_op jit(solution)/shard_map/ppermute | solution.py:36
  31.9 2.0 collective-permute-start.9
  34.6 2.7 collective-permute-done.6
  40.2 8.8 %collective-permute-done.8.refs_5_.w2 = bf16[8,64,512]{2,1,0:T(8,128)(2,1)S(1)} collective-permute-done((bf16[8,64,512]{2,1,0:T(8,128)(2,1)S(1)}, bf16[8,64,512]{2,1,0:T(8,128)(2,1)S(1)}, u32[]{:S(2)}, u32[]{:S(2)}) %collective-permute-start.8) | collective-permute-done | bytes 524320 | tf_op jit(solution)/shard_map/ppermute | solution.py:36
  49.0 9.8 %collective-permute-done.9.refs_14_.refs_16_ = bf16[2,2,4,64,512]{4,3,2,1,0:T(8,128)(2,1)S(1)} collective-permute-done((bf16[2,2,4,64,512]{4,3,2,1,0:T(8,128)(2,1)S(1)}, bf16[2,2,4,64,512]{4,3,2,1,0:T(8,128)(2,1)S(1)}, u32[]{:S(2)}, u32[]{:S(2)}) %collective-permute-start.9) | collective-permute-done | bytes 1048608 | tf_op jit(solution)/shard_map/ppermute | solution.py:741
  61.5 2.1 collective-permute-start.24
  63.5 2.3 fusion.26
  71.8 7.1 %attention_forward.2 = (f32[200,512]{1,0:T(8,128)}, f32[200,512]{1,0:T(8,128)}, bf16[1,200,512]{2,1,0:T(8,128)(2,1)}, bf16[200,1536]{1,0:T(8,128)(2,1)}, bf16[200,512]{1,0:T(8,128)(2,1)}) custom-call(s32[8]{0:T(128)} %xor_multiply_fusion.1.refs_0_.off_ref, bf16[197,512]{1,0:T(8,128)(2,1)} %refs_1_.1, f32[2,512]{1,0:T(2,128)} %get-tuple-element.329.refs_2_.gains, ...), custom_call_target="tpu_custom_call" | custom-call | flops 1 | bytes 1 | tf_op jit(solution)/shard_map/attention_forward/pallas_call | solution.py:285
  78.9 2.0 collective-permute-done.12
  87.0 5.3 %collective-permute-done.15.refs_11_ = bf16[1,200,512]{2,1,0:T(8,128)(2,1)} collective-permute-done((bf16[1,200,512]{2,1,0:T(8,128)(2,1)S(1)}, bf16[1,200,512]{2,1,0:T(8,128)(2,1)}, u32[]{:S(2)}, u32[]{:S(2)}) %collective-permute-start.15) | collective-permute-done | bytes 204832 | tf_op jit(solution)/shard_map/ppermute | solution.py:36
  97.9 2.9 collective-permute-done.18.refs_7_
  100.8 8.6 %collective-permute-done.24.refs_16_.refs_18_ = bf16[2,2,4,64,512]{4,3,2,1,0:T(8,128)(2,1)} collective-permute-done((bf16[2,2,4,64,512]{4,3,2,1,0:T(8,128)(2,1)S(1)}, bf16[2,2,4,64,512]{4,3,2,1,0:T(8,128)(2,1)}, u32[]{:S(2)}, u32[]{:S(2)}) %collective-permute-start.24) | collective-permute-done | bytes 1048608 | tf_op jit(solution)/shard_map/ppermute | solution.py:741
  114.9 10.5 %expert_layer.3 = (bf16[4,200,512]{2,1,0:T(8,128)(2,1)}, bf16[4,200,512]{2,1,0:T(8,128)(2,1)}, bf16[512,512]{1,0:T(8,128)(2,1)}, f32[512,512]{1,0:T(8,128)}) custom-call(s32[8]{0:T(128)} %mul.21.refs_0_, s32[1]{0:T(128)} %bitcast.33.refs_1_, s32[8,200]{1,0:T(8,128)} %copy-done.60, s32[200,8]{1,0:T(8,128)} %bitcast.195, bf16[512,8]{1,0:T(8,128)(2,1)} %bitcast.193, ...), custom_call_target="tpu_custom_call" | custom-call | flops 1 | bytes 1 | tf_op jit(solution)/shard_map/expert_layer/pallas_call | solution.py:612
  126.1 1.9 collective-permute-done.27.odd
  128.9 2.3 add_rows.4
  132.3 4.2 collective-permute-done.31.refs_14_
  139.9 4.2 collective-permute-done.30.refs_5_
  145.2 7.9 %attention_forward.3 = (f32[200,512]{1,0:T(8,128)}, f32[200,512]{1,0:T(8,128)}, bf16[2,200,512]{2,1,0:T(8,128)(2,1)}, bf16[200,1536]{1,0:T(8,128)(2,1)}, bf16[200,512]{1,0:T(8,128)(2,1)}) custom-call(s32[8]{0:T(128)} %xor_multiply_fusion.1.refs_0_.off_ref, f32[200,512]{1,0:T(8,128)} %get-tuple-element.133.refs_1_.hidden_mid, ...), custom_call_target="tpu_custom_call" | custom-call | flops 1 | bytes 1 | tf_op jit(solution)/shard_map/attention_forward/pallas_call | solution.py:285
  158.6 8.0 %collective-permute-done.39.refs_11_ = bf16[2,200,512]{2,1,0:T(8,128)(2,1)S(1)} collective-permute-done((bf16[2,200,512]{2,1,0:T(8,128)(2,1)}, bf16[2,200,512]{2,1,0:T(8,128)(2,1)S(1)}, u32[]{:S(2)}, u32[]{:S(2)}) %collective-permute-start.39) | collective-permute-done | bytes 409632 | tf_op jit(solution)/shard_map/ppermute | solution.py:36
  166.7 4.5 collective-permute-done.37.refs_9_
  171.2 1.9 collective-permute-done.35.refs_7_
  179.0 2.0 gather_fusion.5
  185.1 15.6 %collective-permute-done.42.refs_16_ = bf16[2,2,4,64,512]{4,3,2,1,0:T(8,128)(2,1)S(1)} collective-permute-done((bf16[2,2,4,64,512]{4,3,2,1,0:T(8,128)(2,1)}, bf16[2,2,4,64,512]{4,3,2,1,0:T(8,128)(2,1)S(1)}, u32[]{:S(2)}, u32[]{:S(2)}) %collective-permute-start.42) | collective-permute-done | bytes 1048608 | tf_op jit(solution)/shard_map/ppermute | solution.py:741
  201.7 22.1 %expert_layer.4 = (bf16[4,200,512]{2,1,0:T(8,128)(2,1)}, bf16[4,200,512]{2,1,0:T(8,128)(2,1)}, bf16[4,200,512]{2,1,0:T(8,128)(2,1)}, bf16[4,200,512]{2,1,0:T(8,1...) custom-call(s32[8]{0:T(128)} %mul.21.refs_0_, ...), custom_call_target="tpu_custom_call" | custom-call | flops 1 | bytes 1 | tf_op jit(solution)/shard_map/expert_layer/pallas_call | solution.py:612
  223.9 1.7 collective-permute-start.54
  227.4 2.3 add_rows.5
  233.2 4.0 collective-permute-done.44.p1
  237.2 1.7 collective-permute-done.45.p2
  238.9 3.9 collective-permute-done.46.p3
  243.5 12.4 %attention_backward.2 = (f32[200,512]{1,0:T(8,128)}, bf16[200,512]{1,0:T(8,128)(2,1)}, f32[2,512]{1,0:T(2,128)}, bf16[8,64,512]{2,1,0:T(8,128)(2,1)}, bf16[8,64,...) custom-call(s32[8]{0:T(128)} %xor_multiply_fusion.1.refs_0_.off_ref, f32[197,512]{1,0:T(8,128)} %base.1, ...), custom_call_target="tpu_custom_call" | custom-call | flops 1 | bytes 1 | tf_op jit(solution)/shard_map/attention_backward/pallas_call | solution.py:375
  255.9 2.1 collective-permute-start.52
  259.5 5.6 %collective-permute-done.52.refs_11_ = bf16[1,200,512]{2,1,0:T(8,128)(2,1)S(1)} collective-permute-done((bf16[1,200,512]{2,1,0:T(8,128)(2,1)}, bf16[1,200,512]{2,1,0:T(8,128)(2,1)S(1)}, u32[]{:S(2)}, u32[]{:S(2)}) %collective-permute-start.52) | collective-permute-done | bytes 204832 | tf_op jit(solution)/shard_map/ppermute | solution.py:36
  265.1 2.2 collective-permute-done.50.refs_9_
  267.8 4.8 %collective-permute-done.55 = bf16[2,2,4,64,512]{4,3,2,1,0:T(8,128)(2,1)S(1)} collective-permute-done((bf16[2,2,4,64,512]{4,3,2,1,0:T(8,128)(2,1)}, bf16[2,2,4,64,512]{4,3,2,1,0:T(8,128)(2,1)S(1)}, u32[]{:S(2)}, u32[]{:S(2)}) %collective-permute-start.55) | collective-permute-done | bytes 1048608 | tf_op jit(solution)/shard_map/ppermute | solution.py:741
  273.9 2.1 collective-permute-start.62
  276.0 17.2 %expert_layer.5 = (bf16[4,200,512]{2,1,0:T(8,128)(2,1)}, bf16[4,200,512]{2,1,0:T(8,128)(2,1)}, f32[512,8]{1,0:T(8,128)}, bf16[2,2,4,64,512]{4,3,2,1,0:T(8,128)(2...) custom-call(s32[8]{0:T(128)} %mul.21.refs_0_, ...), custom_call_target="tpu_custom_call" | custom-call | flops 1 | bytes 1 | tf_op jit(solution)/shard_map/expert_layer/pallas_call | solution.py:612
  293.5 1.6 collective-permute-start.57
  295.1 12.8 %collective-permute-done.57 = bf16[8,64,512]{2,1,0:T(8,128)(2,1)} collective-permute-done((bf16[8,64,512]{2,1,0:T(8,128)(2,1)S(1)}, bf16[8,64,512]{2,1,0:T(8,128)(2,1)}, u32[]{:S(2)}, u32[]{:S(2)}) %collective-permute-start.57) | collective-permute-done | bytes 524320 | tf_op jit(solution)/shard_map/ppermute | solution.py:36
  308.9 2.3 add_rows.6
  315.0 3.5 collective-permute-done.59.p1
  318.5 2.5 collective-permute-done.60.p2
  321.0 2.7 collective-permute-done.61.p3
  324.3 2.5 collective-permute-done.64.odd
  327.8 2.3 add_rows.7
  333.6 12.5 %attention_backward.3 = (f32[197,512]{1,0:T(8,128)}, bf16[200,512]{1,0:T(8,128)(2,1)}, f32[2,512]{1,0:T(2,128)}, bf16[8,64,512]{2,1,0:T(8,128)(2,1)}, bf16[8,64,...) custom-call(s32[8]{0:T(128)} %xor_multiply_fusion.1.refs_0_.off_ref, ...), custom_call_target="tpu_custom_call" | custom-call | flops 1 | bytes 1 | tf_op jit(solution)/shard_map/attention_backward/pallas_call | solution.py:375
  346.2 1.8 add_add_fusion.1
  350.2 1.6 collective-permute-start.74
  354.5 9.8 %collective-permute-done.74 = bf16[2,2,64,512]{3,2,0,1:T(8,128)(2,1)S(1)} collective-permute-done((bf16[2,2,64,512]{3,2,0,1:T(8,128)(2,1)S(1)}, bf16[2,2,64,512]{3,2,0,1:T(8,128)(2,1)S(1)}, u32[]{:S(2)}, u32[]{:S(2)}) %collective-permute-start.74) | collective-permute-done | bytes 262176 | tf_op jit(solution)/shard_map/ppermute | solution.py:36
  371.7 2.1 collective-permute-start.81
  373.8 5.0 %collective-permute-done.77 = bf16[8,64,512]{2,1,0:T(8,128)(2,1)} collective-permute-done((bf16[8,64,512]{2,1,0:T(8,128)(2,1)S(1)}, bf16[8,64,512]{2,1,0:T(8,128)(2,1)}, u32[]{:S(2)}, u32[]{:S(2)}) %collective-permute-start.77) | collective-permute-done | bytes 524320 | tf_op jit(solution)/shard_map/ppermute | solution.py:36
  385.4 2.6 collective-permute-done.69
  388.6 1.8 fusion.10
  390.4 3.8 collective-permute-done.70
  396.1 22.8 %collective-permute-done.80 = bf16[2,2,4,64,512]{4,3,2,1,0:T(8,128)(2,1)} collective-permute-done((bf16[2,2,4,64,512]{4,3,2,1,0:T(8,128)(2,1)}, bf16[2,2,4,64,512]{4,3,2,1,0:T(8,128)(2,1)}, u32[]{:S(2)}, u32[]{:S(2)}) %collective-permute-start.80) | collective-permute-done | bytes 1048608 | tf_op jit(solution)/shard_map/ppermute | solution.py:741
  418.9 1.7 add_add_fusion
  420.9 2.1 collective-permute-start.84
  423.5 2.0 collective-permute-done.82
  426.0 2.8 collective-permute-done.84
  429.5 1.9 collective-permute-start.85
  432.6 2.0 collective-permute-start.89
  440.4 1.7 collective-permute-done.87
  (397 shorter events, 125.2 us)
Async XLA Ops:
  2.4 10.8 %collective-permute-start = (bf16[1,2,64,512]{3,2,0,1:T(8,128)(2,1)S(1)}, bf16[1,2,64,512]{3,2,0,1:T(8,128)(2,1)S(1)}, u32[]{:S(2)}, u32[]{:S(2)}) collective-permute-start(bf16[1,2,64,512]{3,2,0,1:T(8,128)(2,1)S(1)} %maximum_bitcast_fusion), channel_id=1, source_target_pairs={{0,16},{1,17},{2,18},{3,19},{4,20},{5,21},{6,22},{7,23},{8,24},{9,... | collective-permute-start | bytes 393224 | tf_op jit(solution)/shard_map/ppermute | solution.py:36
  13.3 8.4 %collective-permute-start.1 = (bf16[2,2,64,512]{3,2,0,1:T(8,128)(2,1)S(1)}, bf16[2,2,64,512]{3,2,0,1:T(8,128)(2,1)S(1)}, u32[]{:S(2)}, u32[]{:S(2)}) collective-permute-start(bf16[2,2,64,512]{3,2,0,1:T(8,128)(2,1)S(1)} %pad_maximum_fusion.16), channel_id=1, source_target_pairs={{0,8},{1,9},{2,10},{3,11},{4,12},{5,13},{6,14},{7,15},{8,0},{9,1},... | collective-permute-start | bytes 786440 | tf_op jit(solution)/shard_map/ppermute | solution.py:36
  15.0 13.7 %collective-permute-start.3 = (bf16[2,2,64,512]{3,2,0,1:T(8,128)(2,1)S(1)}, bf16[2,2,64,512]{3,2,0,1:T(8,128)(2,1)S(1)}, u32[]{:S(2)}, u32[]{:S(2)}) collective-permute-start(bf16[2,2,64,512]{3,2,0,1:T(8,128)(2,1)S(1)} %get-tuple-element.309), channel_id=1, source_target_pairs={{0,2},{1,3},{2,0},{3,1},{4,6},{5,7},{6,4},{7,5},{8,10},{9,11},{10,... | collective-permute-start | bytes 786440 | tf_op jit(solution)/shard_map/ppermute | solution.py:36
  16.6 12.1 %collective-permute-start.5 = (bf16[2,2,64,512]{3,2,0,1:T(8,128)(2,1)S(1)}, bf16[2,2,64,512]{3,2,0,1:T(8,128)(2,1)S(1)}, u32[]{:S(2)}, u32[]{:S(2)}) collective-permute-start(bf16[2,2,64,512]{3,2,0,1:T(8,128)(2,1)S(1)} %get-tuple-element.310), channel_id=1, source_target_pairs={{0,6},{1,7},{2,4},{3,5},{4,2},{5,3},{6,0},{7,1},{8,14},{9,15},{10,... | collective-permute-start | bytes 786440 | tf_op jit(solution)/shard_map/ppermute | solution.py:36
  18.0 11.9 %collective-permute-start.4 = (bf16[2,2,64,512]{3,2,0,1:T(8,128)(2,1)S(1)}, bf16[2,2,64,512]{3,2,0,1:T(8,128)(2,1)S(1)}, u32[]{:S(2)}, u32[]{:S(2)}) collective-permute-start(bf16[2,2,64,512]{3,2,0,1:T(8,128)(2,1)S(1)} %get-tuple-element.311), channel_id=1, source_target_pairs={{0,4},{1,5},{2,6},{3,7},{4,0},{5,1},{6,2},{7,3},{8,12},{9,13},{10,... | collective-permute-start | bytes 786440 | tf_op jit(solution)/shard_map/ppermute | solution.py:36
  31.9 26.9 %collective-permute-start.9 = (bf16[2,2,4,64,512]{4,3,2,1,0:T(8,128)(2,1)S(1)}, bf16[2,2,4,64,512]{4,3,2,1,0:T(8,128)(2,1)S(1)}, u32[]{:S(2)}, u32[]{:S(2)}) collective-permute-start(bf16[2,2,4,64,512]{4,3,2,1,0:T(8,128)(2,1)S(1)} %bitcast.177), channel_id=1, source_target_pairs={{0,16},{1,9},{2,18},{3,11},{4,20},{5,13},{6,22},{7,15},{8,24},{9,1... | collective-permute-start | bytes 3145736 | tf_op jit(solution)/shard_map/ppermute | solution.py:741
  37.3 11.7 %collective-permute-start.8 = (bf16[8,64,512]{2,1,0:T(8,128)(2,1)S(1)}, bf16[8,64,512]{2,1,0:T(8,128)(2,1)S(1)}, u32[]{:S(2)}, u32[]{:S(2)}) collective-permute-start(bf16[8,64,512]{2,1,0:T(8,128)(2,1)S(1)} %pad_maximum_fusion.10.refs_3_.w0), channel_id=1, source_target_pairs={{0,2},{1,3},{2,0},{3,1},{4,6},{5,7},{6,4},{7,5},{8,10},{9,11},{10,... | collective-permute-start | bytes 1572872 | tf_op jit(solution)/shard_map/ppermute | solution.py:36
  61.3 33.8 %collective-permute-start.23 = (bf16[2,2,4,64,512]{4,3,2,1,0:T(8,128)(2,1)S(1)}, bf16[2,2,4,64,512]{4,3,2,1,0:T(8,128)(2,1)}, u32[]{:S(2)}, u32[]{:S(2)}) collective-permute-start(bf16[2,2,4,64,512]{4,3,2,1,0:T(8,128)(2,1)S(1)} %bitcast.178), channel_id=1, source_target_pairs={{0,8},{1,17},{2,10},{3,19},{4,12},{5,21},{6,14},{7,23},{8,0},{9,25... | collective-permute-start | bytes 3145736 | tf_op jit(solution)/shard_map/ppermute | solution.py:741
  61.5 48.0 %collective-permute-start.24 = (bf16[2,2,4,64,512]{4,3,2,1,0:T(8,128)(2,1)S(1)}, bf16[2,2,4,64,512]{4,3,2,1,0:T(8,128)(2,1)}, u32[]{:S(2)}, u32[]{:S(2)}) collective-permute-start(bf16[2,2,4,64,512]{4,3,2,1,0:T(8,128)(2,1)S(1)} %collective-permute-done.9.refs_14_.refs_16_), channel_id=1, source_target_pairs={{0,8},{1,17},{2,10},{3,19},{4,12},{5,21},{6,14},{7,23},{8,0},{9,25... | collective-permute-start | bytes 3145736 | tf_op jit(solution)/shard_map/ppermute | solution.py:741
  65.8 15.1 %collective-permute-start.12 = (bf16[2,2,64,512]{3,2,0,1:T(8,128)(2,1)}, bf16[2,2,64,512]{3,2,0,1:T(8,128)(2,1)}, u32[]{:S(2)}, u32[]{:S(2)}) collective-permute-start(bf16[2,2,64,512]{3,2,0,1:T(8,128)(2,1)} %get-tuple-element.299), channel_id=1, source_target_pairs={{0,2},{1,3},{2,0},{3,1},{4,6},{5,7},{6,4},{7,5},{8,10},{9,11},{10,... | collective-permute-start | bytes 786440 | tf_op jit(solution)/shard_map/ppermute | solution.py:36
  67.4 13.5 %collective-permute-start.14 = (bf16[2,2,64,512]{3,2,0,1:T(8,128)(2,1)}, bf16[2,2,64,512]{3,2,0,1:T(8,128)(2,1)S(1)}, u32[]{:S(2)}, u32[]{:S(2)}) collective-permute-start(bf16[2,2,64,512]{3,2,0,1:T(8,128)(2,1)} %get-tuple-element.300), channel_id=1, source_target_pairs={{0,6},{1,7},{2,4},{3,5},{4,2},{5,3},{6,0},{7,1},{8,14},{9,15},{10,... | collective-permute-start | bytes 786440 | tf_op jit(solution)/shard_map/ppermute | solution.py:36
  69.0 13.0 %collective-permute-start.13 = (bf16[2,2,64,512]{3,2,0,1:T(8,128)(2,1)}, bf16[2,2,64,512]{3,2,0,1:T(8,128)(2,1)S(1)}, u32[]{:S(2)}, u32[]{:S(2)}) collective-permute-start(bf16[2,2,64,512]{3,2,0,1:T(8,128)(2,1)} %get-tuple-element.301), channel_id=1, source_target_pairs={{0,4},{1,5},{2,6},{3,7},{4,0},{5,1},{6,2},{7,3},{8,12},{9,13},{10,... | collective-permute-start | bytes 786440 | tf_op jit(solution)/shard_map/ppermute | solution.py:36
  83.3 9.0 %collective-permute-start.15 = (bf16[1,200,512]{2,1,0:T(8,128)(2,1)S(1)}, bf16[1,200,512]{2,1,0:T(8,128)(2,1)}, u32[]{:S(2)}, u32[]{:S(2)}) collective-permute-start(bf16[1,200,512]{2,1,0:T(8,128)(2,1)S(1)} %copy-done.37), channel_id=1, source_target_pairs={{0,6},{1,7},{2,4},{3,5},{4,2},{5,3},{6,0},{7,1},{8,14},{9,15},{10,... | collective-permute-start | bytes 614408 | tf_op jit(solution)/shard_map/ppermute | solution.py:36
  85.4 11.9 %collective-permute-start.20 = (bf16[1,200,512]{2,1,0:T(8,128)(2,1)S(1)}, bf16[1,200,512]{2,1,0:T(8,128)(2,1)}, u32[]{:S(2)}, u32[]{:S(2)}) collective-permute-start(bf16[1,200,512]{2,1,0:T(8,128)(2,1)S(1)} %copy-done.37), channel_id=1, source_target_pairs={{0,4},{1,5},{2,6},{3,7},{4,0},{5,1},{6,2},{7,3},{8,12},{9,13},{10,... | collective-permute-start | bytes 614408 | tf_op jit(solution)/shard_map/ppermute | solution.py:36
  92.8 16.9 %collective-permute-start.25 = (bf16[4,64,512]{2,1,0:T(8,128)(2,1)S(1)}, bf16[4,64,512]{2,1,0:T(8,128)(2,1)S(1)}, u32[]{:S(2)}, u32[]{:S(2)}) collective-permute-start(bf16[4,64,512]{2,1,0:T(8,128)(2,1)S(1)} %get-tuple-element.144), channel_id=1, source_target_pairs={{0,4},{1,5},{2,6},{3,7},{4,0},{5,1},{6,2},{7,3},{8,12},{9,13},{10,... | collective-permute-start | bytes 786440 | tf_op jit(solution)/shard_map/ppermute | solution.py:36
  96.8 14.3 %collective-permute-start.17 = (bf16[1,200,512]{2,1,0:T(8,128)(2,1)S(1)}, bf16[1,200,512]{2,1,0:T(8,128)(2,1)S(1)}, u32[]{:S(2)}, u32[]{:S(2)}) collective-permute-start(bf16[1,200,512]{2,1,0:T(8,128)(2,1)S(1)} %copy-done.37), channel_id=1, source_target_pairs={{0,1},{1,0},{2,3},{3,2},{4,5},{5,4},{6,7},{7,6},{8,9},{9,8},{10,11... | collective-permute-start | bytes 614408 | tf_op jit(solution)/shard_map/ppermute | solution.py:36
  97.4 16.7 %collective-permute-start.22 = (bf16[1,200,512]{2,1,0:T(8,128)(2,1)}, bf16[1,200,512]{2,1,0:T(8,128)(2,1)S(1)}, u32[]{:S(2)}, u32[]{:S(2)}) collective-permute-start(bf16[1,200,512]{2,1,0:T(8,128)(2,1)} %collective-permute-done.15.refs_11_), channel_id=1, source_target_pairs={{0,1},{1,0},{2,3},{3,2},{4,5},{5,4},{6,7},{7,6},{8,9},{9,8},{10,11... | collective-permute-start | bytes 614408 | tf_op jit(solution)/shard_map/ppermute | solution.py:36
  100.8 13.2 %collective-permute-start.21 = (bf16[1,200,512]{2,1,0:T(8,128)(2,1)}, bf16[1,200,512]{2,1,0:T(8,128)(2,1)S(1)}, u32[]{:S(2)}, u32[]{:S(2)}) collective-permute-start(bf16[1,200,512]{2,1,0:T(8,128)(2,1)} %collective-permute-done.20.refs_9_), channel_id=1, source_target_pairs={{0,1},{1,0},{2,3},{3,2},{4,5},{5,4},{6,7},{7,6},{8,9},{9,8},{10,11... | collective-permute-start | bytes 614408 | tf_op jit(solution)/shard_map/ppermute | solution.py:36
  109.8 26.8 %collective-permute-start.31 = (bf16[2,2,4,64,512]{4,3,2,1,0:T(8,128)(2,1)S(1)}, bf16[2,2,4,64,512]{4,3,2,1,0:T(8,128)(2,1)}, u32[]{:S(2)}, u32[]{:S(2)}) collective-permute-start(bf16[2,2,4,64,512]{4,3,2,1,0:T(8,128)(2,1)S(1)} %bitcast.183), channel_id=1, source_target_pairs={{0,16},{1,9},{2,18},{3,11},{4,20},{5,13},{6,22},{7,15},{8,24},{9,1... | collective-permute-start | bytes 3145736 | tf_op jit(solution)/shard_map/ppermute | solution.py:741
  111.0 14.9 %collective-permute-start.26 = (bf16[8,64,512]{2,1,0:T(8,128)(2,1)}, bf16[8,64,512]{2,1,0:T(8,128)(2,1)S(1)}, u32[]{:S(2)}, u32[]{:S(2)}) collective-permute-start(bf16[8,64,512]{2,1,0:T(8,128)(2,1)} %constant_dynamic-update-slice_fusion.refs_8_.w0), channel_id=1, source_target_pairs={{0,2},{1,3},{2,0},{3,1},{4,6},{5,7},{6,4},{7,5},{8,10},{9,11},{10,... | collective-permute-start | bytes 1572872 | tf_op jit(solution)/shard_map/ppermute | solution.py:36
  125.5 18.7 %collective-permute-start.32 = (bf16[8,64,512]{2,1,0:T(8,128)(2,1)}, bf16[8,64,512]{2,1,0:T(8,128)(2,1)S(1)}, u32[]{:S(2)}, u32[]{:S(2)}) collective-permute-start(bf16[8,64,512]{2,1,0:T(8,128)(2,1)} %constant_dynamic-update-slice_fusion.refs_8_.w0), channel_id=1, source_target_pairs={{0,1},{1,0},{2,3},{3,2},{4,5},{5,4},{6,7},{7,6},{8,9},{9,8},{10,11... | collective-permute-start | bytes 1572872 | tf_op jit(solution)/shard_map/ppermute | solution.py:36
  126.0 18.2 %collective-permute-start.33 = (bf16[8,64,512]{2,1,0:T(8,128)(2,1)S(1)}, bf16[8,64,512]{2,1,0:T(8,128)(2,1)S(1)}, u32[]{:S(2)}, u32[]{:S(2)}) collective-permute-start(bf16[8,64,512]{2,1,0:T(8,128)(2,1)S(1)} %collective-permute-done.26.refs_10_.w2), channel_id=1, source_target_pairs={{0,1},{1,0},{2,3},{3,2},{4,5},{5,4},{6,7},{7,6},{8,9},{9,8},{10,11... | collective-permute-start | bytes 1572872 | tf_op jit(solution)/shard_map/ppermute | solution.py:36
  131.8 8.2 %collective-permute-start.29 = (bf16[200,512]{1,0:T(8,128)(2,1)}, bf16[200,512]{1,0:T(8,128)(2,1)S(1)}, u32[]{:S(2)}, u32[]{:S(2)}) collective-permute-start(bf16[200,512]{1,0:T(8,128)(2,1)} %get-tuple-element.149), channel_id=1, source_target_pairs={{0,4},{1,5},{2,6},{3,7},{4,0},{5,1},{6,2},{7,3},{8,12},{9,13},{10,... | collective-permute-start | bytes 614408 | tf_op jit(solution)/shard_map/ppermute | solution.py:36
  153.0 13.6 %collective-permute-start.39 = (bf16[2,200,512]{2,1,0:T(8,128)(2,1)}, bf16[2,200,512]{2,1,0:T(8,128)(2,1)S(1)}, u32[]{:S(2)}, u32[]{:S(2)}) collective-permute-start(bf16[2,200,512]{2,1,0:T(8,128)(2,1)} %get-tuple-element.158.refs_5_), channel_id=1, source_target_pairs={{0,6},{1,7},{2,4},{3,5},{4,2},{5,3},{6,0},{7,1},{8,14},{9,15},{10,... | collective-permute-start | bytes 1228808 | tf_op jit(solution)/shard_map/ppermute | solution.py:36
  153.9 31.2 %collective-permute-start.41 = (bf16[2,2,4,64,512]{4,3,2,1,0:T(8,128)(2,1)S(1)}, bf16[2,2,4,64,512]{4,3,2,1,0:T(8,128)(2,1)S(1)}, u32[]{:S(2)}, u32[]{:S(2)}) collective-permute-start(bf16[2,2,4,64,512]{4,3,2,1,0:T(8,128)(2,1)S(1)} %bitcast.184), channel_id=1, source_target_pairs={{0,8},{1,17},{2,10},{3,19},{4,12},{5,21},{6,14},{7,23},{8,0},{9,25... | collective-permute-start | bytes 3145736 | tf_op jit(solution)/shard_map/ppermute | solution.py:741
  155.5 45.2 %collective-permute-start.42 = (bf16[2,2,4,64,512]{4,3,2,1,0:T(8,128)(2,1)}, bf16[2,2,4,64,512]{4,3,2,1,0:T(8,128)(2,1)S(1)}, u32[]{:S(2)}, u32[]{:S(2)}) collective-permute-start(bf16[2,2,4,64,512]{4,3,2,1,0:T(8,128)(2,1)} %collective-permute-done.31.refs_14_), channel_id=1, source_target_pairs={{0,8},{1,17},{2,10},{3,19},{4,12},{5,21},{6,14},{7,23},{8,0},{9,25... | collective-permute-start | bytes 3145736 | tf_op jit(solution)/shard_map/ppermute | solution.py:741
  155.9 15.3 %collective-permute-start.37 = (bf16[2,200,512]{2,1,0:T(8,128)(2,1)}, bf16[2,200,512]{2,1,0:T(8,128)(2,1)}, u32[]{:S(2)}, u32[]{:S(2)}) collective-permute-start(bf16[2,200,512]{2,1,0:T(8,128)(2,1)} %get-tuple-element.158.refs_5_), channel_id=1, source_target_pairs={{0,4},{1,5},{2,6},{3,7},{4,0},{5,1},{6,2},{7,3},{8,12},{9,13},{10,... | collective-permute-start | bytes 1228808 | tf_op jit(solution)/shard_map/ppermute | solution.py:36
  157.4 15.7 %collective-permute-start.35 = (bf16[2,200,512]{2,1,0:T(8,128)(2,1)}, bf16[2,200,512]{2,1,0:T(8,128)(2,1)}, u32[]{:S(2)}, u32[]{:S(2)}) collective-permute-start(bf16[2,200,512]{2,1,0:T(8,128)(2,1)} %get-tuple-element.158.refs_5_), channel_id=1, source_target_pairs={{0,2},{1,3},{2,0},{3,1},{4,6},{5,7},{6,4},{7,5},{8,10},{9,11},{10,... | collective-permute-start | bytes 1228808 | tf_op jit(solution)/shard_map/ppermute | solution.py:36
  171.2 13.9 %collective-permute-start.40 = (bf16[2,200,512]{2,1,0:T(8,128)(2,1)S(1)}, bf16[2,200,512]{2,1,0:T(8,128)(2,1)}, u32[]{:S(2)}, u32[]{:S(2)}) collective-permute-start(bf16[2,200,512]{2,1,0:T(8,128)(2,1)S(1)} %collective-permute-done.39.refs_11_), channel_id=1, source_target_pairs={{0,1},{1,0},{2,3},{3,2},{4,5},{5,4},{6,7},{7,6},{8,9},{9,8},{10,11... | collective-permute-start | bytes 1228808 | tf_op jit(solution)/shard_map/ppermute | solution.py:36
  173.1 12.0 %collective-permute-start.38 = (bf16[2,200,512]{2,1,0:T(8,128)(2,1)}, bf16[2,200,512]{2,1,0:T(8,128)(2,1)}, u32[]{:S(2)}, u32[]{:S(2)}) collective-permute-start(bf16[2,200,512]{2,1,0:T(8,128)(2,1)} %collective-permute-done.37.refs_9_), channel_id=1, source_target_pairs={{0,1},{1,0},{2,3},{3,2},{4,5},{5,4},{6,7},{7,6},{8,9},{9,8},{10,11... | collective-permute-start | bytes 1228808 | tf_op jit(solution)/shard_map/ppermute | solution.py:36
  173.1 12.0 %collective-permute-start.36 = (bf16[2,200,512]{2,1,0:T(8,128)(2,1)}, bf16[2,200,512]{2,1,0:T(8,128)(2,1)}, u32[]{:S(2)}, u32[]{:S(2)}) collective-permute-start(bf16[2,200,512]{2,1,0:T(8,128)(2,1)} %collective-permute-done.35.refs_7_), channel_id=1, source_target_pairs={{0,1},{1,0},{2,3},{3,2},{4,5},{5,4},{6,7},{7,6},{8,9},{9,8},{10,11... | collective-permute-start | bytes 1228808 | tf_op jit(solution)/shard_map/ppermute | solution.py:36
  223.9 35.6 %collective-permute-start.54 = (bf16[2,2,4,64,512]{4,3,2,1,0:T(8,128)(2,1)}, bf16[2,2,4,64,512]{4,3,2,1,0:T(8,128)(2,1)S(1)}, u32[]{:S(2)}, u32[]{:S(2)}) collective-permute-start(bf16[2,2,4,64,512]{4,3,2,1,0:T(8,128)(2,1)} %get-tuple-element.173), channel_id=1, source_target_pairs={{0,8},{1,17},{2,10},{3,19},{4,12},{5,21},{6,14},{7,23},{8,0},{9,25... | collective-permute-start | bytes 3145736 | tf_op jit(solution)/shard_map/ppermute | solution.py:741
  225.6 47.1 %collective-permute-start.55 = (bf16[2,2,4,64,512]{4,3,2,1,0:T(8,128)(2,1)}, bf16[2,2,4,64,512]{4,3,2,1,0:T(8,128)(2,1)S(1)}, u32[]{:S(2)}, u32[]{:S(2)}) collective-permute-start(bf16[2,2,4,64,512]{4,3,2,1,0:T(8,128)(2,1)} %get-tuple-element.174), channel_id=1, source_target_pairs={{0,8},{1,17},{2,10},{3,19},{4,12},{5,21},{6,14},{7,23},{8,0},{9,25... | collective-permute-start | bytes 3145736 | tf_op jit(solution)/shard_map/ppermute | solution.py:741
  230.8 8.1 %collective-permute-start.45 = (bf16[200,512]{1,0:T(8,128)(2,1)}, bf16[200,512]{1,0:T(8,128)(2,1)S(1)}, u32[]{:S(2)}, u32[]{:S(2)}) collective-permute-start(bf16[200,512]{1,0:T(8,128)(2,1)} %get-tuple-element.165), channel_id=1, source_target_pairs={{0,4},{1,5},{2,6},{3,7},{4,0},{5,1},{6,2},{7,3},{8,12},{9,13},{10,... | collective-permute-start | bytes 614408 | tf_op jit(solution)/shard_map/ppermute | solution.py:36
  232.2 10.5 %collective-permute-start.46 = (bf16[200,512]{1,0:T(8,128)(2,1)}, bf16[200,512]{1,0:T(8,128)(2,1)S(1)}, u32[]{:S(2)}, u32[]{:S(2)}) collective-permute-start(bf16[200,512]{1,0:T(8,128)(2,1)} %get-tuple-element.166), channel_id=1, source_target_pairs={{0,6},{1,7},{2,4},{3,5},{4,2},{5,3},{6,0},{7,1},{8,14},{9,15},{10,... | collective-permute-start | bytes 614408 | tf_op jit(solution)/shard_map/ppermute | solution.py:36
  255.9 9.2 %collective-permute-start.52 = (bf16[1,200,512]{2,1,0:T(8,128)(2,1)}, bf16[1,200,512]{2,1,0:T(8,128)(2,1)S(1)}, u32[]{:S(2)}, u32[]{:S(2)}) collective-permute-start(bf16[1,200,512]{2,1,0:T(8,128)(2,1)} %bitcast.214), channel_id=1, source_target_pairs={{0,6},{1,7},{2,4},{3,5},{4,2},{5,3},{6,0},{7,1},{8,14},{9,15},{10,... | collective-permute-start | bytes 614408 | tf_op jit(solution)/shard_map/ppermute | solution.py:36
  258.0 9.3 %collective-permute-start.50 = (bf16[1,200,512]{2,1,0:T(8,128)(2,1)}, bf16[1,200,512]{2,1,0:T(8,128)(2,1)S(1)}, u32[]{:S(2)}, u32[]{:S(2)}) collective-permute-start(bf16[1,200,512]{2,1,0:T(8,128)(2,1)} %bitcast.215), channel_id=1, source_target_pairs={{0,4},{1,5},{2,6},{3,7},{4,0},{5,1},{6,2},{7,3},{8,12},{9,13},{10,... | collective-permute-start | bytes 614408 | tf_op jit(solution)/shard_map/ppermute | solution.py:36
  258.5 9.2 %collective-permute-start.48 = (bf16[1,200,512]{2,1,0:T(8,128)(2,1)}, bf16[1,200,512]{2,1,0:T(8,128)(2,1)S(1)}, u32[]{:S(2)}, u32[]{:S(2)}) collective-permute-start(bf16[1,200,512]{2,1,0:T(8,128)(2,1)} %bitcast.216), channel_id=1, source_target_pairs={{0,2},{1,3},{2,0},{3,1},{4,6},{5,7},{6,4},{7,5},{8,10},{9,11},{10,... | collective-permute-start | bytes 614408 | tf_op jit(solution)/shard_map/ppermute | solution.py:36
  259.5 13.2 %collective-permute-start.47 = (bf16[1,200,512]{2,1,0:T(8,128)(2,1)}, bf16[1,200,512]{2,1,0:T(8,128)(2,1)S(1)}, u32[]{:S(2)}, u32[]{:S(2)}) collective-permute-start(bf16[1,200,512]{2,1,0:T(8,128)(2,1)} %bitcast.217), channel_id=1, source_target_pairs={{0,1},{1,0},{2,3},{3,2},{4,5},{5,4},{6,7},{7,6},{8,9},{9,8},{10,11... | collective-permute-start | bytes 614408 | tf_op jit(solution)/shard_map/ppermute | solution.py:36
  273.6 19.8 %collective-permute-start.56 = (bf16[8,64,512]{2,1,0:T(8,128)(2,1)}, bf16[8,64,512]{2,1,0:T(8,128)(2,1)S(1)}, u32[]{:S(2)}, u32[]{:S(2)}) collective-permute-start(bf16[8,64,512]{2,1,0:T(8,128)(2,1)} %get-tuple-element.191), channel_id=1, source_target_pairs={{0,1},{1,0},{2,3},{3,2},{4,5},{5,4},{6,7},{7,6},{8,9},{9,8},{10,11... | collective-permute-start | bytes 1572872 | tf_op jit(solution)/shard_map/ppermute | solution.py:36
  273.9 41.1 %collective-permute-start.62 = (bf16[2,2,4,64,512]{4,3,2,1,0:T(8,128)(2,1)S(1)}, bf16[2,2,4,64,512]{4,3,2,1,0:T(8,128)(2,1)}, u32[]{:S(2)}, u32[]{:S(2)}) collective-permute-start(bf16[2,2,4,64,512]{4,3,2,1,0:T(8,128)(2,1)S(1)} %add.144), channel_id=1, source_target_pairs={{0,16},{1,9},{2,18},{3,11},{4,20},{5,13},{6,22},{7,15},{8,24},{9,1... | collective-permute-start | bytes 3145736 | tf_op jit(solution)/shard_map/ppermute | solution.py:741
  293.3 14.7 %collective-permute-start.58 = (bf16[4,200,512]{2,1,0:T(8,128)(2,1)}, bf16[4,200,512]{2,1,0:T(8,128)(2,1)S(1)}, u32[]{:S(2)}, u32[]{:S(2)}) collective-permute-start(bf16[4,200,512]{2,1,0:T(8,128)(2,1)} %get-tuple-element.193), channel_id=1, source_target_pairs={{0,1},{1,0},{2,3},{3,2},{4,5},{5,4},{6,7},{7,6},{8,9},{9,8},{10,11... | collective-permute-start | bytes 2457608 | tf_op jit(solution)/shard_map/ppermute | solution.py:36
  293.5 14.5 %collective-permute-start.57 = (bf16[8,64,512]{2,1,0:T(8,128)(2,1)S(1)}, bf16[8,64,512]{2,1,0:T(8,128)(2,1)}, u32[]{:S(2)}, u32[]{:S(2)}) collective-permute-start(bf16[8,64,512]{2,1,0:T(8,128)(2,1)S(1)} %add.143), channel_id=1, source_target_pairs={{0,2},{1,3},{2,0},{3,1},{4,6},{5,7},{6,4},{7,5},{8,10},{9,11},{10,... | collective-permute-start | bytes 1572872 | tf_op jit(solution)/shard_map/ppermute | solution.py:36
  312.8 8.2 %collective-permute-start.60 = (bf16[200,512]{1,0:T(8,128)(2,1)}, bf16[200,512]{1,0:T(8,128)(2,1)S(1)}, u32[]{:S(2)}, u32[]{:S(2)}) collective-permute-start(bf16[200,512]{1,0:T(8,128)(2,1)} %get-tuple-element.196), channel_id=1, source_target_pairs={{0,4},{1,5},{2,6},{3,7},{4,0},{5,1},{6,2},{7,3},{8,12},{9,13},{10,... | collective-permute-start | bytes 614408 | tf_op jit(solution)/shard_map/ppermute | solution.py:36
  314.2 9.5 %collective-permute-start.61 = (bf16[200,512]{1,0:T(8,128)(2,1)}, bf16[200,512]{1,0:T(8,128)(2,1)S(1)}, u32[]{:S(2)}, u32[]{:S(2)}) collective-permute-start(bf16[200,512]{1,0:T(8,128)(2,1)} %get-tuple-element.197), channel_id=1, source_target_pairs={{0,6},{1,7},{2,4},{3,5},{4,2},{5,3},{6,0},{7,1},{8,14},{9,15},{10,... | collective-permute-start | bytes 614408 | tf_op jit(solution)/shard_map/ppermute | solution.py:36
  314.7 31.4 %collective-permute-start.63 = (bf16[2,2,4,64,512]{4,3,2,1,0:T(8,128)(2,1)}, bf16[2,2,4,64,512]{4,3,2,1,0:T(8,128)(2,1)S(1)}, u32[]{:S(2)}, u32[]{:S(2)}) collective-permute-start(bf16[2,2,4,64,512]{4,3,2,1,0:T(8,128)(2,1)} %get-tuple-element.212), channel_id=1, source_target_pairs={{0,8},{1,17},{2,10},{3,19},{4,12},{5,21},{6,14},{7,23},{8,0},{9,25... | collective-permute-start | bytes 3145736 | tf_op jit(solution)/shard_map/ppermute | solution.py:741
  330.1 16.0 %collective-permute-start.65 = (bf16[200,512]{1,0:T(8,128)(2,1)}, bf16[200,512]{1,0:T(8,128)(2,1)S(1)}, u32[]{:S(2)}, u32[]{:S(2)}) collective-permute-start(bf16[200,512]{1,0:T(8,128)(2,1)} %get-tuple-element.220), channel_id=1, source_target_pairs={{0,2},{1,3},{2,0},{3,1},{4,6},{5,7},{6,4},{7,5},{8,10},{9,11},{10,... | collective-permute-start | bytes 614408 | tf_op jit(solution)/shard_map/ppermute | solution.py:36
  331.7 14.5 %collective-permute-start.66 = (bf16[200,512]{1,0:T(8,128)(2,1)}, bf16[200,512]{1,0:T(8,128)(2,1)S(1)}, u32[]{:S(2)}, u32[]{:S(2)}) collective-permute-start(bf16[200,512]{1,0:T(8,128)(2,1)} %get-tuple-element.221), channel_id=1, source_target_pairs={{0,4},{1,5},{2,6},{3,7},{4,0},{5,1},{6,2},{7,3},{8,12},{9,13},{10,... | collective-permute-start | bytes 614408 | tf_op jit(solution)/shard_map/ppermute | solution.py:36
  333.1 13.1 %collective-permute-start.67 = (bf16[200,512]{1,0:T(8,128)(2,1)}, bf16[200,512]{1,0:T(8,128)(2,1)S(1)}, u32[]{:S(2)}, u32[]{:S(2)}) collective-permute-start(bf16[200,512]{1,0:T(8,128)(2,1)} %get-tuple-element.222), channel_id=1, source_target_pairs={{0,6},{1,7},{2,4},{3,5},{4,2},{5,3},{6,0},{7,1},{8,14},{9,15},{10,... | collective-permute-start | bytes 614408 | tf_op jit(solution)/shard_map/ppermute | solution.py:36
  350.2 14.0 %collective-permute-start.74 = (bf16[2,2,64,512]{3,2,0,1:T(8,128)(2,1)S(1)}, bf16[2,2,64,512]{3,2,0,1:T(8,128)(2,1)S(1)}, u32[]{:S(2)}, u32[]{:S(2)}) collective-permute-start(bf16[2,2,64,512]{3,2,0,1:T(8,128)(2,1)S(1)} %get-tuple-element.293), channel_id=1, source_target_pairs={{0,2},{1,3},{2,0},{3,1},{4,6},{5,7},{6,4},{7,5},{8,10},{9,11},{10,... | collective-permute-start | bytes 786440 | tf_op jit(solution)/shard_map/ppermute | solution.py:36
  351.9 12.4 %collective-permute-start.76 = (bf16[2,2,64,512]{3,2,0,1:T(8,128)(2,1)S(1)}, bf16[2,2,64,512]{3,2,0,1:T(8,128)(2,1)S(1)}, u32[]{:S(2)}, u32[]{:S(2)}) collective-permute-start(bf16[2,2,64,512]{3,2,0,1:T(8,128)(2,1)S(1)} %get-tuple-element.294), channel_id=1, source_target_pairs={{0,6},{1,7},{2,4},{3,5},{4,2},{5,3},{6,0},{7,1},{8,14},{9,15},{10,... | collective-permute-start | bytes 786440 | tf_op jit(solution)/shard_map/ppermute | solution.py:36
  353.3 12.2 %collective-permute-start.75 = (bf16[2,2,64,512]{3,2,0,1:T(8,128)(2,1)S(1)}, bf16[2,2,64,512]{3,2,0,1:T(8,128)(2,1)S(1)}, u32[]{:S(2)}, u32[]{:S(2)}) collective-permute-start(bf16[2,2,64,512]{3,2,0,1:T(8,128)(2,1)S(1)} %get-tuple-element.295), channel_id=1, source_target_pairs={{0,4},{1,5},{2,6},{3,7},{4,0},{5,1},{6,2},{7,3},{8,12},{9,13},{10,... | collective-permute-start | bytes 786440 | tf_op jit(solution)/shard_map/ppermute | solution.py:36
  353.8 14.5 %collective-permute-start.78 = (bf16[8,64,512]{2,1,0:T(8,128)(2,1)}, bf16[8,64,512]{2,1,0:T(8,128)(2,1)}, u32[]{:S(2)}, u32[]{:S(2)}) collective-permute-start(bf16[8,64,512]{2,1,0:T(8,128)(2,1)} %get-tuple-element.241), channel_id=1, source_target_pairs={{0,1},{1,0},{2,3},{3,2},{4,5},{5,4},{6,7},{7,6},{8,9},{9,8},{10,11... | collective-permute-start | bytes 1572872 | tf_op jit(solution)/shard_map/ppermute | solution.py:36
  353.8 20.0 %collective-permute-start.71 = (bf16[8,64,512]{2,1,0:T(8,128)(2,1)}, bf16[8,64,512]{2,1,0:T(8,128)(2,1)}, u32[]{:S(2)}, u32[]{:S(2)}) collective-permute-start(bf16[8,64,512]{2,1,0:T(8,128)(2,1)} %get-tuple-element.233), channel_id=1, source_target_pairs={{0,1},{1,0},{2,3},{3,2},{4,5},{5,4},{6,7},{7,6},{8,9},{9,8},{10,11... | collective-permute-start | bytes 1572872 | tf_op jit(solution)/shard_map/ppermute | solution.py:36
  365.8 13.0 %collective-permute-start.77 = (bf16[8,64,512]{2,1,0:T(8,128)(2,1)S(1)}, bf16[8,64,512]{2,1,0:T(8,128)(2,1)}, u32[]{:S(2)}, u32[]{:S(2)}) collective-permute-start(bf16[8,64,512]{2,1,0:T(8,128)(2,1)S(1)} %add.153), channel_id=1, source_target_pairs={{0,2},{1,3},{2,0},{3,1},{4,6},{5,7},{6,4},{7,5},{8,10},{9,11},{10,... | collective-permute-start | bytes 1572872 | tf_op jit(solution)/shard_map/ppermute | solution.py:36
  371.3 47.6 %collective-permute-start.80 = (bf16[2,2,4,64,512]{4,3,2,1,0:T(8,128)(2,1)}, bf16[2,2,4,64,512]{4,3,2,1,0:T(8,128)(2,1)}, u32[]{:S(2)}, u32[]{:S(2)}) collective-permute-start(bf16[2,2,4,64,512]{4,3,2,1,0:T(8,128)(2,1)} %add.160), channel_id=1, source_target_pairs={{0,16},{1,9},{2,18},{3,11},{4,20},{5,13},{6,22},{7,15},{8,24},{9,1... | collective-permute-start | bytes 3145736 | tf_op jit(solution)/shard_map/ppermute | solution.py:741
  371.7 47.2 %collective-permute-start.81 = (bf16[2,2,4,64,512]{4,3,2,1,0:T(8,128)(2,1)}, bf16[2,2,4,64,512]{4,3,2,1,0:T(8,128)(2,1)}, u32[]{:S(2)}, u32[]{:S(2)}) collective-permute-start(bf16[2,2,4,64,512]{4,3,2,1,0:T(8,128)(2,1)} %get-tuple-element.245), channel_id=1, source_target_pairs={{0,8},{1,17},{2,10},{3,19},{4,12},{5,21},{6,14},{7,23},{8,0},{9,25... | collective-permute-start | bytes 3145736 | tf_op jit(solution)/shard_map/ppermute | solution.py:741
  381.0 14.0 %collective-permute-start.79 = (bf16[4,2,64,512]{3,2,0,1:T(8,128)(2,1)}, bf16[4,2,64,512]{3,2,0,1:T(8,128)(2,1)}, u32[]{:S(2)}, u32[]{:S(2)}) collective-permute-start(bf16[4,2,64,512]{3,2,0,1:T(8,128)(2,1)} %pad_maximum_fusion.8), channel_id=1, source_target_pairs={{0,4},{1,5},{2,6},{3,7},{4,0},{5,1},{6,2},{7,3},{8,12},{9,13},{10,... | collective-permute-start | bytes 1572872 | tf_op jit(solution)/shard_map/ppermute | solution.py:36
  422.9 8.4 %collective-permute-start.86 = (bf16[2,4,64,512]{3,2,1,0:T(8,128)(2,1)S(1)}, bf16[2,4,64,512]{3,2,1,0:T(8,128)(2,1)S(1)}, u32[]{:S(2)}, u32[]{:S(2)}) collective-permute-start(bf16[2,4,64,512]{3,2,1,0:T(8,128)(2,1)S(1)} %get-tuple-element.291), channel_id=1, source_target_pairs={{0,1},{1,0},{2,3},{3,2},{4,5},{5,4},{6,7},{7,6},{8,9},{9,8},{10,11... | collective-permute-start | bytes 1572872 | tf_op jit(solution)/shard_map/ppermute | solution.py:36
  425.5 10.7 %collective-permute-start.83 = (f32[20,512]{1,0:T(8,128)S(1)}, f32[20,512]{1,0:T(8,128)S(1)}, u32[]{:S(2)}, u32[]{:S(2)}) collective-permute-start(f32[20,512]{1,0:T(8,128)S(1)} %add.161), channel_id=1, source_target_pairs={{0,16},{1,17},{2,18},{3,19},{4,20},{5,21},{6,22},{7,23},{8,24},{9,... | collective-permute-start | bytes 122888 | tf_op jit(solution)/shard_map/ppermute | solution.py:36
  429.5 8.5 %collective-permute-start.85 = (bf16[1,2,64,512]{3,2,0,1:T(8,128)(2,1)}, bf16[1,2,64,512]{3,2,0,1:T(8,128)(2,1)}, u32[]{:S(2)}, u32[]{:S(2)}) collective-permute-start(bf16[1,2,64,512]{3,2,0,1:T(8,128)(2,1)} %slice.327), channel_id=1, source_target_pairs={{0,16},{1,17},{2,18},{3,19},{4,20},{5,21},{6,22},{7,23},{8,24},{9,... | collective-permute-start | bytes 393224 | tf_op jit(solution)/shard_map/ppermute | solution.py:36
  431.4 10.6 %collective-permute-start.87 = (bf16[2,2,64,512]{3,2,0,1:T(8,128)(2,1)S(1)}, bf16[2,2,64,512]{3,2,0,1:T(8,128)(2,1)S(1)}, u32[]{:S(2)}, u32[]{:S(2)}) collective-permute-start(bf16[2,2,64,512]{3,2,0,1:T(8,128)(2,1)S(1)} %get-tuple-element.287), channel_id=1, source_target_pairs={{0,2},{1,3},{2,0},{3,1},{4,6},{5,7},{6,4},{7,5},{8,10},{9,11},{10,... | collective-permute-start | bytes 786440 | tf_op jit(solution)/shard_map/ppermute | solution.py:36
  432.6 9.5 %collective-permute-start.89 = (bf16[2,2,64,512]{3,2,0,1:T(8,128)(2,1)S(1)}, bf16[2,2,64,512]{3,2,0,1:T(8,128)(2,1)S(1)}, u32[]{:S(2)}, u32[]{:S(2)}) collective-permute-start(bf16[2,2,64,512]{3,2,0,1:T(8,128)(2,1)S(1)} %get-tuple-element.288), channel_id=1, source_target_pairs={{0,6},{1,7},{2,4},{3,5},{4,2},{5,3},{6,0},{7,1},{8,14},{9,15},{10,... | collective-permute-start | bytes 786440 | tf_op jit(solution)/shard_map/ppermute | solution.py:36
  434.6 8.9 %collective-permute-start.88 = (bf16[2,2,64,512]{3,2,0,1:T(8,128)(2,1)S(1)}, bf16[2,2,64,512]{3,2,0,1:T(8,128)(2,1)}, u32[]{:S(2)}, u32[]{:S(2)}) collective-permute-start(bf16[2,2,64,512]{3,2,0,1:T(8,128)(2,1)S(1)} %get-tuple-element.289), channel_id=1, source_target_pairs={{0,4},{1,5},{2,6},{3,7},{4,0},{5,1},{6,2},{7,3},{8,12},{9,13},{10,... | collective-permute-start | bytes 786440 | tf_op jit(solution)/shard_map/ppermute | solution.py:36
  (99 other events, 840.4 us)

commit v3 on v2

--- a/solution.py
+++ b/solution.py
@@ -108,28 +108,48 @@
     return got[:, 0], jnp.swapaxes(got[:, 1], 1, 2)
 
 
-def slot_rows(place, ids, ranking, experts):
-    expert_range = jnp.arange(experts, dtype=jnp.int32)[:, None]
-    first = ids[:, 0][None, :] == expert_range
-    second = ids[:, 1][None, :] == expert_range
-    both = jnp.concatenate([first, second]).astype(bf16)
-    earlier = (ranking[:, None] < ranking[None, :]).astype(bf16)
-    counts = mm("et,ts->es", both, earlier)
-    total = jnp.sum(first.astype(f32), axis=1, keepdims=True)
-    slot = jnp.where(first, counts[:experts], jnp.where(second, total + counts[experts:], -1.0))
-    slot = jnp.where(slot < CAP, slot, -1.0).astype(jnp.int32)
-    mine = lax.dynamic_index_in_dim(slot, place.expert, 0, keepdims=False)
-    theirs = lax.dynamic_index_in_dim(slot, place.expert ^ place.tensor_size, 0, keepdims=False)
-    return mine, theirs
-
-
-def slot_tables(place, mine, theirs):
-    groups = jnp.stack([mine, theirs])
-    groups = groups.reshape((2, place.tensor_size, LEN))
-    groups = groups[:, place.tensor ^ jnp.arange(place.tensor_size)]
-    groups = jnp.pad(groups, ((0, 0), (0, 0), (0, ROWS - LEN)), constant_values=-1)
-    table = groups.reshape(-1, ROWS)
-    return table, jnp.swapaxes(table, 0, 1)
+LANES = 256
+
+
+def slot_kernel(experts, mine_ref, ids, rank, mine, theirs):
+    tensor = mine.shape[1]
+    expert, other = mine_ref[0], mine_ref[1]
+    here = mine_ref[2]
+    for l in range(ids.shape[0]):
+        choice = lax.broadcasted_iota(jnp.int32, (experts, tensor * LANES), 0)
+        first, second = ids[l, 0:1, :] == choice, ids[l, 1:2, :] == choice
+        order = rank[l : l + 1, :].astype(f32)
+        column = jnp.broadcast_to(order, (8, tensor * LANES)).T[:, 0:1]
+        earlier = (column < order).astype(f32).astype(bf16)
+        both = jnp.concatenate([first.astype(f32), second.astype(f32)]).astype(bf16)
+        counts = dot(both, earlier)
+        total = jnp.sum(first.astype(f32), axis=1, keepdims=True)
+        slot = jnp.where(first, counts[:experts], jnp.where(second, total + counts[experts:], -1.0))
+        slot = jnp.where(slot < CAP, slot, -1.0)
+        for which, target in ((expert, mine), (other, theirs)):
+            row = jnp.sum(jnp.where(choice == which, slot, 0.0), axis=0, keepdims=True).astype(jnp.int32)
+            for t in range(tensor):
+                target[l, pl.ds(jnp.bitwise_xor(here, t), 1), :] = row[:, t * LANES : (t + 1) * LANES]
+
+
+def slot_tables(place, routes, priority, experts):
+    layers, count, unused = routes.shape
+    spread = ((0, 0), (0, 0), (0, 0), (0, LANES - LEN))
+    ids = jnp.swapaxes(routes, 1, 2).reshape(layers, 2, -1, LEN)
+    ids = jnp.pad(ids, spread, constant_values=-1).reshape(layers, 2, -1)
+    rank = jnp.pad(priority.reshape(layers, 1, -1, LEN), spread).reshape(layers, -1)
+    where = jnp.stack([place.expert, place.expert ^ place.tensor_size, place.tensor]).astype(jnp.int32)
+    shape = jax.ShapeDtypeStruct((layers, place.tensor_size, LANES), jnp.int32)
+    mine, theirs = pl.pallas_call(
+        lambda *refs: slot_kernel(experts, *refs),
+        out_shape=(shape, shape),
+        in_specs=[smem(), vmem(), vmem()],
+        out_specs=(vmem(), vmem()),
+        compiler_params=params(),
+        cost_estimate=pl.CostEstimate(flops=1, transcendentals=0, bytes_accessed=1),
+        name="slots",
+    )(where, ids, rank)
+    return mine, place.swap(theirs, place.tensor_size)
 
 
 def exchange_rows(place, own):
@@ -143,9 +163,9 @@
         target[...] = (even[k].astype(f32) + odd[k].astype(f32)).astype(bf16)
 
 
-def pair_rows(place, parts):
+def pair_rows(place, parts, *others):
     even, odd = parts
-    odd = place.swap(odd, 1)
+    odd, *others = lax.optimization_barrier((place.swap(odd, 1), *others))
     return list(pl.pallas_call(
         add_kernel,
         out_shape=(jax.ShapeDtypeStruct(even.shape[1:], bf16),) * 4,
@@ -153,7 +173,7 @@
         out_specs=(vmem(),) * 4,
         cost_estimate=pl.CostEstimate(flops=1, transcendentals=0, bytes_accessed=1),
         name="add_rows",
-    )(even, odd))
+    )(even, odd)) + others
 
 
 def send_rows(place, sums):
@@ -403,7 +423,7 @@
 CUBE = 0.044715
 
 
-def expert_kernel(plan, off_ref, me_ref, table, table_t, router, *refs):
+def expert_kernel(plan, off_ref, me_ref, mine, theirs, router, *refs):
     forward, backward = plan.images is not None, plan.grads is not None
     piece_count = len(plan.w_in)
     refs = list(refs)
@@ -446,13 +466,17 @@
             for copy in loads(c, which):
                 copy.start()
 
+    def hot_rows(g, t, slot):
+        row = (mine, theirs)[g][plan.layer, t : t + 1, :][:, :ROWS]
+        return (row == slot).astype(f32).astype(bf16)
+
     def gather(images):
         for g in (0, 1):
             total = None
             for t in range(4):
                 j = g * 4 + t
                 slot = lax.broadcasted_iota(jnp.int32, (SLOTS, ROWS), 0)
-                hot = (table[j : j + 1, :] == slot).astype(f32).astype(bf16)
+                hot = hot_rows(g, t, slot)
                 index, layer = images[j]
                 part = dot(hot, tokens[index][layer])
                 total = part if total is None else total + part
@@ -462,9 +486,8 @@
         for g in (0, 1):
             for t in range(4):
                 j = g * 4 + t
-                slot = lax.broadcasted_iota(jnp.int32, (ROWS, SLOTS), 1)
-                hot = (table_t[:, j : j + 1] == slot).astype(f32).astype(bf16)
-                part = dot(hot, slot_rows[g * SLOTS : (g + 1) * SLOTS]).astype(bf16)
+                slot = lax.broadcasted_iota(jnp.int32, (SLOTS, ROWS), 0)
+                part = t_dot(hot_rows(g, t, slot), slot_rows[g * SLOTS : (g + 1) * SLOTS]).astype(bf16)
                 parts[j % 2][j // 2] = part
 
     if forward:
@@ -559,14 +582,14 @@
 
 
 class Plan:
-    def __init__(self, block, images, grads, w_in, w_out, grad_shapes, grad_in, grad_out):
-        self.block = block
+    def __init__(self, layer, block, images, grads, w_in, w_out, grad_shapes, grad_in, grad_out):
+        self.layer, self.block = layer, block
         self.images, self.grads = images, grads
         self.w_in, self.w_out = w_in, w_out
         self.grad_shapes, self.grad_in, self.grad_out = grad_shapes, grad_in, grad_out
 
 
-def expert_layer(plan, offsets, me, tables, router, tokens, saved, weights):
+def expert_layer(plan, offsets, me, tables, router, tokens, saved, weights, flops=1):
     forward, backward = plan.images is not None, plan.grads is not None
     plan.token_arrays, plan.weight_arrays = len(tokens), len(weights)
     width = router.shape[0]
@@ -616,7 +639,7 @@
         out_specs=tuple(out_specs),
         scratch_shapes=scratch,
         compiler_params=params(),
-        cost_estimate=pl.CostEstimate(flops=1, transcendentals=0, bytes_accessed=1),
+        cost_estimate=pl.CostEstimate(flops=flops, transcendentals=0, bytes_accessed=1),
         name="expert_layer",
     )(*operands)
 
@@ -643,14 +666,13 @@
     zero = jnp.zeros((1,), jnp.int32)
     attn_off, expert_off = zero, zero
     me = place.expert.astype(jnp.int32).reshape(1)
-    attn_w, expert_w, tables = [], [], []
+    attn_w, expert_w = [], []
+    tables = slot_tables(place, routes, priority, experts)
     for l in range(LAYERS):
         shard = jnp.concatenate([qkv_weight[l], jnp.swapaxes(out_weight[l], 0, 1)[:, None]], axis=1)
         full = gather_attention(place, shard.reshape(rows, -1))
         attn_w.append([full[j][None] for j in range(4)])
         expert_w.append([w[None] for w in gather_experts(place, expert_in[l], expert_out[l])])
-        mine, theirs = slot_rows(place, routes[l], priority[l, 0], experts)
-        tables.append(slot_tables(place, mine, place.swap(theirs, place.tensor_size)))
     hidden_in, hidden_mid, qkv, ctx = {}, {}, {}, {}
     base, pieces = inputs, []
     saved = None
@@ -666,17 +688,17 @@
         here = [(j, 0) for j in range(8)]
         if last:
             grads = exchange_rows(place, padded_bf16(cotangent)[None])
-            plan = Plan(block, here, [(j + 8, 0) for j in range(8)], *at, [block] * 2, *at)
+            plan = Plan(l, block, here, [(j + 8, 0) for j in range(8)], *at, [block] * 2, *at)
             result = expert_layer(
-                plan, expert_off, me, tables[l], router_weight[l], images + grads, None, expert_w[l]
+                plan, expert_off, me, tables, router_weight[l], images + grads, None, expert_w[l]
             )
             tail = send_rows(place, pair_rows(place, result[:2]))
             result = result[2:]
             outputs = hidden_mid[l] + sum(p.astype(f32) for p in tail)
         else:
-            plan = Plan(block, here, None, *at, None, None, None)
+            plan = Plan(l, block, here, None, *at, None, None, None)
             *result, sent, expert_y = expert_layer(
-                plan, expert_off, me, tables[l], router_weight[l], images, None, expert_w[l]
+                plan, expert_off, me, tables, router_weight[l], images, None, expert_w[l]
             )
             base, pieces = hidden_mid[l], send_rows(place, pair_rows(place, result))
             saved = [sent, expert_y]
@@ -691,9 +713,9 @@
         )
         if l:
             grads = exchange_rows(place, branch[None])
-            plan = Plan(block, None, here, *at, [block] * 2, *at)
+            plan = Plan(l - 1, block, None, here, *at, [block] * 2, *at)
             result = expert_layer(
-                plan, expert_off, me, tables[l - 1], router_weight[l - 1], grads, saved, expert_w[l - 1]
+                plan, expert_off, me, tables, router_weight[l - 1], grads, saved, expert_w[l - 1]
             )
         total = scatter_attention(place, jnp.concatenate(parts), rows)
         attn_list[l] = total.astype(f32).reshape(rows, 4, -1)
@@ -728,12 +750,18 @@
     return jnp.stack([w_in[order], jnp.swapaxes(w_out, 1, 2)[order]])
 
 
+def chip_pairs(place, blocks):
+    return jnp.stack([blocks[:, 0::2], place.swap(blocks[:, 1::2], CORE)], axis=2)
+
+
+def send_pairs(place, pair):
+    two, chips, cores, rows, width = pair.shape
+    got = [pair[:, 0]] + [place.swap(pair[:, k], 2 * k) for k in (1, 2, 3)]
+    return jnp.stack(got, axis=1).reshape(two, 2, chips * cores // 2, rows, width)
+
+
 def plane_blocks(place, blocks):
-    two, count, rows, width = blocks.shape
-    odd = place.swap(blocks[:, 1::2], CORE)
-    pair = jnp.stack([blocks[:, 0::2], odd], axis=2)
-    got = [pair[:, 0]] + [place.swap(pair[:, k], 2 * k) for k in (1, 2, 3)]
-    return jnp.stack(got, axis=1).reshape(two, 2, count // 2, rows, width)
+    return send_pairs(place, chip_pairs(place, blocks))
 
 
 def mixed(place, value, even, odd):
@@ -789,14 +817,18 @@
     me = place.expert.astype(jnp.int32).reshape(1)
     block = (2, place.tensor_size, rows, expert_in.shape[3])
 
-    own0 = plane_blocks(place, expert_blocks(place, expert_in[0], expert_out[0]))
+    pair = chip_pairs(place, expert_blocks(place, expert_in[0], expert_out[0]))
     held = jnp.stack([attention_shard(qkv_weight[l], out_weight[l]) for l in (0, 1)])[None]
+    pair, held = tie(pair, held)
+    own0 = send_pairs(place, pair)
     held = widen(place, widen(place, held, FAR), NEAR)
     held, own0 = tie(held, own0)
     a0 = mixed(place, own0, FAR, NEAR)
-    held0 = widen(place, held[:, 0], X)
+    held = widen(place, held, X)
+    held0, held1 = held[:, 0], held[:, 1]
     over0 = swap(held0, Y)
-    over0, a0, blocks1 = tie(over0, a0, expert_blocks(place, expert_in[1], expert_out[1]))
+    tables = slot_tables(place, routes, priority, experts)
+    over0, a0, blocks1, *tables = tie(over0, a0, expert_blocks(place, expert_in[1], expert_out[1]), *tables)
     b0, c0 = mixed(place, own0, NEAR, FAR), mixed(place, a0, NEAR, FAR)
     weights0 = [held0, swap(held0, CORE), over0, swap(over0, CORE)]
     own1 = plane_blocks(place, blocks1)
@@ -804,36 +836,33 @@
     hidden_in0, hidden_mid0, normed, qkv0, ctx0 = attention_forward(
         attn_off, inputs, [], [], norm_gains[0], weights0
     )
-    normed, own1 = tie(normed, own1)
-    slots = [slot_rows(place, routes[l], priority[l, 0], experts) for l in (0, 1)]
+    normed, own1, held1 = tie(normed, own1, held1)
     images = exchange_rows(place, normed)
-    images[6], held1, theirs = tie(images[6], held[:, 1], jnp.stack([s[1] for s in slots]))
-    theirs = swap(theirs, X)
-    tables = [slot_tables(place, slots[l][0], theirs[l]) for l in (0, 1)]
-    held1 = widen(place, held1, X)
     over1 = swap(held1, Y)
     weights1 = [held1, swap(held1, CORE), over1, swap(over1, CORE)]
+    tied = tie(*images, *weights1)
+    images, weights1 = tied[:8], tied[8:]
     b0, c0, own1 = tie(b0, c0, own1)
-    a1 = mixed(place, own1, FAR, NEAR)
+    a1, b1 = mixed(place, own1, FAR, NEAR), mixed(place, own1, NEAR, FAR)
     first = [(j, 0) for j in range(8)]
     second = [(j, 1) for j in range(8)]
     parts = [[(m, io) for m in range(4)] for io in (0, 1)]
     *rows0, sent, expert_y = expert_layer(
-        Plan(block, first, None, *parts, None, None, None),
-        expert_off, me, tables[0], router_weight[0], images, None, [own0, a0, b0, c0],
-    )
-    rows0[0], weights1[2] = tie(rows0[0], weights1[2])
+        Plan(0, block, first, None, *parts, None, None, None),
+        expert_off, me, tables, router_weight[0], images, None, [own0, a0, b0, c0],
+    )
     pieces = send_rows(place, pair_rows(place, rows0))
-    *pieces, a1, own1 = tie(*pieces, a1, own1)
-    b1, c1 = mixed(place, own1, NEAR, FAR), mixed(place, a1, NEAR, FAR)
     hidden_in1, hidden_mid1, normed, qkv1, ctx1 = attention_forward(
         attn_off, hidden_mid0, pieces, [cotangent], norm_gains[1], weights1
     )
+    normed, a1 = tie(normed, a1)
+    c1 = mixed(place, a1, NEAR, FAR)
     images = exchange_rows(place, normed)
+    images[2], b1 = tie(images[2], b1)
     grad_shapes = [(2,) + block] * 4
     result = expert_layer(
-        Plan(block, first, second, *parts, grad_shapes, *parts),
-        expert_off, me, tables[1], router_weight[1], images, None, [own1, a1, b1, c1],
+        Plan(1, block, first, second, *parts, grad_shapes, *parts),
+        expert_off, me, tables, router_weight[1], images, None, [own1, a1, b1, c1],
     )
     out_rows, back_rows, router1, (own, a, b, c) = result[:2], result[2:4], result[4], result[5:]
 
@@ -842,45 +871,53 @@
     grad1, branch, gains1, *parts1 = attention_backward(
         attn_off, cotangent, pieces, hidden_in1, hidden_mid1, norm_gains[1], weights1, qkv1, ctx1, ROWS
     )
+    far1 = parts1[2] + swap(parts1[3], CORE)
     images = exchange_rows(place, branch[None])
-    tied = tie(*images, a, b, c, *parts1)
-    images, (a, b, c), parts1 = tied[:8], tied[8:11], tied[11:]
+    tied = tie(*images, a, b, c, far1)
+    images, (a, b, c, far1) = tied[:8], tied[8:]
+    far1 = swap(far1, Y)
     a = mixed(place, a + c, FAR, NEAR)
-    near1, far1 = parts1[0] + swap(parts1[1], CORE), parts1[2] + swap(parts1[3], CORE)
-    far1 = swap(far1, Y)
     result = expert_layer(
-        Plan(block, None, first, *parts, grad_shapes, *parts),
-        expert_off, me, tables[0], router_weight[0], images, [sent, expert_y], [own0, a0, b0, c0],
-    )
-    back_rows, router0, (own0, a0, b0, c0) = list(result[:2]), result[2], result[3:]
-    back_rows[0], far1 = tie(back_rows[0], far1)
-    attn_sum1 = near1 + far1
+        Plan(0, block, None, first, *parts, grad_shapes, *parts),
+        expert_off, me, tables, router_weight[0], images, [sent, expert_y], [own0, a0, b0, c0],
+        flops=10**10,
+    )
+    back_rows, router0, (own0, a0, b0, c0) = result[:2], result[2], result[3:]
+    *back_rows, far1 = tie(*back_rows, far1)
     c0 = mixed(place, c0, NEAR, FAR)
     pieces = send_rows(place, pair_rows(place, back_rows))
-    tied = tie(*pieces, a, b, own, *out_rows)
-    pieces, (a, b, own), out_rows = tied[:4], tied[4:7], tied[7:]
-    tail = send_rows(place, pair_rows(place, out_rows))
+    pieces[3], a = tie(pieces[3], a)
     grad0, unused, gains0, *parts0 = attention_backward(
         attn_off, grad1, pieces, hidden_in0, hidden_mid0, norm_gains[0], weights0, qkv0, ctx0, LEN
     )
-    gains0, c0, b0, a, b, own, *tail = tie(gains0, c0, b0, a, b, own, *tail)
+    gains0, c0, b0, a, b, own, *out_rows = tie(gains0, c0, b0, a, b, own, *out_rows)
     a0, b0 = mixed(place, a0 + c0, FAR, NEAR), mixed(place, b0, NEAR, FAR)
-    outputs = hidden_mid1 + sum(p.astype(f32) for p in tail)
-    sum1 = plane_sums(place, own + b + a)
-    near0, far0 = parts0[0] + swap(parts0[1], CORE), parts0[2] + swap(parts0[3], CORE)
-    far0, sum1 = tie(far0, sum1)
-    attn_sum0 = near0 + swap(far0, Y)
-    attn_sum = halve(place, jnp.stack([attn_sum0, attn_sum1], axis=1), X)
     gains, router = jnp.stack([gains0, gains1]), jnp.stack([router0, router1])
     small = jnp.concatenate([gains.reshape(-1), router.reshape(-1)]).reshape(-1, 512)
-    for mask in (CORE, Y, X):
+    recv = [swap(v, CORE) for v in (parts0[3], parts0[1], parts1[1])]
+    *recv, sum1, parts0[0], parts0[2], parts1[0] = tie(
+        *recv, own + b + a, parts0[0], parts0[2], parts1[0]
+    )
+    far0, near0, near1 = parts0[2] + recv[0], parts0[0] + recv[1], parts1[0] + recv[2]
+    far0 = swap(far0, Y)
+    far0, out_rows[0] = tie(far0, out_rows[0])
+    attn_sum = [halve(place, near + far, X) for near, far in ((near0, far0), (near1, far1))]
+    attn_sum = jnp.stack(attn_sum, axis=1)
+    sum1, small, *tail = tie(plane_sums(place, sum1), small, *pair_rows(place, out_rows))
+    tail = send_rows(place, tail)
+    for mask in (CORE, X, Y):
         small = small + swap(small, mask)
-    small, attn_sum, a0, b0 = tie(small, attn_sum, a0, b0)
+    attn_sum, small, sum1, a0, b0, *tail = tie(attn_sum, small, sum1, a0, b0, *tail)
+    outputs = hidden_mid1 + sum(p.astype(f32) for p in tail)
+    sum0 = own0 + a0 + b0
+    pair0 = chip_pairs(place, sum0.reshape((2, -1) + sum0.shape[3:]))
+    pair0, attn_sum, small = tie(pair0, attn_sum, small)
+    sum0 = send_pairs(place, pair0).reshape((2, -1) + sum0.shape[3:])
     for mask in (NEAR, FAR):
         attn_sum = halve(place, attn_sum, mask)
         small = small + swap(small, mask)
     in1, out1 = unpack_sums(place, sum1)
-    in0, out0 = unpack_sums(place, plane_sums(place, own0 + a0 + b0))
+    in0, out0 = unpack_sums(place, sum0)
     small = small.reshape(-1)
     gains, router = small[: gains.size].reshape(gains.shape), small[gains.size :].reshape(router.shape)
     attn = attn_sum.astype(f32).reshape(2, rows, 4, -1)

time: 459 us -> 410 us (0.89)
  waiting for transfers between devices: 198 us -> 147 us
  starting transfers between devices: 80 us -> 92.5 us
  local copies, waits for them, and re-layouts: 44.4 us -> 32.5 us
    ppermute x12, waiting for transfers between devices: 65.9 us -> 30.9 us  [mixed(): return lax.ppermute(value, AXES, pairs)]
    ppermute x78, waiting for transfers between devices: 132 us -> 116 us  [swap(): return lax.ppermute(value, AXES, pairs)]
    ppermute x12, starting transfers between devices: 13.8 us -> 20.7 us  [mixed(): return lax.ppermute(value, AXES, pairs)]
    ppermute x78, starting transfers between devices: 66.2 us -> 71.8 us  [swap(): return lax.ppermute(value, AXES, pairs)]
    reshape x8 -> x3, local copies, waits for them, and re-layouts: 6.28 us -> 0.8 us  [the longest x1 0.63 us: slot_tables(): ids = jnp.pad(ids, spread, constant_values=-1).reshape(layers, 2, -1)]
    unnamed x154 -> x162, local copies, waits for them, and re-layouts: 17.6 us -> 13.4 us
  transfers between devices with their start and end apart: 90 -> 90, of which waited for: 46 -> 45; matrix products, arithmetic and copies ran while one was open for 10% -> 10% of each run, Pallas kernels for 15% -> 20%
where the time goes in v3:
time: 410 us; the launch traced here: 402 us
  waiting for transfers between devices  147 us (36%)
  Pallas kernels  102 us (25%)
  starting transfers between devices  92.5 us (23%)
  local copies, waits for them, and re-layouts  32.5 us (8%)
  other arithmetic  26.5 us (6%)
    ppermute x78, waiting for transfers between devices, swap(): return lax.ppermute(value, AXES, pairs)  116 us
    ppermute x78, starting transfers between devices, swap(): return lax.ppermute(value, AXES, pairs)  71.8 us
    pallas_call x3, Pallas kernels, expert_layer(): pl.pallas_call(lambda *refs: expert_kernel(plan, *refs), out_shape=tuple(...  49.9 us
    ppermute x12, waiting for transfers between devices, mixed(): return lax.ppermute(value, AXES, pairs)  30.9 us
    pallas_call x2, Pallas kernels, attention_backward(): pl.pallas_call(attention_backward_kernel, out_shape=(shape((out_rows, wid...  24.9 us
    ppermute x12, starting transfers between devices, mixed(): return lax.ppermute(value, AXES, pairs)  20.7 us
    pallas_call x2, Pallas kernels, attention_forward(): pl.pallas_call(lambda *refs: attention_forward_kernel(len(pieces), len(ex...  15 us
    unnamed x162, local copies, waits for them, and re-layouts  13.4 us
  transfers between devices with their start and end apart: 90, of which 45 were waited for; matrix products, arithmetic and copies ran while one was open for 10% of the time, Pallas kernels for 20%

profile of v3, /device:TPU:0, one launch (start us, length us, event | category | flops | bytes accessed | tf_op | source)
XLA Modules:
  0.0 402.0 jit_solution(1223086845564989321)
XLA Ops:
  6.6 4.0 %collective-permute-start.1 = (bf16[1,2,64,512]{3,2,0,1:T(8,128)(2,1)S(1)}, bf16[1,2,64,512]{3,2,0,1:T(8,128)(2,1)S(1)}, u32[]{:S(2)}, u32[]{:S(2)}) collective-permute-start(bf16[1,2,64,512]{3,2,0,1:T(8,128)(2,1)S(1)} %maximum_bitcast_fusion), channel_id=1, source_target_pairs={{0,16},{1,17},{2,18},{3,19},{4,20},{5,21},{6,22},{7,23},{8,24},{9,... | collective-permute-start | bytes 393224 | tf_op jit(solution)/shard_map/ppermute | solution.py:36
  10.7 1.6 collective-permute-start.4
  12.3 1.5 collective-permute-start.3
  14.3 3.0 collective-permute-done.1
  18.1 1.9 collective-permute-done.4
  20.0 5.7 %collective-permute-done.3 = bf16[2,2,64,512]{3,2,0,1:T(8,128)(2,1)S(1)} collective-permute-done((bf16[2,2,64,512]{3,2,0,1:T(8,128)(2,1)S(1)}, bf16[2,2,64,512]{3,2,0,1:T(8,128)(2,1)S(1)}, u32[]{:S(2)}, u32[]{:S(2)}) %collective-permute-start.3) | collective-permute-done | bytes 262176 | tf_op jit(solution)/shard_map/ppermute | solution.py:36
  27.3 2.2 collective-permute-start.9
  29.6 9.1 %collective-permute-done.6 = bf16[4,2,64,512]{3,2,0,1:T(8,128)(2,1)S(1)} collective-permute-done((bf16[4,2,64,512]{3,2,0,1:T(8,128)(2,1)S(1)}, bf16[4,2,64,512]{3,2,0,1:T(8,128)(2,1)S(1)}, u32[]{:S(2)}, u32[]{:S(2)}) %collective-permute-start.6) | collective-permute-done | bytes 524320 | tf_op jit(solution)/shard_map/ppermute | solution.py:36
  41.5 2.3 slots.1
  46.7 1.6 gather_fusion.3
  50.7 3.7 collective-permute-done.9.refs_14_.refs_16_
  55.5 1.7 collective-permute-start.27
  62.8 7.1 %attention_forward.2 = (f32[200,512]{1,0:T(8,128)}, f32[200,512]{1,0:T(8,128)}, bf16[1,200,512]{2,1,0:T(8,128)(2,1)}, bf16[200,1536]{1,0:T(8,128)(2,1)}, bf16[200,512]{1,0:T(8,128)(2,1)}) custom-call(s32[8]{0:T(128)} %xor_multiply_fusion.1.refs_0_.off_ref, bf16[197,512]{1,0:T(8,128)(2,1)} %refs_1_.1, f32[2,512]{1,0:T(2,128)} %get-tuple-element.359.refs_2_.gains, ...), custom_call_target="tpu_custom_call" | custom-call | flops 1 | bytes 1 | tf_op jit(solution)/shard_map/attention_forward/pallas_call | solution.py:305
  70.0 3.1 collective-permute-done.13
  78.9 2.4 collective-permute-done.26.refs_15_.refs_17_
  81.3 12.1 %collective-permute-done.24.refs_10_.w2 = bf16[8,64,512]{2,1,0:T(8,128)(2,1)S(1)} collective-permute-done((bf16[8,64,512]{2,1,0:T(8,128)(2,1)S(1)}, bf16[8,64,512]{2,1,0:T(8,128)(2,1)S(1)}, u32[]{:S(2)}, u32[]{:S(2)}) %collective-permute-start.24) | collective-permute-done | bytes 524320 | tf_op jit(solution)/shard_map/ppermute | solution.py:36
  94.7 9.1 %collective-permute-done.27.refs_16_.refs_18_ = bf16[2,2,4,64,512]{4,3,2,1,0:T(8,128)(2,1)} collective-permute-done((bf16[2,2,4,64,512]{4,3,2,1,0:T(8,128)(2,1)}, bf16[2,2,4,64,512]{4,3,2,1,0:T(8,128)(2,1)}, u32[]{:S(2)}, u32[]{:S(2)}) %collective-permute-start.27) | collective-permute-done | bytes 1048608 | tf_op jit(solution)/shard_map/ppermute | solution.py:769
  106.3 1.5 collective-permute-start.32
  111.3 10.9 %expert_layer.3 = (bf16[4,200,512]{2,1,0:T(8,128)(2,1)}, bf16[4,200,512]{2,1,0:T(8,128)(2,1)}, bf16[512,512]{1,0:T(8,128)(2,1)}, f32[512,512]{1,0:T(8,128)}) custom-call(s32[8]{0:T(128)} %mul.21.refs_0_, s32[1]{0:T(128)} %bitcast.31.refs_1_, s32[2,4,256]{2,1,0:T(4,128)} %get-tuple-element.160.refs_2_, s32[2,4,256]{2,1,0:T(4,128)} %copy-done.59, ...), custom_call_target="tpu_custom_call" | custom-call | flops 1 | bytes 1 | tf_op jit(solution)/shard_map/expert_layer/pallas_call | solution.py:635
  122.3 2.3 collective-permute-start.35
  125.8 2.3 add_rows.4
  128.1 1.5 collective-permute-start.29
  131.6 3.8 collective-permute-done.29.refs_3_
  135.4 2.3 collective-permute-done.30.refs_4_
  137.8 3.2 collective-permute-done.31.refs_5_
  141.7 7.9 %attention_forward.3 = (f32[200,512]{1,0:T(8,128)}, f32[200,512]{1,0:T(8,128)}, bf16[2,200,512]{2,1,0:T(8,128)(2,1)}, bf16[200,1536]{1,0:T(8,128)(2,1)}, bf16[200,512]{1,0:T(8,128)(2,1)}) custom-call(s32[8]{0:T(128)} %xor_multiply_fusion.1.refs_0_.off_ref, f32[200,512]{1,0:T(8,128)} %get-tuple-element.159.refs_1_.hidden_mid, ...), custom_call_target="tpu_custom_call" | custom-call | flops 1 | bytes 1 | tf_op jit(solution)/shard_map/attention_forward/pallas_call | solution.py:305
  149.6 2.3 collective-permute-start.41
  156.8 8.7 %collective-permute-done.39.refs_11_ = bf16[2,200,512]{2,1,0:T(8,128)(2,1)S(1)} collective-permute-done((bf16[2,200,512]{2,1,0:T(8,128)(2,1)}, bf16[2,200,512]{2,1,0:T(8,128)(2,1)S(1)}, u32[]{:S(2)}, u32[]{:S(2)}) %collective-permute-start.39) | collective-permute-done | bytes 409632 | tf_op jit(solution)/shard_map/ppermute | solution.py:36
  165.5 6.4 %collective-permute-done.37.refs_9_ = bf16[2,200,512]{2,1,0:T(8,128)(2,1)S(1)} collective-permute-done((bf16[2,200,512]{2,1,0:T(8,128)(2,1)}, bf16[2,200,512]{2,1,0:T(8,128)(2,1)S(1)}, u32[]{:S(2)}, u32[]{:S(2)}) %collective-permute-start.37) | collective-permute-done | bytes 409632 | tf_op jit(solution)/shard_map/ppermute | solution.py:36
  174.3 1.9 collective-permute-done.41.refs_16_
  176.3 22.0 %expert_layer.4 = (bf16[4,200,512]{2,1,0:T(8,128)(2,1)}, bf16[4,200,512]{2,1,0:T(8,128)(2,1)}, bf16[4,200,512]{2,1,0:T(8,128)(2,1)}, bf16[4,200,512]{2,1,0:T(8,1...) custom-call(s32[8]{0:T(128)} %mul.21.refs_0_, ...), custom_call_target="tpu_custom_call" | custom-call | flops 1 | bytes 1 | tf_op jit(solution)/shard_map/expert_layer/pallas_call | solution.py:635
  198.3 1.9 collective-permute-start.42
  200.7 1.6 collective-permute-start.54
  203.4 2.3 add_rows.5
  209.2 4.1 %collective-permute-done.43.p1 = bf16[200,512]{1,0:T(8,128)(2,1)S(1)} collective-permute-done((bf16[200,512]{1,0:T(8,128)(2,1)}, bf16[200,512]{1,0:T(8,128)(2,1)S(1)}, u32[]{:S(2)}, u32[]{:S(2)}) %collective-permute-start.43) | collective-permute-done | bytes 204832 | tf_op jit(solution)/shard_map/ppermute | solution.py:36
  214.8 4.1 %collective-permute-done.45.p3 = bf16[200,512]{1,0:T(8,128)(2,1)S(1)} collective-permute-done((bf16[200,512]{1,0:T(8,128)(2,1)}, bf16[200,512]{1,0:T(8,128)(2,1)S(1)}, u32[]{:S(2)}, u32[]{:S(2)}) %collective-permute-start.45) | collective-permute-done | bytes 204832 | tf_op jit(solution)/shard_map/ppermute | solution.py:36
  219.5 12.5 %attention_backward.2 = (f32[200,512]{1,0:T(8,128)}, bf16[200,512]{1,0:T(8,128)(2,1)}, f32[2,512]{1,0:T(2,128)}, bf16[8,64,512]{2,1,0:T(8,128)(2,1)}, bf16[8,64,...) custom-call(s32[8]{0:T(128)} %xor_multiply_fusion.1.refs_0_.off_ref, f32[197,512]{1,0:T(8,128)} %base.1, ...), custom_call_target="tpu_custom_call" | custom-call | flops 1 | bytes 1 | tf_op jit(solution)/shard_map/attention_backward/pallas_call | solution.py:395
  232.1 1.6 collective-permute-start.51
  235.6 5.5 %collective-permute-done.51.refs_11_ = bf16[1,200,512]{2,1,0:T(8,128)(2,1)S(1)} collective-permute-done((bf16[1,200,512]{2,1,0:T(8,128)(2,1)}, bf16[1,200,512]{2,1,0:T(8,128)(2,1)S(1)}, u32[]{:S(2)}, u32[]{:S(2)}) %collective-permute-start.51) | collective-permute-done | bytes 204832 | tf_op jit(solution)/shard_map/ppermute | solution.py:36
  241.2 3.4 collective-permute-done.49.refs_9_
  246.8 2.2 collective-permute-done.54
  252.1 2.3 collective-permute-start.61
  254.4 17.0 %expert_layer.5 = (bf16[4,200,512]{2,1,0:T(8,128)(2,1)}, bf16[4,200,512]{2,1,0:T(8,128)(2,1)}, f32[512,8]{1,0:T(8,128)}, bf16[2,2,4,64,512]{4,3,2,1,0:T(8,128)(2...) custom-call(s32[8]{0:T(128)} %mul.21.refs_0_, ...), custom_call_target="tpu_custom_call" | custom-call | flops 10000000000 | bytes 1 | tf_op jit(solution)/shard_map/expert_layer/pallas_call | solution.py:635
  271.5 2.4 collective-permute-start.65
  275.0 2.3 add_rows.6
  277.8 1.5 collective-permute-start.58
  280.8 2.8 collective-permute-done.61
  283.6 2.8 collective-permute-done.60.p3
  286.4 2.8 collective-permute-done.58.p1
  290.0 12.5 %attention_backward.3 = (f32[197,512]{1,0:T(8,128)}, bf16[200,512]{1,0:T(8,128)(2,1)}, f32[2,512]{1,0:T(2,128)}, bf16[8,64,512]{2,1,0:T(8,128)(2,1)}, bf16[8,64,...) custom-call(s32[8]{0:T(128)} %xor_multiply_fusion.1.refs_0_.off_ref, ...), custom_call_target="tpu_custom_call" | custom-call | flops 1 | bytes 1 | tf_op jit(solution)/shard_map/attention_backward/pallas_call | solution.py:395
  309.4 1.9 fusion.4
  317.4 11.1 %collective-permute-done.66 = bf16[8,64,512]{2,1,0:T(8,128)(2,1)} collective-permute-done((bf16[8,64,512]{2,1,0:T(8,128)(2,1)}, bf16[8,64,512]{2,1,0:T(8,128)(2,1)}, u32[]{:S(2)}, u32[]{:S(2)}) %collective-permute-start.66) | collective-permute-done | bytes 524320 | tf_op jit(solution)/shard_map/ppermute | solution.py:36
  328.5 2.3 collective-permute-start.78
  330.8 2.3 add_rows.7
  340.7 5.6 %collective-permute-done.75 = f32[20,512]{1,0:T(8,128)S(1)} collective-permute-done((f32[20,512]{1,0:T(8,128)S(1)}, f32[20,512]{1,0:T(8,128)S(1)}, u32[]{:S(2)}, u32[]{:S(2)}) %collective-permute-start.75) | collective-permute-done | bytes 40992 | tf_op jit(solution)/shard_map/ppermute | solution.py:36
  348.5 2.9 collective-permute-done.67
  354.2 4.7 %collective-permute-done.77 = bf16[2,2,4,64,512]{4,3,2,1,0:T(8,128)(2,1)S(1)} collective-permute-done((bf16[2,2,4,64,512]{4,3,2,1,0:T(8,128)(2,1)}, bf16[2,2,4,64,512]{4,3,2,1,0:T(8,128)(2,1)S(1)}, u32[]{:S(2)}, u32[]{:S(2)}) %collective-permute-start.77) | collective-permute-done | bytes 1048608 | tf_op jit(solution)/shard_map/ppermute | solution.py:769
  358.9 3.9 collective-permute-done.78
  366.6 2.9 collective-permute-start.82
  378.4 1.9 collective-permute-start.85
  382.2 4.4 %collective-permute-done.84 = f32[20,512]{1,0:T(8,128)S(1)} collective-permute-done((f32[20,512]{1,0:T(8,128)S(1)}, f32[20,512]{1,0:T(8,128)S(1)}, u32[]{:S(2)}, u32[]{:S(2)}) %collective-permute-start.84) | collective-permute-done | bytes 40992 | tf_op jit(solution)/shard_map/ppermute | solution.py:36
  391.3 3.5 collective-permute-start.86
  396.2 1.5 pad_maximum_fusion.1
  397.8 1.6 pad_maximum_fusion
  (386 shorter events, 114.3 us)
Async XLA Ops:
  6.6 10.6 %collective-permute-start.1 = (bf16[1,2,64,512]{3,2,0,1:T(8,128)(2,1)S(1)}, bf16[1,2,64,512]{3,2,0,1:T(8,128)(2,1)S(1)}, u32[]{:S(2)}, u32[]{:S(2)}) collective-permute-start(bf16[1,2,64,512]{3,2,0,1:T(8,128)(2,1)S(1)} %maximum_bitcast_fusion), channel_id=1, source_target_pairs={{0,16},{1,17},{2,18},{3,19},{4,20},{5,21},{6,22},{7,23},{8,24},{9,... | collective-permute-start | bytes 393224 | tf_op jit(solution)/shard_map/ppermute | solution.py:36
  10.7 9.3 %collective-permute-start.4 = (bf16[2,2,64,512]{3,2,0,1:T(8,128)(2,1)S(1)}, bf16[2,2,64,512]{3,2,0,1:T(8,128)(2,1)S(1)}, u32[]{:S(2)}, u32[]{:S(2)}) collective-permute-start(bf16[2,2,64,512]{3,2,0,1:T(8,128)(2,1)S(1)} %get-tuple-element.348), channel_id=1, source_target_pairs={{0,4},{1,5},{2,6},{3,7},{4,0},{5,1},{6,2},{7,3},{8,12},{9,13},{10,... | collective-permute-start | bytes 786440 | tf_op jit(solution)/shard_map/ppermute | solution.py:36
  12.3 13.4 %collective-permute-start.3 = (bf16[2,2,64,512]{3,2,0,1:T(8,128)(2,1)S(1)}, bf16[2,2,64,512]{3,2,0,1:T(8,128)(2,1)S(1)}, u32[]{:S(2)}, u32[]{:S(2)}) collective-permute-start(bf16[2,2,64,512]{3,2,0,1:T(8,128)(2,1)S(1)} %get-tuple-element.349), channel_id=1, source_target_pairs={{0,2},{1,3},{2,0},{3,1},{4,6},{5,7},{6,4},{7,5},{8,10},{9,11},{10,... | collective-permute-start | bytes 786440 | tf_op jit(solution)/shard_map/ppermute | solution.py:36
  13.8 11.9 %collective-permute-start.5 = (bf16[2,2,64,512]{3,2,0,1:T(8,128)(2,1)S(1)}, bf16[2,2,64,512]{3,2,0,1:T(8,128)(2,1)S(1)}, u32[]{:S(2)}, u32[]{:S(2)}) collective-permute-start(bf16[2,2,64,512]{3,2,0,1:T(8,128)(2,1)S(1)} %slice_bitcast_fusion.18), channel_id=1, source_target_pairs={{0,6},{1,7},{2,4},{3,5},{4,2},{5,3},{6,0},{7,1},{8,14},{9,15},{10,... | collective-permute-start | bytes 786440 | tf_op jit(solution)/shard_map/ppermute | solution.py:36
  17.3 8.7 %collective-permute-start.2 = (bf16[2,2,64,512]{3,2,0,1:T(8,128)(2,1)S(1)}, bf16[2,2,64,512]{3,2,0,1:T(8,128)(2,1)S(1)}, u32[]{:S(2)}, u32[]{:S(2)}) collective-permute-start(bf16[2,2,64,512]{3,2,0,1:T(8,128)(2,1)S(1)} %pad_maximum_fusion.15), channel_id=1, source_target_pairs={{0,8},{1,9},{2,10},{3,11},{4,12},{5,13},{6,14},{7,15},{8,0},{9,1},... | collective-permute-start | bytes 786440 | tf_op jit(solution)/shard_map/ppermute | solution.py:36
  26.1 12.7 %collective-permute-start.6 = (bf16[4,2,64,512]{3,2,0,1:T(8,128)(2,1)S(1)}, bf16[4,2,64,512]{3,2,0,1:T(8,128)(2,1)S(1)}, u32[]{:S(2)}, u32[]{:S(2)}) collective-permute-start(bf16[4,2,64,512]{3,2,0,1:T(8,128)(2,1)S(1)} %pad_maximum_fusion.10), channel_id=1, source_target_pairs={{0,4},{1,5},{2,6},{3,7},{4,0},{5,1},{6,2},{7,3},{8,12},{9,13},{10,... | collective-permute-start | bytes 1572872 | tf_op jit(solution)/shard_map/ppermute | solution.py:36
  27.3 27.1 %collective-permute-start.9 = (bf16[2,2,4,64,512]{4,3,2,1,0:T(8,128)(2,1)S(1)}, bf16[2,2,4,64,512]{4,3,2,1,0:T(8,128)(2,1)}, u32[]{:S(2)}, u32[]{:S(2)}) collective-permute-start(bf16[2,2,4,64,512]{4,3,2,1,0:T(8,128)(2,1)S(1)} %bitcast.163), channel_id=1, source_target_pairs={{0,16},{1,9},{2,18},{3,11},{4,20},{5,13},{6,22},{7,15},{8,24},{9,1... | collective-permute-start | bytes 3145736 | tf_op jit(solution)/shard_map/ppermute | solution.py:769
  38.9 11.8 %collective-permute-start.8 = (bf16[8,64,512]{2,1,0:T(8,128)(2,1)S(1)}, bf16[8,64,512]{2,1,0:T(8,128)(2,1)S(1)}, u32[]{:S(2)}, u32[]{:S(2)}) collective-permute-start(bf16[8,64,512]{2,1,0:T(8,128)(2,1)S(1)} %get-tuple-element.336.refs_3_.w0), channel_id=1, source_target_pairs={{0,2},{1,3},{2,0},{3,1},{4,6},{5,7},{6,4},{7,5},{8,10},{9,11},{10,... | collective-permute-start | bytes 1572872 | tf_op jit(solution)/shard_map/ppermute | solution.py:36
  55.2 26.1 %collective-permute-start.26 = (bf16[2,2,4,64,512]{4,3,2,1,0:T(8,128)(2,1)S(1)}, bf16[2,2,4,64,512]{4,3,2,1,0:T(8,128)(2,1)}, u32[]{:S(2)}, u32[]{:S(2)}) collective-permute-start(bf16[2,2,4,64,512]{4,3,2,1,0:T(8,128)(2,1)S(1)} %bitcast.164), channel_id=1, source_target_pairs={{0,8},{1,17},{2,10},{3,19},{4,12},{5,21},{6,14},{7,23},{8,0},{9,25... | collective-permute-start | bytes 3145736 | tf_op jit(solution)/shard_map/ppermute | solution.py:769
  55.5 48.3 %collective-permute-start.27 = (bf16[2,2,4,64,512]{4,3,2,1,0:T(8,128)(2,1)}, bf16[2,2,4,64,512]{4,3,2,1,0:T(8,128)(2,1)}, u32[]{:S(2)}, u32[]{:S(2)}) collective-permute-start(bf16[2,2,4,64,512]{4,3,2,1,0:T(8,128)(2,1)} %collective-permute-done.9.refs_14_.refs_16_), channel_id=1, source_target_pairs={{0,8},{1,17},{2,10},{3,19},{4,12},{5,21},{6,14},{7,23},{8,0},{9,25... | collective-permute-start | bytes 3145736 | tf_op jit(solution)/shard_map/ppermute | solution.py:769
  58.1 14.9 %collective-permute-start.13 = (bf16[2,2,64,512]{3,2,0,1:T(8,128)(2,1)}, bf16[2,2,64,512]{3,2,0,1:T(8,128)(2,1)}, u32[]{:S(2)}, u32[]{:S(2)}) collective-permute-start(bf16[2,2,64,512]{3,2,0,1:T(8,128)(2,1)} %get-tuple-element.338), channel_id=1, source_target_pairs={{0,2},{1,3},{2,0},{3,1},{4,6},{5,7},{6,4},{7,5},{8,10},{9,11},{10,... | collective-permute-start | bytes 786440 | tf_op jit(solution)/shard_map/ppermute | solution.py:36
  59.0 14.1 %collective-permute-start.15 = (bf16[2,2,64,512]{3,2,0,1:T(8,128)(2,1)}, bf16[2,2,64,512]{3,2,0,1:T(8,128)(2,1)S(1)}, u32[]{:S(2)}, u32[]{:S(2)}) collective-permute-start(bf16[2,2,64,512]{3,2,0,1:T(8,128)(2,1)} %get-tuple-element.339), channel_id=1, source_target_pairs={{0,6},{1,7},{2,4},{3,5},{4,2},{5,3},{6,0},{7,1},{8,14},{9,15},{10,... | collective-permute-start | bytes 786440 | tf_op jit(solution)/shard_map/ppermute | solution.py:36
  60.4 13.8 %collective-permute-start.14 = (bf16[2,2,64,512]{3,2,0,1:T(8,128)(2,1)}, bf16[2,2,64,512]{3,2,0,1:T(8,128)(2,1)S(1)}, u32[]{:S(2)}, u32[]{:S(2)}) collective-permute-start(bf16[2,2,64,512]{3,2,0,1:T(8,128)(2,1)} %get-tuple-element.340), channel_id=1, source_target_pairs={{0,4},{1,5},{2,6},{3,7},{4,0},{5,1},{6,2},{7,3},{8,12},{9,13},{10,... | collective-permute-start | bytes 786440 | tf_op jit(solution)/shard_map/ppermute | solution.py:36
  75.4 18.1 %collective-permute-start.24 = (bf16[8,64,512]{2,1,0:T(8,128)(2,1)S(1)}, bf16[8,64,512]{2,1,0:T(8,128)(2,1)S(1)}, u32[]{:S(2)}, u32[]{:S(2)}) collective-permute-start(bf16[8,64,512]{2,1,0:T(8,128)(2,1)S(1)} %get-tuple-element.184.refs_8_.w0), channel_id=1, source_target_pairs={{0,2},{1,3},{2,0},{3,1},{4,6},{5,7},{6,4},{7,5},{8,10},{9,11},{10,... | collective-permute-start | bytes 1572872 | tf_op jit(solution)/shard_map/ppermute | solution.py:36
  76.3 17.3 %collective-permute-start.21 = (bf16[1,200,512]{2,1,0:T(8,128)(2,1)}, bf16[1,200,512]{2,1,0:T(8,128)(2,1)S(1)}, u32[]{:S(2)}, u32[]{:S(2)}) collective-permute-start(bf16[1,200,512]{2,1,0:T(8,128)(2,1)} %get-tuple-element.166.refs_5_), channel_id=1, source_target_pairs={{0,6},{1,7},{2,4},{3,5},{4,2},{5,3},{6,0},{7,1},{8,14},{9,15},{10,... | collective-permute-start | bytes 614408 | tf_op jit(solution)/shard_map/ppermute | solution.py:36
  77.7 16.7 %collective-permute-start.19 = (bf16[1,200,512]{2,1,0:T(8,128)(2,1)}, bf16[1,200,512]{2,1,0:T(8,128)(2,1)S(1)}, u32[]{:S(2)}, u32[]{:S(2)}) collective-permute-start(bf16[1,200,512]{2,1,0:T(8,128)(2,1)} %get-tuple-element.166.refs_5_), channel_id=1, source_target_pairs={{0,4},{1,5},{2,6},{3,7},{4,0},{5,1},{6,2},{7,3},{8,12},{9,13},{10,... | collective-permute-start | bytes 614408 | tf_op jit(solution)/shard_map/ppermute | solution.py:36
  81.3 29.9 %collective-permute-start.23 = (bf16[8,64,512]{2,1,0:T(8,128)(2,1)S(1)}, bf16[8,64,512]{2,1,0:T(8,128)(2,1)S(1)}, u32[]{:S(2)}, u32[]{:S(2)}) collective-permute-start(bf16[8,64,512]{2,1,0:T(8,128)(2,1)S(1)} %get-tuple-element.184.refs_8_.w0), channel_id=1, source_target_pairs={{0,1},{1,0},{2,3},{3,2},{4,5},{5,4},{6,7},{7,6},{8,9},{9,8},{10,11... | collective-permute-start | bytes 1572872 | tf_op jit(solution)/shard_map/ppermute | solution.py:36
  93.5 17.8 %collective-permute-start.25 = (bf16[8,64,512]{2,1,0:T(8,128)(2,1)S(1)}, bf16[8,64,512]{2,1,0:T(8,128)(2,1)S(1)}, u32[]{:S(2)}, u32[]{:S(2)}) collective-permute-start(bf16[8,64,512]{2,1,0:T(8,128)(2,1)S(1)} %collective-permute-done.24.refs_10_.w2), channel_id=1, source_target_pairs={{0,1},{1,0},{2,3},{3,2},{4,5},{5,4},{6,7},{7,6},{8,9},{9,8},{10,11... | collective-permute-start | bytes 1572872 | tf_op jit(solution)/shard_map/ppermute | solution.py:36
  93.5 11.6 %collective-permute-start.17 = (bf16[1,200,512]{2,1,0:T(8,128)(2,1)}, bf16[1,200,512]{2,1,0:T(8,128)(2,1)}, u32[]{:S(2)}, u32[]{:S(2)}) collective-permute-start(bf16[1,200,512]{2,1,0:T(8,128)(2,1)} %get-tuple-element.166.refs_5_), channel_id=1, source_target_pairs={{0,2},{1,3},{2,0},{3,1},{4,6},{5,7},{6,4},{7,5},{8,10},{9,11},{10,... | collective-permute-start | bytes 614408 | tf_op jit(solution)/shard_map/ppermute | solution.py:36
  94.4 11.2 %collective-permute-start.16 = (bf16[1,200,512]{2,1,0:T(8,128)(2,1)}, bf16[1,200,512]{2,1,0:T(8,128)(2,1)S(1)}, u32[]{:S(2)}, u32[]{:S(2)}) collective-permute-start(bf16[1,200,512]{2,1,0:T(8,128)(2,1)} %get-tuple-element.166.refs_5_), channel_id=1, source_target_pairs={{0,1},{1,0},{2,3},{3,2},{4,5},{5,4},{6,7},{7,6},{8,9},{9,8},{10,11... | collective-permute-start | bytes 614408 | tf_op jit(solution)/shard_map/ppermute | solution.py:36
  106.3 43.2 %collective-permute-start.32 = (bf16[2,2,4,64,512]{4,3,2,1,0:T(8,128)(2,1)S(1)}, bf16[2,2,4,64,512]{4,3,2,1,0:T(8,128)(2,1)}, u32[]{:S(2)}, u32[]{:S(2)}) collective-permute-start(bf16[2,2,4,64,512]{4,3,2,1,0:T(8,128)(2,1)S(1)} %bitcast.169), channel_id=1, source_target_pairs={{0,16},{1,9},{2,18},{3,11},{4,20},{5,13},{6,22},{7,15},{8,24},{9,1... | collective-permute-start | bytes 3145736 | tf_op jit(solution)/shard_map/ppermute | solution.py:769
  122.3 33.1 %collective-permute-start.35 = (bf16[2,2,4,64,512]{4,3,2,1,0:T(8,128)(2,1)S(1)}, bf16[2,2,4,64,512]{4,3,2,1,0:T(8,128)(2,1)S(1)}, u32[]{:S(2)}, u32[]{:S(2)}) collective-permute-start(bf16[2,2,4,64,512]{4,3,2,1,0:T(8,128)(2,1)S(1)} %bitcast.170), channel_id=1, source_target_pairs={{0,8},{1,17},{2,10},{3,19},{4,12},{5,21},{6,14},{7,23},{8,0},{9,25... | collective-permute-start | bytes 3145736 | tf_op jit(solution)/shard_map/ppermute | solution.py:769
  129.6 8.2 %collective-permute-start.30 = (bf16[200,512]{1,0:T(8,128)(2,1)}, bf16[200,512]{1,0:T(8,128)(2,1)S(1)}, u32[]{:S(2)}, u32[]{:S(2)}) collective-permute-start(bf16[200,512]{1,0:T(8,128)(2,1)} %get-tuple-element.182), channel_id=1, source_target_pairs={{0,4},{1,5},{2,6},{3,7},{4,0},{5,1},{6,2},{7,3},{8,12},{9,13},{10,... | collective-permute-start | bytes 614408 | tf_op jit(solution)/shard_map/ppermute | solution.py:36
  130.2 10.9 %collective-permute-start.31 = (bf16[200,512]{1,0:T(8,128)(2,1)}, bf16[200,512]{1,0:T(8,128)(2,1)S(1)}, u32[]{:S(2)}, u32[]{:S(2)}) collective-permute-start(bf16[200,512]{1,0:T(8,128)(2,1)} %get-tuple-element.183), channel_id=1, source_target_pairs={{0,6},{1,7},{2,4},{3,5},{4,2},{5,3},{6,0},{7,1},{8,14},{9,15},{10,... | collective-permute-start | bytes 614408 | tf_op jit(solution)/shard_map/ppermute | solution.py:36
  149.6 26.7 %collective-permute-start.41 = (bf16[2,2,4,64,512]{4,3,2,1,0:T(8,128)(2,1)}, bf16[2,2,4,64,512]{4,3,2,1,0:T(8,128)(2,1)}, u32[]{:S(2)}, u32[]{:S(2)}) collective-permute-start(bf16[2,2,4,64,512]{4,3,2,1,0:T(8,128)(2,1)} %collective-permute-done.32.refs_14_), channel_id=1, source_target_pairs={{0,8},{1,17},{2,10},{3,19},{4,12},{5,21},{6,14},{7,23},{8,0},{9,25... | collective-permute-start | bytes 3145736 | tf_op jit(solution)/shard_map/ppermute | solution.py:769
  151.9 13.6 %collective-permute-start.39 = (bf16[2,200,512]{2,1,0:T(8,128)(2,1)}, bf16[2,200,512]{2,1,0:T(8,128)(2,1)S(1)}, u32[]{:S(2)}, u32[]{:S(2)}) collective-permute-start(bf16[2,200,512]{2,1,0:T(8,128)(2,1)} %get-tuple-element.191.refs_5_), channel_id=1, source_target_pairs={{0,6},{1,7},{2,4},{3,5},{4,2},{5,3},{6,0},{7,1},{8,14},{9,15},{10,... | collective-permute-start | bytes 1228808 | tf_op jit(solution)/shard_map/ppermute | solution.py:36
  153.4 18.4 %collective-permute-start.37 = (bf16[2,200,512]{2,1,0:T(8,128)(2,1)}, bf16[2,200,512]{2,1,0:T(8,128)(2,1)S(1)}, u32[]{:S(2)}, u32[]{:S(2)}) collective-permute-start(bf16[2,200,512]{2,1,0:T(8,128)(2,1)} %get-tuple-element.191.refs_5_), channel_id=1, source_target_pairs={{0,4},{1,5},{2,6},{3,7},{4,0},{5,1},{6,2},{7,3},{8,12},{9,13},{10,... | collective-permute-start | bytes 1228808 | tf_op jit(solution)/shard_map/ppermute | solution.py:36
  154.9 16.9 %collective-permute-start.34 = (bf16[2,200,512]{2,1,0:T(8,128)(2,1)}, bf16[2,200,512]{2,1,0:T(8,128)(2,1)S(1)}, u32[]{:S(2)}, u32[]{:S(2)}) collective-permute-start(bf16[2,200,512]{2,1,0:T(8,128)(2,1)} %get-tuple-element.191.refs_5_), channel_id=1, source_target_pairs={{0,2},{1,3},{2,0},{3,1},{4,6},{5,7},{6,4},{7,5},{8,10},{9,11},{10,... | collective-permute-start | bytes 1228808 | tf_op jit(solution)/shard_map/ppermute | solution.py:36
  155.4 17.7 %collective-permute-start.33 = (bf16[2,200,512]{2,1,0:T(8,128)(2,1)}, bf16[2,200,512]{2,1,0:T(8,128)(2,1)S(1)}, u32[]{:S(2)}, u32[]{:S(2)}) collective-permute-start(bf16[2,200,512]{2,1,0:T(8,128)(2,1)} %get-tuple-element.191.refs_5_), channel_id=1, source_target_pairs={{0,1},{1,0},{2,3},{3,2},{4,5},{5,4},{6,7},{7,6},{8,9},{9,8},{10,11... | collective-permute-start | bytes 1228808 | tf_op jit(solution)/shard_map/ppermute | solution.py:36
  165.5 7.7 %collective-permute-start.40 = (bf16[2,200,512]{2,1,0:T(8,128)(2,1)S(1)}, bf16[2,200,512]{2,1,0:T(8,128)(2,1)S(1)}, u32[]{:S(2)}, u32[]{:S(2)}) collective-permute-start(bf16[2,200,512]{2,1,0:T(8,128)(2,1)S(1)} %collective-permute-done.39.refs_11_), channel_id=1, source_target_pairs={{0,1},{1,0},{2,3},{3,2},{4,5},{5,4},{6,7},{7,6},{8,9},{9,8},{10,11... | collective-permute-start | bytes 1228808 | tf_op jit(solution)/shard_map/ppermute | solution.py:36
  200.3 34.2 %collective-permute-start.53 = (bf16[2,2,4,64,512]{4,3,2,1,0:T(8,128)(2,1)}, bf16[2,2,4,64,512]{4,3,2,1,0:T(8,128)(2,1)S(1)}, u32[]{:S(2)}, u32[]{:S(2)}) collective-permute-start(bf16[2,2,4,64,512]{4,3,2,1,0:T(8,128)(2,1)} %get-tuple-element.207), channel_id=1, source_target_pairs={{0,8},{1,17},{2,10},{3,19},{4,12},{5,21},{6,14},{7,23},{8,0},{9,25... | collective-permute-start | bytes 3145736 | tf_op jit(solution)/shard_map/ppermute | solution.py:769
  200.7 48.3 %collective-permute-start.54 = (bf16[2,2,4,64,512]{4,3,2,1,0:T(8,128)(2,1)}, bf16[2,2,4,64,512]{4,3,2,1,0:T(8,128)(2,1)S(1)}, u32[]{:S(2)}, u32[]{:S(2)}) collective-permute-start(bf16[2,2,4,64,512]{4,3,2,1,0:T(8,128)(2,1)} %get-tuple-element.208), channel_id=1, source_target_pairs={{0,8},{1,17},{2,10},{3,19},{4,12},{5,21},{6,14},{7,23},{8,0},{9,25... | collective-permute-start | bytes 3145736 | tf_op jit(solution)/shard_map/ppermute | solution.py:769
  206.6 8.1 %collective-permute-start.44 = (bf16[200,512]{1,0:T(8,128)(2,1)}, bf16[200,512]{1,0:T(8,128)(2,1)S(1)}, u32[]{:S(2)}, u32[]{:S(2)}) collective-permute-start(bf16[200,512]{1,0:T(8,128)(2,1)} %get-tuple-element.199), channel_id=1, source_target_pairs={{0,4},{1,5},{2,6},{3,7},{4,0},{5,1},{6,2},{7,3},{8,12},{9,13},{10,... | collective-permute-start | bytes 614408 | tf_op jit(solution)/shard_map/ppermute | solution.py:36
  207.8 11.1 %collective-permute-start.45 = (bf16[200,512]{1,0:T(8,128)(2,1)}, bf16[200,512]{1,0:T(8,128)(2,1)S(1)}, u32[]{:S(2)}, u32[]{:S(2)}) collective-permute-start(bf16[200,512]{1,0:T(8,128)(2,1)} %get-tuple-element.200), channel_id=1, source_target_pairs={{0,6},{1,7},{2,4},{3,5},{4,2},{5,3},{6,0},{7,1},{8,14},{9,15},{10,... | collective-permute-start | bytes 614408 | tf_op jit(solution)/shard_map/ppermute | solution.py:36
  232.0 13.1 %collective-permute-start.55 = (bf16[8,64,512]{2,1,0:T(8,128)(2,1)}, bf16[8,64,512]{2,1,0:T(8,128)(2,1)S(1)}, u32[]{:S(2)}, u32[]{:S(2)}) collective-permute-start(bf16[8,64,512]{2,1,0:T(8,128)(2,1)} %get-tuple-element.210), channel_id=1, source_target_pairs={{0,1},{1,0},{2,3},{3,2},{4,5},{5,4},{6,7},{7,6},{8,9},{9,8},{10,11... | collective-permute-start | bytes 1572872 | tf_op jit(solution)/shard_map/ppermute | solution.py:36
  232.1 9.1 %collective-permute-start.51 = (bf16[1,200,512]{2,1,0:T(8,128)(2,1)}, bf16[1,200,512]{2,1,0:T(8,128)(2,1)S(1)}, u32[]{:S(2)}, u32[]{:S(2)}) collective-permute-start(bf16[1,200,512]{2,1,0:T(8,128)(2,1)} %bitcast.201), channel_id=1, source_target_pairs={{0,6},{1,7},{2,4},{3,5},{4,2},{5,3},{6,0},{7,1},{8,14},{9,15},{10,... | collective-permute-start | bytes 614408 | tf_op jit(solution)/shard_map/ppermute | solution.py:36
  233.6 10.9 %collective-permute-start.49 = (bf16[1,200,512]{2,1,0:T(8,128)(2,1)}, bf16[1,200,512]{2,1,0:T(8,128)(2,1)S(1)}, u32[]{:S(2)}, u32[]{:S(2)}) collective-permute-start(bf16[1,200,512]{2,1,0:T(8,128)(2,1)} %bitcast.202), channel_id=1, source_target_pairs={{0,4},{1,5},{2,6},{3,7},{4,0},{5,1},{6,2},{7,3},{8,12},{9,13},{10,... | collective-permute-start | bytes 614408 | tf_op jit(solution)/shard_map/ppermute | solution.py:36
  234.5 10.6 %collective-permute-start.47 = (bf16[1,200,512]{2,1,0:T(8,128)(2,1)}, bf16[1,200,512]{2,1,0:T(8,128)(2,1)S(1)}, u32[]{:S(2)}, u32[]{:S(2)}) collective-permute-start(bf16[1,200,512]{2,1,0:T(8,128)(2,1)} %bitcast.203), channel_id=1, source_target_pairs={{0,2},{1,3},{2,0},{3,1},{4,6},{5,7},{6,4},{7,5},{8,10},{9,11},{10,... | collective-permute-start | bytes 614408 | tf_op jit(solution)/shard_map/ppermute | solution.py:36
  241.2 7.8 %collective-permute-start.46 = (bf16[1,200,512]{2,1,0:T(8,128)(2,1)}, bf16[1,200,512]{2,1,0:T(8,128)(2,1)S(1)}, u32[]{:S(2)}, u32[]{:S(2)}) collective-permute-start(bf16[1,200,512]{2,1,0:T(8,128)(2,1)} %bitcast.204), channel_id=1, source_target_pairs={{0,1},{1,0},{2,3},{3,2},{4,5},{5,4},{6,7},{7,6},{8,9},{9,8},{10,11... | collective-permute-start | bytes 614408 | tf_op jit(solution)/shard_map/ppermute | solution.py:36
  249.9 21.6 %collective-permute-start.56 = (bf16[8,64,512]{2,1,0:T(8,128)(2,1)S(1)}, bf16[8,64,512]{2,1,0:T(8,128)(2,1)}, u32[]{:S(2)}, u32[]{:S(2)}) collective-permute-start(bf16[8,64,512]{2,1,0:T(8,128)(2,1)S(1)} %add.103), channel_id=1, source_target_pairs={{0,2},{1,3},{2,0},{3,1},{4,6},{5,7},{6,4},{7,5},{8,10},{9,11},{10,... | collective-permute-start | bytes 1572872 | tf_op jit(solution)/shard_map/ppermute | solution.py:36
  252.1 31.5 %collective-permute-start.61 = (bf16[2,2,4,64,512]{4,3,2,1,0:T(8,128)(2,1)}, bf16[2,2,4,64,512]{4,3,2,1,0:T(8,128)(2,1)}, u32[]{:S(2)}, u32[]{:S(2)}) collective-permute-start(bf16[2,2,4,64,512]{4,3,2,1,0:T(8,128)(2,1)} %add.104), channel_id=1, source_target_pairs={{0,16},{1,9},{2,18},{3,11},{4,20},{5,13},{6,22},{7,15},{8,24},{9,1... | collective-permute-start | bytes 3145736 | tf_op jit(solution)/shard_map/ppermute | solution.py:769
  271.5 31.5 %collective-permute-start.65 = (bf16[2,2,4,64,512]{4,3,2,1,0:T(8,128)(2,1)}, bf16[2,2,4,64,512]{4,3,2,1,0:T(8,128)(2,1)S(1)}, u32[]{:S(2)}, u32[]{:S(2)}) collective-permute-start(bf16[2,2,4,64,512]{4,3,2,1,0:T(8,128)(2,1)} %get-tuple-element.240), channel_id=1, source_target_pairs={{0,8},{1,17},{2,10},{3,19},{4,12},{5,21},{6,14},{7,23},{8,0},{9,25... | collective-permute-start | bytes 3145736 | tf_op jit(solution)/shard_map/ppermute | solution.py:769
  277.3 9.1 %collective-permute-start.60 = (bf16[200,512]{1,0:T(8,128)(2,1)}, bf16[200,512]{1,0:T(8,128)(2,1)S(1)}, u32[]{:S(2)}, u32[]{:S(2)}) collective-permute-start(bf16[200,512]{1,0:T(8,128)(2,1)} %get-tuple-element.229), channel_id=1, source_target_pairs={{0,6},{1,7},{2,4},{3,5},{4,2},{5,3},{6,0},{7,1},{8,14},{9,15},{10,... | collective-permute-start | bytes 614408 | tf_op jit(solution)/shard_map/ppermute | solution.py:36
  277.8 11.4 %collective-permute-start.58 = (bf16[200,512]{1,0:T(8,128)(2,1)}, bf16[200,512]{1,0:T(8,128)(2,1)S(1)}, u32[]{:S(2)}, u32[]{:S(2)}) collective-permute-start(bf16[200,512]{1,0:T(8,128)(2,1)} %get-tuple-element.227), channel_id=1, source_target_pairs={{0,2},{1,3},{2,0},{3,1},{4,6},{5,7},{6,4},{7,5},{8,10},{9,11},{10,... | collective-permute-start | bytes 614408 | tf_op jit(solution)/shard_map/ppermute | solution.py:36
  279.3 9.9 %collective-permute-start.59 = (bf16[200,512]{1,0:T(8,128)(2,1)}, bf16[200,512]{1,0:T(8,128)(2,1)S(1)}, u32[]{:S(2)}, u32[]{:S(2)}) collective-permute-start(bf16[200,512]{1,0:T(8,128)(2,1)} %get-tuple-element.228), channel_id=1, source_target_pairs={{0,4},{1,5},{2,6},{3,7},{4,0},{5,1},{6,2},{7,3},{8,12},{9,13},{10,... | collective-permute-start | bytes 614408 | tf_op jit(solution)/shard_map/ppermute | solution.py:36
  283.6 20.9 %collective-permute-start.64 = (bf16[8,64,512]{2,1,0:T(8,128)(2,1)}, bf16[8,64,512]{2,1,0:T(8,128)(2,1)}, u32[]{:S(2)}, u32[]{:S(2)}) collective-permute-start(bf16[8,64,512]{2,1,0:T(8,128)(2,1)} %get-tuple-element.238), channel_id=1, source_target_pairs={{0,1},{1,0},{2,3},{3,2},{4,5},{5,4},{6,7},{7,6},{8,9},{9,8},{10,11... | collective-permute-start | bytes 1572872 | tf_op jit(solution)/shard_map/ppermute | solution.py:36
  306.5 9.6 %collective-permute-start.73 = (bf16[4,200,512]{2,1,0:T(8,128)(2,1)}, bf16[4,200,512]{2,1,0:T(8,128)(2,1)}, u32[]{:S(2)}, u32[]{:S(2)}) collective-permute-start(bf16[4,200,512]{2,1,0:T(8,128)(2,1)} %get-tuple-element.268), channel_id=1, source_target_pairs={{0,1},{1,0},{2,3},{3,2},{4,5},{5,4},{6,7},{7,6},{8,9},{9,8},{10,11... | collective-permute-start | bytes 2457608 | tf_op jit(solution)/shard_map/ppermute | solution.py:36
  307.8 20.7 %collective-permute-start.66 = (bf16[8,64,512]{2,1,0:T(8,128)(2,1)}, bf16[8,64,512]{2,1,0:T(8,128)(2,1)}, u32[]{:S(2)}, u32[]{:S(2)}) collective-permute-start(bf16[8,64,512]{2,1,0:T(8,128)(2,1)} %add.108), channel_id=1, source_target_pairs={{0,2},{1,3},{2,0},{3,1},{4,6},{5,7},{6,4},{7,5},{8,10},{9,11},{10,... | collective-permute-start | bytes 1572872 | tf_op jit(solution)/shard_map/ppermute | solution.py:36
  311.2 22.0 %collective-permute-start.70 = (bf16[2,2,64,512]{3,2,0,1:T(8,128)(2,1)}, bf16[2,2,64,512]{3,2,0,1:T(8,128)(2,1)S(1)}, u32[]{:S(2)}, u32[]{:S(2)}) collective-permute-start(bf16[2,2,64,512]{3,2,0,1:T(8,128)(2,1)} %get-tuple-element.330), channel_id=1, source_target_pairs={{0,2},{1,3},{2,0},{3,1},{4,6},{5,7},{6,4},{7,5},{8,10},{9,11},{10,... | collective-permute-start | bytes 786440 | tf_op jit(solution)/shard_map/ppermute | solution.py:36
  312.0 21.2 %collective-permute-start.72 = (bf16[2,2,64,512]{3,2,0,1:T(8,128)(2,1)S(1)}, bf16[2,2,64,512]{3,2,0,1:T(8,128)(2,1)S(1)}, u32[]{:S(2)}, u32[]{:S(2)}) collective-permute-start(bf16[2,2,64,512]{3,2,0,1:T(8,128)(2,1)S(1)} %get-tuple-element.331), channel_id=1, source_target_pairs={{0,6},{1,7},{2,4},{3,5},{4,2},{5,3},{6,0},{7,1},{8,14},{9,15},{10,... | collective-permute-start | bytes 786440 | tf_op jit(solution)/shard_map/ppermute | solution.py:36
  313.2 20.0 %collective-permute-start.71 = (bf16[2,2,64,512]{3,2,0,1:T(8,128)(2,1)S(1)}, bf16[2,2,64,512]{3,2,0,1:T(8,128)(2,1)}, u32[]{:S(2)}, u32[]{:S(2)}) collective-permute-start(bf16[2,2,64,512]{3,2,0,1:T(8,128)(2,1)S(1)} %get-tuple-element.332), channel_id=1, source_target_pairs={{0,4},{1,5},{2,6},{3,7},{4,0},{5,1},{6,2},{7,3},{8,12},{9,13},{10,... | collective-permute-start | bytes 786440 | tf_op jit(solution)/shard_map/ppermute | solution.py:36
  316.1 42.8 %collective-permute-start.77 = (bf16[2,2,4,64,512]{4,3,2,1,0:T(8,128)(2,1)}, bf16[2,2,4,64,512]{4,3,2,1,0:T(8,128)(2,1)S(1)}, u32[]{:S(2)}, u32[]{:S(2)}) collective-permute-start(bf16[2,2,4,64,512]{4,3,2,1,0:T(8,128)(2,1)} %add.117), channel_id=1, source_target_pairs={{0,16},{1,9},{2,18},{3,11},{4,20},{5,13},{6,22},{7,15},{8,24},{9,1... | collective-permute-start | bytes 3145736 | tf_op jit(solution)/shard_map/ppermute | solution.py:769
  328.5 34.3 %collective-permute-start.78 = (bf16[2,2,4,64,512]{4,3,2,1,0:T(8,128)(2,1)}, bf16[2,2,4,64,512]{4,3,2,1,0:T(8,128)(2,1)}, u32[]{:S(2)}, u32[]{:S(2)}) collective-permute-start(bf16[2,2,4,64,512]{4,3,2,1,0:T(8,128)(2,1)} %get-tuple-element.277), channel_id=1, source_target_pairs={{0,8},{1,17},{2,10},{3,19},{4,12},{5,21},{6,14},{7,23},{8,0},{9,25... | collective-permute-start | bytes 3145736 | tf_op jit(solution)/shard_map/ppermute | solution.py:769
  336.0 11.6 %collective-permute-start.68 = (bf16[4,64,512]{2,1,0:T(8,128)(2,1)S(1)}, bf16[4,64,512]{2,1,0:T(8,128)(2,1)S(1)}, u32[]{:S(2)}, u32[]{:S(2)}) collective-permute-start(bf16[4,64,512]{2,1,0:T(8,128)(2,1)S(1)} %slice.252), channel_id=1, source_target_pairs={{0,4},{1,5},{2,6},{3,7},{4,0},{5,1},{6,2},{7,3},{8,12},{9,13},{10,... | collective-permute-start | bytes 786440 | tf_op jit(solution)/shard_map/ppermute | solution.py:36
  337.4 8.9 %collective-permute-start.75 = (f32[20,512]{1,0:T(8,128)S(1)}, f32[20,512]{1,0:T(8,128)S(1)}, u32[]{:S(2)}, u32[]{:S(2)}) collective-permute-start(f32[20,512]{1,0:T(8,128)S(1)} %add.114), channel_id=1, source_target_pairs={{0,4},{1,5},{2,6},{3,7},{4,0},{5,1},{6,2},{7,3},{8,12},{9,13},{10,... | collective-permute-start | bytes 122888 | tf_op jit(solution)/shard_map/ppermute | solution.py:36
  339.4 12.0 %collective-permute-start.67 = (bf16[4,64,512]{2,1,0:T(8,128)(2,1)S(1)}, bf16[4,64,512]{2,1,0:T(8,128)(2,1)S(1)}, u32[]{:S(2)}, u32[]{:S(2)}) collective-permute-start(bf16[4,64,512]{2,1,0:T(8,128)(2,1)S(1)} %slice.250), channel_id=1, source_target_pairs={{0,4},{1,5},{2,6},{3,7},{4,0},{5,1},{6,2},{7,3},{8,12},{9,13},{10,... | collective-permute-start | bytes 786440 | tf_op jit(solution)/shard_map/ppermute | solution.py:36
  347.6 15.2 %collective-permute-start.79 = (bf16[200,512]{1,0:T(8,128)(2,1)S(1)}, bf16[200,512]{1,0:T(8,128)(2,1)S(1)}, u32[]{:S(2)}, u32[]{:S(2)}) collective-permute-start(bf16[200,512]{1,0:T(8,128)(2,1)S(1)} %copy-done.68), channel_id=1, source_target_pairs={{0,2},{1,3},{2,0},{3,1},{4,6},{5,7},{6,4},{7,5},{8,10},{9,11},{10,... | collective-permute-start | bytes 614408 | tf_op jit(solution)/shard_map/ppermute | solution.py:36
  351.4 11.5 %collective-permute-start.80 = (bf16[200,512]{1,0:T(8,128)(2,1)S(1)}, bf16[200,512]{1,0:T(8,128)(2,1)S(1)}, u32[]{:S(2)}, u32[]{:S(2)}) collective-permute-start(bf16[200,512]{1,0:T(8,128)(2,1)S(1)} %copy-done.67), channel_id=1, source_target_pairs={{0,4},{1,5},{2,6},{3,7},{4,0},{5,1},{6,2},{7,3},{8,12},{9,13},{10,... | collective-permute-start | bytes 614408 | tf_op jit(solution)/shard_map/ppermute | solution.py:36
  352.6 10.5 %collective-permute-start.81 = (bf16[200,512]{1,0:T(8,128)(2,1)S(1)}, bf16[200,512]{1,0:T(8,128)(2,1)S(1)}, u32[]{:S(2)}, u32[]{:S(2)}) collective-permute-start(bf16[200,512]{1,0:T(8,128)(2,1)S(1)} %copy-done.66), channel_id=1, source_target_pairs={{0,6},{1,7},{2,4},{3,5},{4,2},{5,3},{6,0},{7,1},{8,14},{9,15},{10,... | collective-permute-start | bytes 614408 | tf_op jit(solution)/shard_map/ppermute | solution.py:36
  372.8 15.5 %collective-permute-start.88 = (bf16[2,2,64,512]{3,2,0,1:T(8,128)(2,1)S(1)}, bf16[2,2,64,512]{3,2,0,1:T(8,128)(2,1)S(1)}, u32[]{:S(2)}, u32[]{:S(2)}) collective-permute-start(bf16[2,2,64,512]{3,2,0,1:T(8,128)(2,1)S(1)} %get-tuple-element.325), channel_id=1, source_target_pairs={{0,4},{1,5},{2,6},{3,7},{4,0},{5,1},{6,2},{7,3},{8,12},{9,13},{10,... | collective-permute-start | bytes 786440 | tf_op jit(solution)/shard_map/ppermute | solution.py:36
  373.6 14.7 %collective-permute-start.87 = (bf16[2,2,64,512]{3,2,0,1:T(8,128)(2,1)S(1)}, bf16[2,2,64,512]{3,2,0,1:T(8,128)(2,1)S(1)}, u32[]{:S(2)}, u32[]{:S(2)}) collective-permute-start(bf16[2,2,64,512]{3,2,0,1:T(8,128)(2,1)S(1)} %get-tuple-element.326), channel_id=1, source_target_pairs={{0,2},{1,3},{2,0},{3,1},{4,6},{5,7},{6,4},{7,5},{8,10},{9,11},{10,... | collective-permute-start | bytes 786440 | tf_op jit(solution)/shard_map/ppermute | solution.py:36
  375.0 13.3 %collective-permute-start.89 = (bf16[2,2,64,512]{3,2,0,1:T(8,128)(2,1)S(1)}, bf16[2,2,64,512]{3,2,0,1:T(8,128)(2,1)}, u32[]{:S(2)}, u32[]{:S(2)}) collective-permute-start(bf16[2,2,64,512]{3,2,0,1:T(8,128)(2,1)S(1)} %slice_bitcast_fusion.17), channel_id=1, source_target_pairs={{0,6},{1,7},{2,4},{3,5},{4,2},{5,3},{6,0},{7,1},{8,14},{9,15},{10,... | collective-permute-start | bytes 786440 | tf_op jit(solution)/shard_map/ppermute | solution.py:36
  378.4 11.9 %collective-permute-start.85 = (bf16[2,2,64,512]{3,2,0,1:T(8,128)(2,1)}, bf16[2,2,64,512]{3,2,0,1:T(8,128)(2,1)S(1)}, u32[]{:S(2)}, u32[]{:S(2)}) collective-permute-start(bf16[2,2,64,512]{3,2,0,1:T(8,128)(2,1)} %slice.212), channel_id=1, source_target_pairs={{0,8},{1,9},{2,10},{3,11},{4,12},{5,13},{6,14},{7,15},{8,0},{9,1},... | collective-permute-start | bytes 786440 | tf_op jit(solution)/shard_map/ppermute | solution.py:36
  391.3 9.0 %collective-permute-start.86 = (bf16[1,2,64,512]{3,2,0,1:T(8,128)(2,1)S(1)}, bf16[1,2,64,512]{3,2,0,1:T(8,128)(2,1)S(1)}, u32[]{:S(2)}, u32[]{:S(2)}) collective-permute-start(bf16[1,2,64,512]{3,2,0,1:T(8,128)(2,1)S(1)} %slice.266), channel_id=1, source_target_pairs={{0,16},{1,17},{2,18},{3,19},{4,20},{5,21},{6,22},{7,23},{8,24},{9,... | collective-permute-start | bytes 393224 | tf_op jit(solution)/shard_map/ppermute | solution.py:36
  (103 other events, 843.2 us)

commit v4 on v3

--- a/solution.py
+++ b/solution.py
@@ -109,6 +109,7 @@
 
 
 LANES = 256
+SPLIT = 2
 
 
 def slot_kernel(experts, mine_ref, ids, rank, mine, theirs):
@@ -264,16 +265,19 @@
     unit, unused = normalized(rows)
     normed_a = (unit * gains[0:1]).astype(bf16)
     low, high = head_masks()
+    for group in copies:
+        for copy in group:
+            copy.wait()
+    for j in range(4):
+        qkv[:, j * 6 * HD : (j + 1) * 6 * HD] = dot(normed_a, wbuf[j, :, : 6 * HD]).astype(bf16)
+    probs = []
+    for j in range(4):
+        part = qkv[:, j * 6 * HD : (j + 1) * 6 * HD]
+        probs.append([head_probs(part[:, : 2 * HD], part[:, 2 * HD : 4 * HD], m).astype(bf16) for m in (low, high)])
     total = rows
     for j in range(4):
-        for copy in copies[j]:
-            copy.wait()
-        part = dot(normed_a, wbuf[j, :, : 6 * HD]).astype(bf16)
-        qkv[:, j * 6 * HD : (j + 1) * 6 * HD] = part
-        queries, keys, values = part[:, : 2 * HD], part[:, 2 * HD : 4 * HD], part[:, 4 * HD :]
-        first = dot(head_probs(queries, keys, low).astype(bf16), values)
-        second = dot(head_probs(queries, keys, high).astype(bf16), values)
-        context = jnp.where(low, first, second).astype(bf16)
+        values = qkv[:, j * 6 * HD + 4 * HD : (j + 1) * 6 * HD]
+        context = jnp.where(low, dot(probs[j][0], values), dot(probs[j][1], values)).astype(bf16)
         ctx[:, j * 2 * HD : (j + 1) * 2 * HD] = context
         total = total + dot_t(context, wbuf[j, :, 6 * HD :])
     mid[...] = total
@@ -343,35 +347,33 @@
     normed_t = (unit * gains[0:1]).astype(bf16).T
     low, high = head_masks()
     scale = HD ** (-0.5)
+    for group in copies:
+        for copy in group:
+            copy.wait()
+    heads = [(j, mask) for j in range(4) for mask in (low, high)]
+    parts = [qkv[:, j * 6 * HD : (j + 1) * 6 * HD] for j in range(4)]
+    queries = [part[:, : 2 * HD] for part in parts]
+    keys = [part[:, 2 * HD : 4 * HD] for part in parts]
+    values = [part[:, 4 * HD :] for part in parts]
+    context_grads = [dot(attn_grad, wbuf[j, :, 6 * HD :]).astype(bf16) for j in range(4)]
+    probs = [head_probs(queries[j], keys[j], mask) for j, mask in heads]
+    probs_grads = [dot_t(only(context_grads[j], mask), values[j]) for j, mask in heads]
+    v_grads = [t_dot(probs[i].astype(bf16), context_grads[j]) for i, (j, mask) in enumerate(heads)]
+    score_grads = [
+        (p * (g - jnp.sum(p * g, axis=-1, keepdims=True))).astype(bf16) for p, g in zip(probs, probs_grads)
+    ]
+    q_grads = [dot(score_grads[i], keys[j]) * scale for i, (j, mask) in enumerate(heads)]
+    k_grads = [t_dot(score_grads[i], queries[j]) * scale for i, (j, mask) in enumerate(heads)]
     normed_part = jnp.zeros_like(grad)
     sends = []
     for j, target in enumerate((g0, g1, g2, g3)):
-        for copy in copies[j]:
-            copy.wait()
-        part = qkv[:, j * 6 * HD : (j + 1) * 6 * HD]
-        queries, keys, values = part[:, : 2 * HD], part[:, 2 * HD : 4 * HD], part[:, 4 * HD :]
+        mixed = jnp.concatenate(
+            [jnp.where(low, g[2 * j], g[2 * j + 1]).astype(bf16) for g in (q_grads, k_grads, v_grads)], axis=1
+        )
         context = ctx[:, j * 2 * HD : (j + 1) * 2 * HD]
-        context_grad = dot(attn_grad, wbuf[j, :, 6 * HD :]).astype(bf16)
-        query_grad, key_grad, value_grad = None, None, None
-        for mask in (low, high):
-            probs = head_probs(queries, keys, mask)
-            v_grad = t_dot(probs.astype(bf16), context_grad)
-            probs_grad = dot_t(only(context_grad, mask), values)
-            inner = jnp.sum(probs * probs_grad, axis=-1, keepdims=True)
-            score_grad = (probs * (probs_grad - inner)).astype(bf16)
-            q_grad = dot(score_grad, keys) * scale
-            k_grad = t_dot(score_grad, queries) * scale
-            if query_grad is None:
-                query_grad, key_grad, value_grad = q_grad, k_grad, v_grad
-            else:
-                query_grad = jnp.where(mask, q_grad, query_grad).astype(bf16)
-                key_grad = jnp.where(mask, k_grad, key_grad).astype(bf16)
-                value_grad = jnp.where(mask, v_grad, value_grad).astype(bf16)
-        for place, mixed in enumerate((query_grad, key_grad, value_grad)):
-            lanes = slice(place * 2 * HD, (place + 1) * 2 * HD)
-            gbuf[j, :, lanes] = dot(normed_t, mixed).astype(bf16)
-            normed_part = normed_part + dot_t(mixed, wbuf[j, :, lanes])
+        gbuf[j, :, : 6 * HD] = dot(normed_t, mixed).astype(bf16)
         gbuf[j, :, 6 * HD :] = dot(attn_grad_t, context).astype(bf16)
+        normed_part = normed_part + dot_t(mixed, wbuf[j, :, : 6 * HD])
         count, rows, unused = target.shape
         for i in range(count):
             send = pltpu.make_async_copy(
@@ -443,7 +445,7 @@
         targets = take(len(plan.grad_shapes))
     in_buf, out_buf, sent_buf, y_buf = take(4)
     if backward:
-        slot_buf, slot_t, sent_t, back_buf, gbuf, out_sems = take(6)
+        slot_buf, branch_buf, slot_t, sent_t, back_buf, gbuf, out_sems = take(7)
     (sems,) = take(1)
 
     near, chunks, rows, width = plan.block
@@ -503,44 +505,16 @@
     is_mine = lax.broadcasted_iota(jnp.int32, probs.shape, 1) == me_ref[0]
     gate = jnp.sum(jnp.where(is_mine, probs, 0.0), axis=-1, keepdims=True)
 
+    if backward:
+        for g, rows_g in gather(plan.grads):
+            part = slice(g * SLOTS, (g + 1) * SLOTS)
+            slot_buf[part] = (gate[part] * rows_g).astype(bf16)
+            branch_buf[part] = rows_g.astype(bf16)
+        slot_t[...] = slot_buf[...].T
+        sent_t[...] = sent.T
+        back_buf[...] = jnp.zeros_like(back_buf)
     if forward:
         y_buf[...] = jnp.zeros_like(y_buf)
-
-        @pl.loop(0, chunks)
-        def _(c):
-            for copy in loads(c, 0):
-                copy.wait()
-            pre = dot(sent_buf[...], in_buf[c])
-            act = (0.5 * pre * (1.0 + jnp.tanh(ROOT * (pre + CUBE * (pre * pre * pre))))).astype(bf16)
-            for copy in loads(c, 1):
-                copy.wait()
-            y_buf[...] += dot_t(act, out_buf[c])
-
-        expert_y = y_buf[...]
-        scatter((gate * expert_y).astype(bf16), parts)
-        if not backward:
-            sent_out[...] = sent
-            y_out[...] = expert_y
-    else:
-        for c in range(chunks):
-            for which in (0, 1):
-                for copy in loads(c, which):
-                    copy.wait()
-        expert_y = y_in[...]
-    if not backward:
-        return
-
-    for g, rows_g in gather(plan.grads):
-        part = slice(g * SLOTS, (g + 1) * SLOTS)
-        slot_buf[part] = (gate[part] * rows_g).astype(bf16)
-        y_buf[part] = rows_g
-    gate_grad = jnp.sum(y_buf[...] * expert_y, axis=-1, keepdims=True)
-    slot_t[...] = slot_buf[...].T
-    sent_t[...] = sent.T
-    logit_grad = gate_grad * gate * (is_mine.astype(f32) - probs)
-    first, second = split(logit_grad)
-    router_grad[...] = dot(sent_t[...], first) + dot(sent_t[...], second)
-    back_buf[...] = dot_t(first, router[...]) + dot_t(second, router[...])
 
     def stores(c, which):
         result = []
@@ -556,29 +530,55 @@
                 )
         return result
 
-    @pl.loop(0, chunks)
-    def _(c):
-        pre = dot(sent_buf[...], in_buf[c])
-        square = pre * pre
-        bend = jnp.tanh(ROOT * (pre + CUBE * (square * pre)))
-        act = (0.5 * pre * (1.0 + bend)).astype(bf16)
-        gbuf[1, c] = dot(slot_t[...], act).astype(bf16)
-        for copy in stores(c, 1):
-            copy.start()
-        slope = 0.5 * (1.0 + bend) + 0.5 * pre * (1.0 - bend * bend) * (ROOT * (1.0 + 3.0 * CUBE * square))
-        pre_grad = (dot(slot_buf[...], out_buf[c]) * slope).astype(bf16)
-        gbuf[0, c] = dot(sent_t[...], pre_grad).astype(bf16)
-        for copy in stores(c, 0):
-            copy.start()
-        back_buf[...] += dot_t(pre_grad, in_buf[c])
-
-    scatter(back_buf[...].astype(bf16), back_parts)
+    halves = [slice(h * width // SPLIT, (h + 1) * width // SPLIT) for h in range(SPLIT)]
 
     @pl.loop(0, chunks)
     def _(c):
         for which in (0, 1):
-            for copy in stores(c, which):
+            for copy in loads(c, which):
                 copy.wait()
+        pres = [dot(sent_buf[...], in_buf[c, :, at]) for at in halves]
+        act_grads = [dot(slot_buf[...], out_buf[c, :, at]) for at in halves] if backward else None
+        for h, at in enumerate(halves):
+            pre = pres[h]
+            square = pre * pre
+            bend = jnp.tanh(pre * (ROOT + ROOT * CUBE * square))
+            rise = 0.5 + 0.5 * bend
+            act = pre * rise
+            low_act = act.astype(bf16)
+            if forward:
+                y_buf[...] += dot_t(low_act, out_buf[c, :, at])
+            if backward:
+                gbuf[1, c, :, at] = dot(slot_t[...], low_act).astype(bf16)
+                slope = rise + act * ((1.0 - bend) * (ROOT + 3.0 * ROOT * CUBE * square))
+                pre_grad = (act_grads[h] * slope).astype(bf16)
+                gbuf[0, c, :, at] = dot(sent_t[...], pre_grad).astype(bf16)
+                back_buf[...] += dot_t(pre_grad, in_buf[c, :, at])
+        if backward:
+            for which in (1, 0):
+                for copy in stores(c, which):
+                    copy.start()
+
+    expert_y = y_buf[...] if forward else y_in[...]
+    if backward:
+        gate_grad = jnp.sum(branch_buf[...].astype(f32) * expert_y, axis=-1, keepdims=True)
+        logit_grad = gate_grad * gate * (is_mine.astype(f32) - probs)
+        first, second = split(logit_grad)
+        router_grad[...] = dot(sent_t[...], first) + dot(sent_t[...], second)
+        back_buf[...] += dot_t(first, router[...]) + dot_t(second, router[...])
+        scatter(back_buf[...].astype(bf16), back_parts)
+    if forward:
+        scatter((gate * expert_y).astype(bf16), parts)
+        if not backward:
+            sent_out[...] = sent
+            y_out[...] = expert_y
+    if backward:
+
+        @pl.loop(0, chunks)
+        def _(c):
+            for which in (0, 1):
+                for copy in stores(c, which):
+                    copy.wait()
 
 
 class Plan:
@@ -624,6 +624,7 @@
     ]
     if backward:
         scratch += [
+            pltpu.VMEM((slots, width), bf16),
             pltpu.VMEM((slots, width), bf16),
             pltpu.VMEM((width, slots), bf16),
             pltpu.VMEM((width, slots), bf16),

time: 410 us -> 400 us (0.976)
  Pallas kernels: 102 us -> 83.3 us
  waiting for transfers between devices: 147 us -> 154 us
    ppermute x12, waiting for transfers between devices: 30.9 us -> 42.1 us  [mixed(): return lax.ppermute(value, AXES, pairs)]
    pallas_call x3, Pallas kernels: 49.9 us -> 42.1 us  [expert_layer(): pl.pallas_call(lambda *refs: expert_kernel(plan, *refs), out_shape=tuple(...]
    pallas_call x2, Pallas kernels: 24.9 us -> 17.6 us  [attention_backward(): pl.pallas_call(attention_backward_kernel, out_shape=(shape((out_rows, wid...]
    ppermute x78, starting transfers between devices: 71.8 us -> 76.7 us  [swap(): return lax.ppermute(value, AXES, pairs)]
    ppermute x78, waiting for transfers between devices: 116 us -> 111 us  [swap(): return lax.ppermute(value, AXES, pairs)]
  transfers between devices with their start and end apart: 90 -> 90, of which waited for: 45 -> 42; matrix products, arithmetic and copies ran while one was open for 10% -> 10% of each run, Pallas kernels for 20% -> 17%
where the time goes in v4:
time: 400 us; the launch traced here: 393 us
  waiting for transfers between devices  154 us (38%)
  starting transfers between devices  95.6 us (24%)
  Pallas kernels  83.3 us (21%)
  local copies, waits for them, and re-layouts  31.8 us (8%)
  other arithmetic  26.5 us (7%)
    ppermute x78, waiting for transfers between devices, swap(): return lax.ppermute(value, AXES, pairs)  111 us
    ppermute x78, starting transfers between devices, swap(): return lax.ppermute(value, AXES, pairs)  76.7 us
    ppermute x12, waiting for transfers between devices, mixed(): return lax.ppermute(value, AXES, pairs)  42.1 us
    pallas_call x3, Pallas kernels, expert_layer(): pl.pallas_call(lambda *refs: expert_kernel(plan, *refs), out_shape=tuple(...  42.1 us
    ppermute x12, starting transfers between devices, mixed(): return lax.ppermute(value, AXES, pairs)  18.9 us
    pallas_call x2, Pallas kernels, attention_backward(): pl.pallas_call(attention_backward_kernel, out_shape=(shape((out_rows, wid...  17.6 us
    unnamed x162, local copies, waits for them, and re-layouts  12.9 us
    pallas_call x2, Pallas kernels, attention_forward(): pl.pallas_call(lambda *refs: attention_forward_kernel(len(pieces), len(ex...  11.9 us
  transfers between devices with their start and end apart: 90, of which 42 were waited for; matrix products, arithmetic and copies ran while one was open for 10% of the time, Pallas kernels for 17%

profile of v4, /device:TPU:0, one launch (start us, length us, event | category | flops | bytes accessed | tf_op | source)
XLA Modules:
  0.0 392.9 jit_solution(13932263577609281353)
XLA Ops:
  6.6 4.0 %collective-permute-start.1 = (bf16[1,2,64,512]{3,2,0,1:T(8,128)(2,1)S(1)}, bf16[1,2,64,512]{3,2,0,1:T(8,128)(2,1)S(1)}, u32[]{:S(2)}, u32[]{:S(2)}) collective-permute-start(bf16[1,2,64,512]{3,2,0,1:T(8,128)(2,1)S(1)} %maximum_bitcast_fusion), channel_id=1, source_target_pairs={{0,16},{1,17},{2,18},{3,19},{4,20},{5,21},{6,22},{7,23},{8,24},{9,... | collective-permute-start | bytes 393224 | tf_op jit(solution)/shard_map/ppermute | solution.py:36
  10.7 1.6 collective-permute-start.4
  12.3 1.5 collective-permute-start.3
  14.3 3.0 collective-permute-done.1
  18.1 1.9 collective-permute-done.4
  20.0 5.7 %collective-permute-done.3 = bf16[2,2,64,512]{3,2,0,1:T(8,128)(2,1)S(1)} collective-permute-done((bf16[2,2,64,512]{3,2,0,1:T(8,128)(2,1)S(1)}, bf16[2,2,64,512]{3,2,0,1:T(8,128)(2,1)S(1)}, u32[]{:S(2)}, u32[]{:S(2)}) %collective-permute-start.3) | collective-permute-done | bytes 262176 | tf_op jit(solution)/shard_map/ppermute | solution.py:36
  27.3 2.2 collective-permute-start.9
  29.6 9.1 %collective-permute-done.6 = bf16[4,2,64,512]{3,2,0,1:T(8,128)(2,1)S(1)} collective-permute-done((bf16[4,2,64,512]{3,2,0,1:T(8,128)(2,1)S(1)}, bf16[4,2,64,512]{3,2,0,1:T(8,128)(2,1)S(1)}, u32[]{:S(2)}, u32[]{:S(2)}) %collective-permute-start.6) | collective-permute-done | bytes 524320 | tf_op jit(solution)/shard_map/ppermute | solution.py:36
  41.5 2.3 slots.1
  46.7 1.6 gather_fusion.3
  50.7 3.7 collective-permute-done.9.refs_14_.refs_16_
  55.5 1.7 collective-permute-start.27
  62.8 5.5 %attention_forward.2 = (f32[200,512]{1,0:T(8,128)}, f32[200,512]{1,0:T(8,128)}, bf16[1,200,512]{2,1,0:T(8,128)(2,1)}, bf16[200,1536]{1,0:T(8,128)(2,1)}, bf16[200,512]{1,0:T(8,128)(2,1)}) custom-call(s32[8]{0:T(128)} %xor_multiply_fusion.1.refs_0_.off_ref, bf16[197,512]{1,0:T(8,128)(2,1)} %refs_1_.1, f32[2,512]{1,0:T(2,128)} %get-tuple-element.359.refs_2_.gains, ...), custom_call_target="tpu_custom_call" | custom-call | flops 1 | bytes 1 | tf_op jit(solution)/shard_map/attention_forward/pallas_call | solution.py:309
  68.4 4.7 %collective-permute-done.13 = bf16[2,2,64,512]{3,2,0,1:T(8,128)(2,1)} collective-permute-done((bf16[2,2,64,512]{3,2,0,1:T(8,128)(2,1)}, bf16[2,2,64,512]{3,2,0,1:T(8,128)(2,1)}, u32[]{:S(2)}, u32[]{:S(2)}) %collective-permute-start.13) | collective-permute-done | bytes 262176 | tf_op jit(solution)/shard_map/ppermute | solution.py:36
  78.9 2.4 collective-permute-done.26.refs_15_.refs_17_
  81.3 12.1 %collective-permute-done.24.refs_10_.w2 = bf16[8,64,512]{2,1,0:T(8,128)(2,1)S(1)} collective-permute-done((bf16[8,64,512]{2,1,0:T(8,128)(2,1)S(1)}, bf16[8,64,512]{2,1,0:T(8,128)(2,1)S(1)}, u32[]{:S(2)}, u32[]{:S(2)}) %collective-permute-start.24) | collective-permute-done | bytes 524320 | tf_op jit(solution)/shard_map/ppermute | solution.py:36
  94.7 9.1 %collective-permute-done.27.refs_16_.refs_18_ = bf16[2,2,4,64,512]{4,3,2,1,0:T(8,128)(2,1)} collective-permute-done((bf16[2,2,4,64,512]{4,3,2,1,0:T(8,128)(2,1)}, bf16[2,2,4,64,512]{4,3,2,1,0:T(8,128)(2,1)}, u32[]{:S(2)}, u32[]{:S(2)}) %collective-permute-start.27) | collective-permute-done | bytes 1048608 | tf_op jit(solution)/shard_map/ppermute | solution.py:770
  106.3 1.5 collective-permute-start.32
  111.3 10.1 %expert_layer.3 = (bf16[4,200,512]{2,1,0:T(8,128)(2,1)}, bf16[4,200,512]{2,1,0:T(8,128)(2,1)}, bf16[512,512]{1,0:T(8,128)(2,1)}, f32[512,512]{1,0:T(8,128)}) custom-call(s32[8]{0:T(128)} %mul.21.refs_0_, s32[1]{0:T(128)} %bitcast.31.refs_1_, s32[2,4,256]{2,1,0:T(4,128)} %get-tuple-element.160.refs_2_, s32[2,4,256]{2,1,0:T(4,128)} %copy-done.59, ...), custom_call_target="tpu_custom_call" | custom-call | flops 1 | bytes 1 | tf_op jit(solution)/shard_map/expert_layer/pallas_call | solution.py:636
  121.6 2.4 collective-permute-start.35
  125.0 2.3 add_rows.4
  127.4 1.5 collective-permute-start.29
  130.9 3.8 collective-permute-done.29.refs_3_
  134.7 2.4 collective-permute-done.30.refs_4_
  137.1 3.2 collective-permute-done.31.refs_5_
  141.0 6.4 %attention_forward.3 = (f32[200,512]{1,0:T(8,128)}, f32[200,512]{1,0:T(8,128)}, bf16[2,200,512]{2,1,0:T(8,128)(2,1)}, bf16[200,1536]{1,0:T(8,128)(2,1)}, bf16[200,512]{1,0:T(8,128)(2,1)}) custom-call(s32[8]{0:T(128)} %xor_multiply_fusion.1.refs_0_.off_ref, f32[200,512]{1,0:T(8,128)} %get-tuple-element.159.refs_1_.hidden_mid, ...), custom_call_target="tpu_custom_call" | custom-call | flops 1 | bytes 1 | tf_op jit(solution)/shard_map/attention_forward/pallas_call | solution.py:309
  147.4 2.4 collective-permute-start.41
  154.0 2.8 collective-permute-start.33
  156.8 6.5 %collective-permute-done.39.refs_11_ = bf16[2,200,512]{2,1,0:T(8,128)(2,1)S(1)} collective-permute-done((bf16[2,200,512]{2,1,0:T(8,128)(2,1)}, bf16[2,200,512]{2,1,0:T(8,128)(2,1)S(1)}, u32[]{:S(2)}, u32[]{:S(2)}) %collective-permute-start.39) | collective-permute-done | bytes 409632 | tf_op jit(solution)/shard_map/ppermute | solution.py:36
  163.3 6.3 %collective-permute-done.37.refs_9_ = bf16[2,200,512]{2,1,0:T(8,128)(2,1)S(1)} collective-permute-done((bf16[2,200,512]{2,1,0:T(8,128)(2,1)}, bf16[2,200,512]{2,1,0:T(8,128)(2,1)S(1)}, u32[]{:S(2)}, u32[]{:S(2)}) %collective-permute-start.37) | collective-permute-done | bytes 409632 | tf_op jit(solution)/shard_map/ppermute | solution.py:36
  172.1 3.0 collective-permute-done.41.refs_16_
  175.1 17.2 %expert_layer.4 = (bf16[4,200,512]{2,1,0:T(8,128)(2,1)}, bf16[4,200,512]{2,1,0:T(8,128)(2,1)}, bf16[4,200,512]{2,1,0:T(8,128)(2,1)}, bf16[4,200,512]{2,1,0:T(8,1...) custom-call(s32[8]{0:T(128)} %mul.21.refs_0_, ...), custom_call_target="tpu_custom_call" | custom-call | flops 1 | bytes 1 | tf_op jit(solution)/shard_map/expert_layer/pallas_call | solution.py:636
  192.3 3.1 collective-permute-start.42
  195.8 1.7 collective-permute-start.54
  198.5 2.3 add_rows.5
  204.3 4.1 %collective-permute-done.43.p1 = bf16[200,512]{1,0:T(8,128)(2,1)S(1)} collective-permute-done((bf16[200,512]{1,0:T(8,128)(2,1)}, bf16[200,512]{1,0:T(8,128)(2,1)S(1)}, u32[]{:S(2)}, u32[]{:S(2)}) %collective-permute-start.43) | collective-permute-done | bytes 204832 | tf_op jit(solution)/shard_map/ppermute | solution.py:36
  209.9 4.1 %collective-permute-done.45.p3 = bf16[200,512]{1,0:T(8,128)(2,1)S(1)} collective-permute-done((bf16[200,512]{1,0:T(8,128)(2,1)}, bf16[200,512]{1,0:T(8,128)(2,1)S(1)}, u32[]{:S(2)}, u32[]{:S(2)}) %collective-permute-start.45) | collective-permute-done | bytes 204832 | tf_op jit(solution)/shard_map/ppermute | solution.py:36
  214.7 8.8 %attention_backward.2 = (f32[200,512]{1,0:T(8,128)}, bf16[200,512]{1,0:T(8,128)(2,1)}, f32[2,512]{1,0:T(2,128)}, bf16[8,64,512]{2,1,0:T(8,128)(2,1)}, bf16[8,64,...) custom-call(s32[8]{0:T(128)} %xor_multiply_fusion.1.refs_0_.off_ref, f32[197,512]{1,0:T(8,128)} %base.1, ...), custom_call_target="tpu_custom_call" | custom-call | flops 1 | bytes 1 | tf_op jit(solution)/shard_map/attention_backward/pallas_call | solution.py:397
  223.6 1.5 collective-permute-start.51
  227.1 5.5 %collective-permute-done.51.refs_11_ = bf16[1,200,512]{2,1,0:T(8,128)(2,1)S(1)} collective-permute-done((bf16[1,200,512]{2,1,0:T(8,128)(2,1)}, bf16[1,200,512]{2,1,0:T(8,128)(2,1)S(1)}, u32[]{:S(2)}, u32[]{:S(2)}) %collective-permute-start.51) | collective-permute-done | bytes 204832 | tf_op jit(solution)/shard_map/ppermute | solution.py:36
  232.7 3.3 collective-permute-done.49.refs_9_
  238.3 5.5 %collective-permute-done.54 = bf16[2,2,4,64,512]{4,3,2,1,0:T(8,128)(2,1)S(1)} collective-permute-done((bf16[2,2,4,64,512]{4,3,2,1,0:T(8,128)(2,1)}, bf16[2,2,4,64,512]{4,3,2,1,0:T(8,128)(2,1)S(1)}, u32[]{:S(2)}, u32[]{:S(2)}) %collective-permute-start.54) | collective-permute-done | bytes 1048608 | tf_op jit(solution)/shard_map/ppermute | solution.py:770
  247.2 1.8 collective-permute-start.61
  249.0 14.8 %expert_layer.5 = (bf16[4,200,512]{2,1,0:T(8,128)(2,1)}, bf16[4,200,512]{2,1,0:T(8,128)(2,1)}, f32[512,8]{1,0:T(8,128)}, bf16[2,2,4,64,512]{4,3,2,1,0:T(8,128)(2...) custom-call(s32[8]{0:T(128)} %mul.21.refs_0_, ...), custom_call_target="tpu_custom_call" | custom-call | flops 10000000000 | bytes 1 | tf_op jit(solution)/shard_map/expert_layer/pallas_call | solution.py:636
  263.8 2.4 collective-permute-start.65
  267.3 2.3 add_rows.6
  273.1 10.0 %collective-permute-done.61 = bf16[2,2,4,64,512]{4,3,2,1,0:T(8,128)(2,1)} collective-permute-done((bf16[2,2,4,64,512]{4,3,2,1,0:T(8,128)(2,1)}, bf16[2,2,4,64,512]{4,3,2,1,0:T(8,128)(2,1)}, u32[]{:S(2)}, u32[]{:S(2)}) %collective-permute-start.61) | collective-permute-done | bytes 1048608 | tf_op jit(solution)/shard_map/ppermute | solution.py:770
  283.9 8.8 %attention_backward.3 = (f32[197,512]{1,0:T(8,128)}, bf16[200,512]{1,0:T(8,128)(2,1)}, f32[2,512]{1,0:T(2,128)}, bf16[8,64,512]{2,1,0:T(8,128)(2,1)}, bf16[8,64,...) custom-call(s32[8]{0:T(128)} %xor_multiply_fusion.1.refs_0_.off_ref, ...), custom_call_target="tpu_custom_call" | custom-call | flops 1 | bytes 1 | tf_op jit(solution)/shard_map/attention_backward/pallas_call | solution.py:397
  296.7 2.3 collective-permute-start.69
  301.1 1.9 fusion.4
  307.9 12.8 %collective-permute-done.66 = bf16[8,64,512]{2,1,0:T(8,128)(2,1)} collective-permute-done((bf16[8,64,512]{2,1,0:T(8,128)(2,1)}, bf16[8,64,512]{2,1,0:T(8,128)(2,1)}, u32[]{:S(2)}, u32[]{:S(2)}) %collective-permute-start.66) | collective-permute-done | bytes 524320 | tf_op jit(solution)/shard_map/ppermute | solution.py:36
  320.7 2.1 collective-permute-start.78
  322.8 2.3 add_rows.7
  332.9 6.0 %collective-permute-done.75 = f32[20,512]{1,0:T(8,128)S(1)} collective-permute-done((f32[20,512]{1,0:T(8,128)S(1)}, f32[20,512]{1,0:T(8,128)S(1)}, u32[]{:S(2)}, u32[]{:S(2)}) %collective-permute-start.75) | collective-permute-done | bytes 40992 | tf_op jit(solution)/shard_map/ppermute | solution.py:36
  341.1 2.9 collective-permute-done.67
  346.3 7.6 %collective-permute-done.78 = bf16[2,2,4,64,512]{4,3,2,1,0:T(8,128)(2,1)} collective-permute-done((bf16[2,2,4,64,512]{4,3,2,1,0:T(8,128)(2,1)}, bf16[2,2,4,64,512]{4,3,2,1,0:T(8,128)(2,1)}, u32[]{:S(2)}, u32[]{:S(2)}) %collective-permute-start.78) | collective-permute-done | bytes 1048608 | tf_op jit(solution)/shard_map/ppermute | solution.py:770
  358.2 3.0 collective-permute-start.82
  365.4 1.6 collective-permute-start.87
  370.3 1.7 collective-permute-start.85
  371.9 2.2 collective-permute-start.84
  374.9 3.2 collective-permute-done.84
  382.8 3.5 collective-permute-start.86
  387.8 1.5 pad_maximum_fusion.1
  389.4 1.6 pad_maximum_fusion
  (386 shorter events, 110.4 us)
Async XLA Ops:
  6.6 10.6 %collective-permute-start.1 = (bf16[1,2,64,512]{3,2,0,1:T(8,128)(2,1)S(1)}, bf16[1,2,64,512]{3,2,0,1:T(8,128)(2,1)S(1)}, u32[]{:S(2)}, u32[]{:S(2)}) collective-permute-start(bf16[1,2,64,512]{3,2,0,1:T(8,128)(2,1)S(1)} %maximum_bitcast_fusion), channel_id=1, source_target_pairs={{0,16},{1,17},{2,18},{3,19},{4,20},{5,21},{6,22},{7,23},{8,24},{9,... | collective-permute-start | bytes 393224 | tf_op jit(solution)/shard_map/ppermute | solution.py:36
  10.7 9.3 %collective-permute-start.4 = (bf16[2,2,64,512]{3,2,0,1:T(8,128)(2,1)S(1)}, bf16[2,2,64,512]{3,2,0,1:T(8,128)(2,1)S(1)}, u32[]{:S(2)}, u32[]{:S(2)}) collective-permute-start(bf16[2,2,64,512]{3,2,0,1:T(8,128)(2,1)S(1)} %get-tuple-element.348), channel_id=1, source_target_pairs={{0,4},{1,5},{2,6},{3,7},{4,0},{5,1},{6,2},{7,3},{8,12},{9,13},{10,... | collective-permute-start | bytes 786440 | tf_op jit(solution)/shard_map/ppermute | solution.py:36
  12.3 13.4 %collective-permute-start.3 = (bf16[2,2,64,512]{3,2,0,1:T(8,128)(2,1)S(1)}, bf16[2,2,64,512]{3,2,0,1:T(8,128)(2,1)S(1)}, u32[]{:S(2)}, u32[]{:S(2)}) collective-permute-start(bf16[2,2,64,512]{3,2,0,1:T(8,128)(2,1)S(1)} %get-tuple-element.349), channel_id=1, source_target_pairs={{0,2},{1,3},{2,0},{3,1},{4,6},{5,7},{6,4},{7,5},{8,10},{9,11},{10,... | collective-permute-start | bytes 786440 | tf_op jit(solution)/shard_map/ppermute | solution.py:36
  13.8 11.9 %collective-permute-start.5 = (bf16[2,2,64,512]{3,2,0,1:T(8,128)(2,1)S(1)}, bf16[2,2,64,512]{3,2,0,1:T(8,128)(2,1)S(1)}, u32[]{:S(2)}, u32[]{:S(2)}) collective-permute-start(bf16[2,2,64,512]{3,2,0,1:T(8,128)(2,1)S(1)} %slice_bitcast_fusion.18), channel_id=1, source_target_pairs={{0,6},{1,7},{2,4},{3,5},{4,2},{5,3},{6,0},{7,1},{8,14},{9,15},{10,... | collective-permute-start | bytes 786440 | tf_op jit(solution)/shard_map/ppermute | solution.py:36
  17.3 8.7 %collective-permute-start.2 = (bf16[2,2,64,512]{3,2,0,1:T(8,128)(2,1)S(1)}, bf16[2,2,64,512]{3,2,0,1:T(8,128)(2,1)S(1)}, u32[]{:S(2)}, u32[]{:S(2)}) collective-permute-start(bf16[2,2,64,512]{3,2,0,1:T(8,128)(2,1)S(1)} %pad_maximum_fusion.15), channel_id=1, source_target_pairs={{0,8},{1,9},{2,10},{3,11},{4,12},{5,13},{6,14},{7,15},{8,0},{9,1},... | collective-permute-start | bytes 786440 | tf_op jit(solution)/shard_map/ppermute | solution.py:36
  26.1 12.7 %collective-permute-start.6 = (bf16[4,2,64,512]{3,2,0,1:T(8,128)(2,1)S(1)}, bf16[4,2,64,512]{3,2,0,1:T(8,128)(2,1)S(1)}, u32[]{:S(2)}, u32[]{:S(2)}) collective-permute-start(bf16[4,2,64,512]{3,2,0,1:T(8,128)(2,1)S(1)} %pad_maximum_fusion.10), channel_id=1, source_target_pairs={{0,4},{1,5},{2,6},{3,7},{4,0},{5,1},{6,2},{7,3},{8,12},{9,13},{10,... | collective-permute-start | bytes 1572872 | tf_op jit(solution)/shard_map/ppermute | solution.py:36
  27.3 27.1 %collective-permute-start.9 = (bf16[2,2,4,64,512]{4,3,2,1,0:T(8,128)(2,1)S(1)}, bf16[2,2,4,64,512]{4,3,2,1,0:T(8,128)(2,1)}, u32[]{:S(2)}, u32[]{:S(2)}) collective-permute-start(bf16[2,2,4,64,512]{4,3,2,1,0:T(8,128)(2,1)S(1)} %bitcast.163), channel_id=1, source_target_pairs={{0,16},{1,9},{2,18},{3,11},{4,20},{5,13},{6,22},{7,15},{8,24},{9,1... | collective-permute-start | bytes 3145736 | tf_op jit(solution)/shard_map/ppermute | solution.py:770
  38.9 11.8 %collective-permute-start.8 = (bf16[8,64,512]{2,1,0:T(8,128)(2,1)S(1)}, bf16[8,64,512]{2,1,0:T(8,128)(2,1)S(1)}, u32[]{:S(2)}, u32[]{:S(2)}) collective-permute-start(bf16[8,64,512]{2,1,0:T(8,128)(2,1)S(1)} %get-tuple-element.336.refs_3_.w0), channel_id=1, source_target_pairs={{0,2},{1,3},{2,0},{3,1},{4,6},{5,7},{6,4},{7,5},{8,10},{9,11},{10,... | collective-permute-start | bytes 1572872 | tf_op jit(solution)/shard_map/ppermute | solution.py:36
  55.2 26.1 %collective-permute-start.26 = (bf16[2,2,4,64,512]{4,3,2,1,0:T(8,128)(2,1)S(1)}, bf16[2,2,4,64,512]{4,3,2,1,0:T(8,128)(2,1)}, u32[]{:S(2)}, u32[]{:S(2)}) collective-permute-start(bf16[2,2,4,64,512]{4,3,2,1,0:T(8,128)(2,1)S(1)} %bitcast.164), channel_id=1, source_target_pairs={{0,8},{1,17},{2,10},{3,19},{4,12},{5,21},{6,14},{7,23},{8,0},{9,25... | collective-permute-start | bytes 3145736 | tf_op jit(solution)/shard_map/ppermute | solution.py:770
  55.5 48.3 %collective-permute-start.27 = (bf16[2,2,4,64,512]{4,3,2,1,0:T(8,128)(2,1)}, bf16[2,2,4,64,512]{4,3,2,1,0:T(8,128)(2,1)}, u32[]{:S(2)}, u32[]{:S(2)}) collective-permute-start(bf16[2,2,4,64,512]{4,3,2,1,0:T(8,128)(2,1)} %collective-permute-done.9.refs_14_.refs_16_), channel_id=1, source_target_pairs={{0,8},{1,17},{2,10},{3,19},{4,12},{5,21},{6,14},{7,23},{8,0},{9,25... | collective-permute-start | bytes 3145736 | tf_op jit(solution)/shard_map/ppermute | solution.py:770
  58.1 14.9 %collective-permute-start.13 = (bf16[2,2,64,512]{3,2,0,1:T(8,128)(2,1)}, bf16[2,2,64,512]{3,2,0,1:T(8,128)(2,1)}, u32[]{:S(2)}, u32[]{:S(2)}) collective-permute-start(bf16[2,2,64,512]{3,2,0,1:T(8,128)(2,1)} %get-tuple-element.338), channel_id=1, source_target_pairs={{0,2},{1,3},{2,0},{3,1},{4,6},{5,7},{6,4},{7,5},{8,10},{9,11},{10,... | collective-permute-start | bytes 786440 | tf_op jit(solution)/shard_map/ppermute | solution.py:36
  59.0 14.1 %collective-permute-start.15 = (bf16[2,2,64,512]{3,2,0,1:T(8,128)(2,1)}, bf16[2,2,64,512]{3,2,0,1:T(8,128)(2,1)S(1)}, u32[]{:S(2)}, u32[]{:S(2)}) collective-permute-start(bf16[2,2,64,512]{3,2,0,1:T(8,128)(2,1)} %get-tuple-element.339), channel_id=1, source_target_pairs={{0,6},{1,7},{2,4},{3,5},{4,2},{5,3},{6,0},{7,1},{8,14},{9,15},{10,... | collective-permute-start | bytes 786440 | tf_op jit(solution)/shard_map/ppermute | solution.py:36
  60.4 13.8 %collective-permute-start.14 = (bf16[2,2,64,512]{3,2,0,1:T(8,128)(2,1)}, bf16[2,2,64,512]{3,2,0,1:T(8,128)(2,1)S(1)}, u32[]{:S(2)}, u32[]{:S(2)}) collective-permute-start(bf16[2,2,64,512]{3,2,0,1:T(8,128)(2,1)} %get-tuple-element.340), channel_id=1, source_target_pairs={{0,4},{1,5},{2,6},{3,7},{4,0},{5,1},{6,2},{7,3},{8,12},{9,13},{10,... | collective-permute-start | bytes 786440 | tf_op jit(solution)/shard_map/ppermute | solution.py:36
  75.4 18.1 %collective-permute-start.24 = (bf16[8,64,512]{2,1,0:T(8,128)(2,1)S(1)}, bf16[8,64,512]{2,1,0:T(8,128)(2,1)S(1)}, u32[]{:S(2)}, u32[]{:S(2)}) collective-permute-start(bf16[8,64,512]{2,1,0:T(8,128)(2,1)S(1)} %get-tuple-element.184.refs_8_.w0), channel_id=1, source_target_pairs={{0,2},{1,3},{2,0},{3,1},{4,6},{5,7},{6,4},{7,5},{8,10},{9,11},{10,... | collective-permute-start | bytes 1572872 | tf_op jit(solution)/shard_map/ppermute | solution.py:36
  76.3 17.3 %collective-permute-start.21 = (bf16[1,200,512]{2,1,0:T(8,128)(2,1)}, bf16[1,200,512]{2,1,0:T(8,128)(2,1)S(1)}, u32[]{:S(2)}, u32[]{:S(2)}) collective-permute-start(bf16[1,200,512]{2,1,0:T(8,128)(2,1)} %get-tuple-element.166.refs_5_), channel_id=1, source_target_pairs={{0,6},{1,7},{2,4},{3,5},{4,2},{5,3},{6,0},{7,1},{8,14},{9,15},{10,... | collective-permute-start | bytes 614408 | tf_op jit(solution)/shard_map/ppermute | solution.py:36
  77.7 16.7 %collective-permute-start.19 = (bf16[1,200,512]{2,1,0:T(8,128)(2,1)}, bf16[1,200,512]{2,1,0:T(8,128)(2,1)S(1)}, u32[]{:S(2)}, u32[]{:S(2)}) collective-permute-start(bf16[1,200,512]{2,1,0:T(8,128)(2,1)} %get-tuple-element.166.refs_5_), channel_id=1, source_target_pairs={{0,4},{1,5},{2,6},{3,7},{4,0},{5,1},{6,2},{7,3},{8,12},{9,13},{10,... | collective-permute-start | bytes 614408 | tf_op jit(solution)/shard_map/ppermute | solution.py:36
  81.3 29.9 %collective-permute-start.23 = (bf16[8,64,512]{2,1,0:T(8,128)(2,1)S(1)}, bf16[8,64,512]{2,1,0:T(8,128)(2,1)S(1)}, u32[]{:S(2)}, u32[]{:S(2)}) collective-permute-start(bf16[8,64,512]{2,1,0:T(8,128)(2,1)S(1)} %get-tuple-element.184.refs_8_.w0), channel_id=1, source_target_pairs={{0,1},{1,0},{2,3},{3,2},{4,5},{5,4},{6,7},{7,6},{8,9},{9,8},{10,11... | collective-permute-start | bytes 1572872 | tf_op jit(solution)/shard_map/ppermute | solution.py:36
  93.5 17.8 %collective-permute-start.25 = (bf16[8,64,512]{2,1,0:T(8,128)(2,1)S(1)}, bf16[8,64,512]{2,1,0:T(8,128)(2,1)S(1)}, u32[]{:S(2)}, u32[]{:S(2)}) collective-permute-start(bf16[8,64,512]{2,1,0:T(8,128)(2,1)S(1)} %collective-permute-done.24.refs_10_.w2), channel_id=1, source_target_pairs={{0,1},{1,0},{2,3},{3,2},{4,5},{5,4},{6,7},{7,6},{8,9},{9,8},{10,11... | collective-permute-start | bytes 1572872 | tf_op jit(solution)/shard_map/ppermute | solution.py:36
  93.5 11.6 %collective-permute-start.17 = (bf16[1,200,512]{2,1,0:T(8,128)(2,1)}, bf16[1,200,512]{2,1,0:T(8,128)(2,1)}, u32[]{:S(2)}, u32[]{:S(2)}) collective-permute-start(bf16[1,200,512]{2,1,0:T(8,128)(2,1)} %get-tuple-element.166.refs_5_), channel_id=1, source_target_pairs={{0,2},{1,3},{2,0},{3,1},{4,6},{5,7},{6,4},{7,5},{8,10},{9,11},{10,... | collective-permute-start | bytes 614408 | tf_op jit(solution)/shard_map/ppermute | solution.py:36
  94.4 11.2 %collective-permute-start.16 = (bf16[1,200,512]{2,1,0:T(8,128)(2,1)}, bf16[1,200,512]{2,1,0:T(8,128)(2,1)S(1)}, u32[]{:S(2)}, u32[]{:S(2)}) collective-permute-start(bf16[1,200,512]{2,1,0:T(8,128)(2,1)} %get-tuple-element.166.refs_5_), channel_id=1, source_target_pairs={{0,1},{1,0},{2,3},{3,2},{4,5},{5,4},{6,7},{7,6},{8,9},{9,8},{10,11... | collective-permute-start | bytes 614408 | tf_op jit(solution)/shard_map/ppermute | solution.py:36
  106.3 41.0 %collective-permute-start.32 = (bf16[2,2,4,64,512]{4,3,2,1,0:T(8,128)(2,1)S(1)}, bf16[2,2,4,64,512]{4,3,2,1,0:T(8,128)(2,1)}, u32[]{:S(2)}, u32[]{:S(2)}) collective-permute-start(bf16[2,2,4,64,512]{4,3,2,1,0:T(8,128)(2,1)S(1)} %bitcast.169), channel_id=1, source_target_pairs={{0,16},{1,9},{2,18},{3,11},{4,20},{5,13},{6,22},{7,15},{8,24},{9,1... | collective-permute-start | bytes 3145736 | tf_op jit(solution)/shard_map/ppermute | solution.py:770
  121.6 32.4 %collective-permute-start.35 = (bf16[2,2,4,64,512]{4,3,2,1,0:T(8,128)(2,1)S(1)}, bf16[2,2,4,64,512]{4,3,2,1,0:T(8,128)(2,1)S(1)}, u32[]{:S(2)}, u32[]{:S(2)}) collective-permute-start(bf16[2,2,4,64,512]{4,3,2,1,0:T(8,128)(2,1)S(1)} %bitcast.170), channel_id=1, source_target_pairs={{0,8},{1,17},{2,10},{3,19},{4,12},{5,21},{6,14},{7,23},{8,0},{9,25... | collective-permute-start | bytes 3145736 | tf_op jit(solution)/shard_map/ppermute | solution.py:770
  128.9 8.2 %collective-permute-start.30 = (bf16[200,512]{1,0:T(8,128)(2,1)}, bf16[200,512]{1,0:T(8,128)(2,1)S(1)}, u32[]{:S(2)}, u32[]{:S(2)}) collective-permute-start(bf16[200,512]{1,0:T(8,128)(2,1)} %get-tuple-element.182), channel_id=1, source_target_pairs={{0,4},{1,5},{2,6},{3,7},{4,0},{5,1},{6,2},{7,3},{8,12},{9,13},{10,... | collective-permute-start | bytes 614408 | tf_op jit(solution)/shard_map/ppermute | solution.py:36
  129.4 10.8 %collective-permute-start.31 = (bf16[200,512]{1,0:T(8,128)(2,1)}, bf16[200,512]{1,0:T(8,128)(2,1)S(1)}, u32[]{:S(2)}, u32[]{:S(2)}) collective-permute-start(bf16[200,512]{1,0:T(8,128)(2,1)} %get-tuple-element.183), channel_id=1, source_target_pairs={{0,6},{1,7},{2,4},{3,5},{4,2},{5,3},{6,0},{7,1},{8,14},{9,15},{10,... | collective-permute-start | bytes 614408 | tf_op jit(solution)/shard_map/ppermute | solution.py:36
  147.4 27.7 %collective-permute-start.41 = (bf16[2,2,4,64,512]{4,3,2,1,0:T(8,128)(2,1)}, bf16[2,2,4,64,512]{4,3,2,1,0:T(8,128)(2,1)}, u32[]{:S(2)}, u32[]{:S(2)}) collective-permute-start(bf16[2,2,4,64,512]{4,3,2,1,0:T(8,128)(2,1)} %collective-permute-done.32.refs_14_), channel_id=1, source_target_pairs={{0,8},{1,17},{2,10},{3,19},{4,12},{5,21},{6,14},{7,23},{8,0},{9,25... | collective-permute-start | bytes 3145736 | tf_op jit(solution)/shard_map/ppermute | solution.py:770
  149.7 13.6 %collective-permute-start.39 = (bf16[2,200,512]{2,1,0:T(8,128)(2,1)}, bf16[2,200,512]{2,1,0:T(8,128)(2,1)S(1)}, u32[]{:S(2)}, u32[]{:S(2)}) collective-permute-start(bf16[2,200,512]{2,1,0:T(8,128)(2,1)} %get-tuple-element.191.refs_5_), channel_id=1, source_target_pairs={{0,6},{1,7},{2,4},{3,5},{4,2},{5,3},{6,0},{7,1},{8,14},{9,15},{10,... | collective-permute-start | bytes 1228808 | tf_op jit(solution)/shard_map/ppermute | solution.py:36
  151.2 18.4 %collective-permute-start.37 = (bf16[2,200,512]{2,1,0:T(8,128)(2,1)}, bf16[2,200,512]{2,1,0:T(8,128)(2,1)S(1)}, u32[]{:S(2)}, u32[]{:S(2)}) collective-permute-start(bf16[2,200,512]{2,1,0:T(8,128)(2,1)} %get-tuple-element.191.refs_5_), channel_id=1, source_target_pairs={{0,4},{1,5},{2,6},{3,7},{4,0},{5,1},{6,2},{7,3},{8,12},{9,13},{10,... | collective-permute-start | bytes 1228808 | tf_op jit(solution)/shard_map/ppermute | solution.py:36
  152.7 16.9 %collective-permute-start.34 = (bf16[2,200,512]{2,1,0:T(8,128)(2,1)}, bf16[2,200,512]{2,1,0:T(8,128)(2,1)S(1)}, u32[]{:S(2)}, u32[]{:S(2)}) collective-permute-start(bf16[2,200,512]{2,1,0:T(8,128)(2,1)} %get-tuple-element.191.refs_5_), channel_id=1, source_target_pairs={{0,2},{1,3},{2,0},{3,1},{4,6},{5,7},{6,4},{7,5},{8,10},{9,11},{10,... | collective-permute-start | bytes 1228808 | tf_op jit(solution)/shard_map/ppermute | solution.py:36
  154.0 17.0 %collective-permute-start.33 = (bf16[2,200,512]{2,1,0:T(8,128)(2,1)}, bf16[2,200,512]{2,1,0:T(8,128)(2,1)S(1)}, u32[]{:S(2)}, u32[]{:S(2)}) collective-permute-start(bf16[2,200,512]{2,1,0:T(8,128)(2,1)} %get-tuple-element.191.refs_5_), channel_id=1, source_target_pairs={{0,1},{1,0},{2,3},{3,2},{4,5},{5,4},{6,7},{7,6},{8,9},{9,8},{10,11... | collective-permute-start | bytes 1228808 | tf_op jit(solution)/shard_map/ppermute | solution.py:36
  195.4 30.5 %collective-permute-start.53 = (bf16[2,2,4,64,512]{4,3,2,1,0:T(8,128)(2,1)}, bf16[2,2,4,64,512]{4,3,2,1,0:T(8,128)(2,1)S(1)}, u32[]{:S(2)}, u32[]{:S(2)}) collective-permute-start(bf16[2,2,4,64,512]{4,3,2,1,0:T(8,128)(2,1)} %get-tuple-element.207), channel_id=1, source_target_pairs={{0,8},{1,17},{2,10},{3,19},{4,12},{5,21},{6,14},{7,23},{8,0},{9,25... | collective-permute-start | bytes 3145736 | tf_op jit(solution)/shard_map/ppermute | solution.py:770
  195.8 48.0 %collective-permute-start.54 = (bf16[2,2,4,64,512]{4,3,2,1,0:T(8,128)(2,1)}, bf16[2,2,4,64,512]{4,3,2,1,0:T(8,128)(2,1)S(1)}, u32[]{:S(2)}, u32[]{:S(2)}) collective-permute-start(bf16[2,2,4,64,512]{4,3,2,1,0:T(8,128)(2,1)} %get-tuple-element.208), channel_id=1, source_target_pairs={{0,8},{1,17},{2,10},{3,19},{4,12},{5,21},{6,14},{7,23},{8,0},{9,25... | collective-permute-start | bytes 3145736 | tf_op jit(solution)/shard_map/ppermute | solution.py:770
  201.7 8.1 %collective-permute-start.44 = (bf16[200,512]{1,0:T(8,128)(2,1)}, bf16[200,512]{1,0:T(8,128)(2,1)S(1)}, u32[]{:S(2)}, u32[]{:S(2)}) collective-permute-start(bf16[200,512]{1,0:T(8,128)(2,1)} %get-tuple-element.199), channel_id=1, source_target_pairs={{0,4},{1,5},{2,6},{3,7},{4,0},{5,1},{6,2},{7,3},{8,12},{9,13},{10,... | collective-permute-start | bytes 614408 | tf_op jit(solution)/shard_map/ppermute | solution.py:36
  202.9 11.1 %collective-permute-start.45 = (bf16[200,512]{1,0:T(8,128)(2,1)}, bf16[200,512]{1,0:T(8,128)(2,1)S(1)}, u32[]{:S(2)}, u32[]{:S(2)}) collective-permute-start(bf16[200,512]{1,0:T(8,128)(2,1)} %get-tuple-element.200), channel_id=1, source_target_pairs={{0,6},{1,7},{2,4},{3,5},{4,2},{5,3},{6,0},{7,1},{8,14},{9,15},{10,... | collective-permute-start | bytes 614408 | tf_op jit(solution)/shard_map/ppermute | solution.py:36
  223.5 13.1 %collective-permute-start.55 = (bf16[8,64,512]{2,1,0:T(8,128)(2,1)}, bf16[8,64,512]{2,1,0:T(8,128)(2,1)S(1)}, u32[]{:S(2)}, u32[]{:S(2)}) collective-permute-start(bf16[8,64,512]{2,1,0:T(8,128)(2,1)} %get-tuple-element.210), channel_id=1, source_target_pairs={{0,1},{1,0},{2,3},{3,2},{4,5},{5,4},{6,7},{7,6},{8,9},{9,8},{10,11... | collective-permute-start | bytes 1572872 | tf_op jit(solution)/shard_map/ppermute | solution.py:36
  223.6 9.1 %collective-permute-start.51 = (bf16[1,200,512]{2,1,0:T(8,128)(2,1)}, bf16[1,200,512]{2,1,0:T(8,128)(2,1)S(1)}, u32[]{:S(2)}, u32[]{:S(2)}) collective-permute-start(bf16[1,200,512]{2,1,0:T(8,128)(2,1)} %bitcast.201), channel_id=1, source_target_pairs={{0,6},{1,7},{2,4},{3,5},{4,2},{5,3},{6,0},{7,1},{8,14},{9,15},{10,... | collective-permute-start | bytes 614408 | tf_op jit(solution)/shard_map/ppermute | solution.py:36
  225.1 10.9 %collective-permute-start.49 = (bf16[1,200,512]{2,1,0:T(8,128)(2,1)}, bf16[1,200,512]{2,1,0:T(8,128)(2,1)S(1)}, u32[]{:S(2)}, u32[]{:S(2)}) collective-permute-start(bf16[1,200,512]{2,1,0:T(8,128)(2,1)} %bitcast.202), channel_id=1, source_target_pairs={{0,4},{1,5},{2,6},{3,7},{4,0},{5,1},{6,2},{7,3},{8,12},{9,13},{10,... | collective-permute-start | bytes 614408 | tf_op jit(solution)/shard_map/ppermute | solution.py:36
  225.9 10.6 %collective-permute-start.47 = (bf16[1,200,512]{2,1,0:T(8,128)(2,1)}, bf16[1,200,512]{2,1,0:T(8,128)(2,1)S(1)}, u32[]{:S(2)}, u32[]{:S(2)}) collective-permute-start(bf16[1,200,512]{2,1,0:T(8,128)(2,1)} %bitcast.203), channel_id=1, source_target_pairs={{0,2},{1,3},{2,0},{3,1},{4,6},{5,7},{6,4},{7,5},{8,10},{9,11},{10,... | collective-permute-start | bytes 614408 | tf_op jit(solution)/shard_map/ppermute | solution.py:36
  232.7 11.1 %collective-permute-start.46 = (bf16[1,200,512]{2,1,0:T(8,128)(2,1)}, bf16[1,200,512]{2,1,0:T(8,128)(2,1)S(1)}, u32[]{:S(2)}, u32[]{:S(2)}) collective-permute-start(bf16[1,200,512]{2,1,0:T(8,128)(2,1)} %bitcast.204), channel_id=1, source_target_pairs={{0,1},{1,0},{2,3},{3,2},{4,5},{5,4},{6,7},{7,6},{8,9},{9,8},{10,11... | collective-permute-start | bytes 614408 | tf_op jit(solution)/shard_map/ppermute | solution.py:36
  236.0 7.8 %collective-permute-start.52 = (bf16[1,200,512]{2,1,0:T(8,128)(2,1)S(1)}, bf16[1,200,512]{2,1,0:T(8,128)(2,1)S(1)}, u32[]{:S(2)}, u32[]{:S(2)}) collective-permute-start(bf16[1,200,512]{2,1,0:T(8,128)(2,1)S(1)} %collective-permute-done.51.refs_11_), channel_id=1, source_target_pairs={{0,1},{1,0},{2,3},{3,2},{4,5},{5,4},{6,7},{7,6},{8,9},{9,8},{10,11... | collective-permute-start | bytes 614408 | tf_op jit(solution)/shard_map/ppermute | solution.py:36
  244.7 19.1 %collective-permute-start.56 = (bf16[8,64,512]{2,1,0:T(8,128)(2,1)S(1)}, bf16[8,64,512]{2,1,0:T(8,128)(2,1)}, u32[]{:S(2)}, u32[]{:S(2)}) collective-permute-start(bf16[8,64,512]{2,1,0:T(8,128)(2,1)S(1)} %add.103), channel_id=1, source_target_pairs={{0,2},{1,3},{2,0},{3,1},{4,6},{5,7},{6,4},{7,5},{8,10},{9,11},{10,... | collective-permute-start | bytes 1572872 | tf_op jit(solution)/shard_map/ppermute | solution.py:36
  247.2 35.8 %collective-permute-start.61 = (bf16[2,2,4,64,512]{4,3,2,1,0:T(8,128)(2,1)}, bf16[2,2,4,64,512]{4,3,2,1,0:T(8,128)(2,1)}, u32[]{:S(2)}, u32[]{:S(2)}) collective-permute-start(bf16[2,2,4,64,512]{4,3,2,1,0:T(8,128)(2,1)} %add.104), channel_id=1, source_target_pairs={{0,16},{1,9},{2,18},{3,11},{4,20},{5,13},{6,22},{7,15},{8,24},{9,1... | collective-permute-start | bytes 3145736 | tf_op jit(solution)/shard_map/ppermute | solution.py:770
  263.8 29.5 %collective-permute-start.65 = (bf16[2,2,4,64,512]{4,3,2,1,0:T(8,128)(2,1)}, bf16[2,2,4,64,512]{4,3,2,1,0:T(8,128)(2,1)S(1)}, u32[]{:S(2)}, u32[]{:S(2)}) collective-permute-start(bf16[2,2,4,64,512]{4,3,2,1,0:T(8,128)(2,1)} %get-tuple-element.240), channel_id=1, source_target_pairs={{0,8},{1,17},{2,10},{3,19},{4,12},{5,21},{6,14},{7,23},{8,0},{9,25... | collective-permute-start | bytes 3145736 | tf_op jit(solution)/shard_map/ppermute | solution.py:770
  269.6 13.4 %collective-permute-start.60 = (bf16[200,512]{1,0:T(8,128)(2,1)}, bf16[200,512]{1,0:T(8,128)(2,1)S(1)}, u32[]{:S(2)}, u32[]{:S(2)}) collective-permute-start(bf16[200,512]{1,0:T(8,128)(2,1)} %get-tuple-element.229), channel_id=1, source_target_pairs={{0,6},{1,7},{2,4},{3,5},{4,2},{5,3},{6,0},{7,1},{8,14},{9,15},{10,... | collective-permute-start | bytes 614408 | tf_op jit(solution)/shard_map/ppermute | solution.py:36
  270.1 13.0 %collective-permute-start.58 = (bf16[200,512]{1,0:T(8,128)(2,1)}, bf16[200,512]{1,0:T(8,128)(2,1)S(1)}, u32[]{:S(2)}, u32[]{:S(2)}) collective-permute-start(bf16[200,512]{1,0:T(8,128)(2,1)} %get-tuple-element.227), channel_id=1, source_target_pairs={{0,2},{1,3},{2,0},{3,1},{4,6},{5,7},{6,4},{7,5},{8,10},{9,11},{10,... | collective-permute-start | bytes 614408 | tf_op jit(solution)/shard_map/ppermute | solution.py:36
  271.6 11.5 %collective-permute-start.59 = (bf16[200,512]{1,0:T(8,128)(2,1)}, bf16[200,512]{1,0:T(8,128)(2,1)S(1)}, u32[]{:S(2)}, u32[]{:S(2)}) collective-permute-start(bf16[200,512]{1,0:T(8,128)(2,1)} %get-tuple-element.228), channel_id=1, source_target_pairs={{0,4},{1,5},{2,6},{3,7},{4,0},{5,1},{6,2},{7,3},{8,12},{9,13},{10,... | collective-permute-start | bytes 614408 | tf_op jit(solution)/shard_map/ppermute | solution.py:36
  283.1 11.7 %collective-permute-start.64 = (bf16[8,64,512]{2,1,0:T(8,128)(2,1)}, bf16[8,64,512]{2,1,0:T(8,128)(2,1)}, u32[]{:S(2)}, u32[]{:S(2)}) collective-permute-start(bf16[8,64,512]{2,1,0:T(8,128)(2,1)} %get-tuple-element.238), channel_id=1, source_target_pairs={{0,1},{1,0},{2,3},{3,2},{4,5},{5,4},{6,7},{7,6},{8,9},{9,8},{10,11... | collective-permute-start | bytes 1572872 | tf_op jit(solution)/shard_map/ppermute | solution.py:36
  299.1 8.8 %collective-permute-start.73 = (bf16[4,200,512]{2,1,0:T(8,128)(2,1)}, bf16[4,200,512]{2,1,0:T(8,128)(2,1)}, u32[]{:S(2)}, u32[]{:S(2)}) collective-permute-start(bf16[4,200,512]{2,1,0:T(8,128)(2,1)} %get-tuple-element.268), channel_id=1, source_target_pairs={{0,1},{1,0},{2,3},{3,2},{4,5},{5,4},{6,7},{7,6},{8,9},{9,8},{10,11... | collective-permute-start | bytes 2457608 | tf_op jit(solution)/shard_map/ppermute | solution.py:36
  300.0 20.7 %collective-permute-start.66 = (bf16[8,64,512]{2,1,0:T(8,128)(2,1)}, bf16[8,64,512]{2,1,0:T(8,128)(2,1)}, u32[]{:S(2)}, u32[]{:S(2)}) collective-permute-start(bf16[8,64,512]{2,1,0:T(8,128)(2,1)} %add.108), channel_id=1, source_target_pairs={{0,2},{1,3},{2,0},{3,1},{4,6},{5,7},{6,4},{7,5},{8,10},{9,11},{10,... | collective-permute-start | bytes 1572872 | tf_op jit(solution)/shard_map/ppermute | solution.py:36
  303.0 22.8 %collective-permute-start.70 = (bf16[2,2,64,512]{3,2,0,1:T(8,128)(2,1)}, bf16[2,2,64,512]{3,2,0,1:T(8,128)(2,1)S(1)}, u32[]{:S(2)}, u32[]{:S(2)}) collective-permute-start(bf16[2,2,64,512]{3,2,0,1:T(8,128)(2,1)} %get-tuple-element.330), channel_id=1, source_target_pairs={{0,2},{1,3},{2,0},{3,1},{4,6},{5,7},{6,4},{7,5},{8,10},{9,11},{10,... | collective-permute-start | bytes 786440 | tf_op jit(solution)/shard_map/ppermute | solution.py:36
  304.2 21.6 %collective-permute-start.72 = (bf16[2,2,64,512]{3,2,0,1:T(8,128)(2,1)S(1)}, bf16[2,2,64,512]{3,2,0,1:T(8,128)(2,1)S(1)}, u32[]{:S(2)}, u32[]{:S(2)}) collective-permute-start(bf16[2,2,64,512]{3,2,0,1:T(8,128)(2,1)S(1)} %get-tuple-element.331), channel_id=1, source_target_pairs={{0,6},{1,7},{2,4},{3,5},{4,2},{5,3},{6,0},{7,1},{8,14},{9,15},{10,... | collective-permute-start | bytes 786440 | tf_op jit(solution)/shard_map/ppermute | solution.py:36
  305.1 20.6 %collective-permute-start.71 = (bf16[2,2,64,512]{3,2,0,1:T(8,128)(2,1)S(1)}, bf16[2,2,64,512]{3,2,0,1:T(8,128)(2,1)}, u32[]{:S(2)}, u32[]{:S(2)}) collective-permute-start(bf16[2,2,64,512]{3,2,0,1:T(8,128)(2,1)S(1)} %get-tuple-element.332), channel_id=1, source_target_pairs={{0,4},{1,5},{2,6},{3,7},{4,0},{5,1},{6,2},{7,3},{8,12},{9,13},{10,... | collective-permute-start | bytes 786440 | tf_op jit(solution)/shard_map/ppermute | solution.py:36
  307.9 38.4 %collective-permute-start.77 = (bf16[2,2,4,64,512]{4,3,2,1,0:T(8,128)(2,1)}, bf16[2,2,4,64,512]{4,3,2,1,0:T(8,128)(2,1)S(1)}, u32[]{:S(2)}, u32[]{:S(2)}) collective-permute-start(bf16[2,2,4,64,512]{4,3,2,1,0:T(8,128)(2,1)} %add.117), channel_id=1, source_target_pairs={{0,16},{1,9},{2,18},{3,11},{4,20},{5,13},{6,22},{7,15},{8,24},{9,1... | collective-permute-start | bytes 3145736 | tf_op jit(solution)/shard_map/ppermute | solution.py:770
  320.7 33.3 %collective-permute-start.78 = (bf16[2,2,4,64,512]{4,3,2,1,0:T(8,128)(2,1)}, bf16[2,2,4,64,512]{4,3,2,1,0:T(8,128)(2,1)}, u32[]{:S(2)}, u32[]{:S(2)}) collective-permute-start(bf16[2,2,4,64,512]{4,3,2,1,0:T(8,128)(2,1)} %get-tuple-element.277), channel_id=1, source_target_pairs={{0,8},{1,17},{2,10},{3,19},{4,12},{5,21},{6,14},{7,23},{8,0},{9,25... | collective-permute-start | bytes 3145736 | tf_op jit(solution)/shard_map/ppermute | solution.py:770
  328.6 11.2 %collective-permute-start.68 = (bf16[4,64,512]{2,1,0:T(8,128)(2,1)S(1)}, bf16[4,64,512]{2,1,0:T(8,128)(2,1)S(1)}, u32[]{:S(2)}, u32[]{:S(2)}) collective-permute-start(bf16[4,64,512]{2,1,0:T(8,128)(2,1)S(1)} %slice.252), channel_id=1, source_target_pairs={{0,4},{1,5},{2,6},{3,7},{4,0},{5,1},{6,2},{7,3},{8,12},{9,13},{10,... | collective-permute-start | bytes 786440 | tf_op jit(solution)/shard_map/ppermute | solution.py:36
  329.5 9.3 %collective-permute-start.75 = (f32[20,512]{1,0:T(8,128)S(1)}, f32[20,512]{1,0:T(8,128)S(1)}, u32[]{:S(2)}, u32[]{:S(2)}) collective-permute-start(f32[20,512]{1,0:T(8,128)S(1)} %add.114), channel_id=1, source_target_pairs={{0,4},{1,5},{2,6},{3,7},{4,0},{5,1},{6,2},{7,3},{8,12},{9,13},{10,... | collective-permute-start | bytes 122888 | tf_op jit(solution)/shard_map/ppermute | solution.py:36
  331.9 12.0 %collective-permute-start.67 = (bf16[4,64,512]{2,1,0:T(8,128)(2,1)S(1)}, bf16[4,64,512]{2,1,0:T(8,128)(2,1)S(1)}, u32[]{:S(2)}, u32[]{:S(2)}) collective-permute-start(bf16[4,64,512]{2,1,0:T(8,128)(2,1)S(1)} %slice.250), channel_id=1, source_target_pairs={{0,4},{1,5},{2,6},{3,7},{4,0},{5,1},{6,2},{7,3},{8,12},{9,13},{10,... | collective-permute-start | bytes 786440 | tf_op jit(solution)/shard_map/ppermute | solution.py:36
  339.8 14.1 %collective-permute-start.79 = (bf16[200,512]{1,0:T(8,128)(2,1)S(1)}, bf16[200,512]{1,0:T(8,128)(2,1)S(1)}, u32[]{:S(2)}, u32[]{:S(2)}) collective-permute-start(bf16[200,512]{1,0:T(8,128)(2,1)S(1)} %copy-done.68), channel_id=1, source_target_pairs={{0,2},{1,3},{2,0},{3,1},{4,6},{5,7},{6,4},{7,5},{8,10},{9,11},{10,... | collective-permute-start | bytes 614408 | tf_op jit(solution)/shard_map/ppermute | solution.py:36
  343.9 10.0 %collective-permute-start.80 = (bf16[200,512]{1,0:T(8,128)(2,1)S(1)}, bf16[200,512]{1,0:T(8,128)(2,1)S(1)}, u32[]{:S(2)}, u32[]{:S(2)}) collective-permute-start(bf16[200,512]{1,0:T(8,128)(2,1)S(1)} %copy-done.67), channel_id=1, source_target_pairs={{0,4},{1,5},{2,6},{3,7},{4,0},{5,1},{6,2},{7,3},{8,12},{9,13},{10,... | collective-permute-start | bytes 614408 | tf_op jit(solution)/shard_map/ppermute | solution.py:36
  344.8 10.4 %collective-permute-start.81 = (bf16[200,512]{1,0:T(8,128)(2,1)S(1)}, bf16[200,512]{1,0:T(8,128)(2,1)S(1)}, u32[]{:S(2)}, u32[]{:S(2)}) collective-permute-start(bf16[200,512]{1,0:T(8,128)(2,1)S(1)} %copy-done.66), channel_id=1, source_target_pairs={{0,6},{1,7},{2,4},{3,5},{4,2},{5,3},{6,0},{7,1},{8,14},{9,15},{10,... | collective-permute-start | bytes 614408 | tf_op jit(solution)/shard_map/ppermute | solution.py:36
  364.8 15.1 %collective-permute-start.88 = (bf16[2,2,64,512]{3,2,0,1:T(8,128)(2,1)S(1)}, bf16[2,2,64,512]{3,2,0,1:T(8,128)(2,1)S(1)}, u32[]{:S(2)}, u32[]{:S(2)}) collective-permute-start(bf16[2,2,64,512]{3,2,0,1:T(8,128)(2,1)S(1)} %get-tuple-element.325), channel_id=1, source_target_pairs={{0,4},{1,5},{2,6},{3,7},{4,0},{5,1},{6,2},{7,3},{8,12},{9,13},{10,... | collective-permute-start | bytes 786440 | tf_op jit(solution)/shard_map/ppermute | solution.py:36
  365.4 14.5 %collective-permute-start.87 = (bf16[2,2,64,512]{3,2,0,1:T(8,128)(2,1)S(1)}, bf16[2,2,64,512]{3,2,0,1:T(8,128)(2,1)S(1)}, u32[]{:S(2)}, u32[]{:S(2)}) collective-permute-start(bf16[2,2,64,512]{3,2,0,1:T(8,128)(2,1)S(1)} %get-tuple-element.326), channel_id=1, source_target_pairs={{0,2},{1,3},{2,0},{3,1},{4,6},{5,7},{6,4},{7,5},{8,10},{9,11},{10,... | collective-permute-start | bytes 786440 | tf_op jit(solution)/shard_map/ppermute | solution.py:36
  367.0 13.0 %collective-permute-start.89 = (bf16[2,2,64,512]{3,2,0,1:T(8,128)(2,1)S(1)}, bf16[2,2,64,512]{3,2,0,1:T(8,128)(2,1)}, u32[]{:S(2)}, u32[]{:S(2)}) collective-permute-start(bf16[2,2,64,512]{3,2,0,1:T(8,128)(2,1)S(1)} %slice_bitcast_fusion.17), channel_id=1, source_target_pairs={{0,6},{1,7},{2,4},{3,5},{4,2},{5,3},{6,0},{7,1},{8,14},{9,15},{10,... | collective-permute-start | bytes 786440 | tf_op jit(solution)/shard_map/ppermute | solution.py:36
  370.3 11.6 %collective-permute-start.85 = (bf16[2,2,64,512]{3,2,0,1:T(8,128)(2,1)}, bf16[2,2,64,512]{3,2,0,1:T(8,128)(2,1)S(1)}, u32[]{:S(2)}, u32[]{:S(2)}) collective-permute-start(bf16[2,2,64,512]{3,2,0,1:T(8,128)(2,1)} %slice.212), channel_id=1, source_target_pairs={{0,8},{1,9},{2,10},{3,11},{4,12},{5,13},{6,14},{7,15},{8,0},{9,1},... | collective-permute-start | bytes 786440 | tf_op jit(solution)/shard_map/ppermute | solution.py:36
  382.8 8.1 %collective-permute-start.86 = (bf16[1,2,64,512]{3,2,0,1:T(8,128)(2,1)S(1)}, bf16[1,2,64,512]{3,2,0,1:T(8,128)(2,1)S(1)}, u32[]{:S(2)}, u32[]{:S(2)}) collective-permute-start(bf16[1,2,64,512]{3,2,0,1:T(8,128)(2,1)S(1)} %slice.266), channel_id=1, source_target_pairs={{0,16},{1,17},{2,18},{3,19},{4,20},{5,21},{6,22},{7,23},{8,24},{9,... | collective-permute-start | bytes 393224 | tf_op jit(solution)/shard_map/ppermute | solution.py:36
  (103 other events, 869.8 us)

commit v5 on v4

--- a/solution.py
+++ b/solution.py
@@ -784,14 +784,47 @@
     return held[:half] + place.swap(held[half:], mask)
 
 
-def plane_sums(place, mine):
-    shape = mine.shape
-    return plane_blocks(place, mine.reshape((2, -1) + shape[3:])).reshape((2, -1) + shape[3:])
-
-
-def unpack_sums(place, got):
-    got = got[:, place.expert ^ jnp.arange(got.shape[1])].astype(f32)
-    return got[0], jnp.swapaxes(got[1], 1, 2)
+def send_sums(place, pair):
+    return [pair[:, 0]] + [place.swap(pair[:, k], 2 * k) for k in (1, 2, 3)]
+
+
+def unpack_kernel(layer, filled, me_ref, *refs):
+    pieces, refs = refs[:4], refs[4 + 2 * filled :]
+    in_ref, out_ref, in_buf, out_buf, sems = refs
+    copies = []
+    for k, piece in enumerate(pieces):
+        for core in (0, 1):
+            j = 2 * k + core
+            expert = jnp.bitwise_xor(me_ref[0], j)
+            in_buf[j] = piece[0, core].astype(f32)
+            out_buf[j] = piece[1, core].astype(f32)
+            copies.append(pltpu.make_async_copy(in_buf.at[j], in_ref.at[layer, expert], sems.at[0, j]))
+            copies.append(pltpu.make_async_copy(out_buf.at[j], out_ref.at[layer, expert], sems.at[1, j]))
+            for copy in copies[-2:]:
+                copy.start()
+    for copy in copies:
+        copy.wait()
+
+
+def unpack_sums(me, pieces, layer, layers, before=()):
+    unused, cores, rows, width = pieces[0].shape
+    experts = cores * len(pieces)
+    shape = jax.ShapeDtypeStruct
+    return pl.pallas_call(
+        lambda *refs: unpack_kernel(layer, len(before) // 2, *refs),
+        out_shape=(shape((layers, experts, rows, width), f32),) * 2,
+        in_specs=[smem()] + [vmem()] * len(pieces) + [hbm()] * len(before),
+        out_specs=(hbm(), hbm()),
+        scratch_shapes=[
+            pltpu.VMEM((experts, rows, width), f32),
+            pltpu.VMEM((experts, rows, width), f32),
+            pltpu.SemaphoreType.DMA((2, experts)),
+        ],
+        input_output_aliases={5: 0, 6: 1} if before else {},
+        compiler_params=params(),
+        cost_estimate=pl.CostEstimate(flops=1, transcendentals=0, bytes_accessed=1),
+        name="unpack",
+    )(me, *pieces, *before)
 
 
 def per_device_plane(
@@ -860,65 +893,67 @@
     c1 = mixed(place, a1, NEAR, FAR)
     images = exchange_rows(place, normed)
     images[2], b1 = tie(images[2], b1)
-    grad_shapes = [(2,) + block] * 4
+    grad_shapes = [(2,) + block, (2,) + block, (2, 2) + block]
+    grad_parts = [[(0, io), (1, io), (2, (0, io)), (2, (1, io))] for io in (0, 1)]
     result = expert_layer(
-        Plan(1, block, first, second, *parts, grad_shapes, *parts),
+        Plan(1, block, first, second, *parts, grad_shapes, *grad_parts),
         expert_off, me, tables, router_weight[1], images, None, [own1, a1, b1, c1],
     )
-    out_rows, back_rows, router1, (own, a, b, c) = result[:2], result[2:4], result[4], result[5:]
-
-    b, c = mixed(place, b, NEAR, FAR), mixed(place, c, NEAR, FAR)
+    out_rows, back_rows, router1, (own, a, bc) = result[:2], result[2:4], result[4], result[5:]
+    bc = mixed(place, bc, NEAR, FAR)
     pieces = send_rows(place, pair_rows(place, back_rows))
     grad1, branch, gains1, *parts1 = attention_backward(
         attn_off, cotangent, pieces, hidden_in1, hidden_mid1, norm_gains[1], weights1, qkv1, ctx1, ROWS
     )
     far1 = parts1[2] + swap(parts1[3], CORE)
     images = exchange_rows(place, branch[None])
-    tied = tie(*images, a, b, c, far1)
-    images, (a, b, c, far1) = tied[:8], tied[8:]
+    tied = tie(*images, a, bc, far1)
+    images, (a, bc, far1) = tied[:8], tied[8:]
     far1 = swap(far1, Y)
-    a = mixed(place, a + c, FAR, NEAR)
+    a = mixed(place, a + bc[1], FAR, NEAR)
     result = expert_layer(
-        Plan(0, block, None, first, *parts, grad_shapes, *parts),
+        Plan(0, block, None, first, *parts, grad_shapes, *grad_parts),
         expert_off, me, tables, router_weight[0], images, [sent, expert_y], [own0, a0, b0, c0],
         flops=10**10,
     )
-    back_rows, router0, (own0, a0, b0, c0) = result[:2], result[2], result[3:]
+    back_rows, router0, (own0, a0, bc0) = result[:2], result[2], result[3:]
     *back_rows, far1 = tie(*back_rows, far1)
-    c0 = mixed(place, c0, NEAR, FAR)
+    bc0 = mixed(place, bc0, NEAR, FAR)
     pieces = send_rows(place, pair_rows(place, back_rows))
     pieces[3], a = tie(pieces[3], a)
     grad0, unused, gains0, *parts0 = attention_backward(
         attn_off, grad1, pieces, hidden_in0, hidden_mid0, norm_gains[0], weights0, qkv0, ctx0, LEN
     )
-    gains0, c0, b0, a, b, own, *out_rows = tie(gains0, c0, b0, a, b, own, *out_rows)
-    a0, b0 = mixed(place, a0 + c0, FAR, NEAR), mixed(place, b0, NEAR, FAR)
+    gains0, a0, a, bc, own, *out_rows = tie(gains0, a0, a, bc, own, *out_rows)
     gains, router = jnp.stack([gains0, gains1]), jnp.stack([router0, router1])
     small = jnp.concatenate([gains.reshape(-1), router.reshape(-1)]).reshape(-1, 512)
     recv = [swap(v, CORE) for v in (parts0[3], parts0[1], parts1[1])]
     *recv, sum1, parts0[0], parts0[2], parts1[0] = tie(
-        *recv, own + b + a, parts0[0], parts0[2], parts1[0]
+        *recv, own + bc[0] + a, parts0[0], parts0[2], parts1[0]
     )
     far0, near0, near1 = parts0[2] + recv[0], parts0[0] + recv[1], parts1[0] + recv[2]
     far0 = swap(far0, Y)
-    far0, out_rows[0] = tie(far0, out_rows[0])
+    far0, out_rows[0], a0, bc0 = tie(far0, out_rows[0], a0, bc0)
+    a0 = mixed(place, a0 + bc0[1], FAR, NEAR)
     attn_sum = [halve(place, near + far, X) for near, far in ((near0, far0), (near1, far1))]
     attn_sum = jnp.stack(attn_sum, axis=1)
-    sum1, small, *tail = tie(plane_sums(place, sum1), small, *pair_rows(place, out_rows))
+    sum1 = send_sums(place, chip_pairs(place, sum1.reshape((2, -1) + sum1.shape[3:])))
+    sum1[3], small, *tail = tie(sum1[3], small, *pair_rows(place, out_rows))
     tail = send_rows(place, tail)
     for mask in (CORE, X, Y):
         small = small + swap(small, mask)
-    attn_sum, small, sum1, a0, b0, *tail = tie(attn_sum, small, sum1, a0, b0, *tail)
+    grads1 = unpack_sums(me, sum1, 1, LAYERS)
+    tied = tie(attn_sum, small, a0, *grads1, *tail)
+    (attn_sum, small, a0), grads1, tail = tied[:3], tied[3:5], tied[5:]
     outputs = hidden_mid1 + sum(p.astype(f32) for p in tail)
-    sum0 = own0 + a0 + b0
+    sum0 = own0 + a0 + bc0[0]
     pair0 = chip_pairs(place, sum0.reshape((2, -1) + sum0.shape[3:]))
     pair0, attn_sum, small = tie(pair0, attn_sum, small)
-    sum0 = send_pairs(place, pair0).reshape((2, -1) + sum0.shape[3:])
+    sum0 = send_sums(place, pair0)
     for mask in (NEAR, FAR):
         attn_sum = halve(place, attn_sum, mask)
         small = small + swap(small, mask)
-    in1, out1 = unpack_sums(place, sum1)
-    in0, out0 = unpack_sums(place, sum0)
+    in_grads, out_grads = unpack_sums(me, sum0, 0, LAYERS, grads1)
     small = small.reshape(-1)
     gains, router = small[: gains.size].reshape(gains.shape), small[gains.size :].reshape(router.shape)
     attn = attn_sum.astype(f32).reshape(2, rows, 4, -1)
@@ -929,8 +964,8 @@
         attn[:, :, :3],
         jnp.swapaxes(attn[:, :, 3], 1, 2),
         router,
-        jnp.stack([in0, in1]),
-        jnp.stack([out0, out1]),
+        in_grads,
+        jnp.swapaxes(out_grads, 2, 3),
     )
 
 

time: 400 us -> 384 us (0.960)
  the two profiles are of different devices: /device:TPU:0 before, /device:TPU:28 now
where the time goes in v5:
time: 384 us; the launch traced here: 377 us
  waiting for transfers between devices  154 us (40%)
  Pallas kernels  88.5 us (23%)
  starting transfers between devices  83.5 us (22%)
  local copies, waits for them, and re-layouts  28.1 us (7%)
  other arithmetic  20.3 us (5%)
    ppermute x78, waiting for transfers between devices, swap(): return lax.ppermute(value, AXES, pairs)  111 us
    ppermute x78, starting transfers between devices, swap(): return lax.ppermute(value, AXES, pairs)  71.3 us
    ppermute x10, waiting for transfers between devices, mixed(): return lax.ppermute(value, AXES, pairs)  43.2 us
    pallas_call x3, Pallas kernels, expert_layer(): pl.pallas_call(lambda *refs: expert_kernel(plan, *refs), out_shape=tuple(...  42.2 us
    pallas_call x2, Pallas kernels, attention_backward(): pl.pallas_call(attention_backward_kernel, out_shape=(shape((out_rows, wid...  17.6 us
    ppermute x10, starting transfers between devices, mixed(): return lax.ppermute(value, AXES, pairs)  12.2 us
    pallas_call x2, Pallas kernels, attention_forward(): pl.pallas_call(lambda *refs: attention_forward_kernel(len(pieces), len(ex...  11.9 us
    unnamed x146, local copies, waits for them, and re-layouts  11.4 us
  transfers between devices with their start and end apart: 88, of which 45 were waited for; matrix products, arithmetic and copies ran while one was open for 9% of the time, Pallas kernels for 19%

profile of v5, /device:TPU:28, one launch (start us, length us, event | category | flops | bytes accessed | tf_op | source)
XLA Modules:
  0.0 376.6 jit_solution(18273480450072532698)
XLA Ops:
  0.7 2.2 slice_bitcast_fusion.6
  6.9 1.6 collective-permute-start.4
  10.5 5.1 %collective-permute-done.1 = bf16[1,2,64,512]{3,2,0,1:T(8,128)(2,1)S(1)} collective-permute-done((bf16[1,2,64,512]{3,2,0,1:T(8,128)(2,1)S(1)}, bf16[1,2,64,512]{3,2,0,1:T(8,128)(2,1)S(1)}, u32[]{:S(2)}, u32[]{:S(2)}) %collective-permute-start.1) | collective-permute-done | bytes 131104 | tf_op jit(solution)/shard_map/ppermute | solution.py:36
  16.2 5.7 %collective-permute-done.3 = bf16[2,2,64,512]{3,2,0,1:T(8,128)(2,1)S(1)} collective-permute-done((bf16[2,2,64,512]{3,2,0,1:T(8,128)(2,1)S(1)}, bf16[2,2,64,512]{3,2,0,1:T(8,128)(2,1)S(1)}, u32[]{:S(2)}, u32[]{:S(2)}) %collective-permute-start.3) | collective-permute-done | bytes 262176 | tf_op jit(solution)/shard_map/ppermute | solution.py:36
  22.1 1.8 collective-permute-done.2
  24.0 1.6 collective-permute-start.6
  25.7 11.5 %collective-permute-done.6 = bf16[4,2,64,512]{3,2,0,1:T(8,128)(2,1)S(1)} collective-permute-done((bf16[4,2,64,512]{3,2,0,1:T(8,128)(2,1)S(1)}, bf16[4,2,64,512]{3,2,0,1:T(8,128)(2,1)S(1)}, u32[]{:S(2)}, u32[]{:S(2)}) %collective-permute-start.6) | collective-permute-done | bytes 524320 | tf_op jit(solution)/shard_map/ppermute | solution.py:36
  39.9 2.3 slots.1
  43.8 2.4 gather_fusion.2
  49.6 3.0 collective-permute-done.9.refs_14_.refs_16_
  53.3 2.0 collective-permute-start.27
  60.9 5.5 %attention_forward.2 = (f32[200,512]{1,0:T(8,128)}, f32[200,512]{1,0:T(8,128)}, bf16[1,200,512]{2,1,0:T(8,128)(2,1)}, bf16[200,1536]{1,0:T(8,128)(2,1)}, bf16[200,512]{1,0:T(8,128)(2,1)}) custom-call(s32[8]{0:T(128)} %xor_multiply_fusion.1.refs_0_.off_ref, bf16[197,512]{1,0:T(8,128)(2,1)} %refs_1_.1, f32[2,512]{1,0:T(2,128)} %get-tuple-element.360.refs_2_.gains, ...), custom_call_target="tpu_custom_call" | custom-call | flops 1 | bytes 1 | tf_op jit(solution)/shard_map/attention_forward/pallas_call | solution.py:309
  66.5 4.7 %collective-permute-done.13 = bf16[2,2,64,512]{3,2,0,1:T(8,128)(2,1)} collective-permute-done((bf16[2,2,64,512]{3,2,0,1:T(8,128)(2,1)}, bf16[2,2,64,512]{3,2,0,1:T(8,128)(2,1)}, u32[]{:S(2)}, u32[]{:S(2)}) %collective-permute-start.13) | collective-permute-done | bytes 262176 | tf_op jit(solution)/shard_map/ppermute | solution.py:36
  77.0 2.1 collective-permute-done.26.refs_15_.refs_17_
  79.8 11.8 %collective-permute-done.24.refs_10_.w2 = bf16[8,64,512]{2,1,0:T(8,128)(2,1)S(1)} collective-permute-done((bf16[8,64,512]{2,1,0:T(8,128)(2,1)S(1)}, bf16[8,64,512]{2,1,0:T(8,128)(2,1)S(1)}, u32[]{:S(2)}, u32[]{:S(2)}) %collective-permute-start.24) | collective-permute-done | bytes 524320 | tf_op jit(solution)/shard_map/ppermute | solution.py:36
  92.4 9.5 %collective-permute-done.27.refs_16_.refs_18_ = bf16[2,2,4,64,512]{4,3,2,1,0:T(8,128)(2,1)} collective-permute-done((bf16[2,2,4,64,512]{4,3,2,1,0:T(8,128)(2,1)}, bf16[2,2,4,64,512]{4,3,2,1,0:T(8,128)(2,1)}, u32[]{:S(2)}, u32[]{:S(2)}) %collective-permute-start.27) | collective-permute-done | bytes 1048608 | tf_op jit(solution)/shard_map/ppermute | solution.py:770
  108.6 10.1 %expert_layer.3 = (bf16[4,200,512]{2,1,0:T(8,128)(2,1)}, bf16[4,200,512]{2,1,0:T(8,128)(2,1)}, bf16[512,512]{1,0:T(8,128)(2,1)}, f32[512,512]{1,0:T(8,128)}) custom-call(s32[8]{0:T(128)} %mul.21.refs_0_, s32[1]{0:T(128)} %bitcast.31.refs_1_.refs_0_, s32[2,4,256]{2,1,0:T(4,128)} %get-tuple-element.162.refs_2_, s32[2,4,256]{2,1,0:T(4,128)} %copy-done.55, ...), custom_call_target="tpu_custom_call" | custom-call | flops 1 | bytes 1 | tf_op jit(solution)/shard_map/expert_layer/pallas_call | solution.py:636
  122.3 2.3 add_rows.4
  125.7 2.5 collective-permute-start.31
  128.2 3.8 %collective-permute-done.29.refs_3_ = bf16[200,512]{1,0:T(8,128)(2,1)S(1)} collective-permute-done((bf16[200,512]{1,0:T(8,128)(2,1)}, bf16[200,512]{1,0:T(8,128)(2,1)S(1)}, u32[]{:S(2)}, u32[]{:S(2)}) %collective-permute-start.29) | collective-permute-done | bytes 204832 | tf_op jit(solution)/shard_map/ppermute | solution.py:36
  133.4 4.2 %collective-permute-done.31.refs_5_ = bf16[200,512]{1,0:T(8,128)(2,1)S(1)} collective-permute-done((bf16[200,512]{1,0:T(8,128)(2,1)}, bf16[200,512]{1,0:T(8,128)(2,1)S(1)}, u32[]{:S(2)}, u32[]{:S(2)}) %collective-permute-start.31) | collective-permute-done | bytes 204832 | tf_op jit(solution)/shard_map/ppermute | solution.py:36
  138.3 6.4 %attention_forward.3 = (f32[200,512]{1,0:T(8,128)}, f32[200,512]{1,0:T(8,128)}, bf16[2,200,512]{2,1,0:T(8,128)(2,1)}, bf16[200,1536]{1,0:T(8,128)(2,1)}, bf16[200,512]{1,0:T(8,128)(2,1)}) custom-call(s32[8]{0:T(128)} %xor_multiply_fusion.1.refs_0_.off_ref, f32[200,512]{1,0:T(8,128)} %get-tuple-element.161.refs_1_.hidden_mid, ...), custom_call_target="tpu_custom_call" | custom-call | flops 1 | bytes 1 | tf_op jit(solution)/shard_map/attention_forward/pallas_call | solution.py:309
  147.6 1.5 collective-permute-start.34
  150.4 6.4 %collective-permute-start.33 = (bf16[2,200,512]{2,1,0:T(8,128)(2,1)}, bf16[2,200,512]{2,1,0:T(8,128)(2,1)S(1)}, u32[]{:S(2)}, u32[]{:S(2)}) collective-permute-start(bf16[2,200,512]{2,1,0:T(8,128)(2,1)} %get-tuple-element.193.refs_5_), channel_id=1, source_target_pairs={{0,1},{1,0},{2,3},{3,2},{4,5},{5,4},{6,7},{7,6},{8,9},{9,8},{10,11... | collective-permute-start | bytes 1228808 | tf_op jit(solution)/shard_map/ppermute | solution.py:36
  156.9 2.3 collective-permute-done.39.refs_11_
  159.2 6.9 %collective-permute-done.37.refs_9_ = bf16[2,200,512]{2,1,0:T(8,128)(2,1)S(1)} collective-permute-done((bf16[2,200,512]{2,1,0:T(8,128)(2,1)}, bf16[2,200,512]{2,1,0:T(8,128)(2,1)S(1)}, u32[]{:S(2)}, u32[]{:S(2)}) %collective-permute-start.37) | collective-permute-done | bytes 409632 | tf_op jit(solution)/shard_map/ppermute | solution.py:36
  168.8 3.5 collective-permute-done.41.refs_16_
  172.4 17.1 %expert_layer.4 = (bf16[4,200,512]{2,1,0:T(8,128)(2,1)}, bf16[4,200,512]{2,1,0:T(8,128)(2,1)}, bf16[4,200,512]{2,1,0:T(8,128)(2,1)}, bf16[4,200,512]{2,1,0:T(8,1...) custom-call(s32[8]{0:T(128)} %mul.21.refs_0_, ...), custom_call_target="tpu_custom_call" | custom-call | flops 1 | bytes 1 | tf_op jit(solution)/shard_map/expert_layer/pallas_call | solution.py:636
  189.5 2.5 collective-permute-start.53
  193.2 2.2 collective-permute-done.42.odd
  196.2 2.3 add_rows.5
  199.6 2.5 collective-permute-start.45
  202.1 4.1 %collective-permute-done.43.p1 = bf16[200,512]{1,0:T(8,128)(2,1)S(1)} collective-permute-done((bf16[200,512]{1,0:T(8,128)(2,1)}, bf16[200,512]{1,0:T(8,128)(2,1)S(1)}, u32[]{:S(2)}, u32[]{:S(2)}) %collective-permute-start.43) | collective-permute-done | bytes 204832 | tf_op jit(solution)/shard_map/ppermute | solution.py:36
  207.3 4.5 %collective-permute-done.45.p3 = bf16[200,512]{1,0:T(8,128)(2,1)S(1)} collective-permute-done((bf16[200,512]{1,0:T(8,128)(2,1)}, bf16[200,512]{1,0:T(8,128)(2,1)S(1)}, u32[]{:S(2)}, u32[]{:S(2)}) %collective-permute-start.45) | collective-permute-done | bytes 204832 | tf_op jit(solution)/shard_map/ppermute | solution.py:36
  212.4 8.8 %attention_backward.2 = (f32[200,512]{1,0:T(8,128)}, bf16[200,512]{1,0:T(8,128)(2,1)}, f32[2,512]{1,0:T(2,128)}, bf16[8,64,512]{2,1,0:T(8,128)(2,1)}, bf16[8,64,...) custom-call(s32[8]{0:T(128)} %xor_multiply_fusion.1.refs_0_.off_ref, f32[197,512]{1,0:T(8,128)} %base.1, ...), custom_call_target="tpu_custom_call" | custom-call | flops 1 | bytes 1 | tf_op jit(solution)/shard_map/attention_backward/pallas_call | solution.py:397
  223.3 1.5 collective-permute-start.47
  224.9 5.5 %collective-permute-done.51.refs_11_ = bf16[1,200,512]{2,1,0:T(8,128)(2,1)S(1)} collective-permute-done((bf16[1,200,512]{2,1,0:T(8,128)(2,1)}, bf16[1,200,512]{2,1,0:T(8,128)(2,1)S(1)}, u32[]{:S(2)}, u32[]{:S(2)}) %collective-permute-start.51) | collective-permute-done | bytes 204832 | tf_op jit(solution)/shard_map/ppermute | solution.py:36
  230.4 3.0 collective-permute-done.49.refs_9_
  236.1 2.0 collective-permute-done.53
  239.8 2.5 collective-permute-start.60
  242.3 14.9 %expert_layer.5 = (bf16[4,200,512]{2,1,0:T(8,128)(2,1)}, bf16[4,200,512]{2,1,0:T(8,128)(2,1)}, f32[512,8]{1,0:T(8,128)}, bf16[2,2,4,64,512]{4,3,2,1,0:T(8,128)(2...) custom-call(s32[8]{0:T(128)} %mul.21.refs_0_, s32[1]{0:T(128)} %bitcast.31.refs_1_.refs_0_, ...), custom_call_target="tpu_custom_call" | custom-call | flops 10000000000 | bytes 1 | tf_op jit(solution)/shard_map/expert_layer/pallas_call | solution.py:636
  259.9 2.3 add_rows.6
  262.3 1.5 collective-permute-start.59
  265.7 4.5 %collective-permute-done.60 = bf16[2,2,4,64,512]{4,3,2,1,0:T(8,128)(2,1)S(1)} collective-permute-done((bf16[2,2,4,64,512]{4,3,2,1,0:T(8,128)(2,1)}, bf16[2,2,4,64,512]{4,3,2,1,0:T(8,128)(2,1)S(1)}, u32[]{:S(2)}, u32[]{:S(2)}) %collective-permute-start.60) | collective-permute-done | bytes 1048608 | tf_op jit(solution)/shard_map/ppermute | solution.py:770
  270.3 4.4 %collective-permute-start.63 = (bf16[8,64,512]{2,1,0:T(8,128)(2,1)}, bf16[8,64,512]{2,1,0:T(8,128)(2,1)S(1)}, u32[]{:S(2)}, u32[]{:S(2)}) collective-permute-start(bf16[8,64,512]{2,1,0:T(8,128)(2,1)} %get-tuple-element.239), channel_id=1, source_target_pairs={{0,1},{1,0},{2,3},{3,2},{4,5},{5,4},{6,7},{7,6},{8,9},{9,8},{10,11... | collective-permute-start | bytes 1572872 | tf_op jit(solution)/shard_map/ppermute | solution.py:36
  275.7 8.8 %attention_backward.3 = (f32[197,512]{1,0:T(8,128)}, bf16[200,512]{1,0:T(8,128)(2,1)}, f32[2,512]{1,0:T(2,128)}, bf16[8,64,512]{2,1,0:T(8,128)(2,1)}, bf16[8,64,...) custom-call(s32[8]{0:T(128)} %xor_multiply_fusion.1.refs_0_.off_ref, ...), custom_call_target="tpu_custom_call" | custom-call | flops 1 | bytes 1 | tf_op jit(solution)/shard_map/attention_backward/pallas_call | solution.py:397
  285.0 1.7 fusion
  291.0 2.2 fusion.14
  294.5 17.3 %collective-permute-done.65 = bf16[2,2,2,4,64,512]{5,4,3,2,1,0:T(8,128)(2,1)S(1)} collective-permute-done((bf16[2,2,2,4,64,512]{5,4,3,2,1,0:T(8,128)(2,1)}, bf16[2,2,2,4,64,512]{5,4,3,2,1,0:T(8,128)(2,1)S(1)}, u32[]{:S(2)}, u32[]{:S(2)}) %collective-permute-start.65) | collective-permute-done | bytes 2097184 | tf_op jit(solution)/shard_map/ppermute | solution.py:770
  313.0 1.5 collective-permute-start.74
  318.4 2.3 add_rows.7
  327.6 4.0 %collective-permute-done.76.refs_3_ = bf16[2,2,64,512]{3,2,1,0:T(8,128)(2,1)} collective-permute-done((bf16[2,2,64,512]{3,2,1,0:T(8,128)(2,1)}, bf16[2,2,64,512]{3,2,1,0:T(8,128)(2,1)}, u32[]{:S(2)}, u32[]{:S(2)}) %collective-permute-start.76) | collective-permute-done | bytes 262176 | tf_op jit(solution)/shard_map/ppermute | solution.py:36
  332.9 2.4 collective-permute-done.66
  336.1 1.8 collective-permute-start.79
  339.0 2.6 unpack.2
  342.4 2.8 collective-permute-done.79
  345.2 1.7 bitcast_add_fusion
  347.1 1.9 collective-permute-done.80
  349.2 3.4 collective-permute-start.83
  354.7 2.3 collective-permute-start.85
  357.0 3.3 collective-permute-done.81
  361.7 1.7 collective-permute-start.84
  364.2 5.1 %collective-permute-done.82 = f32[20,512]{1,0:T(8,128)S(1)} collective-permute-done((f32[20,512]{1,0:T(8,128)S(1)}, f32[20,512]{1,0:T(8,128)S(1)}, u32[]{:S(2)}, u32[]{:S(2)}) %collective-permute-start.82) | collective-permute-done | bytes 40992 | tf_op jit(solution)/shard_map/ppermute | solution.py:36
  372.0 2.6 unpack.3
  (357 shorter events, 96.0 us)
Async XLA Ops:
  6.4 9.2 %collective-permute-start.1 = (bf16[1,2,64,512]{3,2,0,1:T(8,128)(2,1)S(1)}, bf16[1,2,64,512]{3,2,0,1:T(8,128)(2,1)S(1)}, u32[]{:S(2)}, u32[]{:S(2)}) collective-permute-start(bf16[1,2,64,512]{3,2,0,1:T(8,128)(2,1)S(1)} %maximum_bitcast_fusion), channel_id=1, source_target_pairs={{0,16},{1,17},{2,18},{3,19},{4,20},{5,21},{6,22},{7,23},{8,24},{9,... | collective-permute-start | bytes 393224 | tf_op jit(solution)/shard_map/ppermute | solution.py:36
  6.9 9.3 %collective-permute-start.4 = (bf16[2,2,64,512]{3,2,0,1:T(8,128)(2,1)S(1)}, bf16[2,2,64,512]{3,2,0,1:T(8,128)(2,1)S(1)}, u32[]{:S(2)}, u32[]{:S(2)}) collective-permute-start(bf16[2,2,64,512]{3,2,0,1:T(8,128)(2,1)S(1)} %get-tuple-element.349), channel_id=1, source_target_pairs={{0,4},{1,5},{2,6},{3,7},{4,0},{5,1},{6,2},{7,3},{8,12},{9,13},{10,... | collective-permute-start | bytes 786440 | tf_op jit(solution)/shard_map/ppermute | solution.py:36
  8.5 13.4 %collective-permute-start.3 = (bf16[2,2,64,512]{3,2,0,1:T(8,128)(2,1)S(1)}, bf16[2,2,64,512]{3,2,0,1:T(8,128)(2,1)S(1)}, u32[]{:S(2)}, u32[]{:S(2)}) collective-permute-start(bf16[2,2,64,512]{3,2,0,1:T(8,128)(2,1)S(1)} %get-tuple-element.350), channel_id=1, source_target_pairs={{0,2},{1,3},{2,0},{3,1},{4,6},{5,7},{6,4},{7,5},{8,10},{9,11},{10,... | collective-permute-start | bytes 786440 | tf_op jit(solution)/shard_map/ppermute | solution.py:36
  9.0 12.9 %collective-permute-start.5 = (bf16[2,2,64,512]{3,2,0,1:T(8,128)(2,1)S(1)}, bf16[2,2,64,512]{3,2,0,1:T(8,128)(2,1)S(1)}, u32[]{:S(2)}, u32[]{:S(2)}) collective-permute-start(bf16[2,2,64,512]{3,2,0,1:T(8,128)(2,1)S(1)} %slice_bitcast_fusion.16), channel_id=1, source_target_pairs={{0,6},{1,7},{2,4},{3,5},{4,2},{5,3},{6,0},{7,1},{8,14},{9,15},{10,... | collective-permute-start | bytes 786440 | tf_op jit(solution)/shard_map/ppermute | solution.py:36
  15.7 8.3 %collective-permute-start.2 = (bf16[2,2,64,512]{3,2,0,1:T(8,128)(2,1)S(1)}, bf16[2,2,64,512]{3,2,0,1:T(8,128)(2,1)S(1)}, u32[]{:S(2)}, u32[]{:S(2)}) collective-permute-start(bf16[2,2,64,512]{3,2,0,1:T(8,128)(2,1)S(1)} %pad_maximum_fusion.11), channel_id=1, source_target_pairs={{0,8},{1,9},{2,10},{3,11},{4,12},{5,13},{6,14},{7,15},{8,0},{9,1},... | collective-permute-start | bytes 786440 | tf_op jit(solution)/shard_map/ppermute | solution.py:36
  24.0 13.1 %collective-permute-start.6 = (bf16[4,2,64,512]{3,2,0,1:T(8,128)(2,1)S(1)}, bf16[4,2,64,512]{3,2,0,1:T(8,128)(2,1)S(1)}, u32[]{:S(2)}, u32[]{:S(2)}) collective-permute-start(bf16[4,2,64,512]{3,2,0,1:T(8,128)(2,1)S(1)} %pad_maximum_fusion.6), channel_id=1, source_target_pairs={{0,4},{1,5},{2,6},{3,7},{4,0},{5,1},{6,2},{7,3},{8,12},{9,13},{10,... | collective-permute-start | bytes 1572872 | tf_op jit(solution)/shard_map/ppermute | solution.py:36
  25.6 26.9 %collective-permute-start.9 = (bf16[2,2,4,64,512]{4,3,2,1,0:T(8,128)(2,1)S(1)}, bf16[2,2,4,64,512]{4,3,2,1,0:T(8,128)(2,1)}, u32[]{:S(2)}, u32[]{:S(2)}) collective-permute-start(bf16[2,2,4,64,512]{4,3,2,1,0:T(8,128)(2,1)S(1)} %bitcast.150), channel_id=1, source_target_pairs={{0,16},{1,9},{2,18},{3,11},{4,20},{5,13},{6,22},{7,15},{8,24},{9,1... | collective-permute-start | bytes 3145736 | tf_op jit(solution)/shard_map/ppermute | solution.py:770
  37.3 12.3 %collective-permute-start.8 = (bf16[8,64,512]{2,1,0:T(8,128)(2,1)S(1)}, bf16[8,64,512]{2,1,0:T(8,128)(2,1)S(1)}, u32[]{:S(2)}, u32[]{:S(2)}) collective-permute-start(bf16[8,64,512]{2,1,0:T(8,128)(2,1)S(1)} %get-tuple-element.337.refs_3_.w0), channel_id=1, source_target_pairs={{0,2},{1,3},{2,0},{3,1},{4,6},{5,7},{6,4},{7,5},{8,10},{9,11},{10,... | collective-permute-start | bytes 1572872 | tf_op jit(solution)/shard_map/ppermute | solution.py:36
  53.3 25.8 %collective-permute-start.26 = (bf16[2,2,4,64,512]{4,3,2,1,0:T(8,128)(2,1)S(1)}, bf16[2,2,4,64,512]{4,3,2,1,0:T(8,128)(2,1)}, u32[]{:S(2)}, u32[]{:S(2)}) collective-permute-start(bf16[2,2,4,64,512]{4,3,2,1,0:T(8,128)(2,1)S(1)} %bitcast.151), channel_id=1, source_target_pairs={{0,8},{1,17},{2,10},{3,19},{4,12},{5,21},{6,14},{7,23},{8,0},{9,25... | collective-permute-start | bytes 3145736 | tf_op jit(solution)/shard_map/ppermute | solution.py:770
  53.3 48.6 %collective-permute-start.27 = (bf16[2,2,4,64,512]{4,3,2,1,0:T(8,128)(2,1)}, bf16[2,2,4,64,512]{4,3,2,1,0:T(8,128)(2,1)}, u32[]{:S(2)}, u32[]{:S(2)}) collective-permute-start(bf16[2,2,4,64,512]{4,3,2,1,0:T(8,128)(2,1)} %collective-permute-done.9.refs_14_.refs_16_), channel_id=1, source_target_pairs={{0,8},{1,17},{2,10},{3,19},{4,12},{5,21},{6,14},{7,23},{8,0},{9,25... | collective-permute-start | bytes 3145736 | tf_op jit(solution)/shard_map/ppermute | solution.py:770
  56.2 14.9 %collective-permute-start.13 = (bf16[2,2,64,512]{3,2,0,1:T(8,128)(2,1)}, bf16[2,2,64,512]{3,2,0,1:T(8,128)(2,1)}, u32[]{:S(2)}, u32[]{:S(2)}) collective-permute-start(bf16[2,2,64,512]{3,2,0,1:T(8,128)(2,1)} %get-tuple-element.339), channel_id=1, source_target_pairs={{0,2},{1,3},{2,0},{3,1},{4,6},{5,7},{6,4},{7,5},{8,10},{9,11},{10,... | collective-permute-start | bytes 786440 | tf_op jit(solution)/shard_map/ppermute | solution.py:36
  56.8 14.4 %collective-permute-start.15 = (bf16[2,2,64,512]{3,2,0,1:T(8,128)(2,1)}, bf16[2,2,64,512]{3,2,0,1:T(8,128)(2,1)S(1)}, u32[]{:S(2)}, u32[]{:S(2)}) collective-permute-start(bf16[2,2,64,512]{3,2,0,1:T(8,128)(2,1)} %get-tuple-element.340), channel_id=1, source_target_pairs={{0,6},{1,7},{2,4},{3,5},{4,2},{5,3},{6,0},{7,1},{8,14},{9,15},{10,... | collective-permute-start | bytes 786440 | tf_op jit(solution)/shard_map/ppermute | solution.py:36
  58.2 14.0 %collective-permute-start.14 = (bf16[2,2,64,512]{3,2,0,1:T(8,128)(2,1)}, bf16[2,2,64,512]{3,2,0,1:T(8,128)(2,1)S(1)}, u32[]{:S(2)}, u32[]{:S(2)}) collective-permute-start(bf16[2,2,64,512]{3,2,0,1:T(8,128)(2,1)} %get-tuple-element.341), channel_id=1, source_target_pairs={{0,4},{1,5},{2,6},{3,7},{4,0},{5,1},{6,2},{7,3},{8,12},{9,13},{10,... | collective-permute-start | bytes 786440 | tf_op jit(solution)/shard_map/ppermute | solution.py:36
  73.5 18.1 %collective-permute-start.24 = (bf16[8,64,512]{2,1,0:T(8,128)(2,1)S(1)}, bf16[8,64,512]{2,1,0:T(8,128)(2,1)S(1)}, u32[]{:S(2)}, u32[]{:S(2)}) collective-permute-start(bf16[8,64,512]{2,1,0:T(8,128)(2,1)S(1)} %get-tuple-element.186.refs_8_.w0), channel_id=1, source_target_pairs={{0,2},{1,3},{2,0},{3,1},{4,6},{5,7},{6,4},{7,5},{8,10},{9,11},{10,... | collective-permute-start | bytes 1572872 | tf_op jit(solution)/shard_map/ppermute | solution.py:36
  74.0 17.6 %collective-permute-start.21 = (bf16[1,200,512]{2,1,0:T(8,128)(2,1)}, bf16[1,200,512]{2,1,0:T(8,128)(2,1)S(1)}, u32[]{:S(2)}, u32[]{:S(2)}) collective-permute-start(bf16[1,200,512]{2,1,0:T(8,128)(2,1)} %get-tuple-element.168.refs_5_), channel_id=1, source_target_pairs={{0,6},{1,7},{2,4},{3,5},{4,2},{5,3},{6,0},{7,1},{8,14},{9,15},{10,... | collective-permute-start | bytes 614408 | tf_op jit(solution)/shard_map/ppermute | solution.py:36
  75.5 16.7 %collective-permute-start.19 = (bf16[1,200,512]{2,1,0:T(8,128)(2,1)}, bf16[1,200,512]{2,1,0:T(8,128)(2,1)S(1)}, u32[]{:S(2)}, u32[]{:S(2)}) collective-permute-start(bf16[1,200,512]{2,1,0:T(8,128)(2,1)} %get-tuple-element.168.refs_5_), channel_id=1, source_target_pairs={{0,4},{1,5},{2,6},{3,7},{4,0},{5,1},{6,2},{7,3},{8,12},{9,13},{10,... | collective-permute-start | bytes 614408 | tf_op jit(solution)/shard_map/ppermute | solution.py:36
  79.1 29.5 %collective-permute-start.23 = (bf16[8,64,512]{2,1,0:T(8,128)(2,1)S(1)}, bf16[8,64,512]{2,1,0:T(8,128)(2,1)S(1)}, u32[]{:S(2)}, u32[]{:S(2)}) collective-permute-start(bf16[8,64,512]{2,1,0:T(8,128)(2,1)S(1)} %get-tuple-element.186.refs_8_.w0), channel_id=1, source_target_pairs={{0,1},{1,0},{2,3},{3,2},{4,5},{5,4},{6,7},{7,6},{8,9},{9,8},{10,11... | collective-permute-start | bytes 1572872 | tf_op jit(solution)/shard_map/ppermute | solution.py:36
  91.6 17.0 %collective-permute-start.25 = (bf16[8,64,512]{2,1,0:T(8,128)(2,1)S(1)}, bf16[8,64,512]{2,1,0:T(8,128)(2,1)S(1)}, u32[]{:S(2)}, u32[]{:S(2)}) collective-permute-start(bf16[8,64,512]{2,1,0:T(8,128)(2,1)S(1)} %collective-permute-done.24.refs_10_.w2), channel_id=1, source_target_pairs={{0,1},{1,0},{2,3},{3,2},{4,5},{5,4},{6,7},{7,6},{8,9},{9,8},{10,11... | collective-permute-start | bytes 1572872 | tf_op jit(solution)/shard_map/ppermute | solution.py:36
  91.6 11.6 %collective-permute-start.17 = (bf16[1,200,512]{2,1,0:T(8,128)(2,1)}, bf16[1,200,512]{2,1,0:T(8,128)(2,1)}, u32[]{:S(2)}, u32[]{:S(2)}) collective-permute-start(bf16[1,200,512]{2,1,0:T(8,128)(2,1)} %get-tuple-element.168.refs_5_), channel_id=1, source_target_pairs={{0,2},{1,3},{2,0},{3,1},{4,6},{5,7},{6,4},{7,5},{8,10},{9,11},{10,... | collective-permute-start | bytes 614408 | tf_op jit(solution)/shard_map/ppermute | solution.py:36
  92.2 11.5 %collective-permute-start.16 = (bf16[1,200,512]{2,1,0:T(8,128)(2,1)}, bf16[1,200,512]{2,1,0:T(8,128)(2,1)S(1)}, u32[]{:S(2)}, u32[]{:S(2)}) collective-permute-start(bf16[1,200,512]{2,1,0:T(8,128)(2,1)} %get-tuple-element.168.refs_5_), channel_id=1, source_target_pairs={{0,1},{1,0},{2,3},{3,2},{4,5},{5,4},{6,7},{7,6},{8,9},{9,8},{10,11... | collective-permute-start | bytes 614408 | tf_op jit(solution)/shard_map/ppermute | solution.py:36
  104.4 40.2 %collective-permute-start.32 = (bf16[2,2,4,64,512]{4,3,2,1,0:T(8,128)(2,1)S(1)}, bf16[2,2,4,64,512]{4,3,2,1,0:T(8,128)(2,1)}, u32[]{:S(2)}, u32[]{:S(2)}) collective-permute-start(bf16[2,2,4,64,512]{4,3,2,1,0:T(8,128)(2,1)S(1)} %bitcast.156), channel_id=1, source_target_pairs={{0,16},{1,9},{2,18},{3,11},{4,20},{5,13},{6,22},{7,15},{8,24},{9,1... | collective-permute-start | bytes 3145736 | tf_op jit(solution)/shard_map/ppermute | solution.py:770
  118.9 31.5 %collective-permute-start.35 = (bf16[2,2,4,64,512]{4,3,2,1,0:T(8,128)(2,1)S(1)}, bf16[2,2,4,64,512]{4,3,2,1,0:T(8,128)(2,1)S(1)}, u32[]{:S(2)}, u32[]{:S(2)}) collective-permute-start(bf16[2,2,4,64,512]{4,3,2,1,0:T(8,128)(2,1)S(1)} %bitcast.157), channel_id=1, source_target_pairs={{0,8},{1,17},{2,10},{3,19},{4,12},{5,21},{6,14},{7,23},{8,0},{9,25... | collective-permute-start | bytes 3145736 | tf_op jit(solution)/shard_map/ppermute | solution.py:770
  124.7 7.3 %collective-permute-start.29 = (bf16[200,512]{1,0:T(8,128)(2,1)}, bf16[200,512]{1,0:T(8,128)(2,1)S(1)}, u32[]{:S(2)}, u32[]{:S(2)}) collective-permute-start(bf16[200,512]{1,0:T(8,128)(2,1)} %get-tuple-element.183), channel_id=1, source_target_pairs={{0,2},{1,3},{2,0},{3,1},{4,6},{5,7},{6,4},{7,5},{8,10},{9,11},{10,... | collective-permute-start | bytes 614408 | tf_op jit(solution)/shard_map/ppermute | solution.py:36
  125.2 8.2 %collective-permute-start.30 = (bf16[200,512]{1,0:T(8,128)(2,1)}, bf16[200,512]{1,0:T(8,128)(2,1)S(1)}, u32[]{:S(2)}, u32[]{:S(2)}) collective-permute-start(bf16[200,512]{1,0:T(8,128)(2,1)} %get-tuple-element.184), channel_id=1, source_target_pairs={{0,4},{1,5},{2,6},{3,7},{4,0},{5,1},{6,2},{7,3},{8,12},{9,13},{10,... | collective-permute-start | bytes 614408 | tf_op jit(solution)/shard_map/ppermute | solution.py:36
  125.7 11.9 %collective-permute-start.31 = (bf16[200,512]{1,0:T(8,128)(2,1)}, bf16[200,512]{1,0:T(8,128)(2,1)S(1)}, u32[]{:S(2)}, u32[]{:S(2)}) collective-permute-start(bf16[200,512]{1,0:T(8,128)(2,1)} %get-tuple-element.185), channel_id=1, source_target_pairs={{0,6},{1,7},{2,4},{3,5},{4,2},{5,3},{6,0},{7,1},{8,14},{9,15},{10,... | collective-permute-start | bytes 614408 | tf_op jit(solution)/shard_map/ppermute | solution.py:36
  144.7 27.7 %collective-permute-start.41 = (bf16[2,2,4,64,512]{4,3,2,1,0:T(8,128)(2,1)}, bf16[2,2,4,64,512]{4,3,2,1,0:T(8,128)(2,1)}, u32[]{:S(2)}, u32[]{:S(2)}) collective-permute-start(bf16[2,2,4,64,512]{4,3,2,1,0:T(8,128)(2,1)} %collective-permute-done.32.refs_14_), channel_id=1, source_target_pairs={{0,8},{1,17},{2,10},{3,19},{4,12},{5,21},{6,14},{7,23},{8,0},{9,25... | collective-permute-start | bytes 3145736 | tf_op jit(solution)/shard_map/ppermute | solution.py:770
  145.7 13.5 %collective-permute-start.39 = (bf16[2,200,512]{2,1,0:T(8,128)(2,1)}, bf16[2,200,512]{2,1,0:T(8,128)(2,1)S(1)}, u32[]{:S(2)}, u32[]{:S(2)}) collective-permute-start(bf16[2,200,512]{2,1,0:T(8,128)(2,1)} %get-tuple-element.193.refs_5_), channel_id=1, source_target_pairs={{0,6},{1,7},{2,4},{3,5},{4,2},{5,3},{6,0},{7,1},{8,14},{9,15},{10,... | collective-permute-start | bytes 1228808 | tf_op jit(solution)/shard_map/ppermute | solution.py:36
  146.1 19.9 %collective-permute-start.37 = (bf16[2,200,512]{2,1,0:T(8,128)(2,1)}, bf16[2,200,512]{2,1,0:T(8,128)(2,1)S(1)}, u32[]{:S(2)}, u32[]{:S(2)}) collective-permute-start(bf16[2,200,512]{2,1,0:T(8,128)(2,1)} %get-tuple-element.193.refs_5_), channel_id=1, source_target_pairs={{0,4},{1,5},{2,6},{3,7},{4,0},{5,1},{6,2},{7,3},{8,12},{9,13},{10,... | collective-permute-start | bytes 1228808 | tf_op jit(solution)/shard_map/ppermute | solution.py:36
  147.6 19.3 %collective-permute-start.34 = (bf16[2,200,512]{2,1,0:T(8,128)(2,1)}, bf16[2,200,512]{2,1,0:T(8,128)(2,1)S(1)}, u32[]{:S(2)}, u32[]{:S(2)}) collective-permute-start(bf16[2,200,512]{2,1,0:T(8,128)(2,1)} %get-tuple-element.193.refs_5_), channel_id=1, source_target_pairs={{0,2},{1,3},{2,0},{3,1},{4,6},{5,7},{6,4},{7,5},{8,10},{9,11},{10,... | collective-permute-start | bytes 1228808 | tf_op jit(solution)/shard_map/ppermute | solution.py:36
  150.4 17.5 %collective-permute-start.33 = (bf16[2,200,512]{2,1,0:T(8,128)(2,1)}, bf16[2,200,512]{2,1,0:T(8,128)(2,1)S(1)}, u32[]{:S(2)}, u32[]{:S(2)}) collective-permute-start(bf16[2,200,512]{2,1,0:T(8,128)(2,1)} %get-tuple-element.193.refs_5_), channel_id=1, source_target_pairs={{0,1},{1,0},{2,3},{3,2},{4,5},{5,4},{6,7},{7,6},{8,9},{9,8},{10,11... | collective-permute-start | bytes 1228808 | tf_op jit(solution)/shard_map/ppermute | solution.py:36
  159.2 8.7 %collective-permute-start.40 = (bf16[2,200,512]{2,1,0:T(8,128)(2,1)S(1)}, bf16[2,200,512]{2,1,0:T(8,128)(2,1)S(1)}, u32[]{:S(2)}, u32[]{:S(2)}) collective-permute-start(bf16[2,200,512]{2,1,0:T(8,128)(2,1)S(1)} %collective-permute-done.39.refs_11_), channel_id=1, source_target_pairs={{0,1},{1,0},{2,3},{3,2},{4,5},{5,4},{6,7},{7,6},{8,9},{9,8},{10,11... | collective-permute-start | bytes 1228808 | tf_op jit(solution)/shard_map/ppermute | solution.py:36
  189.5 48.6 %collective-permute-start.53 = (bf16[2,2,2,4,64,512]{5,4,3,2,1,0:T(8,128)(2,1)}, bf16[2,2,2,4,64,512]{5,4,3,2,1,0:T(8,128)(2,1)S(1)}, u32[]{:S(2)}, u32[]{:S(2)}) collective-permute-start(bf16[2,2,2,4,64,512]{5,4,3,2,1,0:T(8,128)(2,1)} %get-tuple-element.209), channel_id=1, source_target_pairs={{0,8},{1,17},{2,10},{3,19},{4,12},{5,21},{6,14},{7,23},{8,0},{9,25... | collective-permute-start | bytes 6291464 | tf_op jit(solution)/shard_map/ppermute | solution.py:770
  198.6 7.6 %collective-permute-start.43 = (bf16[200,512]{1,0:T(8,128)(2,1)}, bf16[200,512]{1,0:T(8,128)(2,1)S(1)}, u32[]{:S(2)}, u32[]{:S(2)}) collective-permute-start(bf16[200,512]{1,0:T(8,128)(2,1)} %get-tuple-element.200), channel_id=1, source_target_pairs={{0,2},{1,3},{2,0},{3,1},{4,6},{5,7},{6,4},{7,5},{8,10},{9,11},{10,... | collective-permute-start | bytes 614408 | tf_op jit(solution)/shard_map/ppermute | solution.py:36
  199.1 8.1 %collective-permute-start.44 = (bf16[200,512]{1,0:T(8,128)(2,1)}, bf16[200,512]{1,0:T(8,128)(2,1)S(1)}, u32[]{:S(2)}, u32[]{:S(2)}) collective-permute-start(bf16[200,512]{1,0:T(8,128)(2,1)} %get-tuple-element.201), channel_id=1, source_target_pairs={{0,4},{1,5},{2,6},{3,7},{4,0},{5,1},{6,2},{7,3},{8,12},{9,13},{10,... | collective-permute-start | bytes 614408 | tf_op jit(solution)/shard_map/ppermute | solution.py:36
  199.6 12.1 %collective-permute-start.45 = (bf16[200,512]{1,0:T(8,128)(2,1)}, bf16[200,512]{1,0:T(8,128)(2,1)S(1)}, u32[]{:S(2)}, u32[]{:S(2)}) collective-permute-start(bf16[200,512]{1,0:T(8,128)(2,1)} %get-tuple-element.202), channel_id=1, source_target_pairs={{0,6},{1,7},{2,4},{3,5},{4,2},{5,3},{6,0},{7,1},{8,14},{9,15},{10,... | collective-permute-start | bytes 614408 | tf_op jit(solution)/shard_map/ppermute | solution.py:36
  221.2 13.1 %collective-permute-start.54 = (bf16[8,64,512]{2,1,0:T(8,128)(2,1)}, bf16[8,64,512]{2,1,0:T(8,128)(2,1)S(1)}, u32[]{:S(2)}, u32[]{:S(2)}) collective-permute-start(bf16[8,64,512]{2,1,0:T(8,128)(2,1)} %get-tuple-element.211), channel_id=1, source_target_pairs={{0,1},{1,0},{2,3},{3,2},{4,5},{5,4},{6,7},{7,6},{8,9},{9,8},{10,11... | collective-permute-start | bytes 1572872 | tf_op jit(solution)/shard_map/ppermute | solution.py:36
  221.3 9.1 %collective-permute-start.51 = (bf16[1,200,512]{2,1,0:T(8,128)(2,1)}, bf16[1,200,512]{2,1,0:T(8,128)(2,1)S(1)}, u32[]{:S(2)}, u32[]{:S(2)}) collective-permute-start(bf16[1,200,512]{2,1,0:T(8,128)(2,1)} %bitcast.184), channel_id=1, source_target_pairs={{0,6},{1,7},{2,4},{3,5},{4,2},{5,3},{6,0},{7,1},{8,14},{9,15},{10,... | collective-permute-start | bytes 614408 | tf_op jit(solution)/shard_map/ppermute | solution.py:36
  221.8 11.5 %collective-permute-start.49 = (bf16[1,200,512]{2,1,0:T(8,128)(2,1)}, bf16[1,200,512]{2,1,0:T(8,128)(2,1)S(1)}, u32[]{:S(2)}, u32[]{:S(2)}) collective-permute-start(bf16[1,200,512]{2,1,0:T(8,128)(2,1)} %bitcast.185), channel_id=1, source_target_pairs={{0,4},{1,5},{2,6},{3,7},{4,0},{5,1},{6,2},{7,3},{8,12},{9,13},{10,... | collective-permute-start | bytes 614408 | tf_op jit(solution)/shard_map/ppermute | solution.py:36
  223.3 11.0 %collective-permute-start.47 = (bf16[1,200,512]{2,1,0:T(8,128)(2,1)}, bf16[1,200,512]{2,1,0:T(8,128)(2,1)S(1)}, u32[]{:S(2)}, u32[]{:S(2)}) collective-permute-start(bf16[1,200,512]{2,1,0:T(8,128)(2,1)} %bitcast.186), channel_id=1, source_target_pairs={{0,2},{1,3},{2,0},{3,1},{4,6},{5,7},{6,4},{7,5},{8,10},{9,11},{10,... | collective-permute-start | bytes 614408 | tf_op jit(solution)/shard_map/ppermute | solution.py:36
  238.1 19.1 %collective-permute-start.55 = (bf16[8,64,512]{2,1,0:T(8,128)(2,1)S(1)}, bf16[8,64,512]{2,1,0:T(8,128)(2,1)}, u32[]{:S(2)}, u32[]{:S(2)}) collective-permute-start(bf16[8,64,512]{2,1,0:T(8,128)(2,1)S(1)} %add.101), channel_id=1, source_target_pairs={{0,2},{1,3},{2,0},{3,1},{4,6},{5,7},{6,4},{7,5},{8,10},{9,11},{10,... | collective-permute-start | bytes 1572872 | tf_op jit(solution)/shard_map/ppermute | solution.py:36
  239.8 30.5 %collective-permute-start.60 = (bf16[2,2,4,64,512]{4,3,2,1,0:T(8,128)(2,1)}, bf16[2,2,4,64,512]{4,3,2,1,0:T(8,128)(2,1)S(1)}, u32[]{:S(2)}, u32[]{:S(2)}) collective-permute-start(bf16[2,2,4,64,512]{4,3,2,1,0:T(8,128)(2,1)} %bitcast_add_fusion.3), channel_id=1, source_target_pairs={{0,16},{1,9},{2,18},{3,11},{4,20},{5,13},{6,22},{7,15},{8,24},{9,1... | collective-permute-start | bytes 3145736 | tf_op jit(solution)/shard_map/ppermute | solution.py:770
  257.3 54.6 %collective-permute-start.65 = (bf16[2,2,2,4,64,512]{5,4,3,2,1,0:T(8,128)(2,1)}, bf16[2,2,2,4,64,512]{5,4,3,2,1,0:T(8,128)(2,1)S(1)}, u32[]{:S(2)}, u32[]{:S(2)}) collective-permute-start(bf16[2,2,2,4,64,512]{5,4,3,2,1,0:T(8,128)(2,1)} %get-tuple-element.258), channel_id=1, source_target_pairs={{0,8},{1,17},{2,10},{3,19},{4,12},{5,21},{6,14},{7,23},{8,0},{9,25... | collective-permute-start | bytes 6291464 | tf_op jit(solution)/shard_map/ppermute | solution.py:770
  262.3 12.4 %collective-permute-start.59 = (bf16[200,512]{1,0:T(8,128)(2,1)}, bf16[200,512]{1,0:T(8,128)(2,1)S(1)}, u32[]{:S(2)}, u32[]{:S(2)}) collective-permute-start(bf16[200,512]{1,0:T(8,128)(2,1)} %get-tuple-element.230), channel_id=1, source_target_pairs={{0,6},{1,7},{2,4},{3,5},{4,2},{5,3},{6,0},{7,1},{8,14},{9,15},{10,... | collective-permute-start | bytes 614408 | tf_op jit(solution)/shard_map/ppermute | solution.py:36
  263.8 11.1 %collective-permute-start.57 = (bf16[200,512]{1,0:T(8,128)(2,1)}, bf16[200,512]{1,0:T(8,128)(2,1)S(1)}, u32[]{:S(2)}, u32[]{:S(2)}) collective-permute-start(bf16[200,512]{1,0:T(8,128)(2,1)} %get-tuple-element.228), channel_id=1, source_target_pairs={{0,2},{1,3},{2,0},{3,1},{4,6},{5,7},{6,4},{7,5},{8,10},{9,11},{10,... | collective-permute-start | bytes 614408 | tf_op jit(solution)/shard_map/ppermute | solution.py:36
  264.3 10.6 %collective-permute-start.58 = (bf16[200,512]{1,0:T(8,128)(2,1)}, bf16[200,512]{1,0:T(8,128)(2,1)S(1)}, u32[]{:S(2)}, u32[]{:S(2)}) collective-permute-start(bf16[200,512]{1,0:T(8,128)(2,1)} %get-tuple-element.229), channel_id=1, source_target_pairs={{0,4},{1,5},{2,6},{3,7},{4,0},{5,1},{6,2},{7,3},{8,12},{9,13},{10,... | collective-permute-start | bytes 614408 | tf_op jit(solution)/shard_map/ppermute | solution.py:36
  270.3 16.4 %collective-permute-start.63 = (bf16[8,64,512]{2,1,0:T(8,128)(2,1)}, bf16[8,64,512]{2,1,0:T(8,128)(2,1)S(1)}, u32[]{:S(2)}, u32[]{:S(2)}) collective-permute-start(bf16[8,64,512]{2,1,0:T(8,128)(2,1)} %get-tuple-element.239), channel_id=1, source_target_pairs={{0,1},{1,0},{2,3},{3,2},{4,5},{5,4},{6,7},{7,6},{8,9},{9,8},{10,11... | collective-permute-start | bytes 1572872 | tf_op jit(solution)/shard_map/ppermute | solution.py:36
  289.7 22.2 %collective-permute-start.64 = (bf16[8,64,512]{2,1,0:T(8,128)(2,1)}, bf16[8,64,512]{2,1,0:T(8,128)(2,1)}, u32[]{:S(2)}, u32[]{:S(2)}) collective-permute-start(bf16[8,64,512]{2,1,0:T(8,128)(2,1)} %add.106), channel_id=1, source_target_pairs={{0,2},{1,3},{2,0},{3,1},{4,6},{5,7},{6,4},{7,5},{8,10},{9,11},{10,... | collective-permute-start | bytes 1572872 | tf_op jit(solution)/shard_map/ppermute | solution.py:36
  290.9 26.1 %collective-permute-start.70 = (bf16[4,200,512]{2,1,0:T(8,128)(2,1)}, bf16[4,200,512]{2,1,0:T(8,128)(2,1)S(1)}, u32[]{:S(2)}, u32[]{:S(2)}) collective-permute-start(bf16[4,200,512]{2,1,0:T(8,128)(2,1)} %get-tuple-element.269), channel_id=1, source_target_pairs={{0,1},{1,0},{2,3},{3,2},{4,5},{5,4},{6,7},{7,6},{8,9},{9,8},{10,11... | collective-permute-start | bytes 2457608 | tf_op jit(solution)/shard_map/ppermute | solution.py:36
  293.2 27.5 %collective-permute-start.69 = (bf16[2,2,64,512]{3,2,1,0:T(8,128)(2,1)}, bf16[2,2,64,512]{3,2,1,0:T(8,128)(2,1)}, u32[]{:S(2)}, u32[]{:S(2)}) collective-permute-start(bf16[2,2,64,512]{3,2,1,0:T(8,128)(2,1)} %get-tuple-element.331), channel_id=1, source_target_pairs={{0,6},{1,7},{2,4},{3,5},{4,2},{5,3},{6,0},{7,1},{8,14},{9,15},{10,... | collective-permute-start | bytes 786440 | tf_op jit(solution)/shard_map/ppermute | solution.py:36
  313.0 32.2 %collective-permute-start.74 = (bf16[2,2,4,64,512]{4,3,2,1,0:T(8,128)(2,1)}, bf16[2,2,4,64,512]{4,3,2,1,0:T(8,128)(2,1)}, u32[]{:S(2)}, u32[]{:S(2)}) collective-permute-start(bf16[2,2,4,64,512]{4,3,2,1,0:T(8,128)(2,1)} %bitcast_add_fusion.1), channel_id=1, source_target_pairs={{0,16},{1,9},{2,18},{3,11},{4,20},{5,13},{6,22},{7,15},{8,24},{9,1... | collective-permute-start | bytes 3145736 | tf_op jit(solution)/shard_map/ppermute | solution.py:770
  316.4 9.6 %collective-permute-start.67 = (bf16[4,64,512]{2,1,0:T(8,128)(2,1)}, bf16[4,64,512]{2,1,0:T(8,128)(2,1)}, u32[]{:S(2)}, u32[]{:S(2)}) collective-permute-start(bf16[4,64,512]{2,1,0:T(8,128)(2,1)} %slice.248), channel_id=1, source_target_pairs={{0,4},{1,5},{2,6},{3,7},{4,0},{5,1},{6,2},{7,3},{8,12},{9,13},{10,... | collective-permute-start | bytes 786440 | tf_op jit(solution)/shard_map/ppermute | solution.py:36
  317.0 14.5 %collective-permute-start.76 = (bf16[2,2,64,512]{3,2,1,0:T(8,128)(2,1)}, bf16[2,2,64,512]{3,2,1,0:T(8,128)(2,1)}, u32[]{:S(2)}, u32[]{:S(2)}) collective-permute-start(bf16[2,2,64,512]{3,2,1,0:T(8,128)(2,1)} %get-tuple-element.330), channel_id=1, source_target_pairs={{0,4},{1,5},{2,6},{3,7},{4,0},{5,1},{6,2},{7,3},{8,12},{9,13},{10,... | collective-permute-start | bytes 786440 | tf_op jit(solution)/shard_map/ppermute | solution.py:36
  322.3 13.0 %collective-permute-start.66 = (bf16[4,64,512]{2,1,0:T(8,128)(2,1)S(1)}, bf16[4,64,512]{2,1,0:T(8,128)(2,1)S(1)}, u32[]{:S(2)}, u32[]{:S(2)}) collective-permute-start(bf16[4,64,512]{2,1,0:T(8,128)(2,1)S(1)} %slice.246), channel_id=1, source_target_pairs={{0,4},{1,5},{2,6},{3,7},{4,0},{5,1},{6,2},{7,3},{8,12},{9,13},{10,... | collective-permute-start | bytes 786440 | tf_op jit(solution)/shard_map/ppermute | solution.py:36
  323.2 14.7 %collective-permute-start.75 = (bf16[2,2,64,512]{3,2,1,0:T(8,128)(2,1)S(1)}, bf16[2,2,64,512]{3,2,1,0:T(8,128)(2,1)S(1)}, u32[]{:S(2)}, u32[]{:S(2)}) collective-permute-start(bf16[2,2,64,512]{3,2,1,0:T(8,128)(2,1)S(1)} %copy-done.34), channel_id=1, source_target_pairs={{0,2},{1,3},{2,0},{3,1},{4,6},{5,7},{6,4},{7,5},{8,10},{9,11},{10,... | collective-permute-start | bytes 786440 | tf_op jit(solution)/shard_map/ppermute | solution.py:36
  325.9 10.1 %collective-permute-start.72 = (f32[20,512]{1,0:T(8,128)S(1)}, f32[20,512]{1,0:T(8,128)S(1)}, u32[]{:S(2)}, u32[]{:S(2)}) collective-permute-start(f32[20,512]{1,0:T(8,128)S(1)} %add.112), channel_id=1, source_target_pairs={{0,4},{1,5},{2,6},{3,7},{4,0},{5,1},{6,2},{7,3},{8,12},{9,13},{10,... | collective-permute-start | bytes 122888 | tf_op jit(solution)/shard_map/ppermute | solution.py:36
  331.6 10.7 %collective-permute-start.77 = (bf16[200,512]{1,0:T(8,128)(2,1)}, bf16[200,512]{1,0:T(8,128)(2,1)S(1)}, u32[]{:S(2)}, u32[]{:S(2)}) collective-permute-start(bf16[200,512]{1,0:T(8,128)(2,1)} %get-tuple-element.281), channel_id=1, source_target_pairs={{0,2},{1,3},{2,0},{3,1},{4,6},{5,7},{6,4},{7,5},{8,10},{9,11},{10,... | collective-permute-start | bytes 614408 | tf_op jit(solution)/shard_map/ppermute | solution.py:36
  336.1 9.1 %collective-permute-start.79 = (bf16[200,512]{1,0:T(8,128)(2,1)}, bf16[200,512]{1,0:T(8,128)(2,1)S(1)}, u32[]{:S(2)}, u32[]{:S(2)}) collective-permute-start(bf16[200,512]{1,0:T(8,128)(2,1)} %get-tuple-element.283), channel_id=1, source_target_pairs={{0,6},{1,7},{2,4},{3,5},{4,2},{5,3},{6,0},{7,1},{8,14},{9,15},{10,... | collective-permute-start | bytes 614408 | tf_op jit(solution)/shard_map/ppermute | solution.py:36
  349.2 12.5 %collective-permute-start.83 = (bf16[2,2,64,512]{3,2,0,1:T(8,128)(2,1)S(1)}, bf16[2,2,64,512]{3,2,0,1:T(8,128)(2,1)S(1)}, u32[]{:S(2)}, u32[]{:S(2)}) collective-permute-start(bf16[2,2,64,512]{3,2,0,1:T(8,128)(2,1)S(1)} %slice.216), channel_id=1, source_target_pairs={{0,8},{1,9},{2,10},{3,11},{4,12},{5,13},{6,14},{7,15},{8,0},{9,1},... | collective-permute-start | bytes 786440 | tf_op jit(solution)/shard_map/ppermute | solution.py:36
  352.6 7.7 %collective-permute-start.81 = (f32[20,512]{1,0:T(8,128)S(1)}, f32[20,512]{1,0:T(8,128)S(1)}, u32[]{:S(2)}, u32[]{:S(2)}) collective-permute-start(f32[20,512]{1,0:T(8,128)S(1)} %add.114), channel_id=1, source_target_pairs={{0,8},{1,9},{2,10},{3,11},{4,12},{5,13},{6,14},{7,15},{8,0},{9,1},... | collective-permute-start | bytes 122888 | tf_op jit(solution)/shard_map/ppermute | solution.py:36
  353.5 17.6 %collective-permute-start.87 = (bf16[2,2,64,512]{3,2,1,0:T(8,128)(2,1)S(1)}, bf16[2,2,64,512]{3,2,1,0:T(8,128)(2,1)S(1)}, u32[]{:S(2)}, u32[]{:S(2)}) collective-permute-start(bf16[2,2,64,512]{3,2,1,0:T(8,128)(2,1)S(1)} %get-tuple-element.324), channel_id=1, source_target_pairs={{0,6},{1,7},{2,4},{3,5},{4,2},{5,3},{6,0},{7,1},{8,14},{9,15},{10,... | collective-permute-start | bytes 786440 | tf_op jit(solution)/shard_map/ppermute | solution.py:36
  353.5 17.6 %collective-permute-start.86 = (bf16[2,2,64,512]{3,2,1,0:T(8,128)(2,1)S(1)}, bf16[2,2,64,512]{3,2,1,0:T(8,128)(2,1)S(1)}, u32[]{:S(2)}, u32[]{:S(2)}) collective-permute-start(bf16[2,2,64,512]{3,2,1,0:T(8,128)(2,1)S(1)} %get-tuple-element.325), channel_id=1, source_target_pairs={{0,4},{1,5},{2,6},{3,7},{4,0},{5,1},{6,2},{7,3},{8,12},{9,13},{10,... | collective-permute-start | bytes 786440 | tf_op jit(solution)/shard_map/ppermute | solution.py:36
  354.7 16.4 %collective-permute-start.85 = (bf16[2,2,64,512]{3,2,1,0:T(8,128)(2,1)S(1)}, bf16[2,2,64,512]{3,2,1,0:T(8,128)(2,1)S(1)}, u32[]{:S(2)}, u32[]{:S(2)}) collective-permute-start(bf16[2,2,64,512]{3,2,1,0:T(8,128)(2,1)S(1)} %get-tuple-element.326), channel_id=1, source_target_pairs={{0,2},{1,3},{2,0},{3,1},{4,6},{5,7},{6,4},{7,5},{8,10},{9,11},{10,... | collective-permute-start | bytes 786440 | tf_op jit(solution)/shard_map/ppermute | solution.py:36
  360.3 9.1 %collective-permute-start.82 = (f32[20,512]{1,0:T(8,128)S(1)}, f32[20,512]{1,0:T(8,128)S(1)}, u32[]{:S(2)}, u32[]{:S(2)}) collective-permute-start(f32[20,512]{1,0:T(8,128)S(1)} %add.122), channel_id=1, source_target_pairs={{0,16},{1,17},{2,18},{3,19},{4,20},{5,21},{6,22},{7,23},{8,24},{9,... | collective-permute-start | bytes 122888 | tf_op jit(solution)/shard_map/ppermute | solution.py:36
  361.7 12.9 %collective-permute-start.84 = (bf16[1,2,64,512]{3,2,0,1:T(8,128)(2,1)S(1)}, bf16[1,2,64,512]{3,2,0,1:T(8,128)(2,1)S(1)}, u32[]{:S(2)}, u32[]{:S(2)}) collective-permute-start(bf16[1,2,64,512]{3,2,0,1:T(8,128)(2,1)S(1)} %slice.262), channel_id=1, source_target_pairs={{0,16},{1,17},{2,18},{3,19},{4,20},{5,21},{6,22},{7,23},{8,24},{9,... | collective-permute-start | bytes 393224 | tf_op jit(solution)/shard_map/ppermute | solution.py:36
  (93 other events, 688.8 us)

commit v6 on v5

--- a/solution.py
+++ b/solution.py
@@ -463,7 +463,8 @@
                 )
         return result
 
-    for c in range(chunks):
+    @pl.loop(0, chunks)
+    def _(c):
         for which in (0, 1):
             for copy in loads(c, which):
                 copy.start()
@@ -498,7 +499,7 @@
     else:
         sent_buf[...] = sent_in[...]
     sent = sent_buf[...]
-    logits = dot(sent, router[...])
+    logits = dot_t(sent, router[plan.layer])
     top = jnp.max(logits, axis=-1, keepdims=True)
     weights = jnp.exp(logits - top)
     probs = weights / jnp.sum(weights, axis=-1, keepdims=True)
@@ -564,8 +565,8 @@
         gate_grad = jnp.sum(branch_buf[...].astype(f32) * expert_y, axis=-1, keepdims=True)
         logit_grad = gate_grad * gate * (is_mine.astype(f32) - probs)
         first, second = split(logit_grad)
-        router_grad[...] = dot(sent_t[...], first) + dot(sent_t[...], second)
-        back_buf[...] += dot_t(first, router[...]) + dot_t(second, router[...])
+        router_grad[...] = t_dot(first, sent) + t_dot(second, sent)
+        back_buf[...] += dot(first, router[plan.layer]) + dot(second, router[plan.layer])
         scatter(back_buf[...].astype(bf16), back_parts)
     if forward:
         scatter((gate * expert_y).astype(bf16), parts)
@@ -592,7 +593,7 @@
 def expert_layer(plan, offsets, me, tables, router, tokens, saved, weights, flops=1):
     forward, backward = plan.images is not None, plan.grads is not None
     plan.token_arrays, plan.weight_arrays = len(tokens), len(weights)
-    width = router.shape[0]
+    width = router.shape[2]
     count = len(plan.w_in)
     near, chunks, rows, hidden = plan.block
     slots = 2 * SLOTS
@@ -611,7 +612,7 @@
     if forward and not backward:
         out_shape += [shape((slots, width), bf16), shape((slots, width), f32)]
     if backward:
-        out_shape += [token_part] * 2 + [shape(router.shape, f32)]
+        out_shape += [token_part] * 2 + [shape(router.shape[1:], f32)]
     out_specs += [vmem()] * len(out_shape)
     if backward:
         out_shape += [shape(s, bf16) for s in plan.grad_shapes]
@@ -667,6 +668,7 @@
     zero = jnp.zeros((1,), jnp.int32)
     attn_off, expert_off = zero, zero
     me = place.expert.astype(jnp.int32).reshape(1)
+    routers = jnp.swapaxes(router_weight, 1, 2)
     attn_w, expert_w = [], []
     tables = slot_tables(place, routes, priority, experts)
     for l in range(LAYERS):
@@ -691,7 +693,7 @@
             grads = exchange_rows(place, padded_bf16(cotangent)[None])
             plan = Plan(l, block, here, [(j + 8, 0) for j in range(8)], *at, [block] * 2, *at)
             result = expert_layer(
-                plan, expert_off, me, tables, router_weight[l], images + grads, None, expert_w[l]
+                plan, expert_off, me, tables, routers, images + grads, None, expert_w[l]
             )
             tail = send_rows(place, pair_rows(place, result[:2]))
             result = result[2:]
@@ -699,7 +701,7 @@
         else:
             plan = Plan(l, block, here, None, *at, None, None, None)
             *result, sent, expert_y = expert_layer(
-                plan, expert_off, me, tables, router_weight[l], images, None, expert_w[l]
+                plan, expert_off, me, tables, routers, images, None, expert_w[l]
             )
             base, pieces = hidden_mid[l], send_rows(place, pair_rows(place, result))
             saved = [sent, expert_y]
@@ -716,7 +718,7 @@
             grads = exchange_rows(place, branch[None])
             plan = Plan(l - 1, block, None, here, *at, [block] * 2, *at)
             result = expert_layer(
-                plan, expert_off, me, tables, router_weight[l - 1], grads, saved, expert_w[l - 1]
+                plan, expert_off, me, tables, routers, grads, saved, expert_w[l - 1]
             )
         total = scatter_attention(place, jnp.concatenate(parts), rows)
         attn_list[l] = total.astype(f32).reshape(rows, 4, -1)
@@ -733,7 +735,7 @@
         gains,
         jnp.stack([attn_list[l][:, :3] for l in range(LAYERS)]),
         jnp.stack([jnp.swapaxes(attn_list[l][:, 3], 0, 1) for l in range(LAYERS)]),
-        router,
+        jnp.swapaxes(router, 1, 2),
         jnp.stack([in_list[l] for l in range(LAYERS)]),
         jnp.stack([out_list[l] for l in range(LAYERS)]),
     )
@@ -849,6 +851,7 @@
     replica = jnp.stack([jnp.zeros_like(core), 4 - 2 * core, 2 + 2 * core, 6 + 0 * core])
     expert_off = ((place.dp ^ replica[:, None] ^ jnp.arange(2)[None, :]) * rows).reshape(-1).astype(jnp.int32)
     me = place.expert.astype(jnp.int32).reshape(1)
+    routers = jnp.swapaxes(router_weight, 1, 2)
     block = (2, place.tensor_size, rows, expert_in.shape[3])
 
     pair = chip_pairs(place, expert_blocks(place, expert_in[0], expert_out[0]))
@@ -862,7 +865,9 @@
     held0, held1 = held[:, 0], held[:, 1]
     over0 = swap(held0, Y)
     tables = slot_tables(place, routes, priority, experts)
-    over0, a0, blocks1, *tables = tie(over0, a0, expert_blocks(place, expert_in[1], expert_out[1]), *tables)
+    over0, a0, blocks1, me, expert_off, *tables = tie(
+        over0, a0, expert_blocks(place, expert_in[1], expert_out[1]), me, expert_off, *tables
+    )
     b0, c0 = mixed(place, own0, NEAR, FAR), mixed(place, a0, NEAR, FAR)
     weights0 = [held0, swap(held0, CORE), over0, swap(over0, CORE)]
     own1 = plane_blocks(place, blocks1)
@@ -883,7 +888,7 @@
     parts = [[(m, io) for m in range(4)] for io in (0, 1)]
     *rows0, sent, expert_y = expert_layer(
         Plan(0, block, first, None, *parts, None, None, None),
-        expert_off, me, tables, router_weight[0], images, None, [own0, a0, b0, c0],
+        expert_off, me, tables, routers, images, None, [own0, a0, b0, c0],
     )
     pieces = send_rows(place, pair_rows(place, rows0))
     hidden_in1, hidden_mid1, normed, qkv1, ctx1 = attention_forward(
@@ -897,7 +902,7 @@
     grad_parts = [[(0, io), (1, io), (2, (0, io)), (2, (1, io))] for io in (0, 1)]
     result = expert_layer(
         Plan(1, block, first, second, *parts, grad_shapes, *grad_parts),
-        expert_off, me, tables, router_weight[1], images, None, [own1, a1, b1, c1],
+        expert_off, me, tables, routers, images, None, [own1, a1, b1, c1],
     )
     out_rows, back_rows, router1, (own, a, bc) = result[:2], result[2:4], result[4], result[5:]
     bc = mixed(place, bc, NEAR, FAR)
@@ -913,7 +918,7 @@
     a = mixed(place, a + bc[1], FAR, NEAR)
     result = expert_layer(
         Plan(0, block, None, first, *parts, grad_shapes, *grad_parts),
-        expert_off, me, tables, router_weight[0], images, [sent, expert_y], [own0, a0, b0, c0],
+        expert_off, me, tables, routers, images, [sent, expert_y], [own0, a0, b0, c0],
         flops=10**10,
     )
     back_rows, router0, (own0, a0, bc0) = result[:2], result[2], result[3:]
@@ -933,13 +938,13 @@
     )
     far0, near0, near1 = parts0[2] + recv[0], parts0[0] + recv[1], parts1[0] + recv[2]
     far0 = swap(far0, Y)
-    far0, out_rows[0], a0, bc0 = tie(far0, out_rows[0], a0, bc0)
-    a0 = mixed(place, a0 + bc0[1], FAR, NEAR)
+    sum1 = send_sums(place, chip_pairs(place, sum1.reshape((2, -1) + sum1.shape[3:])))
     attn_sum = [halve(place, near + far, X) for near, far in ((near0, far0), (near1, far1))]
     attn_sum = jnp.stack(attn_sum, axis=1)
-    sum1 = send_sums(place, chip_pairs(place, sum1.reshape((2, -1) + sum1.shape[3:])))
-    sum1[3], small, *tail = tie(sum1[3], small, *pair_rows(place, out_rows))
-    tail = send_rows(place, tail)
+    tied = tie(*sum1, bc0, a0, small, *out_rows)
+    sum1, (bc0, a0, small), out_rows = tied[:4], tied[4:7], tied[7:]
+    a0 = mixed(place, a0 + bc0[1], FAR, NEAR)
+    tail = send_rows(place, pair_rows(place, out_rows))
     for mask in (CORE, X, Y):
         small = small + swap(small, mask)
     grads1 = unpack_sums(me, sum1, 1, LAYERS)
@@ -963,7 +968,7 @@
         gains,
         attn[:, :, :3],
         jnp.swapaxes(attn[:, :, 3], 1, 2),
-        router,
+        jnp.swapaxes(router, 1, 2),
         in_grads,
         jnp.swapaxes(out_grads, 2, 3),
     )

time: 384 us -> 376 us (0.979)
  the two profiles are of different devices: /device:TPU:28 before, /device:TPU:0 now
where the time goes in v6:
time: 376 us; the launch traced here: 369 us
  waiting for transfers between devices  159 us (42%)
  Pallas kernels  86.6 us (23%)
  starting transfers between devices  84.9 us (23%)
  local copies, waits for them, and re-layouts  20.3 us (5%)
  other arithmetic  16.7 us (4%)
    ppermute x78, waiting for transfers between devices, swap(): return lax.ppermute(value, AXES, pairs)  112 us
    ppermute x78, starting transfers between devices, swap(): return lax.ppermute(value, AXES, pairs)  68.4 us
    ppermute x10, waiting for transfers between devices, mixed(): return lax.ppermute(value, AXES, pairs)  46.4 us
    pallas_call x3, Pallas kernels, expert_layer(): pl.pallas_call(lambda *refs: expert_kernel(plan, *refs), out_shape=tuple(...  40.3 us
    pallas_call x2, Pallas kernels, attention_backward(): pl.pallas_call(attention_backward_kernel, out_shape=(shape((out_rows, wid...  17.5 us
    ppermute x10, starting transfers between devices, mixed(): return lax.ppermute(value, AXES, pairs)  16.5 us
    pallas_call x2, Pallas kernels, attention_forward(): pl.pallas_call(lambda *refs: attention_forward_kernel(len(pieces), len(ex...  11.9 us
    pallas_call x4, Pallas kernels, pair_rows(): pl.pallas_call(add_kernel, out_shape=(jax.ShapeDtypeStruct(even.shape[1:]...  9.33 us
  transfers between devices with their start and end apart: 88, of which 51 were waited for; matrix products, arithmetic and copies ran while one was open for 6% of the time, Pallas kernels for 19%

profile of v6, /device:TPU:0, one launch (start us, length us, event | category | flops | bytes accessed | tf_op | source)
XLA Modules:
  0.0 369.5 jit_solution(5718826955629032891)
XLA Ops:
  5.8 4.0 %collective-permute-start.1 = (bf16[1,2,64,512]{3,2,0,1:T(8,128)(2,1)S(1)}, bf16[1,2,64,512]{3,2,0,1:T(8,128)(2,1)S(1)}, u32[]{:S(2)}, u32[]{:S(2)}) collective-permute-start(bf16[1,2,64,512]{3,2,0,1:T(8,128)(2,1)S(1)} %maximum_bitcast_fusion), channel_id=1, source_target_pairs={{0,16},{1,17},{2,18},{3,19},{4,20},{5,21},{6,22},{7,23},{8,24},{9,... | collective-permute-start | bytes 393224 | tf_op jit(solution)/shard_map/ppermute | solution.py:36
  13.5 3.0 collective-permute-done.1
  17.3 1.9 collective-permute-done.4
  19.2 5.7 %collective-permute-done.3 = bf16[2,2,64,512]{3,2,0,1:T(8,128)(2,1)S(1)} collective-permute-done((bf16[2,2,64,512]{3,2,0,1:T(8,128)(2,1)S(1)}, bf16[2,2,64,512]{3,2,0,1:T(8,128)(2,1)S(1)}, u32[]{:S(2)}, u32[]{:S(2)}) %collective-permute-start.3) | collective-permute-done | bytes 262176 | tf_op jit(solution)/shard_map/ppermute | solution.py:36
  26.7 2.3 collective-permute-start.9
  29.0 8.9 %collective-permute-done.6 = bf16[4,2,64,512]{3,2,0,1:T(8,128)(2,1)S(1)} collective-permute-done((bf16[4,2,64,512]{3,2,0,1:T(8,128)(2,1)S(1)}, bf16[4,2,64,512]{3,2,0,1:T(8,128)(2,1)S(1)}, u32[]{:S(2)}, u32[]{:S(2)}) %collective-permute-start.6) | collective-permute-done | bytes 524320 | tf_op jit(solution)/shard_map/ppermute | solution.py:36
  40.6 2.3 slots.1
  50.0 3.8 %collective-permute-done.9.refs_14_.refs_16_ = bf16[2,2,4,64,512]{4,3,2,1,0:T(8,128)(2,1)} collective-permute-done((bf16[2,2,4,64,512]{4,3,2,1,0:T(8,128)(2,1)S(1)}, bf16[2,2,4,64,512]{4,3,2,1,0:T(8,128)(2,1)}, u32[]{:S(2)}, u32[]{:S(2)}) %collective-permute-start.9) | collective-permute-done | bytes 1048608 | tf_op jit(solution)/shard_map/ppermute | solution.py:772
  62.2 5.5 %attention_forward.2 = (f32[200,512]{1,0:T(8,128)}, f32[200,512]{1,0:T(8,128)}, bf16[1,200,512]{2,1,0:T(8,128)(2,1)}, bf16[200,1536]{1,0:T(8,128)(2,1)}, bf16[200,512]{1,0:T(8,128)(2,1)}) custom-call(s32[8]{0:T(128)} %xor_multiply_fusion.1.refs_0_.off_ref, bf16[197,512]{1,0:T(8,128)(2,1)} %refs_1_.1, f32[2,512]{1,0:T(2,128)} %get-tuple-element.336.refs_2_.gains, ...), custom_call_target="tpu_custom_call" | custom-call | flops 1 | bytes 1 | tf_op jit(solution)/shard_map/attention_forward/pallas_call | solution.py:309
  67.7 3.3 collective-permute-done.13
  77.0 3.7 %collective-permute-done.26.refs_15_.refs_17_ = bf16[2,2,4,64,512]{4,3,2,1,0:T(8,128)(2,1)} collective-permute-done((bf16[2,2,4,64,512]{4,3,2,1,0:T(8,128)(2,1)S(1)}, bf16[2,2,4,64,512]{4,3,2,1,0:T(8,128)(2,1)}, u32[]{:S(2)}, u32[]{:S(2)}) %collective-permute-start.26) | collective-permute-done | bytes 1048608 | tf_op jit(solution)/shard_map/ppermute | solution.py:772
  80.7 10.1 %collective-permute-done.24.refs_10_.w2 = bf16[8,64,512]{2,1,0:T(8,128)(2,1)S(1)} collective-permute-done((bf16[8,64,512]{2,1,0:T(8,128)(2,1)S(1)}, bf16[8,64,512]{2,1,0:T(8,128)(2,1)S(1)}, u32[]{:S(2)}, u32[]{:S(2)}) %collective-permute-start.24) | collective-permute-done | bytes 524320 | tf_op jit(solution)/shard_map/ppermute | solution.py:36
  91.9 6.4 %collective-permute-done.17.refs_7_ = bf16[1,200,512]{2,1,0:T(8,128)(2,1)S(1)} collective-permute-done((bf16[1,200,512]{2,1,0:T(8,128)(2,1)S(1)}, bf16[1,200,512]{2,1,0:T(8,128)(2,1)S(1)}, u32[]{:S(2)}, u32[]{:S(2)}) %collective-permute-start.17) | collective-permute-done | bytes 204832 | tf_op jit(solution)/shard_map/ppermute | solution.py:36
  98.9 4.3 %collective-permute-done.27.refs_16_.refs_18_ = bf16[2,2,4,64,512]{4,3,2,1,0:T(8,128)(2,1)} collective-permute-done((bf16[2,2,4,64,512]{4,3,2,1,0:T(8,128)(2,1)}, bf16[2,2,4,64,512]{4,3,2,1,0:T(8,128)(2,1)}, u32[]{:S(2)}, u32[]{:S(2)}) %collective-permute-start.27) | collective-permute-done | bytes 1048608 | tf_op jit(solution)/shard_map/ppermute | solution.py:772
  105.6 9.3 %expert_layer.3 = (bf16[4,200,512]{2,1,0:T(8,128)(2,1)}, bf16[4,200,512]{2,1,0:T(8,128)(2,1)}, bf16[512,512]{1,0:T(8,128)(2,1)}, f32[512,512]{1,0:T(8,128)}) custom-call(s32[8]{0:T(128)} %mul.21.refs_0_, s32[1]{0:T(128)} %bitcast.31.refs_1_.refs_0_, s32[2,4,256]{2,1,0:T(4,128)} %get-tuple-element.165.refs_2_, s32[2,4,256]{2,1,0:T(4,128)} %copy-done.57, ...), custom_call_target="tpu_custom_call" | custom-call | flops 1 | bytes 1 | tf_op jit(solution)/shard_map/expert_layer/pallas_call | solution.py:637
  115.0 2.4 collective-permute-start.35
  118.5 2.3 add_rows.4
  124.3 3.8 %collective-permute-done.29.refs_3_ = bf16[200,512]{1,0:T(8,128)(2,1)S(1)} collective-permute-done((bf16[200,512]{1,0:T(8,128)(2,1)}, bf16[200,512]{1,0:T(8,128)(2,1)S(1)}, u32[]{:S(2)}, u32[]{:S(2)}) %collective-permute-start.29) | collective-permute-done | bytes 204832 | tf_op jit(solution)/shard_map/ppermute | solution.py:36
  128.1 2.4 collective-permute-done.30.refs_4_
  130.5 3.2 collective-permute-done.31.refs_5_
  134.4 6.4 %attention_forward.3 = (f32[200,512]{1,0:T(8,128)}, f32[200,512]{1,0:T(8,128)}, bf16[2,200,512]{2,1,0:T(8,128)(2,1)}, bf16[200,1536]{1,0:T(8,128)(2,1)}, bf16[200,512]{1,0:T(8,128)(2,1)}) custom-call(s32[8]{0:T(128)} %xor_multiply_fusion.1.refs_0_.off_ref, f32[200,512]{1,0:T(8,128)} %get-tuple-element.162.refs_1_.hidden_mid, ...), custom_call_target="tpu_custom_call" | custom-call | flops 1 | bytes 1 | tf_op jit(solution)/shard_map/attention_forward/pallas_call | solution.py:309
  141.2 3.2 collective-permute-start.41
  147.8 3.1 collective-permute-done.35.refs_15_
  150.9 2.0 collective-permute-start.33
  153.0 4.9 %collective-permute-done.39.refs_11_ = bf16[2,200,512]{2,1,0:T(8,128)(2,1)S(1)} collective-permute-done((bf16[2,200,512]{2,1,0:T(8,128)(2,1)}, bf16[2,200,512]{2,1,0:T(8,128)(2,1)S(1)}, u32[]{:S(2)}, u32[]{:S(2)}) %collective-permute-start.39) | collective-permute-done | bytes 409632 | tf_op jit(solution)/shard_map/ppermute | solution.py:36
  157.9 5.6 %collective-permute-done.37.refs_9_ = bf16[2,200,512]{2,1,0:T(8,128)(2,1)S(1)} collective-permute-done((bf16[2,200,512]{2,1,0:T(8,128)(2,1)}, bf16[2,200,512]{2,1,0:T(8,128)(2,1)S(1)}, u32[]{:S(2)}, u32[]{:S(2)}) %collective-permute-start.37) | collective-permute-done | bytes 409632 | tf_op jit(solution)/shard_map/ppermute | solution.py:36
  166.6 5.7 %collective-permute-done.41.refs_16_ = bf16[2,2,4,64,512]{4,3,2,1,0:T(8,128)(2,1)} collective-permute-done((bf16[2,2,4,64,512]{4,3,2,1,0:T(8,128)(2,1)}, bf16[2,2,4,64,512]{4,3,2,1,0:T(8,128)(2,1)}, u32[]{:S(2)}, u32[]{:S(2)}) %collective-permute-start.41) | collective-permute-done | bytes 1048608 | tf_op jit(solution)/shard_map/ppermute | solution.py:772
  172.3 16.7 %expert_layer.4 = (bf16[4,200,512]{2,1,0:T(8,128)(2,1)}, bf16[4,200,512]{2,1,0:T(8,128)(2,1)}, bf16[4,200,512]{2,1,0:T(8,128)(2,1)}, bf16[4,200,512]{2,1,0:T(8,1...) custom-call(s32[8]{0:T(128)} %mul.21.refs_0_, ...), custom_call_target="tpu_custom_call" | custom-call | flops 1 | bytes 1 | tf_op jit(solution)/shard_map/expert_layer/pallas_call | solution.py:637
  188.9 2.4 collective-permute-start.53
  191.9 2.2 collective-permute-done.42.odd
  195.0 2.3 add_rows.5
  200.8 4.1 %collective-permute-done.43.p1 = bf16[200,512]{1,0:T(8,128)(2,1)S(1)} collective-permute-done((bf16[200,512]{1,0:T(8,128)(2,1)}, bf16[200,512]{1,0:T(8,128)(2,1)S(1)}, u32[]{:S(2)}, u32[]{:S(2)}) %collective-permute-start.43) | collective-permute-done | bytes 204832 | tf_op jit(solution)/shard_map/ppermute | solution.py:36
  204.9 1.9 collective-permute-done.44.p2
  206.8 3.7 %collective-permute-done.45.p3 = bf16[200,512]{1,0:T(8,128)(2,1)S(1)} collective-permute-done((bf16[200,512]{1,0:T(8,128)(2,1)}, bf16[200,512]{1,0:T(8,128)(2,1)S(1)}, u32[]{:S(2)}, u32[]{:S(2)}) %collective-permute-start.45) | collective-permute-done | bytes 204832 | tf_op jit(solution)/shard_map/ppermute | solution.py:36
  211.2 8.8 %attention_backward.2 = (f32[200,512]{1,0:T(8,128)}, bf16[200,512]{1,0:T(8,128)(2,1)}, f32[2,512]{1,0:T(2,128)}, bf16[8,64,512]{2,1,0:T(8,128)(2,1)}, bf16[8,64,...) custom-call(s32[8]{0:T(128)} %xor_multiply_fusion.1.refs_0_.off_ref, f32[197,512]{1,0:T(8,128)} %base.1, ...), custom_call_target="tpu_custom_call" | custom-call | flops 1 | bytes 1 | tf_op jit(solution)/shard_map/attention_backward/pallas_call | solution.py:397
  220.0 1.8 collective-permute-start.51
  223.6 5.5 %collective-permute-done.51.refs_11_ = bf16[1,200,512]{2,1,0:T(8,128)(2,1)S(1)} collective-permute-done((bf16[1,200,512]{2,1,0:T(8,128)(2,1)}, bf16[1,200,512]{2,1,0:T(8,128)(2,1)S(1)}, u32[]{:S(2)}, u32[]{:S(2)}) %collective-permute-start.51) | collective-permute-done | bytes 204832 | tf_op jit(solution)/shard_map/ppermute | solution.py:36
  229.1 3.5 collective-permute-done.49.refs_9_
  234.8 2.7 collective-permute-done.53
  237.5 1.8 collective-permute-start.55
  240.4 3.6 collective-permute-start.60
  244.0 14.3 %expert_layer.5 = (bf16[4,200,512]{2,1,0:T(8,128)(2,1)}, bf16[4,200,512]{2,1,0:T(8,128)(2,1)}, f32[8,512]{1,0:T(8,128)}, bf16[2,2,4,64,512]{4,3,2,1,0:T(8,128)(2...) custom-call(s32[8]{0:T(128)} %mul.21.refs_0_, s32[1]{0:T(128)} %bitcast.31.refs_1_.refs_0_, ...), custom_call_target="tpu_custom_call" | custom-call | flops 10000000000 | bytes 1 | tf_op jit(solution)/shard_map/expert_layer/pallas_call | solution.py:637
  258.5 2.6 collective-permute-done.56.odd
  261.1 2.3 add_rows.6
  266.9 8.2 %collective-permute-done.60 = bf16[2,2,4,64,512]{4,3,2,1,0:T(8,128)(2,1)S(1)} collective-permute-done((bf16[2,2,4,64,512]{4,3,2,1,0:T(8,128)(2,1)}, bf16[2,2,4,64,512]{4,3,2,1,0:T(8,128)(2,1)S(1)}, u32[]{:S(2)}, u32[]{:S(2)}) %collective-permute-start.60) | collective-permute-done | bytes 1048608 | tf_op jit(solution)/shard_map/ppermute | solution.py:772
  276.5 8.8 %attention_backward.3 = (f32[197,512]{1,0:T(8,128)}, bf16[200,512]{1,0:T(8,128)(2,1)}, f32[2,512]{1,0:T(2,128)}, bf16[8,64,512]{2,1,0:T(8,128)(2,1)}, bf16[8,64,...) custom-call(s32[8]{0:T(128)} %xor_multiply_fusion.1.refs_0_.off_ref, ...), custom_call_target="tpu_custom_call" | custom-call | flops 1 | bytes 1 | tf_op jit(solution)/shard_map/attention_backward/pallas_call | solution.py:397
  285.8 1.7 fusion
  289.2 1.7 collective-permute-done.67
  297.9 13.5 %collective-permute-done.71 = bf16[2,2,2,4,64,512]{5,4,3,2,1,0:T(8,128)(2,1)S(1)} collective-permute-done((bf16[2,2,2,4,64,512]{5,4,3,2,1,0:T(8,128)(2,1)}, bf16[2,2,2,4,64,512]{5,4,3,2,1,0:T(8,128)(2,1)S(1)}, u32[]{:S(2)}, u32[]{:S(2)}) %collective-permute-start.71) | collective-permute-done | bytes 2097184 | tf_op jit(solution)/shard_map/ppermute | solution.py:772
  311.3 1.7 collective-permute-start.76
  319.3 5.3 %collective-permute-done.66 = bf16[4,64,512]{2,1,0:T(8,128)(2,1)S(1)} collective-permute-done((bf16[4,64,512]{2,1,0:T(8,128)(2,1)S(1)}, bf16[4,64,512]{2,1,0:T(8,128)(2,1)S(1)}, u32[]{:S(2)}, u32[]{:S(2)}) %collective-permute-start.66) | collective-permute-done | bytes 262176 | tf_op jit(solution)/shard_map/ppermute | solution.py:36
  326.2 2.3 add_rows.7
  330.3 1.8 collective-permute-start.79
  333.0 2.6 unpack.2
  337.6 2.8 collective-permute-done.79
  341.3 1.7 bitcast_add_fusion
  343.3 1.9 collective-permute-done.80
  345.5 2.1 collective-permute-start.83
  348.3 1.7 collective-permute-done.81
  350.9 1.9 collective-permute-start.87
  356.0 2.3 collective-permute-start.84
  358.9 2.2 collective-permute-done.87.refs_4_
  361.1 2.9 collective-permute-done.86.refs_3_
  364.9 2.6 unpack.3
  (360 shorter events, 98.0 us)
Async XLA Ops:
  5.8 10.6 %collective-permute-start.1 = (bf16[1,2,64,512]{3,2,0,1:T(8,128)(2,1)S(1)}, bf16[1,2,64,512]{3,2,0,1:T(8,128)(2,1)S(1)}, u32[]{:S(2)}, u32[]{:S(2)}) collective-permute-start(bf16[1,2,64,512]{3,2,0,1:T(8,128)(2,1)S(1)} %maximum_bitcast_fusion), channel_id=1, source_target_pairs={{0,16},{1,17},{2,18},{3,19},{4,20},{5,21},{6,22},{7,23},{8,24},{9,... | collective-permute-start | bytes 393224 | tf_op jit(solution)/shard_map/ppermute | solution.py:36
  10.0 9.3 %collective-permute-start.4 = (bf16[2,2,64,512]{3,2,0,1:T(8,128)(2,1)S(1)}, bf16[2,2,64,512]{3,2,0,1:T(8,128)(2,1)S(1)}, u32[]{:S(2)}, u32[]{:S(2)}) collective-permute-start(bf16[2,2,64,512]{3,2,0,1:T(8,128)(2,1)S(1)} %get-tuple-element.327), channel_id=1, source_target_pairs={{0,4},{1,5},{2,6},{3,7},{4,0},{5,1},{6,2},{7,3},{8,12},{9,13},{10,... | collective-permute-start | bytes 786440 | tf_op jit(solution)/shard_map/ppermute | solution.py:36
  11.5 13.4 %collective-permute-start.3 = (bf16[2,2,64,512]{3,2,0,1:T(8,128)(2,1)S(1)}, bf16[2,2,64,512]{3,2,0,1:T(8,128)(2,1)S(1)}, u32[]{:S(2)}, u32[]{:S(2)}) collective-permute-start(bf16[2,2,64,512]{3,2,0,1:T(8,128)(2,1)S(1)} %get-tuple-element.328), channel_id=1, source_target_pairs={{0,2},{1,3},{2,0},{3,1},{4,6},{5,7},{6,4},{7,5},{8,10},{9,11},{10,... | collective-permute-start | bytes 786440 | tf_op jit(solution)/shard_map/ppermute | solution.py:36
  13.0 11.9 %collective-permute-start.5 = (bf16[2,2,64,512]{3,2,0,1:T(8,128)(2,1)S(1)}, bf16[2,2,64,512]{3,2,0,1:T(8,128)(2,1)S(1)}, u32[]{:S(2)}, u32[]{:S(2)}) collective-permute-start(bf16[2,2,64,512]{3,2,0,1:T(8,128)(2,1)S(1)} %slice_bitcast_fusion.16), channel_id=1, source_target_pairs={{0,6},{1,7},{2,4},{3,5},{4,2},{5,3},{6,0},{7,1},{8,14},{9,15},{10,... | collective-permute-start | bytes 786440 | tf_op jit(solution)/shard_map/ppermute | solution.py:36
  16.5 8.7 %collective-permute-start.2 = (bf16[2,2,64,512]{3,2,0,1:T(8,128)(2,1)S(1)}, bf16[2,2,64,512]{3,2,0,1:T(8,128)(2,1)S(1)}, u32[]{:S(2)}, u32[]{:S(2)}) collective-permute-start(bf16[2,2,64,512]{3,2,0,1:T(8,128)(2,1)S(1)} %pad_maximum_fusion.10), channel_id=1, source_target_pairs={{0,8},{1,9},{2,10},{3,11},{4,12},{5,13},{6,14},{7,15},{8,0},{9,1},... | collective-permute-start | bytes 786440 | tf_op jit(solution)/shard_map/ppermute | solution.py:36
  25.2 12.7 %collective-permute-start.6 = (bf16[4,2,64,512]{3,2,0,1:T(8,128)(2,1)S(1)}, bf16[4,2,64,512]{3,2,0,1:T(8,128)(2,1)S(1)}, u32[]{:S(2)}, u32[]{:S(2)}) collective-permute-start(bf16[4,2,64,512]{3,2,0,1:T(8,128)(2,1)S(1)} %pad_maximum_fusion.6), channel_id=1, source_target_pairs={{0,4},{1,5},{2,6},{3,7},{4,0},{5,1},{6,2},{7,3},{8,12},{9,13},{10,... | collective-permute-start | bytes 1572872 | tf_op jit(solution)/shard_map/ppermute | solution.py:36
  26.7 27.1 %collective-permute-start.9 = (bf16[2,2,4,64,512]{4,3,2,1,0:T(8,128)(2,1)S(1)}, bf16[2,2,4,64,512]{4,3,2,1,0:T(8,128)(2,1)}, u32[]{:S(2)}, u32[]{:S(2)}) collective-permute-start(bf16[2,2,4,64,512]{4,3,2,1,0:T(8,128)(2,1)S(1)} %bitcast.156), channel_id=1, source_target_pairs={{0,16},{1,9},{2,18},{3,11},{4,20},{5,13},{6,22},{7,15},{8,24},{9,1... | collective-permute-start | bytes 3145736 | tf_op jit(solution)/shard_map/ppermute | solution.py:772
  38.1 12.0 %collective-permute-start.8 = (bf16[8,64,512]{2,1,0:T(8,128)(2,1)S(1)}, bf16[8,64,512]{2,1,0:T(8,128)(2,1)}, u32[]{:S(2)}, u32[]{:S(2)}) collective-permute-start(bf16[8,64,512]{2,1,0:T(8,128)(2,1)S(1)} %get-tuple-element.315.refs_3_.w0), channel_id=1, source_target_pairs={{0,2},{1,3},{2,0},{3,1},{4,6},{5,7},{6,4},{7,5},{8,10},{9,11},{10,... | collective-permute-start | bytes 1572872 | tf_op jit(solution)/shard_map/ppermute | solution.py:36
  54.5 6.4 %collective-permute-start.11 = (bf16[8,64,512]{2,1,0:T(8,128)(2,1)}, bf16[8,64,512]{2,1,0:T(8,128)(2,1)S(1)}, u32[]{:S(2)}, u32[]{:S(2)}) collective-permute-start(bf16[8,64,512]{2,1,0:T(8,128)(2,1)} %collective-permute-done.8.refs_5_.w2), channel_id=1, source_target_pairs={{0,1},{1,0},{2,3},{3,2},{4,5},{5,4},{6,7},{7,6},{8,9},{9,8},{10,11... | collective-permute-start | bytes 1572872 | tf_op jit(solution)/shard_map/ppermute | solution.py:36
  54.6 26.1 %collective-permute-start.26 = (bf16[2,2,4,64,512]{4,3,2,1,0:T(8,128)(2,1)S(1)}, bf16[2,2,4,64,512]{4,3,2,1,0:T(8,128)(2,1)}, u32[]{:S(2)}, u32[]{:S(2)}) collective-permute-start(bf16[2,2,4,64,512]{4,3,2,1,0:T(8,128)(2,1)S(1)} %bitcast.157), channel_id=1, source_target_pairs={{0,8},{1,17},{2,10},{3,19},{4,12},{5,21},{6,14},{7,23},{8,0},{9,25... | collective-permute-start | bytes 3145736 | tf_op jit(solution)/shard_map/ppermute | solution.py:772
  56.8 14.2 %collective-permute-start.13 = (bf16[2,2,64,512]{3,2,0,1:T(8,128)(2,1)}, bf16[2,2,64,512]{3,2,0,1:T(8,128)(2,1)S(1)}, u32[]{:S(2)}, u32[]{:S(2)}) collective-permute-start(bf16[2,2,64,512]{3,2,0,1:T(8,128)(2,1)} %get-tuple-element.317), channel_id=1, source_target_pairs={{0,2},{1,3},{2,0},{3,1},{4,6},{5,7},{6,4},{7,5},{8,10},{9,11},{10,... | collective-permute-start | bytes 786440 | tf_op jit(solution)/shard_map/ppermute | solution.py:36
  57.6 13.3 %collective-permute-start.15 = (bf16[2,2,64,512]{3,2,0,1:T(8,128)(2,1)}, bf16[2,2,64,512]{3,2,0,1:T(8,128)(2,1)}, u32[]{:S(2)}, u32[]{:S(2)}) collective-permute-start(bf16[2,2,64,512]{3,2,0,1:T(8,128)(2,1)} %get-tuple-element.318), channel_id=1, source_target_pairs={{0,6},{1,7},{2,4},{3,5},{4,2},{5,3},{6,0},{7,1},{8,14},{9,15},{10,... | collective-permute-start | bytes 786440 | tf_op jit(solution)/shard_map/ppermute | solution.py:36
  59.1 13.1 %collective-permute-start.14 = (bf16[2,2,64,512]{3,2,0,1:T(8,128)(2,1)S(1)}, bf16[2,2,64,512]{3,2,0,1:T(8,128)(2,1)S(1)}, u32[]{:S(2)}, u32[]{:S(2)}) collective-permute-start(bf16[2,2,64,512]{3,2,0,1:T(8,128)(2,1)S(1)} %get-tuple-element.319), channel_id=1, source_target_pairs={{0,4},{1,5},{2,6},{3,7},{4,0},{5,1},{6,2},{7,3},{8,12},{9,13},{10,... | collective-permute-start | bytes 786440 | tf_op jit(solution)/shard_map/ppermute | solution.py:36
  60.9 42.3 %collective-permute-start.27 = (bf16[2,2,4,64,512]{4,3,2,1,0:T(8,128)(2,1)}, bf16[2,2,4,64,512]{4,3,2,1,0:T(8,128)(2,1)}, u32[]{:S(2)}, u32[]{:S(2)}) collective-permute-start(bf16[2,2,4,64,512]{4,3,2,1,0:T(8,128)(2,1)} %collective-permute-done.9.refs_14_.refs_16_), channel_id=1, source_target_pairs={{0,8},{1,17},{2,10},{3,19},{4,12},{5,21},{6,14},{7,23},{8,0},{9,25... | collective-permute-start | bytes 3145736 | tf_op jit(solution)/shard_map/ppermute | solution.py:772
  73.4 17.4 %collective-permute-start.24 = (bf16[8,64,512]{2,1,0:T(8,128)(2,1)S(1)}, bf16[8,64,512]{2,1,0:T(8,128)(2,1)S(1)}, u32[]{:S(2)}, u32[]{:S(2)}) collective-permute-start(bf16[8,64,512]{2,1,0:T(8,128)(2,1)S(1)} %get-tuple-element.189.refs_8_.w0), channel_id=1, source_target_pairs={{0,2},{1,3},{2,0},{3,1},{4,6},{5,7},{6,4},{7,5},{8,10},{9,11},{10,... | collective-permute-start | bytes 1572872 | tf_op jit(solution)/shard_map/ppermute | solution.py:36
  74.3 16.5 %collective-permute-start.21 = (bf16[1,200,512]{2,1,0:T(8,128)(2,1)S(1)}, bf16[1,200,512]{2,1,0:T(8,128)(2,1)S(1)}, u32[]{:S(2)}, u32[]{:S(2)}) collective-permute-start(bf16[1,200,512]{2,1,0:T(8,128)(2,1)S(1)} %copy-done.38), channel_id=1, source_target_pairs={{0,6},{1,7},{2,4},{3,5},{4,2},{5,3},{6,0},{7,1},{8,14},{9,15},{10,... | collective-permute-start | bytes 614408 | tf_op jit(solution)/shard_map/ppermute | solution.py:36
  75.8 16.0 %collective-permute-start.19 = (bf16[1,200,512]{2,1,0:T(8,128)(2,1)S(1)}, bf16[1,200,512]{2,1,0:T(8,128)(2,1)S(1)}, u32[]{:S(2)}, u32[]{:S(2)}) collective-permute-start(bf16[1,200,512]{2,1,0:T(8,128)(2,1)S(1)} %copy-done.38), channel_id=1, source_target_pairs={{0,4},{1,5},{2,6},{3,7},{4,0},{5,1},{6,2},{7,3},{8,12},{9,13},{10,... | collective-permute-start | bytes 614408 | tf_op jit(solution)/shard_map/ppermute | solution.py:36
  80.7 24.1 %collective-permute-start.23 = (bf16[8,64,512]{2,1,0:T(8,128)(2,1)S(1)}, bf16[8,64,512]{2,1,0:T(8,128)(2,1)S(1)}, u32[]{:S(2)}, u32[]{:S(2)}) collective-permute-start(bf16[8,64,512]{2,1,0:T(8,128)(2,1)S(1)} %get-tuple-element.189.refs_8_.w0), channel_id=1, source_target_pairs={{0,1},{1,0},{2,3},{3,2},{4,5},{5,4},{6,7},{7,6},{8,9},{9,8},{10,11... | collective-permute-start | bytes 1572872 | tf_op jit(solution)/shard_map/ppermute | solution.py:36
  90.9 14.0 %collective-permute-start.25 = (bf16[8,64,512]{2,1,0:T(8,128)(2,1)S(1)}, bf16[8,64,512]{2,1,0:T(8,128)(2,1)S(1)}, u32[]{:S(2)}, u32[]{:S(2)}) collective-permute-start(bf16[8,64,512]{2,1,0:T(8,128)(2,1)S(1)} %collective-permute-done.24.refs_10_.w2), channel_id=1, source_target_pairs={{0,1},{1,0},{2,3},{3,2},{4,5},{5,4},{6,7},{7,6},{8,9},{9,8},{10,11... | collective-permute-start | bytes 1572872 | tf_op jit(solution)/shard_map/ppermute | solution.py:36
  90.9 7.5 %collective-permute-start.17 = (bf16[1,200,512]{2,1,0:T(8,128)(2,1)S(1)}, bf16[1,200,512]{2,1,0:T(8,128)(2,1)S(1)}, u32[]{:S(2)}, u32[]{:S(2)}) collective-permute-start(bf16[1,200,512]{2,1,0:T(8,128)(2,1)S(1)} %copy-done.38), channel_id=1, source_target_pairs={{0,2},{1,3},{2,0},{3,1},{4,6},{5,7},{6,4},{7,5},{8,10},{9,11},{10,... | collective-permute-start | bytes 614408 | tf_op jit(solution)/shard_map/ppermute | solution.py:36
  91.8 6.6 %collective-permute-start.16 = (bf16[1,200,512]{2,1,0:T(8,128)(2,1)S(1)}, bf16[1,200,512]{2,1,0:T(8,128)(2,1)S(1)}, u32[]{:S(2)}, u32[]{:S(2)}) collective-permute-start(bf16[1,200,512]{2,1,0:T(8,128)(2,1)S(1)} %copy-done.38), channel_id=1, source_target_pairs={{0,1},{1,0},{2,3},{3,2},{4,5},{5,4},{6,7},{7,6},{8,9},{9,8},{10,11... | collective-permute-start | bytes 614408 | tf_op jit(solution)/shard_map/ppermute | solution.py:36
  98.4 6.4 %collective-permute-start.20 = (bf16[1,200,512]{2,1,0:T(8,128)(2,1)S(1)}, bf16[1,200,512]{2,1,0:T(8,128)(2,1)S(1)}, u32[]{:S(2)}, u32[]{:S(2)}) collective-permute-start(bf16[1,200,512]{2,1,0:T(8,128)(2,1)S(1)} %collective-permute-done.19.refs_9_), channel_id=1, source_target_pairs={{0,1},{1,0},{2,3},{3,2},{4,5},{5,4},{6,7},{7,6},{8,9},{9,8},{10,11... | collective-permute-start | bytes 614408 | tf_op jit(solution)/shard_map/ppermute | solution.py:36
  103.2 38.0 %collective-permute-start.32 = (bf16[2,2,4,64,512]{4,3,2,1,0:T(8,128)(2,1)S(1)}, bf16[2,2,4,64,512]{4,3,2,1,0:T(8,128)(2,1)}, u32[]{:S(2)}, u32[]{:S(2)}) collective-permute-start(bf16[2,2,4,64,512]{4,3,2,1,0:T(8,128)(2,1)S(1)} %bitcast.162), channel_id=1, source_target_pairs={{0,16},{1,9},{2,18},{3,11},{4,20},{5,13},{6,22},{7,15},{8,24},{9,1... | collective-permute-start | bytes 3145736 | tf_op jit(solution)/shard_map/ppermute | solution.py:772
  115.0 35.9 %collective-permute-start.35 = (bf16[2,2,4,64,512]{4,3,2,1,0:T(8,128)(2,1)S(1)}, bf16[2,2,4,64,512]{4,3,2,1,0:T(8,128)(2,1)S(1)}, u32[]{:S(2)}, u32[]{:S(2)}) collective-permute-start(bf16[2,2,4,64,512]{4,3,2,1,0:T(8,128)(2,1)S(1)} %bitcast.163), channel_id=1, source_target_pairs={{0,8},{1,17},{2,10},{3,19},{4,12},{5,21},{6,14},{7,23},{8,0},{9,25... | collective-permute-start | bytes 3145736 | tf_op jit(solution)/shard_map/ppermute | solution.py:772
  120.8 7.3 %collective-permute-start.29 = (bf16[200,512]{1,0:T(8,128)(2,1)}, bf16[200,512]{1,0:T(8,128)(2,1)S(1)}, u32[]{:S(2)}, u32[]{:S(2)}) collective-permute-start(bf16[200,512]{1,0:T(8,128)(2,1)} %get-tuple-element.186), channel_id=1, source_target_pairs={{0,2},{1,3},{2,0},{3,1},{4,6},{5,7},{6,4},{7,5},{8,10},{9,11},{10,... | collective-permute-start | bytes 614408 | tf_op jit(solution)/shard_map/ppermute | solution.py:36
  122.3 8.2 %collective-permute-start.30 = (bf16[200,512]{1,0:T(8,128)(2,1)}, bf16[200,512]{1,0:T(8,128)(2,1)S(1)}, u32[]{:S(2)}, u32[]{:S(2)}) collective-permute-start(bf16[200,512]{1,0:T(8,128)(2,1)} %get-tuple-element.187), channel_id=1, source_target_pairs={{0,4},{1,5},{2,6},{3,7},{4,0},{5,1},{6,2},{7,3},{8,12},{9,13},{10,... | collective-permute-start | bytes 614408 | tf_op jit(solution)/shard_map/ppermute | solution.py:36
  122.8 10.8 %collective-permute-start.31 = (bf16[200,512]{1,0:T(8,128)(2,1)}, bf16[200,512]{1,0:T(8,128)(2,1)S(1)}, u32[]{:S(2)}, u32[]{:S(2)}) collective-permute-start(bf16[200,512]{1,0:T(8,128)(2,1)} %get-tuple-element.188), channel_id=1, source_target_pairs={{0,6},{1,7},{2,4},{3,5},{4,2},{5,3},{6,0},{7,1},{8,14},{9,15},{10,... | collective-permute-start | bytes 614408 | tf_op jit(solution)/shard_map/ppermute | solution.py:36
  141.2 31.0 %collective-permute-start.41 = (bf16[2,2,4,64,512]{4,3,2,1,0:T(8,128)(2,1)}, bf16[2,2,4,64,512]{4,3,2,1,0:T(8,128)(2,1)}, u32[]{:S(2)}, u32[]{:S(2)}) collective-permute-start(bf16[2,2,4,64,512]{4,3,2,1,0:T(8,128)(2,1)} %collective-permute-done.32.refs_14_), channel_id=1, source_target_pairs={{0,8},{1,17},{2,10},{3,19},{4,12},{5,21},{6,14},{7,23},{8,0},{9,25... | collective-permute-start | bytes 3145736 | tf_op jit(solution)/shard_map/ppermute | solution.py:772
  144.3 13.5 %collective-permute-start.39 = (bf16[2,200,512]{2,1,0:T(8,128)(2,1)}, bf16[2,200,512]{2,1,0:T(8,128)(2,1)S(1)}, u32[]{:S(2)}, u32[]{:S(2)}) collective-permute-start(bf16[2,200,512]{2,1,0:T(8,128)(2,1)} %get-tuple-element.196.refs_5_), channel_id=1, source_target_pairs={{0,6},{1,7},{2,4},{3,5},{4,2},{5,3},{6,0},{7,1},{8,14},{9,15},{10,... | collective-permute-start | bytes 1228808 | tf_op jit(solution)/shard_map/ppermute | solution.py:36
  145.8 17.6 %collective-permute-start.37 = (bf16[2,200,512]{2,1,0:T(8,128)(2,1)}, bf16[2,200,512]{2,1,0:T(8,128)(2,1)S(1)}, u32[]{:S(2)}, u32[]{:S(2)}) collective-permute-start(bf16[2,200,512]{2,1,0:T(8,128)(2,1)} %get-tuple-element.196.refs_5_), channel_id=1, source_target_pairs={{0,4},{1,5},{2,6},{3,7},{4,0},{5,1},{6,2},{7,3},{8,12},{9,13},{10,... | collective-permute-start | bytes 1228808 | tf_op jit(solution)/shard_map/ppermute | solution.py:36
  147.3 16.1 %collective-permute-start.34 = (bf16[2,200,512]{2,1,0:T(8,128)(2,1)}, bf16[2,200,512]{2,1,0:T(8,128)(2,1)S(1)}, u32[]{:S(2)}, u32[]{:S(2)}) collective-permute-start(bf16[2,200,512]{2,1,0:T(8,128)(2,1)} %get-tuple-element.196.refs_5_), channel_id=1, source_target_pairs={{0,2},{1,3},{2,0},{3,1},{4,6},{5,7},{6,4},{7,5},{8,10},{9,11},{10,... | collective-permute-start | bytes 1228808 | tf_op jit(solution)/shard_map/ppermute | solution.py:36
  150.9 13.0 %collective-permute-start.33 = (bf16[2,200,512]{2,1,0:T(8,128)(2,1)}, bf16[2,200,512]{2,1,0:T(8,128)(2,1)S(1)}, u32[]{:S(2)}, u32[]{:S(2)}) collective-permute-start(bf16[2,200,512]{2,1,0:T(8,128)(2,1)} %get-tuple-element.196.refs_5_), channel_id=1, source_target_pairs={{0,1},{1,0},{2,3},{3,2},{4,5},{5,4},{6,7},{7,6},{8,9},{9,8},{10,11... | collective-permute-start | bytes 1228808 | tf_op jit(solution)/shard_map/ppermute | solution.py:36
  188.9 48.6 %collective-permute-start.53 = (bf16[2,2,2,4,64,512]{5,4,3,2,1,0:T(8,128)(2,1)}, bf16[2,2,2,4,64,512]{5,4,3,2,1,0:T(8,128)(2,1)S(1)}, u32[]{:S(2)}, u32[]{:S(2)}) collective-permute-start(bf16[2,2,2,4,64,512]{5,4,3,2,1,0:T(8,128)(2,1)} %get-tuple-element.212), channel_id=1, source_target_pairs={{0,8},{1,17},{2,10},{3,19},{4,12},{5,21},{6,14},{7,23},{8,0},{9,25... | collective-permute-start | bytes 6291464 | tf_op jit(solution)/shard_map/ppermute | solution.py:772
  197.3 7.6 %collective-permute-start.43 = (bf16[200,512]{1,0:T(8,128)(2,1)}, bf16[200,512]{1,0:T(8,128)(2,1)S(1)}, u32[]{:S(2)}, u32[]{:S(2)}) collective-permute-start(bf16[200,512]{1,0:T(8,128)(2,1)} %get-tuple-element.203), channel_id=1, source_target_pairs={{0,2},{1,3},{2,0},{3,1},{4,6},{5,7},{6,4},{7,5},{8,10},{9,11},{10,... | collective-permute-start | bytes 614408 | tf_op jit(solution)/shard_map/ppermute | solution.py:36
  198.6 8.2 %collective-permute-start.44 = (bf16[200,512]{1,0:T(8,128)(2,1)}, bf16[200,512]{1,0:T(8,128)(2,1)S(1)}, u32[]{:S(2)}, u32[]{:S(2)}) collective-permute-start(bf16[200,512]{1,0:T(8,128)(2,1)} %get-tuple-element.204), channel_id=1, source_target_pairs={{0,4},{1,5},{2,6},{3,7},{4,0},{5,1},{6,2},{7,3},{8,12},{9,13},{10,... | collective-permute-start | bytes 614408 | tf_op jit(solution)/shard_map/ppermute | solution.py:36
  199.7 10.8 %collective-permute-start.45 = (bf16[200,512]{1,0:T(8,128)(2,1)}, bf16[200,512]{1,0:T(8,128)(2,1)S(1)}, u32[]{:S(2)}, u32[]{:S(2)}) collective-permute-start(bf16[200,512]{1,0:T(8,128)(2,1)} %get-tuple-element.205), channel_id=1, source_target_pairs={{0,6},{1,7},{2,4},{3,5},{4,2},{5,3},{6,0},{7,1},{8,14},{9,15},{10,... | collective-permute-start | bytes 614408 | tf_op jit(solution)/shard_map/ppermute | solution.py:36
  219.9 13.2 %collective-permute-start.54 = (bf16[8,64,512]{2,1,0:T(8,128)(2,1)}, bf16[8,64,512]{2,1,0:T(8,128)(2,1)S(1)}, u32[]{:S(2)}, u32[]{:S(2)}) collective-permute-start(bf16[8,64,512]{2,1,0:T(8,128)(2,1)} %get-tuple-element.214), channel_id=1, source_target_pairs={{0,1},{1,0},{2,3},{3,2},{4,5},{5,4},{6,7},{7,6},{8,9},{9,8},{10,11... | collective-permute-start | bytes 1572872 | tf_op jit(solution)/shard_map/ppermute | solution.py:36
  220.0 9.1 %collective-permute-start.51 = (bf16[1,200,512]{2,1,0:T(8,128)(2,1)}, bf16[1,200,512]{2,1,0:T(8,128)(2,1)S(1)}, u32[]{:S(2)}, u32[]{:S(2)}) collective-permute-start(bf16[1,200,512]{2,1,0:T(8,128)(2,1)} %bitcast.192), channel_id=1, source_target_pairs={{0,6},{1,7},{2,4},{3,5},{4,2},{5,3},{6,0},{7,1},{8,14},{9,15},{10,... | collective-permute-start | bytes 614408 | tf_op jit(solution)/shard_map/ppermute | solution.py:36
  221.9 10.8 %collective-permute-start.49 = (bf16[1,200,512]{2,1,0:T(8,128)(2,1)}, bf16[1,200,512]{2,1,0:T(8,128)(2,1)S(1)}, u32[]{:S(2)}, u32[]{:S(2)}) collective-permute-start(bf16[1,200,512]{2,1,0:T(8,128)(2,1)} %bitcast.193), channel_id=1, source_target_pairs={{0,4},{1,5},{2,6},{3,7},{4,0},{5,1},{6,2},{7,3},{8,12},{9,13},{10,... | collective-permute-start | bytes 614408 | tf_op jit(solution)/shard_map/ppermute | solution.py:36
  222.6 10.4 %collective-permute-start.47 = (bf16[1,200,512]{2,1,0:T(8,128)(2,1)}, bf16[1,200,512]{2,1,0:T(8,128)(2,1)S(1)}, u32[]{:S(2)}, u32[]{:S(2)}) collective-permute-start(bf16[1,200,512]{2,1,0:T(8,128)(2,1)} %bitcast.194), channel_id=1, source_target_pairs={{0,2},{1,3},{2,0},{3,1},{4,6},{5,7},{6,4},{7,5},{8,10},{9,11},{10,... | collective-permute-start | bytes 614408 | tf_op jit(solution)/shard_map/ppermute | solution.py:36
  237.5 20.8 %collective-permute-start.55 = (bf16[8,64,512]{2,1,0:T(8,128)(2,1)S(1)}, bf16[8,64,512]{2,1,0:T(8,128)(2,1)}, u32[]{:S(2)}, u32[]{:S(2)}) collective-permute-start(bf16[8,64,512]{2,1,0:T(8,128)(2,1)S(1)} %add.101), channel_id=1, source_target_pairs={{0,2},{1,3},{2,0},{3,1},{4,6},{5,7},{6,4},{7,5},{8,10},{9,11},{10,... | collective-permute-start | bytes 1572872 | tf_op jit(solution)/shard_map/ppermute | solution.py:36
  240.4 34.7 %collective-permute-start.60 = (bf16[2,2,4,64,512]{4,3,2,1,0:T(8,128)(2,1)}, bf16[2,2,4,64,512]{4,3,2,1,0:T(8,128)(2,1)S(1)}, u32[]{:S(2)}, u32[]{:S(2)}) collective-permute-start(bf16[2,2,4,64,512]{4,3,2,1,0:T(8,128)(2,1)} %bitcast_add_fusion.3), channel_id=1, source_target_pairs={{0,16},{1,9},{2,18},{3,11},{4,20},{5,13},{6,22},{7,15},{8,24},{9,1... | collective-permute-start | bytes 3145736 | tf_op jit(solution)/shard_map/ppermute | solution.py:772
  258.4 52.9 %collective-permute-start.71 = (bf16[2,2,2,4,64,512]{5,4,3,2,1,0:T(8,128)(2,1)}, bf16[2,2,2,4,64,512]{5,4,3,2,1,0:T(8,128)(2,1)S(1)}, u32[]{:S(2)}, u32[]{:S(2)}) collective-permute-start(bf16[2,2,2,4,64,512]{5,4,3,2,1,0:T(8,128)(2,1)} %get-tuple-element.263), channel_id=1, source_target_pairs={{0,8},{1,17},{2,10},{3,19},{4,12},{5,21},{6,14},{7,23},{8,0},{9,25... | collective-permute-start | bytes 6291464 | tf_op jit(solution)/shard_map/ppermute | solution.py:772
  263.4 11.7 %collective-permute-start.59 = (bf16[200,512]{1,0:T(8,128)(2,1)}, bf16[200,512]{1,0:T(8,128)(2,1)S(1)}, u32[]{:S(2)}, u32[]{:S(2)}) collective-permute-start(bf16[200,512]{1,0:T(8,128)(2,1)} %get-tuple-element.233), channel_id=1, source_target_pairs={{0,6},{1,7},{2,4},{3,5},{4,2},{5,3},{6,0},{7,1},{8,14},{9,15},{10,... | collective-permute-start | bytes 614408 | tf_op jit(solution)/shard_map/ppermute | solution.py:36
  263.9 11.4 %collective-permute-start.57 = (bf16[200,512]{1,0:T(8,128)(2,1)}, bf16[200,512]{1,0:T(8,128)(2,1)S(1)}, u32[]{:S(2)}, u32[]{:S(2)}) collective-permute-start(bf16[200,512]{1,0:T(8,128)(2,1)} %get-tuple-element.231), channel_id=1, source_target_pairs={{0,2},{1,3},{2,0},{3,1},{4,6},{5,7},{6,4},{7,5},{8,10},{9,11},{10,... | collective-permute-start | bytes 614408 | tf_op jit(solution)/shard_map/ppermute | solution.py:36
  265.4 9.9 %collective-permute-start.58 = (bf16[200,512]{1,0:T(8,128)(2,1)}, bf16[200,512]{1,0:T(8,128)(2,1)S(1)}, u32[]{:S(2)}, u32[]{:S(2)}) collective-permute-start(bf16[200,512]{1,0:T(8,128)(2,1)} %get-tuple-element.232), channel_id=1, source_target_pairs={{0,4},{1,5},{2,6},{3,7},{4,0},{5,1},{6,2},{7,3},{8,12},{9,13},{10,... | collective-permute-start | bytes 614408 | tf_op jit(solution)/shard_map/ppermute | solution.py:36
  275.1 12.4 %collective-permute-start.63 = (bf16[8,64,512]{2,1,0:T(8,128)(2,1)}, bf16[8,64,512]{2,1,0:T(8,128)(2,1)S(1)}, u32[]{:S(2)}, u32[]{:S(2)}) collective-permute-start(bf16[8,64,512]{2,1,0:T(8,128)(2,1)} %get-tuple-element.242), channel_id=1, source_target_pairs={{0,1},{1,0},{2,3},{3,2},{4,5},{5,4},{6,7},{7,6},{8,9},{9,8},{10,11... | collective-permute-start | bytes 1572872 | tf_op jit(solution)/shard_map/ppermute | solution.py:36
  291.9 19.4 %collective-permute-start.70 = (bf16[2,2,64,512]{3,2,1,0:T(8,128)(2,1)}, bf16[2,2,64,512]{3,2,1,0:T(8,128)(2,1)S(1)}, u32[]{:S(2)}, u32[]{:S(2)}) collective-permute-start(bf16[2,2,64,512]{3,2,1,0:T(8,128)(2,1)} %get-tuple-element.308), channel_id=1, source_target_pairs={{0,6},{1,7},{2,4},{3,5},{4,2},{5,3},{6,0},{7,1},{8,14},{9,15},{10,... | collective-permute-start | bytes 786440 | tf_op jit(solution)/shard_map/ppermute | solution.py:36
  292.8 18.5 %collective-permute-start.68 = (bf16[2,2,64,512]{3,2,1,0:T(8,128)(2,1)}, bf16[2,2,64,512]{3,2,1,0:T(8,128)(2,1)}, u32[]{:S(2)}, u32[]{:S(2)}) collective-permute-start(bf16[2,2,64,512]{3,2,1,0:T(8,128)(2,1)} %get-tuple-element.310), channel_id=1, source_target_pairs={{0,2},{1,3},{2,0},{3,1},{4,6},{5,7},{6,4},{7,5},{8,10},{9,11},{10,... | collective-permute-start | bytes 786440 | tf_op jit(solution)/shard_map/ppermute | solution.py:36
  294.3 17.0 %collective-permute-start.69 = (bf16[2,2,64,512]{3,2,1,0:T(8,128)(2,1)}, bf16[2,2,64,512]{3,2,1,0:T(8,128)(2,1)}, u32[]{:S(2)}, u32[]{:S(2)}) collective-permute-start(bf16[2,2,64,512]{3,2,1,0:T(8,128)(2,1)} %get-tuple-element.311), channel_id=1, source_target_pairs={{0,4},{1,5},{2,6},{3,7},{4,0},{5,1},{6,2},{7,3},{8,12},{9,13},{10,... | collective-permute-start | bytes 786440 | tf_op jit(solution)/shard_map/ppermute | solution.py:36
  296.9 21.0 %collective-permute-start.64 = (bf16[8,64,512]{2,1,0:T(8,128)(2,1)S(1)}, bf16[8,64,512]{2,1,0:T(8,128)(2,1)S(1)}, u32[]{:S(2)}, u32[]{:S(2)}) collective-permute-start(bf16[8,64,512]{2,1,0:T(8,128)(2,1)S(1)} %add.106), channel_id=1, source_target_pairs={{0,2},{1,3},{2,0},{3,1},{4,6},{5,7},{6,4},{7,5},{8,10},{9,11},{10,... | collective-permute-start | bytes 1572872 | tf_op jit(solution)/shard_map/ppermute | solution.py:36
  311.3 14.9 %collective-permute-start.76 = (bf16[4,200,512]{2,1,0:T(8,128)(2,1)}, bf16[4,200,512]{2,1,0:T(8,128)(2,1)}, u32[]{:S(2)}, u32[]{:S(2)}) collective-permute-start(bf16[4,200,512]{2,1,0:T(8,128)(2,1)} %get-tuple-element.281), channel_id=1, source_target_pairs={{0,1},{1,0},{2,3},{3,2},{4,5},{5,4},{6,7},{7,6},{8,9},{9,8},{10,11... | collective-permute-start | bytes 2457608 | tf_op jit(solution)/shard_map/ppermute | solution.py:36
  314.1 27.2 %collective-permute-start.75 = (bf16[2,2,4,64,512]{4,3,2,1,0:T(8,128)(2,1)}, bf16[2,2,4,64,512]{4,3,2,1,0:T(8,128)(2,1)}, u32[]{:S(2)}, u32[]{:S(2)}) collective-permute-start(bf16[2,2,4,64,512]{4,3,2,1,0:T(8,128)(2,1)} %bitcast_add_fusion.1), channel_id=1, source_target_pairs={{0,16},{1,9},{2,18},{3,11},{4,20},{5,13},{6,22},{7,15},{8,24},{9,1... | collective-permute-start | bytes 3145736 | tf_op jit(solution)/shard_map/ppermute | solution.py:772
  315.4 9.2 %collective-permute-start.66 = (bf16[4,64,512]{2,1,0:T(8,128)(2,1)S(1)}, bf16[4,64,512]{2,1,0:T(8,128)(2,1)S(1)}, u32[]{:S(2)}, u32[]{:S(2)}) collective-permute-start(bf16[4,64,512]{2,1,0:T(8,128)(2,1)S(1)} %slice.239), channel_id=1, source_target_pairs={{0,4},{1,5},{2,6},{3,7},{4,0},{5,1},{6,2},{7,3},{8,12},{9,13},{10,... | collective-permute-start | bytes 786440 | tf_op jit(solution)/shard_map/ppermute | solution.py:36
  318.0 12.3 %collective-permute-start.65 = (bf16[4,64,512]{2,1,0:T(8,128)(2,1)S(1)}, bf16[4,64,512]{2,1,0:T(8,128)(2,1)S(1)}, u32[]{:S(2)}, u32[]{:S(2)}) collective-permute-start(bf16[4,64,512]{2,1,0:T(8,128)(2,1)S(1)} %slice.237), channel_id=1, source_target_pairs={{0,4},{1,5},{2,6},{3,7},{4,0},{5,1},{6,2},{7,3},{8,12},{9,13},{10,... | collective-permute-start | bytes 786440 | tf_op jit(solution)/shard_map/ppermute | solution.py:36
  324.7 7.4 %collective-permute-start.73 = (f32[20,512]{1,0:T(8,128)S(1)}, f32[20,512]{1,0:T(8,128)S(1)}, u32[]{:S(2)}, u32[]{:S(2)}) collective-permute-start(f32[20,512]{1,0:T(8,128)S(1)} %add.112), channel_id=1, source_target_pairs={{0,4},{1,5},{2,6},{3,7},{4,0},{5,1},{6,2},{7,3},{8,12},{9,13},{10,... | collective-permute-start | bytes 122888 | tf_op jit(solution)/shard_map/ppermute | solution.py:36
  328.6 8.6 %collective-permute-start.77 = (bf16[200,512]{1,0:T(8,128)(2,1)}, bf16[200,512]{1,0:T(8,128)(2,1)S(1)}, u32[]{:S(2)}, u32[]{:S(2)}) collective-permute-start(bf16[200,512]{1,0:T(8,128)(2,1)} %get-tuple-element.283), channel_id=1, source_target_pairs={{0,2},{1,3},{2,0},{3,1},{4,6},{5,7},{6,4},{7,5},{8,10},{9,11},{10,... | collective-permute-start | bytes 614408 | tf_op jit(solution)/shard_map/ppermute | solution.py:36
  329.3 8.2 %collective-permute-start.78 = (bf16[200,512]{1,0:T(8,128)(2,1)}, bf16[200,512]{1,0:T(8,128)(2,1)S(1)}, u32[]{:S(2)}, u32[]{:S(2)}) collective-permute-start(bf16[200,512]{1,0:T(8,128)(2,1)} %get-tuple-element.284), channel_id=1, source_target_pairs={{0,4},{1,5},{2,6},{3,7},{4,0},{5,1},{6,2},{7,3},{8,12},{9,13},{10,... | collective-permute-start | bytes 614408 | tf_op jit(solution)/shard_map/ppermute | solution.py:36
  330.3 10.1 %collective-permute-start.79 = (bf16[200,512]{1,0:T(8,128)(2,1)}, bf16[200,512]{1,0:T(8,128)(2,1)S(1)}, u32[]{:S(2)}, u32[]{:S(2)}) collective-permute-start(bf16[200,512]{1,0:T(8,128)(2,1)} %get-tuple-element.285), channel_id=1, source_target_pairs={{0,6},{1,7},{2,4},{3,5},{4,2},{5,3},{6,0},{7,1},{8,14},{9,15},{10,... | collective-permute-start | bytes 614408 | tf_op jit(solution)/shard_map/ppermute | solution.py:36
  345.5 10.5 %collective-permute-start.83 = (bf16[2,2,64,512]{3,2,0,1:T(8,128)(2,1)S(1)}, bf16[2,2,64,512]{3,2,0,1:T(8,128)(2,1)S(1)}, u32[]{:S(2)}, u32[]{:S(2)}) collective-permute-start(bf16[2,2,64,512]{3,2,0,1:T(8,128)(2,1)S(1)} %slice.207), channel_id=1, source_target_pairs={{0,8},{1,9},{2,10},{3,11},{4,12},{5,13},{6,14},{7,15},{8,0},{9,1},... | collective-permute-start | bytes 786440 | tf_op jit(solution)/shard_map/ppermute | solution.py:36
  350.9 10.2 %collective-permute-start.87 = (bf16[2,2,64,512]{3,2,1,0:T(8,128)(2,1)S(1)}, bf16[2,2,64,512]{3,2,1,0:T(8,128)(2,1)S(1)}, u32[]{:S(2)}, u32[]{:S(2)}) collective-permute-start(bf16[2,2,64,512]{3,2,1,0:T(8,128)(2,1)S(1)} %get-tuple-element.302), channel_id=1, source_target_pairs={{0,6},{1,7},{2,4},{3,5},{4,2},{5,3},{6,0},{7,1},{8,14},{9,15},{10,... | collective-permute-start | bytes 786440 | tf_op jit(solution)/shard_map/ppermute | solution.py:36
  352.8 11.2 %collective-permute-start.86 = (bf16[2,2,64,512]{3,2,1,0:T(8,128)(2,1)S(1)}, bf16[2,2,64,512]{3,2,1,0:T(8,128)(2,1)S(1)}, u32[]{:S(2)}, u32[]{:S(2)}) collective-permute-start(bf16[2,2,64,512]{3,2,1,0:T(8,128)(2,1)S(1)} %get-tuple-element.303), channel_id=1, source_target_pairs={{0,4},{1,5},{2,6},{3,7},{4,0},{5,1},{6,2},{7,3},{8,12},{9,13},{10,... | collective-permute-start | bytes 786440 | tf_op jit(solution)/shard_map/ppermute | solution.py:36
  353.6 10.6 %collective-permute-start.85 = (bf16[2,2,64,512]{3,2,1,0:T(8,128)(2,1)S(1)}, bf16[2,2,64,512]{3,2,1,0:T(8,128)(2,1)S(1)}, u32[]{:S(2)}, u32[]{:S(2)}) collective-permute-start(bf16[2,2,64,512]{3,2,1,0:T(8,128)(2,1)S(1)} %get-tuple-element.304), channel_id=1, source_target_pairs={{0,2},{1,3},{2,0},{3,1},{4,6},{5,7},{6,4},{7,5},{8,10},{9,11},{10,... | collective-permute-start | bytes 786440 | tf_op jit(solution)/shard_map/ppermute | solution.py:36
  356.0 11.5 %collective-permute-start.84 = (bf16[1,2,64,512]{3,2,0,1:T(8,128)(2,1)S(1)}, bf16[1,2,64,512]{3,2,0,1:T(8,128)(2,1)S(1)}, u32[]{:S(2)}, u32[]{:S(2)}) collective-permute-start(bf16[1,2,64,512]{3,2,0,1:T(8,128)(2,1)S(1)} %slice.253), channel_id=1, source_target_pairs={{0,16},{1,17},{2,18},{3,19},{4,20},{5,21},{6,22},{7,23},{8,24},{9,... | collective-permute-start | bytes 393224 | tf_op jit(solution)/shard_map/ppermute | solution.py:36
  (97 other events, 646.7 us)

commit v7 on v6

--- a/solution.py
+++ b/solution.py
@@ -109,7 +109,7 @@
 
 
 LANES = 256
-SPLIT = 2
+SPLIT = 1
 
 
 def slot_kernel(experts, mine_ref, ids, rank, mine, theirs):
@@ -268,8 +268,11 @@
     for group in copies:
         for copy in group:
             copy.wait()
-    for j in range(4):
-        qkv[:, j * 6 * HD : (j + 1) * 6 * HD] = dot(normed_a, wbuf[j, :, : 6 * HD]).astype(bf16)
+
+    @pl.loop(0, 4)
+    def _(j):
+        qkv[:, pl.ds(pl.multiple_of(j * 6 * HD, 6 * HD), 6 * HD)] = dot(normed_a, wbuf[j, :, : 6 * HD]).astype(bf16)
+
     probs = []
     for j in range(4):
         part = qkv[:, j * 6 * HD : (j + 1) * 6 * HD]
@@ -330,7 +333,7 @@
 
 def attention_backward_kernel(
     off_ref, base, p0, p1, p2, p3, hidden_in, hidden_mid, gains, w0, w1, w2, w3, qkv, ctx,
-    grad_out, branch, gain_out, g0, g1, g2, g3, scratch, wbuf, gbuf, sems, out_sems,
+    grad_out, branch, gain_out, g0, g1, g2, g3, scratch, wbuf, gbuf, mixed_buf, back_buf, sems, out_sems,
 ):
     copies = weight_copies(off_ref, (w0, w1, w2, w3), wbuf, sems)
     for group in copies:
@@ -355,7 +358,12 @@
     queries = [part[:, : 2 * HD] for part in parts]
     keys = [part[:, 2 * HD : 4 * HD] for part in parts]
     values = [part[:, 4 * HD :] for part in parts]
-    context_grads = [dot(attn_grad, wbuf[j, :, 6 * HD :]).astype(bf16) for j in range(4)]
+
+    @pl.loop(0, 4)
+    def _(j):
+        back_buf[j] = dot(attn_grad, wbuf[j, :, 6 * HD :]).astype(bf16)
+
+    context_grads = [back_buf[j] for j in range(4)]
     probs = [head_probs(queries[j], keys[j], mask) for j, mask in heads]
     probs_grads = [dot_t(only(context_grads[j], mask), values[j]) for j, mask in heads]
     v_grads = [t_dot(probs[i].astype(bf16), context_grads[j]) for i, (j, mask) in enumerate(heads)]
@@ -364,16 +372,23 @@
     ]
     q_grads = [dot(score_grads[i], keys[j]) * scale for i, (j, mask) in enumerate(heads)]
     k_grads = [t_dot(score_grads[i], queries[j]) * scale for i, (j, mask) in enumerate(heads)]
-    normed_part = jnp.zeros_like(grad)
+    for j in range(4):
+        mixed_buf[j] = jnp.concatenate(
+            [jnp.where(low, g[2 * j], g[2 * j + 1]).astype(bf16) for g in (q_grads, k_grads, v_grads)], axis=1
+        )
+    scratch[...] = jnp.zeros_like(scratch)
+
+    @pl.loop(0, 4)
+    def _(j):
+        mixed = mixed_buf[j]
+        context = ctx[:, pl.ds(pl.multiple_of(j * 2 * HD, 2 * HD), 2 * HD)]
+        gbuf[j, :, : 6 * HD] = dot(normed_t, mixed).astype(bf16)
+        gbuf[j, :, 6 * HD :] = dot(attn_grad_t, context).astype(bf16)
+        scratch[...] += dot_t(mixed, wbuf[j, :, : 6 * HD])
+
+    normed_part = scratch[...]
     sends = []
     for j, target in enumerate((g0, g1, g2, g3)):
-        mixed = jnp.concatenate(
-            [jnp.where(low, g[2 * j], g[2 * j + 1]).astype(bf16) for g in (q_grads, k_grads, v_grads)], axis=1
-        )
-        context = ctx[:, j * 2 * HD : (j + 1) * 2 * HD]
-        gbuf[j, :, : 6 * HD] = dot(normed_t, mixed).astype(bf16)
-        gbuf[j, :, 6 * HD :] = dot(attn_grad_t, context).astype(bf16)
-        normed_part = normed_part + dot_t(mixed, wbuf[j, :, : 6 * HD])
         count, rows, unused = target.shape
         for i in range(count):
             send = pltpu.make_async_copy(
@@ -407,6 +422,8 @@
             pltpu.VMEM((ROWS, width), f32),
             pltpu.VMEM((4, width, width), bf16),
             pltpu.VMEM((4, width, width), bf16),
+            pltpu.VMEM((4, ROWS, 6 * HD), bf16),
+            pltpu.VMEM((4, ROWS, 2 * HD), bf16),
             pltpu.SemaphoreType.DMA((4, blocks[0])),
             pltpu.SemaphoreType.DMA((4, blocks[0])),
         ],

time: 376 us -> 370 us (0.984); the launches traced: 369 us -> 369 us
  Pallas kernels: 86.6 us -> 91.6 us
  waiting for transfers between devices: 159 us -> 154 us
    ppermute x10, waiting for transfers between devices: 46.4 us -> 42.3 us  [mixed(): return lax.ppermute(value, AXES, pairs)]
    pallas_call x2, Pallas kernels: 17.5 us -> 21.6 us  [attention_backward(): pl.pallas_call(attention_backward_kernel, out_shape=(shape((out_rows, wid...]
  transfers between devices with their start and end apart: 88 -> 88, of which waited for: 51 -> 50; matrix products, arithmetic and copies ran while one was open for 6% -> 6% of each run, Pallas kernels for 19% -> 20%
where the time goes in v7:
time: 370 us; the launch traced here: 369 us
  waiting for transfers between devices  154 us (42%)
  Pallas kernels  91.6 us (25%)
  starting transfers between devices  84.5 us (23%)
  local copies, waits for them, and re-layouts  20.5 us (6%)
  other arithmetic  16.7 us (5%)
    ppermute x78, waiting for transfers between devices, swap(): return lax.ppermute(value, AXES, pairs)  112 us
    ppermute x78, starting transfers between devices, swap(): return lax.ppermute(value, AXES, pairs)  68 us
    ppermute x10, waiting for transfers between devices, mixed(): return lax.ppermute(value, AXES, pairs)  42.3 us
    pallas_call x3, Pallas kernels, expert_layer(): pl.pallas_call(lambda *refs: expert_kernel(plan, *refs), out_shape=tuple(...  40.2 us
    pallas_call x2, Pallas kernels, attention_backward(): pl.pallas_call(attention_backward_kernel, out_shape=(shape((out_rows, wid...  21.6 us
    ppermute x10, starting transfers between devices, mixed(): return lax.ppermute(value, AXES, pairs)  16.5 us
    pallas_call x2, Pallas kernels, attention_forward(): pl.pallas_call(lambda *refs: attention_forward_kernel(len(pieces), len(ex...  12.9 us
    pallas_call x4, Pallas kernels, pair_rows(): pl.pallas_call(add_kernel, out_shape=(jax.ShapeDtypeStruct(even.shape[1:]...  9.33 us
  transfers between devices with their start and end apart: 88, of which 50 were waited for; matrix products, arithmetic and copies ran while one was open for 6% of the time, Pallas kernels for 20%

profile of v7, /device:TPU:0, one launch (start us, length us, event | category | flops | bytes accessed | tf_op | source)
XLA Modules:
  0.0 369.1 jit_solution(18283586894454478182)
XLA Ops:
  5.8 4.0 %collective-permute-start.1 = (bf16[1,2,64,512]{3,2,0,1:T(8,128)(2,1)S(1)}, bf16[1,2,64,512]{3,2,0,1:T(8,128)(2,1)S(1)}, u32[]{:S(2)}, u32[]{:S(2)}) collective-permute-start(bf16[1,2,64,512]{3,2,0,1:T(8,128)(2,1)S(1)} %maximum_bitcast_fusion), channel_id=1, source_target_pairs={{0,16},{1,17},{2,18},{3,19},{4,20},{5,21},{6,22},{7,23},{8,24},{9,... | collective-permute-start | bytes 393224 | tf_op jit(solution)/shard_map/ppermute | solution.py:36
  13.5 3.0 collective-permute-done.1
  17.3 1.9 collective-permute-done.4
  19.2 5.7 %collective-permute-done.3 = bf16[2,2,64,512]{3,2,0,1:T(8,128)(2,1)S(1)} collective-permute-done((bf16[2,2,64,512]{3,2,0,1:T(8,128)(2,1)S(1)}, bf16[2,2,64,512]{3,2,0,1:T(8,128)(2,1)S(1)}, u32[]{:S(2)}, u32[]{:S(2)}) %collective-permute-start.3) | collective-permute-done | bytes 262176 | tf_op jit(solution)/shard_map/ppermute | solution.py:36
  26.7 2.3 collective-permute-start.9
  29.0 8.9 %collective-permute-done.6 = bf16[4,2,64,512]{3,2,0,1:T(8,128)(2,1)S(1)} collective-permute-done((bf16[4,2,64,512]{3,2,0,1:T(8,128)(2,1)S(1)}, bf16[4,2,64,512]{3,2,0,1:T(8,128)(2,1)S(1)}, u32[]{:S(2)}, u32[]{:S(2)}) %collective-permute-start.6) | collective-permute-done | bytes 524320 | tf_op jit(solution)/shard_map/ppermute | solution.py:36
  40.6 2.3 slots.1
  50.0 3.8 %collective-permute-done.9.refs_14_.refs_16_ = bf16[2,2,4,64,512]{4,3,2,1,0:T(8,128)(2,1)} collective-permute-done((bf16[2,2,4,64,512]{4,3,2,1,0:T(8,128)(2,1)S(1)}, bf16[2,2,4,64,512]{4,3,2,1,0:T(8,128)(2,1)}, u32[]{:S(2)}, u32[]{:S(2)}) %collective-permute-start.9) | collective-permute-done | bytes 1048608 | tf_op jit(solution)/shard_map/ppermute | solution.py:789
  62.2 6.1 %attention_forward.2 = (f32[200,512]{1,0:T(8,128)}, f32[200,512]{1,0:T(8,128)}, bf16[1,200,512]{2,1,0:T(8,128)(2,1)}, bf16[200,1536]{1,0:T(8,128)(2,1)}, bf16[200,512]{1,0:T(8,128)(2,1)}) custom-call(s32[8]{0:T(128)} %xor_multiply_fusion.1.refs_0_.off_ref, bf16[197,512]{1,0:T(8,128)(2,1)} %refs_1_.1, f32[2,512]{1,0:T(2,128)} %get-tuple-element.336.refs_2_.gains, ...), custom_call_target="tpu_custom_call" | custom-call | flops 1 | bytes 1 | tf_op jit(solution)/shard_map/attention_forward/pallas_call | solution.py:312
  68.3 2.7 collective-permute-done.13
  77.0 3.7 %collective-permute-done.26.refs_15_.refs_17_ = bf16[2,2,4,64,512]{4,3,2,1,0:T(8,128)(2,1)} collective-permute-done((bf16[2,2,4,64,512]{4,3,2,1,0:T(8,128)(2,1)S(1)}, bf16[2,2,4,64,512]{4,3,2,1,0:T(8,128)(2,1)}, u32[]{:S(2)}, u32[]{:S(2)}) %collective-permute-start.26) | collective-permute-done | bytes 1048608 | tf_op jit(solution)/shard_map/ppermute | solution.py:789
  80.7 10.1 %collective-permute-done.24.refs_10_.w2 = bf16[8,64,512]{2,1,0:T(8,128)(2,1)S(1)} collective-permute-done((bf16[8,64,512]{2,1,0:T(8,128)(2,1)S(1)}, bf16[8,64,512]{2,1,0:T(8,128)(2,1)S(1)}, u32[]{:S(2)}, u32[]{:S(2)}) %collective-permute-start.24) | collective-permute-done | bytes 524320 | tf_op jit(solution)/shard_map/ppermute | solution.py:36
  91.9 6.4 %collective-permute-done.17.refs_7_ = bf16[1,200,512]{2,1,0:T(8,128)(2,1)S(1)} collective-permute-done((bf16[1,200,512]{2,1,0:T(8,128)(2,1)S(1)}, bf16[1,200,512]{2,1,0:T(8,128)(2,1)S(1)}, u32[]{:S(2)}, u32[]{:S(2)}) %collective-permute-start.17) | collective-permute-done | bytes 204832 | tf_op jit(solution)/shard_map/ppermute | solution.py:36
  98.9 4.3 %collective-permute-done.27.refs_16_.refs_18_ = bf16[2,2,4,64,512]{4,3,2,1,0:T(8,128)(2,1)} collective-permute-done((bf16[2,2,4,64,512]{4,3,2,1,0:T(8,128)(2,1)}, bf16[2,2,4,64,512]{4,3,2,1,0:T(8,128)(2,1)}, u32[]{:S(2)}, u32[]{:S(2)}) %collective-permute-start.27) | collective-permute-done | bytes 1048608 | tf_op jit(solution)/shard_map/ppermute | solution.py:789
  103.2 1.6 collective-permute-start.32
  105.6 9.2 %expert_layer.3 = (bf16[4,200,512]{2,1,0:T(8,128)(2,1)}, bf16[4,200,512]{2,1,0:T(8,128)(2,1)}, bf16[512,512]{1,0:T(8,128)(2,1)}, f32[512,512]{1,0:T(8,128)}) custom-call(s32[8]{0:T(128)} %mul.21.refs_0_, s32[1]{0:T(128)} %bitcast.31.refs_1_.refs_0_, s32[2,4,256]{2,1,0:T(4,128)} %get-tuple-element.165.refs_2_, s32[2,4,256]{2,1,0:T(4,128)} %copy-done.57, ...), custom_call_target="tpu_custom_call" | custom-call | flops 1 | bytes 1 | tf_op jit(solution)/shard_map/expert_layer/pallas_call | solution.py:654
  114.9 2.4 collective-permute-start.35
  118.3 2.3 add_rows.4
  124.1 3.8 %collective-permute-done.29.refs_3_ = bf16[200,512]{1,0:T(8,128)(2,1)S(1)} collective-permute-done((bf16[200,512]{1,0:T(8,128)(2,1)}, bf16[200,512]{1,0:T(8,128)(2,1)S(1)}, u32[]{:S(2)}, u32[]{:S(2)}) %collective-permute-start.29) | collective-permute-done | bytes 204832 | tf_op jit(solution)/shard_map/ppermute | solution.py:36
  128.0 2.4 collective-permute-done.30.refs_4_
  130.3 3.2 collective-permute-done.31.refs_5_
  134.2 6.8 %attention_forward.3 = (f32[200,512]{1,0:T(8,128)}, f32[200,512]{1,0:T(8,128)}, bf16[2,200,512]{2,1,0:T(8,128)(2,1)}, bf16[200,1536]{1,0:T(8,128)(2,1)}, bf16[200,512]{1,0:T(8,128)(2,1)}) custom-call(s32[8]{0:T(128)} %xor_multiply_fusion.1.refs_0_.off_ref, f32[200,512]{1,0:T(8,128)} %get-tuple-element.162.refs_1_.hidden_mid, ...), custom_call_target="tpu_custom_call" | custom-call | flops 1 | bytes 1 | tf_op jit(solution)/shard_map/attention_forward/pallas_call | solution.py:312
  141.3 3.2 collective-permute-start.41
  148.0 2.9 collective-permute-done.35.refs_15_
  150.9 2.0 collective-permute-start.33
  153.0 5.1 %collective-permute-done.39.refs_11_ = bf16[2,200,512]{2,1,0:T(8,128)(2,1)S(1)} collective-permute-done((bf16[2,200,512]{2,1,0:T(8,128)(2,1)}, bf16[2,200,512]{2,1,0:T(8,128)(2,1)S(1)}, u32[]{:S(2)}, u32[]{:S(2)}) %collective-permute-start.39) | collective-permute-done | bytes 409632 | tf_op jit(solution)/shard_map/ppermute | solution.py:36
  158.1 5.6 %collective-permute-done.37.refs_9_ = bf16[2,200,512]{2,1,0:T(8,128)(2,1)S(1)} collective-permute-done((bf16[2,200,512]{2,1,0:T(8,128)(2,1)}, bf16[2,200,512]{2,1,0:T(8,128)(2,1)S(1)}, u32[]{:S(2)}, u32[]{:S(2)}) %collective-permute-start.37) | collective-permute-done | bytes 409632 | tf_op jit(solution)/shard_map/ppermute | solution.py:36
  166.8 5.4 %collective-permute-done.41.refs_16_ = bf16[2,2,4,64,512]{4,3,2,1,0:T(8,128)(2,1)} collective-permute-done((bf16[2,2,4,64,512]{4,3,2,1,0:T(8,128)(2,1)}, bf16[2,2,4,64,512]{4,3,2,1,0:T(8,128)(2,1)}, u32[]{:S(2)}, u32[]{:S(2)}) %collective-permute-start.41) | collective-permute-done | bytes 1048608 | tf_op jit(solution)/shard_map/ppermute | solution.py:789
  172.3 16.7 %expert_layer.4 = (bf16[4,200,512]{2,1,0:T(8,128)(2,1)}, bf16[4,200,512]{2,1,0:T(8,128)(2,1)}, bf16[4,200,512]{2,1,0:T(8,128)(2,1)}, bf16[4,200,512]{2,1,0:T(8,1...) custom-call(s32[8]{0:T(128)} %mul.21.refs_0_, ...), custom_call_target="tpu_custom_call" | custom-call | flops 1 | bytes 1 | tf_op jit(solution)/shard_map/expert_layer/pallas_call | solution.py:654
  189.0 2.4 collective-permute-start.53
  192.0 2.2 collective-permute-done.42.odd
  195.0 2.3 add_rows.5
  200.9 4.1 %collective-permute-done.43.p1 = bf16[200,512]{1,0:T(8,128)(2,1)S(1)} collective-permute-done((bf16[200,512]{1,0:T(8,128)(2,1)}, bf16[200,512]{1,0:T(8,128)(2,1)S(1)}, u32[]{:S(2)}, u32[]{:S(2)}) %collective-permute-start.43) | collective-permute-done | bytes 204832 | tf_op jit(solution)/shard_map/ppermute | solution.py:36
  204.9 1.9 collective-permute-done.44.p2
  206.8 3.7 %collective-permute-done.45.p3 = bf16[200,512]{1,0:T(8,128)(2,1)S(1)} collective-permute-done((bf16[200,512]{1,0:T(8,128)(2,1)}, bf16[200,512]{1,0:T(8,128)(2,1)S(1)}, u32[]{:S(2)}, u32[]{:S(2)}) %collective-permute-start.45) | collective-permute-done | bytes 204832 | tf_op jit(solution)/shard_map/ppermute | solution.py:36
  211.2 10.8 %attention_backward.2 = (f32[200,512]{1,0:T(8,128)}, bf16[200,512]{1,0:T(8,128)(2,1)}, f32[2,512]{1,0:T(2,128)}, bf16[8,64,512]{2,1,0:T(8,128)(2,1)}, bf16[8,64,...) custom-call(s32[8]{0:T(128)} %xor_multiply_fusion.1.refs_0_.off_ref, f32[197,512]{1,0:T(8,128)} %base.1, ...), custom_call_target="tpu_custom_call" | custom-call | flops 1 | bytes 1 | tf_op jit(solution)/shard_map/attention_backward/pallas_call | solution.py:412
  222.0 1.8 collective-permute-start.51
  225.6 5.5 %collective-permute-done.51.refs_11_ = bf16[1,200,512]{2,1,0:T(8,128)(2,1)S(1)} collective-permute-done((bf16[1,200,512]{2,1,0:T(8,128)(2,1)}, bf16[1,200,512]{2,1,0:T(8,128)(2,1)S(1)}, u32[]{:S(2)}, u32[]{:S(2)}) %collective-permute-start.51) | collective-permute-done | bytes 204832 | tf_op jit(solution)/shard_map/ppermute | solution.py:36
  231.1 3.5 collective-permute-done.49.refs_9_
  237.6 1.8 collective-permute-start.55
  240.5 3.6 collective-permute-start.60
  244.0 14.4 %expert_layer.5 = (bf16[4,200,512]{2,1,0:T(8,128)(2,1)}, bf16[4,200,512]{2,1,0:T(8,128)(2,1)}, f32[8,512]{1,0:T(8,128)}, bf16[2,2,4,64,512]{4,3,2,1,0:T(8,128)(2...) custom-call(s32[8]{0:T(128)} %mul.21.refs_0_, s32[1]{0:T(128)} %bitcast.31.refs_1_.refs_0_, ...), custom_call_target="tpu_custom_call" | custom-call | flops 10000000000 | bytes 1 | tf_op jit(solution)/shard_map/expert_layer/pallas_call | solution.py:654
  258.6 2.6 collective-permute-done.56.odd
  261.2 2.3 add_rows.6
  267.0 8.5 %collective-permute-done.60 = bf16[2,2,4,64,512]{4,3,2,1,0:T(8,128)(2,1)S(1)} collective-permute-done((bf16[2,2,4,64,512]{4,3,2,1,0:T(8,128)(2,1)}, bf16[2,2,4,64,512]{4,3,2,1,0:T(8,128)(2,1)S(1)}, u32[]{:S(2)}, u32[]{:S(2)}) %collective-permute-start.60) | collective-permute-done | bytes 1048608 | tf_op jit(solution)/shard_map/ppermute | solution.py:789
  276.8 10.8 %attention_backward.3 = (f32[197,512]{1,0:T(8,128)}, bf16[200,512]{1,0:T(8,128)(2,1)}, f32[2,512]{1,0:T(2,128)}, bf16[8,64,512]{2,1,0:T(8,128)(2,1)}, bf16[8,64,...) custom-call(s32[8]{0:T(128)} %xor_multiply_fusion.1.refs_0_.off_ref, ...), custom_call_target="tpu_custom_call" | custom-call | flops 1 | bytes 1 | tf_op jit(solution)/shard_map/attention_backward/pallas_call | solution.py:412
  288.2 1.7 fusion
  291.6 1.7 collective-permute-done.67
  300.0 11.3 %collective-permute-done.71 = bf16[2,2,2,4,64,512]{5,4,3,2,1,0:T(8,128)(2,1)S(1)} collective-permute-done((bf16[2,2,2,4,64,512]{5,4,3,2,1,0:T(8,128)(2,1)}, bf16[2,2,2,4,64,512]{5,4,3,2,1,0:T(8,128)(2,1)S(1)}, u32[]{:S(2)}, u32[]{:S(2)}) %collective-permute-start.71) | collective-permute-done | bytes 2097184 | tf_op jit(solution)/shard_map/ppermute | solution.py:789
  311.4 1.8 collective-permute-start.76
  317.0 3.1 collective-permute-done.64
  321.5 3.3 collective-permute-done.66
  326.2 2.3 add_rows.7
  330.4 1.6 collective-permute-start.79
  333.1 2.6 unpack.2
  337.6 2.7 collective-permute-done.79
  341.5 1.7 bitcast_add_fusion
  343.5 1.9 collective-permute-done.80
  345.6 2.1 collective-permute-start.83
  348.5 1.7 collective-permute-done.81
  356.1 2.3 collective-permute-start.84
  359.0 2.2 collective-permute-done.87.refs_4_
  361.2 2.8 collective-permute-done.86.refs_3_
  365.0 2.6 unpack.3
  (360 shorter events, 98.0 us)
Async XLA Ops:
  5.8 10.6 %collective-permute-start.1 = (bf16[1,2,64,512]{3,2,0,1:T(8,128)(2,1)S(1)}, bf16[1,2,64,512]{3,2,0,1:T(8,128)(2,1)S(1)}, u32[]{:S(2)}, u32[]{:S(2)}) collective-permute-start(bf16[1,2,64,512]{3,2,0,1:T(8,128)(2,1)S(1)} %maximum_bitcast_fusion), channel_id=1, source_target_pairs={{0,16},{1,17},{2,18},{3,19},{4,20},{5,21},{6,22},{7,23},{8,24},{9,... | collective-permute-start | bytes 393224 | tf_op jit(solution)/shard_map/ppermute | solution.py:36
  10.0 9.3 %collective-permute-start.4 = (bf16[2,2,64,512]{3,2,0,1:T(8,128)(2,1)S(1)}, bf16[2,2,64,512]{3,2,0,1:T(8,128)(2,1)S(1)}, u32[]{:S(2)}, u32[]{:S(2)}) collective-permute-start(bf16[2,2,64,512]{3,2,0,1:T(8,128)(2,1)S(1)} %get-tuple-element.327), channel_id=1, source_target_pairs={{0,4},{1,5},{2,6},{3,7},{4,0},{5,1},{6,2},{7,3},{8,12},{9,13},{10,... | collective-permute-start | bytes 786440 | tf_op jit(solution)/shard_map/ppermute | solution.py:36
  11.5 13.4 %collective-permute-start.3 = (bf16[2,2,64,512]{3,2,0,1:T(8,128)(2,1)S(1)}, bf16[2,2,64,512]{3,2,0,1:T(8,128)(2,1)S(1)}, u32[]{:S(2)}, u32[]{:S(2)}) collective-permute-start(bf16[2,2,64,512]{3,2,0,1:T(8,128)(2,1)S(1)} %get-tuple-element.328), channel_id=1, source_target_pairs={{0,2},{1,3},{2,0},{3,1},{4,6},{5,7},{6,4},{7,5},{8,10},{9,11},{10,... | collective-permute-start | bytes 786440 | tf_op jit(solution)/shard_map/ppermute | solution.py:36
  13.0 11.9 %collective-permute-start.5 = (bf16[2,2,64,512]{3,2,0,1:T(8,128)(2,1)S(1)}, bf16[2,2,64,512]{3,2,0,1:T(8,128)(2,1)S(1)}, u32[]{:S(2)}, u32[]{:S(2)}) collective-permute-start(bf16[2,2,64,512]{3,2,0,1:T(8,128)(2,1)S(1)} %slice_bitcast_fusion.16), channel_id=1, source_target_pairs={{0,6},{1,7},{2,4},{3,5},{4,2},{5,3},{6,0},{7,1},{8,14},{9,15},{10,... | collective-permute-start | bytes 786440 | tf_op jit(solution)/shard_map/ppermute | solution.py:36
  16.5 8.7 %collective-permute-start.2 = (bf16[2,2,64,512]{3,2,0,1:T(8,128)(2,1)S(1)}, bf16[2,2,64,512]{3,2,0,1:T(8,128)(2,1)S(1)}, u32[]{:S(2)}, u32[]{:S(2)}) collective-permute-start(bf16[2,2,64,512]{3,2,0,1:T(8,128)(2,1)S(1)} %pad_maximum_fusion.10), channel_id=1, source_target_pairs={{0,8},{1,9},{2,10},{3,11},{4,12},{5,13},{6,14},{7,15},{8,0},{9,1},... | collective-permute-start | bytes 786440 | tf_op jit(solution)/shard_map/ppermute | solution.py:36
  25.2 12.7 %collective-permute-start.6 = (bf16[4,2,64,512]{3,2,0,1:T(8,128)(2,1)S(1)}, bf16[4,2,64,512]{3,2,0,1:T(8,128)(2,1)S(1)}, u32[]{:S(2)}, u32[]{:S(2)}) collective-permute-start(bf16[4,2,64,512]{3,2,0,1:T(8,128)(2,1)S(1)} %pad_maximum_fusion.6), channel_id=1, source_target_pairs={{0,4},{1,5},{2,6},{3,7},{4,0},{5,1},{6,2},{7,3},{8,12},{9,13},{10,... | collective-permute-start | bytes 1572872 | tf_op jit(solution)/shard_map/ppermute | solution.py:36
  26.7 27.1 %collective-permute-start.9 = (bf16[2,2,4,64,512]{4,3,2,1,0:T(8,128)(2,1)S(1)}, bf16[2,2,4,64,512]{4,3,2,1,0:T(8,128)(2,1)}, u32[]{:S(2)}, u32[]{:S(2)}) collective-permute-start(bf16[2,2,4,64,512]{4,3,2,1,0:T(8,128)(2,1)S(1)} %bitcast.156), channel_id=1, source_target_pairs={{0,16},{1,9},{2,18},{3,11},{4,20},{5,13},{6,22},{7,15},{8,24},{9,1... | collective-permute-start | bytes 3145736 | tf_op jit(solution)/shard_map/ppermute | solution.py:789
  38.1 12.0 %collective-permute-start.8 = (bf16[8,64,512]{2,1,0:T(8,128)(2,1)S(1)}, bf16[8,64,512]{2,1,0:T(8,128)(2,1)}, u32[]{:S(2)}, u32[]{:S(2)}) collective-permute-start(bf16[8,64,512]{2,1,0:T(8,128)(2,1)S(1)} %get-tuple-element.315.refs_3_.w0), channel_id=1, source_target_pairs={{0,2},{1,3},{2,0},{3,1},{4,6},{5,7},{6,4},{7,5},{8,10},{9,11},{10,... | collective-permute-start | bytes 1572872 | tf_op jit(solution)/shard_map/ppermute | solution.py:36
  54.5 6.4 %collective-permute-start.11 = (bf16[8,64,512]{2,1,0:T(8,128)(2,1)}, bf16[8,64,512]{2,1,0:T(8,128)(2,1)S(1)}, u32[]{:S(2)}, u32[]{:S(2)}) collective-permute-start(bf16[8,64,512]{2,1,0:T(8,128)(2,1)} %collective-permute-done.8.refs_5_.w2), channel_id=1, source_target_pairs={{0,1},{1,0},{2,3},{3,2},{4,5},{5,4},{6,7},{7,6},{8,9},{9,8},{10,11... | collective-permute-start | bytes 1572872 | tf_op jit(solution)/shard_map/ppermute | solution.py:36
  54.6 26.1 %collective-permute-start.26 = (bf16[2,2,4,64,512]{4,3,2,1,0:T(8,128)(2,1)S(1)}, bf16[2,2,4,64,512]{4,3,2,1,0:T(8,128)(2,1)}, u32[]{:S(2)}, u32[]{:S(2)}) collective-permute-start(bf16[2,2,4,64,512]{4,3,2,1,0:T(8,128)(2,1)S(1)} %bitcast.157), channel_id=1, source_target_pairs={{0,8},{1,17},{2,10},{3,19},{4,12},{5,21},{6,14},{7,23},{8,0},{9,25... | collective-permute-start | bytes 3145736 | tf_op jit(solution)/shard_map/ppermute | solution.py:789
  56.8 14.2 %collective-permute-start.13 = (bf16[2,2,64,512]{3,2,0,1:T(8,128)(2,1)}, bf16[2,2,64,512]{3,2,0,1:T(8,128)(2,1)S(1)}, u32[]{:S(2)}, u32[]{:S(2)}) collective-permute-start(bf16[2,2,64,512]{3,2,0,1:T(8,128)(2,1)} %get-tuple-element.317), channel_id=1, source_target_pairs={{0,2},{1,3},{2,0},{3,1},{4,6},{5,7},{6,4},{7,5},{8,10},{9,11},{10,... | collective-permute-start | bytes 786440 | tf_op jit(solution)/shard_map/ppermute | solution.py:36
  57.6 13.3 %collective-permute-start.15 = (bf16[2,2,64,512]{3,2,0,1:T(8,128)(2,1)}, bf16[2,2,64,512]{3,2,0,1:T(8,128)(2,1)}, u32[]{:S(2)}, u32[]{:S(2)}) collective-permute-start(bf16[2,2,64,512]{3,2,0,1:T(8,128)(2,1)} %get-tuple-element.318), channel_id=1, source_target_pairs={{0,6},{1,7},{2,4},{3,5},{4,2},{5,3},{6,0},{7,1},{8,14},{9,15},{10,... | collective-permute-start | bytes 786440 | tf_op jit(solution)/shard_map/ppermute | solution.py:36
  59.1 13.1 %collective-permute-start.14 = (bf16[2,2,64,512]{3,2,0,1:T(8,128)(2,1)S(1)}, bf16[2,2,64,512]{3,2,0,1:T(8,128)(2,1)S(1)}, u32[]{:S(2)}, u32[]{:S(2)}) collective-permute-start(bf16[2,2,64,512]{3,2,0,1:T(8,128)(2,1)S(1)} %get-tuple-element.319), channel_id=1, source_target_pairs={{0,4},{1,5},{2,6},{3,7},{4,0},{5,1},{6,2},{7,3},{8,12},{9,13},{10,... | collective-permute-start | bytes 786440 | tf_op jit(solution)/shard_map/ppermute | solution.py:36
  60.9 42.3 %collective-permute-start.27 = (bf16[2,2,4,64,512]{4,3,2,1,0:T(8,128)(2,1)}, bf16[2,2,4,64,512]{4,3,2,1,0:T(8,128)(2,1)}, u32[]{:S(2)}, u32[]{:S(2)}) collective-permute-start(bf16[2,2,4,64,512]{4,3,2,1,0:T(8,128)(2,1)} %collective-permute-done.9.refs_14_.refs_16_), channel_id=1, source_target_pairs={{0,8},{1,17},{2,10},{3,19},{4,12},{5,21},{6,14},{7,23},{8,0},{9,25... | collective-permute-start | bytes 3145736 | tf_op jit(solution)/shard_map/ppermute | solution.py:789
  73.4 17.4 %collective-permute-start.24 = (bf16[8,64,512]{2,1,0:T(8,128)(2,1)S(1)}, bf16[8,64,512]{2,1,0:T(8,128)(2,1)S(1)}, u32[]{:S(2)}, u32[]{:S(2)}) collective-permute-start(bf16[8,64,512]{2,1,0:T(8,128)(2,1)S(1)} %get-tuple-element.189.refs_8_.w0), channel_id=1, source_target_pairs={{0,2},{1,3},{2,0},{3,1},{4,6},{5,7},{6,4},{7,5},{8,10},{9,11},{10,... | collective-permute-start | bytes 1572872 | tf_op jit(solution)/shard_map/ppermute | solution.py:36
  74.3 16.5 %collective-permute-start.21 = (bf16[1,200,512]{2,1,0:T(8,128)(2,1)S(1)}, bf16[1,200,512]{2,1,0:T(8,128)(2,1)S(1)}, u32[]{:S(2)}, u32[]{:S(2)}) collective-permute-start(bf16[1,200,512]{2,1,0:T(8,128)(2,1)S(1)} %copy-done.38), channel_id=1, source_target_pairs={{0,6},{1,7},{2,4},{3,5},{4,2},{5,3},{6,0},{7,1},{8,14},{9,15},{10,... | collective-permute-start | bytes 614408 | tf_op jit(solution)/shard_map/ppermute | solution.py:36
  75.8 16.0 %collective-permute-start.19 = (bf16[1,200,512]{2,1,0:T(8,128)(2,1)S(1)}, bf16[1,200,512]{2,1,0:T(8,128)(2,1)S(1)}, u32[]{:S(2)}, u32[]{:S(2)}) collective-permute-start(bf16[1,200,512]{2,1,0:T(8,128)(2,1)S(1)} %copy-done.38), channel_id=1, source_target_pairs={{0,4},{1,5},{2,6},{3,7},{4,0},{5,1},{6,2},{7,3},{8,12},{9,13},{10,... | collective-permute-start | bytes 614408 | tf_op jit(solution)/shard_map/ppermute | solution.py:36
  80.7 24.1 %collective-permute-start.23 = (bf16[8,64,512]{2,1,0:T(8,128)(2,1)S(1)}, bf16[8,64,512]{2,1,0:T(8,128)(2,1)S(1)}, u32[]{:S(2)}, u32[]{:S(2)}) collective-permute-start(bf16[8,64,512]{2,1,0:T(8,128)(2,1)S(1)} %get-tuple-element.189.refs_8_.w0), channel_id=1, source_target_pairs={{0,1},{1,0},{2,3},{3,2},{4,5},{5,4},{6,7},{7,6},{8,9},{9,8},{10,11... | collective-permute-start | bytes 1572872 | tf_op jit(solution)/shard_map/ppermute | solution.py:36
  90.9 14.0 %collective-permute-start.25 = (bf16[8,64,512]{2,1,0:T(8,128)(2,1)S(1)}, bf16[8,64,512]{2,1,0:T(8,128)(2,1)S(1)}, u32[]{:S(2)}, u32[]{:S(2)}) collective-permute-start(bf16[8,64,512]{2,1,0:T(8,128)(2,1)S(1)} %collective-permute-done.24.refs_10_.w2), channel_id=1, source_target_pairs={{0,1},{1,0},{2,3},{3,2},{4,5},{5,4},{6,7},{7,6},{8,9},{9,8},{10,11... | collective-permute-start | bytes 1572872 | tf_op jit(solution)/shard_map/ppermute | solution.py:36
  90.9 7.5 %collective-permute-start.17 = (bf16[1,200,512]{2,1,0:T(8,128)(2,1)S(1)}, bf16[1,200,512]{2,1,0:T(8,128)(2,1)S(1)}, u32[]{:S(2)}, u32[]{:S(2)}) collective-permute-start(bf16[1,200,512]{2,1,0:T(8,128)(2,1)S(1)} %copy-done.38), channel_id=1, source_target_pairs={{0,2},{1,3},{2,0},{3,1},{4,6},{5,7},{6,4},{7,5},{8,10},{9,11},{10,... | collective-permute-start | bytes 614408 | tf_op jit(solution)/shard_map/ppermute | solution.py:36
  91.8 6.6 %collective-permute-start.16 = (bf16[1,200,512]{2,1,0:T(8,128)(2,1)S(1)}, bf16[1,200,512]{2,1,0:T(8,128)(2,1)S(1)}, u32[]{:S(2)}, u32[]{:S(2)}) collective-permute-start(bf16[1,200,512]{2,1,0:T(8,128)(2,1)S(1)} %copy-done.38), channel_id=1, source_target_pairs={{0,1},{1,0},{2,3},{3,2},{4,5},{5,4},{6,7},{7,6},{8,9},{9,8},{10,11... | collective-permute-start | bytes 614408 | tf_op jit(solution)/shard_map/ppermute | solution.py:36
  98.4 6.4 %collective-permute-start.20 = (bf16[1,200,512]{2,1,0:T(8,128)(2,1)S(1)}, bf16[1,200,512]{2,1,0:T(8,128)(2,1)S(1)}, u32[]{:S(2)}, u32[]{:S(2)}) collective-permute-start(bf16[1,200,512]{2,1,0:T(8,128)(2,1)S(1)} %collective-permute-done.19.refs_9_), channel_id=1, source_target_pairs={{0,1},{1,0},{2,3},{3,2},{4,5},{5,4},{6,7},{7,6},{8,9},{9,8},{10,11... | collective-permute-start | bytes 614408 | tf_op jit(solution)/shard_map/ppermute | solution.py:36
  103.2 38.1 %collective-permute-start.32 = (bf16[2,2,4,64,512]{4,3,2,1,0:T(8,128)(2,1)S(1)}, bf16[2,2,4,64,512]{4,3,2,1,0:T(8,128)(2,1)}, u32[]{:S(2)}, u32[]{:S(2)}) collective-permute-start(bf16[2,2,4,64,512]{4,3,2,1,0:T(8,128)(2,1)S(1)} %bitcast.162), channel_id=1, source_target_pairs={{0,16},{1,9},{2,18},{3,11},{4,20},{5,13},{6,22},{7,15},{8,24},{9,1... | collective-permute-start | bytes 3145736 | tf_op jit(solution)/shard_map/ppermute | solution.py:789
  114.9 36.1 %collective-permute-start.35 = (bf16[2,2,4,64,512]{4,3,2,1,0:T(8,128)(2,1)S(1)}, bf16[2,2,4,64,512]{4,3,2,1,0:T(8,128)(2,1)S(1)}, u32[]{:S(2)}, u32[]{:S(2)}) collective-permute-start(bf16[2,2,4,64,512]{4,3,2,1,0:T(8,128)(2,1)S(1)} %bitcast.163), channel_id=1, source_target_pairs={{0,8},{1,17},{2,10},{3,19},{4,12},{5,21},{6,14},{7,23},{8,0},{9,25... | collective-permute-start | bytes 3145736 | tf_op jit(solution)/shard_map/ppermute | solution.py:789
  120.6 7.3 %collective-permute-start.29 = (bf16[200,512]{1,0:T(8,128)(2,1)}, bf16[200,512]{1,0:T(8,128)(2,1)S(1)}, u32[]{:S(2)}, u32[]{:S(2)}) collective-permute-start(bf16[200,512]{1,0:T(8,128)(2,1)} %get-tuple-element.186), channel_id=1, source_target_pairs={{0,2},{1,3},{2,0},{3,1},{4,6},{5,7},{6,4},{7,5},{8,10},{9,11},{10,... | collective-permute-start | bytes 614408 | tf_op jit(solution)/shard_map/ppermute | solution.py:36
  122.1 8.2 %collective-permute-start.30 = (bf16[200,512]{1,0:T(8,128)(2,1)}, bf16[200,512]{1,0:T(8,128)(2,1)S(1)}, u32[]{:S(2)}, u32[]{:S(2)}) collective-permute-start(bf16[200,512]{1,0:T(8,128)(2,1)} %get-tuple-element.187), channel_id=1, source_target_pairs={{0,4},{1,5},{2,6},{3,7},{4,0},{5,1},{6,2},{7,3},{8,12},{9,13},{10,... | collective-permute-start | bytes 614408 | tf_op jit(solution)/shard_map/ppermute | solution.py:36
  122.7 10.9 %collective-permute-start.31 = (bf16[200,512]{1,0:T(8,128)(2,1)}, bf16[200,512]{1,0:T(8,128)(2,1)S(1)}, u32[]{:S(2)}, u32[]{:S(2)}) collective-permute-start(bf16[200,512]{1,0:T(8,128)(2,1)} %get-tuple-element.188), channel_id=1, source_target_pairs={{0,6},{1,7},{2,4},{3,5},{4,2},{5,3},{6,0},{7,1},{8,14},{9,15},{10,... | collective-permute-start | bytes 614408 | tf_op jit(solution)/shard_map/ppermute | solution.py:36
  141.3 30.9 %collective-permute-start.41 = (bf16[2,2,4,64,512]{4,3,2,1,0:T(8,128)(2,1)}, bf16[2,2,4,64,512]{4,3,2,1,0:T(8,128)(2,1)}, u32[]{:S(2)}, u32[]{:S(2)}) collective-permute-start(bf16[2,2,4,64,512]{4,3,2,1,0:T(8,128)(2,1)} %collective-permute-done.32.refs_14_), channel_id=1, source_target_pairs={{0,8},{1,17},{2,10},{3,19},{4,12},{5,21},{6,14},{7,23},{8,0},{9,25... | collective-permute-start | bytes 3145736 | tf_op jit(solution)/shard_map/ppermute | solution.py:789
  144.5 13.5 %collective-permute-start.39 = (bf16[2,200,512]{2,1,0:T(8,128)(2,1)}, bf16[2,200,512]{2,1,0:T(8,128)(2,1)S(1)}, u32[]{:S(2)}, u32[]{:S(2)}) collective-permute-start(bf16[2,200,512]{2,1,0:T(8,128)(2,1)} %get-tuple-element.196.refs_5_), channel_id=1, source_target_pairs={{0,6},{1,7},{2,4},{3,5},{4,2},{5,3},{6,0},{7,1},{8,14},{9,15},{10,... | collective-permute-start | bytes 1228808 | tf_op jit(solution)/shard_map/ppermute | solution.py:36
  146.0 17.7 %collective-permute-start.37 = (bf16[2,200,512]{2,1,0:T(8,128)(2,1)}, bf16[2,200,512]{2,1,0:T(8,128)(2,1)S(1)}, u32[]{:S(2)}, u32[]{:S(2)}) collective-permute-start(bf16[2,200,512]{2,1,0:T(8,128)(2,1)} %get-tuple-element.196.refs_5_), channel_id=1, source_target_pairs={{0,4},{1,5},{2,6},{3,7},{4,0},{5,1},{6,2},{7,3},{8,12},{9,13},{10,... | collective-permute-start | bytes 1228808 | tf_op jit(solution)/shard_map/ppermute | solution.py:36
  147.5 16.2 %collective-permute-start.34 = (bf16[2,200,512]{2,1,0:T(8,128)(2,1)}, bf16[2,200,512]{2,1,0:T(8,128)(2,1)S(1)}, u32[]{:S(2)}, u32[]{:S(2)}) collective-permute-start(bf16[2,200,512]{2,1,0:T(8,128)(2,1)} %get-tuple-element.196.refs_5_), channel_id=1, source_target_pairs={{0,2},{1,3},{2,0},{3,1},{4,6},{5,7},{6,4},{7,5},{8,10},{9,11},{10,... | collective-permute-start | bytes 1228808 | tf_op jit(solution)/shard_map/ppermute | solution.py:36
  150.9 13.3 %collective-permute-start.33 = (bf16[2,200,512]{2,1,0:T(8,128)(2,1)}, bf16[2,200,512]{2,1,0:T(8,128)(2,1)S(1)}, u32[]{:S(2)}, u32[]{:S(2)}) collective-permute-start(bf16[2,200,512]{2,1,0:T(8,128)(2,1)} %get-tuple-element.196.refs_5_), channel_id=1, source_target_pairs={{0,1},{1,0},{2,3},{3,2},{4,5},{5,4},{6,7},{7,6},{8,9},{9,8},{10,11... | collective-permute-start | bytes 1228808 | tf_op jit(solution)/shard_map/ppermute | solution.py:36
  189.0 48.6 %collective-permute-start.53 = (bf16[2,2,2,4,64,512]{5,4,3,2,1,0:T(8,128)(2,1)}, bf16[2,2,2,4,64,512]{5,4,3,2,1,0:T(8,128)(2,1)S(1)}, u32[]{:S(2)}, u32[]{:S(2)}) collective-permute-start(bf16[2,2,2,4,64,512]{5,4,3,2,1,0:T(8,128)(2,1)} %get-tuple-element.212), channel_id=1, source_target_pairs={{0,8},{1,17},{2,10},{3,19},{4,12},{5,21},{6,14},{7,23},{8,0},{9,25... | collective-permute-start | bytes 6291464 | tf_op jit(solution)/shard_map/ppermute | solution.py:789
  197.3 7.6 %collective-permute-start.43 = (bf16[200,512]{1,0:T(8,128)(2,1)}, bf16[200,512]{1,0:T(8,128)(2,1)S(1)}, u32[]{:S(2)}, u32[]{:S(2)}) collective-permute-start(bf16[200,512]{1,0:T(8,128)(2,1)} %get-tuple-element.203), channel_id=1, source_target_pairs={{0,2},{1,3},{2,0},{3,1},{4,6},{5,7},{6,4},{7,5},{8,10},{9,11},{10,... | collective-permute-start | bytes 614408 | tf_op jit(solution)/shard_map/ppermute | solution.py:36
  198.6 8.2 %collective-permute-start.44 = (bf16[200,512]{1,0:T(8,128)(2,1)}, bf16[200,512]{1,0:T(8,128)(2,1)S(1)}, u32[]{:S(2)}, u32[]{:S(2)}) collective-permute-start(bf16[200,512]{1,0:T(8,128)(2,1)} %get-tuple-element.204), channel_id=1, source_target_pairs={{0,4},{1,5},{2,6},{3,7},{4,0},{5,1},{6,2},{7,3},{8,12},{9,13},{10,... | collective-permute-start | bytes 614408 | tf_op jit(solution)/shard_map/ppermute | solution.py:36
  199.7 10.8 %collective-permute-start.45 = (bf16[200,512]{1,0:T(8,128)(2,1)}, bf16[200,512]{1,0:T(8,128)(2,1)S(1)}, u32[]{:S(2)}, u32[]{:S(2)}) collective-permute-start(bf16[200,512]{1,0:T(8,128)(2,1)} %get-tuple-element.205), channel_id=1, source_target_pairs={{0,6},{1,7},{2,4},{3,5},{4,2},{5,3},{6,0},{7,1},{8,14},{9,15},{10,... | collective-permute-start | bytes 614408 | tf_op jit(solution)/shard_map/ppermute | solution.py:36
  222.0 13.2 %collective-permute-start.54 = (bf16[8,64,512]{2,1,0:T(8,128)(2,1)}, bf16[8,64,512]{2,1,0:T(8,128)(2,1)S(1)}, u32[]{:S(2)}, u32[]{:S(2)}) collective-permute-start(bf16[8,64,512]{2,1,0:T(8,128)(2,1)} %get-tuple-element.214), channel_id=1, source_target_pairs={{0,1},{1,0},{2,3},{3,2},{4,5},{5,4},{6,7},{7,6},{8,9},{9,8},{10,11... | collective-permute-start | bytes 1572872 | tf_op jit(solution)/shard_map/ppermute | solution.py:36
  222.0 9.1 %collective-permute-start.51 = (bf16[1,200,512]{2,1,0:T(8,128)(2,1)}, bf16[1,200,512]{2,1,0:T(8,128)(2,1)S(1)}, u32[]{:S(2)}, u32[]{:S(2)}) collective-permute-start(bf16[1,200,512]{2,1,0:T(8,128)(2,1)} %bitcast.192), channel_id=1, source_target_pairs={{0,6},{1,7},{2,4},{3,5},{4,2},{5,3},{6,0},{7,1},{8,14},{9,15},{10,... | collective-permute-start | bytes 614408 | tf_op jit(solution)/shard_map/ppermute | solution.py:36
  223.9 10.8 %collective-permute-start.49 = (bf16[1,200,512]{2,1,0:T(8,128)(2,1)}, bf16[1,200,512]{2,1,0:T(8,128)(2,1)S(1)}, u32[]{:S(2)}, u32[]{:S(2)}) collective-permute-start(bf16[1,200,512]{2,1,0:T(8,128)(2,1)} %bitcast.193), channel_id=1, source_target_pairs={{0,4},{1,5},{2,6},{3,7},{4,0},{5,1},{6,2},{7,3},{8,12},{9,13},{10,... | collective-permute-start | bytes 614408 | tf_op jit(solution)/shard_map/ppermute | solution.py:36
  224.6 10.4 %collective-permute-start.47 = (bf16[1,200,512]{2,1,0:T(8,128)(2,1)}, bf16[1,200,512]{2,1,0:T(8,128)(2,1)S(1)}, u32[]{:S(2)}, u32[]{:S(2)}) collective-permute-start(bf16[1,200,512]{2,1,0:T(8,128)(2,1)} %bitcast.194), channel_id=1, source_target_pairs={{0,2},{1,3},{2,0},{3,1},{4,6},{5,7},{6,4},{7,5},{8,10},{9,11},{10,... | collective-permute-start | bytes 614408 | tf_op jit(solution)/shard_map/ppermute | solution.py:36
  237.6 20.8 %collective-permute-start.55 = (bf16[8,64,512]{2,1,0:T(8,128)(2,1)S(1)}, bf16[8,64,512]{2,1,0:T(8,128)(2,1)}, u32[]{:S(2)}, u32[]{:S(2)}) collective-permute-start(bf16[8,64,512]{2,1,0:T(8,128)(2,1)S(1)} %add.101), channel_id=1, source_target_pairs={{0,2},{1,3},{2,0},{3,1},{4,6},{5,7},{6,4},{7,5},{8,10},{9,11},{10,... | collective-permute-start | bytes 1572872 | tf_op jit(solution)/shard_map/ppermute | solution.py:36
  240.5 35.0 %collective-permute-start.60 = (bf16[2,2,4,64,512]{4,3,2,1,0:T(8,128)(2,1)}, bf16[2,2,4,64,512]{4,3,2,1,0:T(8,128)(2,1)S(1)}, u32[]{:S(2)}, u32[]{:S(2)}) collective-permute-start(bf16[2,2,4,64,512]{4,3,2,1,0:T(8,128)(2,1)} %bitcast_add_fusion.3), channel_id=1, source_target_pairs={{0,16},{1,9},{2,18},{3,11},{4,20},{5,13},{6,22},{7,15},{8,24},{9,1... | collective-permute-start | bytes 3145736 | tf_op jit(solution)/shard_map/ppermute | solution.py:789
  258.5 52.8 %collective-permute-start.71 = (bf16[2,2,2,4,64,512]{5,4,3,2,1,0:T(8,128)(2,1)}, bf16[2,2,2,4,64,512]{5,4,3,2,1,0:T(8,128)(2,1)S(1)}, u32[]{:S(2)}, u32[]{:S(2)}) collective-permute-start(bf16[2,2,2,4,64,512]{5,4,3,2,1,0:T(8,128)(2,1)} %get-tuple-element.263), channel_id=1, source_target_pairs={{0,8},{1,17},{2,10},{3,19},{4,12},{5,21},{6,14},{7,23},{8,0},{9,25... | collective-permute-start | bytes 6291464 | tf_op jit(solution)/shard_map/ppermute | solution.py:789
  263.5 12.0 %collective-permute-start.59 = (bf16[200,512]{1,0:T(8,128)(2,1)}, bf16[200,512]{1,0:T(8,128)(2,1)S(1)}, u32[]{:S(2)}, u32[]{:S(2)}) collective-permute-start(bf16[200,512]{1,0:T(8,128)(2,1)} %get-tuple-element.233), channel_id=1, source_target_pairs={{0,6},{1,7},{2,4},{3,5},{4,2},{5,3},{6,0},{7,1},{8,14},{9,15},{10,... | collective-permute-start | bytes 614408 | tf_op jit(solution)/shard_map/ppermute | solution.py:36
  264.0 11.5 %collective-permute-start.57 = (bf16[200,512]{1,0:T(8,128)(2,1)}, bf16[200,512]{1,0:T(8,128)(2,1)S(1)}, u32[]{:S(2)}, u32[]{:S(2)}) collective-permute-start(bf16[200,512]{1,0:T(8,128)(2,1)} %get-tuple-element.231), channel_id=1, source_target_pairs={{0,2},{1,3},{2,0},{3,1},{4,6},{5,7},{6,4},{7,5},{8,10},{9,11},{10,... | collective-permute-start | bytes 614408 | tf_op jit(solution)/shard_map/ppermute | solution.py:36
  265.5 10.0 %collective-permute-start.58 = (bf16[200,512]{1,0:T(8,128)(2,1)}, bf16[200,512]{1,0:T(8,128)(2,1)S(1)}, u32[]{:S(2)}, u32[]{:S(2)}) collective-permute-start(bf16[200,512]{1,0:T(8,128)(2,1)} %get-tuple-element.232), channel_id=1, source_target_pairs={{0,4},{1,5},{2,6},{3,7},{4,0},{5,1},{6,2},{7,3},{8,12},{9,13},{10,... | collective-permute-start | bytes 614408 | tf_op jit(solution)/shard_map/ppermute | solution.py:36
  275.5 14.4 %collective-permute-start.63 = (bf16[8,64,512]{2,1,0:T(8,128)(2,1)}, bf16[8,64,512]{2,1,0:T(8,128)(2,1)S(1)}, u32[]{:S(2)}, u32[]{:S(2)}) collective-permute-start(bf16[8,64,512]{2,1,0:T(8,128)(2,1)} %get-tuple-element.242), channel_id=1, source_target_pairs={{0,1},{1,0},{2,3},{3,2},{4,5},{5,4},{6,7},{7,6},{8,9},{9,8},{10,11... | collective-permute-start | bytes 1572872 | tf_op jit(solution)/shard_map/ppermute | solution.py:36
  294.4 17.0 %collective-permute-start.70 = (bf16[2,2,64,512]{3,2,1,0:T(8,128)(2,1)}, bf16[2,2,64,512]{3,2,1,0:T(8,128)(2,1)S(1)}, u32[]{:S(2)}, u32[]{:S(2)}) collective-permute-start(bf16[2,2,64,512]{3,2,1,0:T(8,128)(2,1)} %get-tuple-element.308), channel_id=1, source_target_pairs={{0,6},{1,7},{2,4},{3,5},{4,2},{5,3},{6,0},{7,1},{8,14},{9,15},{10,... | collective-permute-start | bytes 786440 | tf_op jit(solution)/shard_map/ppermute | solution.py:36
  295.0 16.4 %collective-permute-start.68 = (bf16[2,2,64,512]{3,2,1,0:T(8,128)(2,1)}, bf16[2,2,64,512]{3,2,1,0:T(8,128)(2,1)}, u32[]{:S(2)}, u32[]{:S(2)}) collective-permute-start(bf16[2,2,64,512]{3,2,1,0:T(8,128)(2,1)} %get-tuple-element.310), channel_id=1, source_target_pairs={{0,2},{1,3},{2,0},{3,1},{4,6},{5,7},{6,4},{7,5},{8,10},{9,11},{10,... | collective-permute-start | bytes 786440 | tf_op jit(solution)/shard_map/ppermute | solution.py:36
  296.5 14.9 %collective-permute-start.69 = (bf16[2,2,64,512]{3,2,1,0:T(8,128)(2,1)}, bf16[2,2,64,512]{3,2,1,0:T(8,128)(2,1)}, u32[]{:S(2)}, u32[]{:S(2)}) collective-permute-start(bf16[2,2,64,512]{3,2,1,0:T(8,128)(2,1)} %get-tuple-element.311), channel_id=1, source_target_pairs={{0,4},{1,5},{2,6},{3,7},{4,0},{5,1},{6,2},{7,3},{8,12},{9,13},{10,... | collective-permute-start | bytes 786440 | tf_op jit(solution)/shard_map/ppermute | solution.py:36
  299.3 20.7 %collective-permute-start.64 = (bf16[8,64,512]{2,1,0:T(8,128)(2,1)S(1)}, bf16[8,64,512]{2,1,0:T(8,128)(2,1)S(1)}, u32[]{:S(2)}, u32[]{:S(2)}) collective-permute-start(bf16[8,64,512]{2,1,0:T(8,128)(2,1)S(1)} %add.106), channel_id=1, source_target_pairs={{0,2},{1,3},{2,0},{3,1},{4,6},{5,7},{6,4},{7,5},{8,10},{9,11},{10,... | collective-permute-start | bytes 1572872 | tf_op jit(solution)/shard_map/ppermute | solution.py:36
  311.4 14.8 %collective-permute-start.76 = (bf16[4,200,512]{2,1,0:T(8,128)(2,1)}, bf16[4,200,512]{2,1,0:T(8,128)(2,1)}, u32[]{:S(2)}, u32[]{:S(2)}) collective-permute-start(bf16[4,200,512]{2,1,0:T(8,128)(2,1)} %get-tuple-element.281), channel_id=1, source_target_pairs={{0,1},{1,0},{2,3},{3,2},{4,5},{5,4},{6,7},{7,6},{8,9},{9,8},{10,11... | collective-permute-start | bytes 2457608 | tf_op jit(solution)/shard_map/ppermute | solution.py:36
  314.2 27.2 %collective-permute-start.75 = (bf16[2,2,4,64,512]{4,3,2,1,0:T(8,128)(2,1)}, bf16[2,2,4,64,512]{4,3,2,1,0:T(8,128)(2,1)}, u32[]{:S(2)}, u32[]{:S(2)}) collective-permute-start(bf16[2,2,4,64,512]{4,3,2,1,0:T(8,128)(2,1)} %bitcast_add_fusion.1), channel_id=1, source_target_pairs={{0,16},{1,9},{2,18},{3,11},{4,20},{5,13},{6,22},{7,15},{8,24},{9,1... | collective-permute-start | bytes 3145736 | tf_op jit(solution)/shard_map/ppermute | solution.py:789
  315.5 9.2 %collective-permute-start.66 = (bf16[4,64,512]{2,1,0:T(8,128)(2,1)S(1)}, bf16[4,64,512]{2,1,0:T(8,128)(2,1)S(1)}, u32[]{:S(2)}, u32[]{:S(2)}) collective-permute-start(bf16[4,64,512]{2,1,0:T(8,128)(2,1)S(1)} %slice.239), channel_id=1, source_target_pairs={{0,4},{1,5},{2,6},{3,7},{4,0},{5,1},{6,2},{7,3},{8,12},{9,13},{10,... | collective-permute-start | bytes 786440 | tf_op jit(solution)/shard_map/ppermute | solution.py:36
  320.2 10.2 %collective-permute-start.65 = (bf16[4,64,512]{2,1,0:T(8,128)(2,1)S(1)}, bf16[4,64,512]{2,1,0:T(8,128)(2,1)S(1)}, u32[]{:S(2)}, u32[]{:S(2)}) collective-permute-start(bf16[4,64,512]{2,1,0:T(8,128)(2,1)S(1)} %slice.237), channel_id=1, source_target_pairs={{0,4},{1,5},{2,6},{3,7},{4,0},{5,1},{6,2},{7,3},{8,12},{9,13},{10,... | collective-permute-start | bytes 786440 | tf_op jit(solution)/shard_map/ppermute | solution.py:36
  324.8 7.2 %collective-permute-start.73 = (f32[20,512]{1,0:T(8,128)S(1)}, f32[20,512]{1,0:T(8,128)S(1)}, u32[]{:S(2)}, u32[]{:S(2)}) collective-permute-start(f32[20,512]{1,0:T(8,128)S(1)} %add.112), channel_id=1, source_target_pairs={{0,4},{1,5},{2,6},{3,7},{4,0},{5,1},{6,2},{7,3},{8,12},{9,13},{10,... | collective-permute-start | bytes 122888 | tf_op jit(solution)/shard_map/ppermute | solution.py:36
  328.5 8.6 %collective-permute-start.77 = (bf16[200,512]{1,0:T(8,128)(2,1)}, bf16[200,512]{1,0:T(8,128)(2,1)S(1)}, u32[]{:S(2)}, u32[]{:S(2)}) collective-permute-start(bf16[200,512]{1,0:T(8,128)(2,1)} %get-tuple-element.283), channel_id=1, source_target_pairs={{0,2},{1,3},{2,0},{3,1},{4,6},{5,7},{6,4},{7,5},{8,10},{9,11},{10,... | collective-permute-start | bytes 614408 | tf_op jit(solution)/shard_map/ppermute | solution.py:36
  329.4 8.2 %collective-permute-start.78 = (bf16[200,512]{1,0:T(8,128)(2,1)}, bf16[200,512]{1,0:T(8,128)(2,1)S(1)}, u32[]{:S(2)}, u32[]{:S(2)}) collective-permute-start(bf16[200,512]{1,0:T(8,128)(2,1)} %get-tuple-element.284), channel_id=1, source_target_pairs={{0,4},{1,5},{2,6},{3,7},{4,0},{5,1},{6,2},{7,3},{8,12},{9,13},{10,... | collective-permute-start | bytes 614408 | tf_op jit(solution)/shard_map/ppermute | solution.py:36
  330.4 9.9 %collective-permute-start.79 = (bf16[200,512]{1,0:T(8,128)(2,1)}, bf16[200,512]{1,0:T(8,128)(2,1)S(1)}, u32[]{:S(2)}, u32[]{:S(2)}) collective-permute-start(bf16[200,512]{1,0:T(8,128)(2,1)} %get-tuple-element.285), channel_id=1, source_target_pairs={{0,6},{1,7},{2,4},{3,5},{4,2},{5,3},{6,0},{7,1},{8,14},{9,15},{10,... | collective-permute-start | bytes 614408 | tf_op jit(solution)/shard_map/ppermute | solution.py:36
  345.6 10.5 %collective-permute-start.83 = (bf16[2,2,64,512]{3,2,0,1:T(8,128)(2,1)S(1)}, bf16[2,2,64,512]{3,2,0,1:T(8,128)(2,1)S(1)}, u32[]{:S(2)}, u32[]{:S(2)}) collective-permute-start(bf16[2,2,64,512]{3,2,0,1:T(8,128)(2,1)S(1)} %slice.207), channel_id=1, source_target_pairs={{0,8},{1,9},{2,10},{3,11},{4,12},{5,13},{6,14},{7,15},{8,0},{9,1},... | collective-permute-start | bytes 786440 | tf_op jit(solution)/shard_map/ppermute | solution.py:36
  351.0 10.2 %collective-permute-start.87 = (bf16[2,2,64,512]{3,2,1,0:T(8,128)(2,1)S(1)}, bf16[2,2,64,512]{3,2,1,0:T(8,128)(2,1)S(1)}, u32[]{:S(2)}, u32[]{:S(2)}) collective-permute-start(bf16[2,2,64,512]{3,2,1,0:T(8,128)(2,1)S(1)} %get-tuple-element.302), channel_id=1, source_target_pairs={{0,6},{1,7},{2,4},{3,5},{4,2},{5,3},{6,0},{7,1},{8,14},{9,15},{10,... | collective-permute-start | bytes 786440 | tf_op jit(solution)/shard_map/ppermute | solution.py:36
  352.5 11.5 %collective-permute-start.86 = (bf16[2,2,64,512]{3,2,1,0:T(8,128)(2,1)S(1)}, bf16[2,2,64,512]{3,2,1,0:T(8,128)(2,1)S(1)}, u32[]{:S(2)}, u32[]{:S(2)}) collective-permute-start(bf16[2,2,64,512]{3,2,1,0:T(8,128)(2,1)S(1)} %get-tuple-element.303), channel_id=1, source_target_pairs={{0,4},{1,5},{2,6},{3,7},{4,0},{5,1},{6,2},{7,3},{8,12},{9,13},{10,... | collective-permute-start | bytes 786440 | tf_op jit(solution)/shard_map/ppermute | solution.py:36
  353.4 10.8 %collective-permute-start.85 = (bf16[2,2,64,512]{3,2,1,0:T(8,128)(2,1)S(1)}, bf16[2,2,64,512]{3,2,1,0:T(8,128)(2,1)S(1)}, u32[]{:S(2)}, u32[]{:S(2)}) collective-permute-start(bf16[2,2,64,512]{3,2,1,0:T(8,128)(2,1)S(1)} %get-tuple-element.304), channel_id=1, source_target_pairs={{0,2},{1,3},{2,0},{3,1},{4,6},{5,7},{6,4},{7,5},{8,10},{9,11},{10,... | collective-permute-start | bytes 786440 | tf_op jit(solution)/shard_map/ppermute | solution.py:36
  356.1 11.5 %collective-permute-start.84 = (bf16[1,2,64,512]{3,2,0,1:T(8,128)(2,1)S(1)}, bf16[1,2,64,512]{3,2,0,1:T(8,128)(2,1)S(1)}, u32[]{:S(2)}, u32[]{:S(2)}) collective-permute-start(bf16[1,2,64,512]{3,2,0,1:T(8,128)(2,1)S(1)} %slice.253), channel_id=1, source_target_pairs={{0,16},{1,17},{2,18},{3,19},{4,20},{5,21},{6,22},{7,23},{8,24},{9,... | collective-permute-start | bytes 393224 | tf_op jit(solution)/shard_map/ppermute | solution.py:36
  (97 other events, 628.6 us)

commit v8 on v7

--- a/solution.py
+++ b/solution.py
@@ -454,7 +454,7 @@
     tokens = take(plan.token_arrays)
     sent_in, y_in = take(2) if not forward else (None, None)
     sources = take(plan.weight_arrays)
-    parts = take(2) if forward else None
+    parts = take(1 if backward else 2) if forward else None
     sent_out, y_out = take(2) if forward and not backward else (None, None)
     if backward:
         back_parts = take(2)
@@ -586,8 +586,10 @@
         back_buf[...] += dot(first, router[plan.layer]) + dot(second, router[plan.layer])
         scatter(back_buf[...].astype(bf16), back_parts)
     if forward:
-        scatter((gate * expert_y).astype(bf16), parts)
-        if not backward:
+        if backward:
+            parts[0][...] = (gate * expert_y).astype(bf16)
+        else:
+            scatter((gate * expert_y).astype(bf16), parts)
             sent_out[...] = sent
             y_out[...] = expert_y
     if backward:
@@ -597,6 +599,33 @@
             for which in (0, 1):
                 for copy in stores(c, which):
                     copy.wait()
+
+
+def place_kernel(layer, mine, theirs, rows, even, odd, tables):
+    tables[0] = mine[layer]
+    tables[1] = theirs[layer]
+
+    @pl.loop(0, 2)
+    def _(g):
+        slot = lax.broadcasted_iota(jnp.int32, (SLOTS, ROWS), 0)
+        group = rows[pl.ds(pl.multiple_of(g * SLOTS, SLOTS), SLOTS)]
+        for t in range(4):
+            hot = (tables[g, t : t + 1, :][:, :ROWS] == slot).astype(f32).astype(bf16)
+            (even, odd)[t % 2][g * 2 + t // 2] = t_dot(hot, group).astype(bf16)
+
+
+def place_rows(layer, tables, rows):
+    part = jax.ShapeDtypeStruct((4, ROWS, rows.shape[1]), bf16)
+    return pl.pallas_call(
+        lambda *refs: place_kernel(layer, *refs),
+        out_shape=(part, part),
+        in_specs=[vmem()] * 3,
+        out_specs=(vmem(), vmem()),
+        scratch_shapes=[pltpu.VMEM((2, 4, LANES), jnp.int32)],
+        compiler_params=params(),
+        cost_estimate=pl.CostEstimate(flops=1, transcendentals=0, bytes_accessed=1),
+        name="place_rows",
+    )(*tables, rows)
 
 
 class Plan:
@@ -625,7 +654,7 @@
     in_specs += [hbm()] * len(weights)
     out_shape, out_specs = [], []
     if forward:
-        out_shape += [token_part] * 2
+        out_shape += [shape((slots, width), bf16)] if backward else [token_part] * 2
     if forward and not backward:
         out_shape += [shape((slots, width), bf16), shape((slots, width), f32)]
     if backward:
@@ -712,8 +741,8 @@
             result = expert_layer(
                 plan, expert_off, me, tables, routers, images + grads, None, expert_w[l]
             )
-            tail = send_rows(place, pair_rows(place, result[:2]))
-            result = result[2:]
+            tail = send_rows(place, pair_rows(place, place_rows(l, tables, result[0])))
+            result = result[1:]
             outputs = hidden_mid[l] + sum(p.astype(f32) for p in tail)
         else:
             plan = Plan(l, block, here, None, *at, None, None, None)
@@ -921,7 +950,7 @@
         Plan(1, block, first, second, *parts, grad_shapes, *grad_parts),
         expert_off, me, tables, routers, images, None, [own1, a1, b1, c1],
     )
-    out_rows, back_rows, router1, (own, a, bc) = result[:2], result[2:4], result[4], result[5:]
+    out_rows, back_rows, router1, (own, a, bc) = result[0], result[1:3], result[3], result[4:]
     bc = mixed(place, bc, NEAR, FAR)
     pieces = send_rows(place, pair_rows(place, back_rows))
     grad1, branch, gains1, *parts1 = attention_backward(
@@ -946,9 +975,11 @@
     grad0, unused, gains0, *parts0 = attention_backward(
         attn_off, grad1, pieces, hidden_in0, hidden_mid0, norm_gains[0], weights0, qkv0, ctx0, LEN
     )
-    gains0, a0, a, bc, own, *out_rows = tie(gains0, a0, a, bc, own, *out_rows)
+    gains0, a0, a, bc, own, out_rows = tie(gains0, a0, a, bc, own, out_rows)
+    out_rows = place_rows(1, tables, out_rows)
     gains, router = jnp.stack([gains0, gains1]), jnp.stack([router0, router1])
     small = jnp.concatenate([gains.reshape(-1), router.reshape(-1)]).reshape(-1, 512)
+    small = jnp.pad(small, ((0, -small.shape[0] % 8), (0, 0)))
     recv = [swap(v, CORE) for v in (parts0[3], parts0[1], parts1[1])]
     *recv, sum1, parts0[0], parts0[2], parts1[0] = tie(
         *recv, own + bc[0] + a, parts0[0], parts0[2], parts1[0]
@@ -972,12 +1003,16 @@
     pair0 = chip_pairs(place, sum0.reshape((2, -1) + sum0.shape[3:]))
     pair0, attn_sum, small = tie(pair0, attn_sum, small)
     sum0 = send_sums(place, pair0)
+    shape = attn_sum.shape
+    attn_sum = attn_sum.reshape(-1, shape[-1])
     for mask in (NEAR, FAR):
-        attn_sum = halve(place, attn_sum, mask)
-        small = small + swap(small, mask)
+        keep, count = attn_sum.shape[0] // 2, small.shape[0]
+        got = swap(jnp.concatenate([attn_sum[keep:], *split(small)]), mask)
+        attn_sum = attn_sum[:keep] + got[:keep]
+        small = small + got[keep : keep + count].astype(f32) + got[keep + count :].astype(f32)
     in_grads, out_grads = unpack_sums(me, sum0, 0, LAYERS, grads1)
     small = small.reshape(-1)
-    gains, router = small[: gains.size].reshape(gains.shape), small[gains.size :].reshape(router.shape)
+    gains, router = small[: gains.size].reshape(gains.shape), small[gains.size : gains.size + router.size].reshape(router.shape)
     attn = attn_sum.astype(f32).reshape(2, rows, 4, -1)
     return (
         outputs[:LEN].astype(bf16),

time: 370 us -> 369 us (level)
  starting transfers between devices: 84.5 us -> 79.8 us
    ppermute x78 -> x76, starting transfers between devices: 68 us -> 63.3 us  [swap(): return lax.ppermute(value, AXES, pairs)]
    ppermute x78 -> x76, waiting for transfers between devices: 112 us -> 114 us  [swap(): return lax.ppermute(value, AXES, pairs)]
  transfers between devices with their start and end apart: 88 -> 86, of which waited for: 50 -> 49; matrix products, arithmetic and copies ran while one was open for 6% -> 6% of each run, Pallas kernels for 20% -> 21%
where the time goes in v8:
time: 369 us; the launch traced here: 368 us
  waiting for transfers between devices  154 us (42%)
  Pallas kernels  93.9 us (25%)
  starting transfers between devices  79.8 us (22%)
  local copies, waits for them, and re-layouts  20.4 us (6%)
  other arithmetic  17.8 us (5%)
    ppermute x76, waiting for transfers between devices, swap(): return lax.ppermute(value, AXES, pairs)  114 us
    ppermute x76, starting transfers between devices, swap(): return lax.ppermute(value, AXES, pairs)  63.3 us
    ppermute x10, waiting for transfers between devices, mixed(): return lax.ppermute(value, AXES, pairs)  39.8 us
    pallas_call x3, Pallas kernels, expert_layer(): pl.pallas_call(lambda *refs: expert_kernel(plan, *refs), out_shape=tuple(...  39.2 us
    pallas_call x2, Pallas kernels, attention_backward(): pl.pallas_call(attention_backward_kernel, out_shape=(shape((out_rows, wid...  21.8 us
    ppermute x10, starting transfers between devices, mixed(): return lax.ppermute(value, AXES, pairs)  16.5 us
    pallas_call x2, Pallas kernels, attention_forward(): pl.pallas_call(lambda *refs: attention_forward_kernel(len(pieces), len(ex...  12.9 us
    pallas_call x4, Pallas kernels, pair_rows(): pl.pallas_call(add_kernel, out_shape=(jax.ShapeDtypeStruct(even.shape[1:]...  9.28 us
  transfers between devices with their start and end apart: 86, of which 49 were waited for; matrix products, arithmetic and copies ran while one was open for 6% of the time, Pallas kernels for 21%

profile of v8, /device:TPU:0, one launch (start us, length us, event | category | flops | bytes accessed | tf_op | source)
XLA Modules:
  0.0 367.8 jit_solution(15852851952270858832)
XLA Ops:
  5.8 4.0 %collective-permute-start.1 = (bf16[1,2,64,512]{3,2,0,1:T(8,128)(2,1)S(1)}, bf16[1,2,64,512]{3,2,0,1:T(8,128)(2,1)S(1)}, u32[]{:S(2)}, u32[]{:S(2)}) collective-permute-start(bf16[1,2,64,512]{3,2,0,1:T(8,128)(2,1)S(1)} %maximum_bitcast_fusion), channel_id=1, source_target_pairs={{0,16},{1,17},{2,18},{3,19},{4,20},{5,21},{6,22},{7,23},{8,24},{9,... | collective-permute-start | bytes 393224 | tf_op jit(solution)/shard_map/ppermute | solution.py:36
  13.5 3.0 collective-permute-done.1
  17.3 1.9 collective-permute-done.4
  19.2 5.7 %collective-permute-done.3 = bf16[2,2,64,512]{3,2,0,1:T(8,128)(2,1)S(1)} collective-permute-done((bf16[2,2,64,512]{3,2,0,1:T(8,128)(2,1)S(1)}, bf16[2,2,64,512]{3,2,0,1:T(8,128)(2,1)S(1)}, u32[]{:S(2)}, u32[]{:S(2)}) %collective-permute-start.3) | collective-permute-done | bytes 262176 | tf_op jit(solution)/shard_map/ppermute | solution.py:36
  26.7 2.3 collective-permute-start.9
  29.0 8.9 %collective-permute-done.6 = bf16[4,2,64,512]{3,2,0,1:T(8,128)(2,1)S(1)} collective-permute-done((bf16[4,2,64,512]{3,2,0,1:T(8,128)(2,1)S(1)}, bf16[4,2,64,512]{3,2,0,1:T(8,128)(2,1)S(1)}, u32[]{:S(2)}, u32[]{:S(2)}) %collective-permute-start.6) | collective-permute-done | bytes 524320 | tf_op jit(solution)/shard_map/ppermute | solution.py:36
  40.6 2.3 slots.1
  50.0 3.8 %collective-permute-done.9.refs_14_.refs_16_ = bf16[2,2,4,64,512]{4,3,2,1,0:T(8,128)(2,1)} collective-permute-done((bf16[2,2,4,64,512]{4,3,2,1,0:T(8,128)(2,1)S(1)}, bf16[2,2,4,64,512]{4,3,2,1,0:T(8,128)(2,1)}, u32[]{:S(2)}, u32[]{:S(2)}) %collective-permute-start.9) | collective-permute-done | bytes 1048608 | tf_op jit(solution)/shard_map/ppermute | solution.py:818
  62.2 6.1 %attention_forward.2 = (f32[200,512]{1,0:T(8,128)}, f32[200,512]{1,0:T(8,128)}, bf16[1,200,512]{2,1,0:T(8,128)(2,1)}, bf16[200,1536]{1,0:T(8,128)(2,1)}, bf16[200,512]{1,0:T(8,128)(2,1)}) custom-call(s32[8]{0:T(128)} %xor_multiply_fusion.1.refs_0_.off_ref, bf16[197,512]{1,0:T(8,128)(2,1)} %refs_1_.1, f32[2,512]{1,0:T(2,128)} %get-tuple-element.358.refs_2_.gains, ...), custom_call_target="tpu_custom_call" | custom-call | flops 1 | bytes 1 | tf_op jit(solution)/shard_map/attention_forward/pallas_call | solution.py:312
  68.3 2.7 collective-permute-done.13
  77.0 3.7 %collective-permute-done.26.refs_15_.refs_17_ = bf16[2,2,4,64,512]{4,3,2,1,0:T(8,128)(2,1)} collective-permute-done((bf16[2,2,4,64,512]{4,3,2,1,0:T(8,128)(2,1)S(1)}, bf16[2,2,4,64,512]{4,3,2,1,0:T(8,128)(2,1)}, u32[]{:S(2)}, u32[]{:S(2)}) %collective-permute-start.26) | collective-permute-done | bytes 1048608 | tf_op jit(solution)/shard_map/ppermute | solution.py:818
  80.7 10.1 %collective-permute-done.24.refs_10_.w2 = bf16[8,64,512]{2,1,0:T(8,128)(2,1)S(1)} collective-permute-done((bf16[8,64,512]{2,1,0:T(8,128)(2,1)S(1)}, bf16[8,64,512]{2,1,0:T(8,128)(2,1)S(1)}, u32[]{:S(2)}, u32[]{:S(2)}) %collective-permute-start.24) | collective-permute-done | bytes 524320 | tf_op jit(solution)/shard_map/ppermute | solution.py:36
  91.9 6.4 %collective-permute-done.17.refs_7_ = bf16[1,200,512]{2,1,0:T(8,128)(2,1)S(1)} collective-permute-done((bf16[1,200,512]{2,1,0:T(8,128)(2,1)S(1)}, bf16[1,200,512]{2,1,0:T(8,128)(2,1)S(1)}, u32[]{:S(2)}, u32[]{:S(2)}) %collective-permute-start.17) | collective-permute-done | bytes 204832 | tf_op jit(solution)/shard_map/ppermute | solution.py:36
  98.9 4.3 %collective-permute-done.27.refs_16_.refs_18_ = bf16[2,2,4,64,512]{4,3,2,1,0:T(8,128)(2,1)} collective-permute-done((bf16[2,2,4,64,512]{4,3,2,1,0:T(8,128)(2,1)}, bf16[2,2,4,64,512]{4,3,2,1,0:T(8,128)(2,1)}, u32[]{:S(2)}, u32[]{:S(2)}) %collective-permute-start.27) | collective-permute-done | bytes 1048608 | tf_op jit(solution)/shard_map/ppermute | solution.py:818
  103.2 1.6 collective-permute-start.32
  105.6 9.2 %expert_layer.3 = (bf16[4,200,512]{2,1,0:T(8,128)(2,1)}, bf16[4,200,512]{2,1,0:T(8,128)(2,1)}, bf16[512,512]{1,0:T(8,128)(2,1)}, f32[512,512]{1,0:T(8,128)}) custom-call(s32[8]{0:T(128)} %mul.21.refs_0_, s32[1]{0:T(128)} %bitcast.31.refs_1_.refs_0_, s32[2,4,256]{2,1,0:T(4,128)} %get-tuple-element.165.refs_2_.refs_0_, s32[2,4,256]{2,1,0:T(4,128)} %copy-done.56, ...), custom_call_target="tpu_custom_call" | custom-call | flops 1 | bytes 1 | tf_op jit(solution)/shard_map/expert_layer/pallas_call | solution.py:683
  114.9 2.4 collective-permute-start.35
  118.3 2.3 add_rows.4
  124.1 3.8 %collective-permute-done.29.refs_3_ = bf16[200,512]{1,0:T(8,128)(2,1)S(1)} collective-permute-done((bf16[200,512]{1,0:T(8,128)(2,1)}, bf16[200,512]{1,0:T(8,128)(2,1)S(1)}, u32[]{:S(2)}, u32[]{:S(2)}) %collective-permute-start.29) | collective-permute-done | bytes 204832 | tf_op jit(solution)/shard_map/ppermute | solution.py:36
  127.9 2.4 collective-permute-done.30.refs_4_
  130.3 3.2 collective-permute-done.31.refs_5_
  134.2 6.8 %attention_forward.3 = (f32[200,512]{1,0:T(8,128)}, f32[200,512]{1,0:T(8,128)}, bf16[2,200,512]{2,1,0:T(8,128)(2,1)}, bf16[200,1536]{1,0:T(8,128)(2,1)}, bf16[200,512]{1,0:T(8,128)(2,1)}) custom-call(s32[8]{0:T(128)} %xor_multiply_fusion.1.refs_0_.off_ref, f32[200,512]{1,0:T(8,128)} %get-tuple-element.162.refs_1_.hidden_mid, ...), custom_call_target="tpu_custom_call" | custom-call | flops 1 | bytes 1 | tf_op jit(solution)/shard_map/attention_forward/pallas_call | solution.py:312
  141.3 3.2 collective-permute-start.41
  148.0 2.9 collective-permute-done.35.refs_15_
  150.9 2.0 collective-permute-start.33
  153.0 5.1 %collective-permute-done.39.refs_11_ = bf16[2,200,512]{2,1,0:T(8,128)(2,1)S(1)} collective-permute-done((bf16[2,200,512]{2,1,0:T(8,128)(2,1)}, bf16[2,200,512]{2,1,0:T(8,128)(2,1)S(1)}, u32[]{:S(2)}, u32[]{:S(2)}) %collective-permute-start.39) | collective-permute-done | bytes 409632 | tf_op jit(solution)/shard_map/ppermute | solution.py:36
  158.1 5.6 %collective-permute-done.37.refs_9_ = bf16[2,200,512]{2,1,0:T(8,128)(2,1)S(1)} collective-permute-done((bf16[2,200,512]{2,1,0:T(8,128)(2,1)}, bf16[2,200,512]{2,1,0:T(8,128)(2,1)S(1)}, u32[]{:S(2)}, u32[]{:S(2)}) %collective-permute-start.37) | collective-permute-done | bytes 409632 | tf_op jit(solution)/shard_map/ppermute | solution.py:36
  166.8 5.5 %collective-permute-done.41.refs_16_ = bf16[2,2,4,64,512]{4,3,2,1,0:T(8,128)(2,1)} collective-permute-done((bf16[2,2,4,64,512]{4,3,2,1,0:T(8,128)(2,1)}, bf16[2,2,4,64,512]{4,3,2,1,0:T(8,128)(2,1)}, u32[]{:S(2)}, u32[]{:S(2)}) %collective-permute-start.41) | collective-permute-done | bytes 1048608 | tf_op jit(solution)/shard_map/ppermute | solution.py:818
  172.3 15.9 %expert_layer.4 = (bf16[512,512]{1,0:T(8,128)(2,1)}, bf16[4,200,512]{2,1,0:T(8,128)(2,1)}, bf16[4,200,512]{2,1,0:T(8,128)(2,1)}, f32[8,512]{1,0:T(8,128)}, bf16[...) custom-call(s32[8]{0:T(128)} %mul.21.refs_0_, ...), custom_call_target="tpu_custom_call" | custom-call | flops 1 | bytes 1 | tf_op jit(solution)/shard_map/expert_layer/pallas_call | solution.py:683
  188.2 2.4 collective-permute-start.53
  191.2 2.2 collective-permute-done.42.odd
  194.3 2.3 add_rows.5
  200.1 4.1 %collective-permute-done.43.p1 = bf16[200,512]{1,0:T(8,128)(2,1)S(1)} collective-permute-done((bf16[200,512]{1,0:T(8,128)(2,1)}, bf16[200,512]{1,0:T(8,128)(2,1)S(1)}, u32[]{:S(2)}, u32[]{:S(2)}) %collective-permute-start.43) | collective-permute-done | bytes 204832 | tf_op jit(solution)/shard_map/ppermute | solution.py:36
  204.2 1.9 collective-permute-done.44.p2
  206.1 3.7 %collective-permute-done.45.p3 = bf16[200,512]{1,0:T(8,128)(2,1)S(1)} collective-permute-done((bf16[200,512]{1,0:T(8,128)(2,1)}, bf16[200,512]{1,0:T(8,128)(2,1)S(1)}, u32[]{:S(2)}, u32[]{:S(2)}) %collective-permute-start.45) | collective-permute-done | bytes 204832 | tf_op jit(solution)/shard_map/ppermute | solution.py:36
  210.4 10.8 %attention_backward.2 = (f32[200,512]{1,0:T(8,128)}, bf16[200,512]{1,0:T(8,128)(2,1)}, f32[2,512]{1,0:T(2,128)}, bf16[8,64,512]{2,1,0:T(8,128)(2,1)}, bf16[8,64,...) custom-call(s32[8]{0:T(128)} %xor_multiply_fusion.1.refs_0_.off_ref, f32[197,512]{1,0:T(8,128)} %base.1, ...), custom_call_target="tpu_custom_call" | custom-call | flops 1 | bytes 1 | tf_op jit(solution)/shard_map/attention_backward/pallas_call | solution.py:412
  221.3 1.8 collective-permute-start.51
  224.8 5.5 %collective-permute-done.51.refs_11_ = bf16[1,200,512]{2,1,0:T(8,128)(2,1)S(1)} collective-permute-done((bf16[1,200,512]{2,1,0:T(8,128)(2,1)}, bf16[1,200,512]{2,1,0:T(8,128)(2,1)S(1)}, u32[]{:S(2)}, u32[]{:S(2)}) %collective-permute-start.51) | collective-permute-done | bytes 204832 | tf_op jit(solution)/shard_map/ppermute | solution.py:36
  230.4 3.5 collective-permute-done.49.refs_9_
  236.9 1.8 collective-permute-start.55
  239.7 3.6 collective-permute-start.60
  243.3 14.1 %expert_layer.5 = (bf16[4,200,512]{2,1,0:T(8,128)(2,1)}, bf16[4,200,512]{2,1,0:T(8,128)(2,1)}, f32[8,512]{1,0:T(8,128)}, bf16[2,2,4,64,512]{4,3,2,1,0:T(8,128)(2...) custom-call(s32[8]{0:T(128)} %mul.21.refs_0_, s32[1]{0:T(128)} %bitcast.31.refs_1_.refs_0_, ...), custom_call_target="tpu_custom_call" | custom-call | flops 10000000000 | bytes 1 | tf_op jit(solution)/shard_map/expert_layer/pallas_call | solution.py:683
  257.6 2.6 collective-permute-done.56.odd
  260.2 2.3 add_rows.6
  266.0 9.0 %collective-permute-done.60 = bf16[2,2,4,64,512]{4,3,2,1,0:T(8,128)(2,1)S(1)} collective-permute-done((bf16[2,2,4,64,512]{4,3,2,1,0:T(8,128)(2,1)}, bf16[2,2,4,64,512]{4,3,2,1,0:T(8,128)(2,1)S(1)}, u32[]{:S(2)}, u32[]{:S(2)}) %collective-permute-start.60) | collective-permute-done | bytes 1048608 | tf_op jit(solution)/shard_map/ppermute | solution.py:818
  276.2 11.1 %attention_backward.3 = (f32[197,512]{1,0:T(8,128)}, bf16[200,512]{1,0:T(8,128)(2,1)}, f32[2,512]{1,0:T(2,128)}, bf16[8,64,512]{2,1,0:T(8,128)(2,1)}, bf16[8,64,...) custom-call(s32[8]{0:T(128)} %xor_multiply_fusion.1.refs_0_.off_ref, ...), custom_call_target="tpu_custom_call" | custom-call | flops 1 | bytes 1 | tf_op jit(solution)/shard_map/attention_backward/pallas_call | solution.py:412
  287.8 1.7 fusion
  291.2 1.7 collective-permute-done.67
  295.6 1.8 collective-permute-start.69
  297.4 3.1 place_rows.1
  302.3 8.4 %collective-permute-done.71 = bf16[2,2,2,4,64,512]{5,4,3,2,1,0:T(8,128)(2,1)S(1)} collective-permute-done((bf16[2,2,2,4,64,512]{5,4,3,2,1,0:T(8,128)(2,1)}, bf16[2,2,2,4,64,512]{5,4,3,2,1,0:T(8,128)(2,1)S(1)}, u32[]{:S(2)}, u32[]{:S(2)}) %collective-permute-start.71) | collective-permute-done | bytes 2097184 | tf_op jit(solution)/shard_map/ppermute | solution.py:818
  310.7 1.8 collective-permute-start.76
  316.3 3.1 collective-permute-done.64
  320.6 3.4 collective-permute-done.66
  325.6 2.3 add_rows.7
  329.7 1.7 collective-permute-start.79
  332.3 2.6 unpack.2
  337.0 2.7 collective-permute-done.79
  340.8 1.7 bitcast_add_fusion
  342.7 1.9 collective-permute-done.80
  349.3 5.1 %collective-permute-done.81 = bf16[304,512]{1,0:T(8,128)(2,1)S(1)} collective-permute-done((bf16[304,512]{1,0:T(8,128)(2,1)S(1)}, bf16[304,512]{1,0:T(8,128)(2,1)S(1)}, u32[]{:S(2)}, u32[]{:S(2)}) %collective-permute-start.81) | collective-permute-done | bytes 311328 | tf_op jit(solution)/shard_map/ppermute | solution.py:36
  354.7 1.8 fusion.1
  356.5 3.3 collective-permute-done.84.refs_3_
  361.4 2.6 unpack.3
  (363 shorter events, 95.6 us)
Async XLA Ops:
  5.8 10.6 %collective-permute-start.1 = (bf16[1,2,64,512]{3,2,0,1:T(8,128)(2,1)S(1)}, bf16[1,2,64,512]{3,2,0,1:T(8,128)(2,1)S(1)}, u32[]{:S(2)}, u32[]{:S(2)}) collective-permute-start(bf16[1,2,64,512]{3,2,0,1:T(8,128)(2,1)S(1)} %maximum_bitcast_fusion), channel_id=1, source_target_pairs={{0,16},{1,17},{2,18},{3,19},{4,20},{5,21},{6,22},{7,23},{8,24},{9,... | collective-permute-start | bytes 393224 | tf_op jit(solution)/shard_map/ppermute | solution.py:36
  10.0 9.3 %collective-permute-start.4 = (bf16[2,2,64,512]{3,2,0,1:T(8,128)(2,1)S(1)}, bf16[2,2,64,512]{3,2,0,1:T(8,128)(2,1)S(1)}, u32[]{:S(2)}, u32[]{:S(2)}) collective-permute-start(bf16[2,2,64,512]{3,2,0,1:T(8,128)(2,1)S(1)} %get-tuple-element.347), channel_id=1, source_target_pairs={{0,4},{1,5},{2,6},{3,7},{4,0},{5,1},{6,2},{7,3},{8,12},{9,13},{10,... | collective-permute-start | bytes 786440 | tf_op jit(solution)/shard_map/ppermute | solution.py:36
  11.5 13.4 %collective-permute-start.3 = (bf16[2,2,64,512]{3,2,0,1:T(8,128)(2,1)S(1)}, bf16[2,2,64,512]{3,2,0,1:T(8,128)(2,1)S(1)}, u32[]{:S(2)}, u32[]{:S(2)}) collective-permute-start(bf16[2,2,64,512]{3,2,0,1:T(8,128)(2,1)S(1)} %get-tuple-element.348), channel_id=1, source_target_pairs={{0,2},{1,3},{2,0},{3,1},{4,6},{5,7},{6,4},{7,5},{8,10},{9,11},{10,... | collective-permute-start | bytes 786440 | tf_op jit(solution)/shard_map/ppermute | solution.py:36
  13.0 11.9 %collective-permute-start.5 = (bf16[2,2,64,512]{3,2,0,1:T(8,128)(2,1)S(1)}, bf16[2,2,64,512]{3,2,0,1:T(8,128)(2,1)S(1)}, u32[]{:S(2)}, u32[]{:S(2)}) collective-permute-start(bf16[2,2,64,512]{3,2,0,1:T(8,128)(2,1)S(1)} %slice_bitcast_fusion.16), channel_id=1, source_target_pairs={{0,6},{1,7},{2,4},{3,5},{4,2},{5,3},{6,0},{7,1},{8,14},{9,15},{10,... | collective-permute-start | bytes 786440 | tf_op jit(solution)/shard_map/ppermute | solution.py:36
  16.5 8.7 %collective-permute-start.2 = (bf16[2,2,64,512]{3,2,0,1:T(8,128)(2,1)S(1)}, bf16[2,2,64,512]{3,2,0,1:T(8,128)(2,1)S(1)}, u32[]{:S(2)}, u32[]{:S(2)}) collective-permute-start(bf16[2,2,64,512]{3,2,0,1:T(8,128)(2,1)S(1)} %pad_maximum_fusion.11), channel_id=1, source_target_pairs={{0,8},{1,9},{2,10},{3,11},{4,12},{5,13},{6,14},{7,15},{8,0},{9,1},... | collective-permute-start | bytes 786440 | tf_op jit(solution)/shard_map/ppermute | solution.py:36
  25.2 12.7 %collective-permute-start.6 = (bf16[4,2,64,512]{3,2,0,1:T(8,128)(2,1)S(1)}, bf16[4,2,64,512]{3,2,0,1:T(8,128)(2,1)S(1)}, u32[]{:S(2)}, u32[]{:S(2)}) collective-permute-start(bf16[4,2,64,512]{3,2,0,1:T(8,128)(2,1)S(1)} %pad_maximum_fusion.6), channel_id=1, source_target_pairs={{0,4},{1,5},{2,6},{3,7},{4,0},{5,1},{6,2},{7,3},{8,12},{9,13},{10,... | collective-permute-start | bytes 1572872 | tf_op jit(solution)/shard_map/ppermute | solution.py:36
  26.7 27.1 %collective-permute-start.9 = (bf16[2,2,4,64,512]{4,3,2,1,0:T(8,128)(2,1)S(1)}, bf16[2,2,4,64,512]{4,3,2,1,0:T(8,128)(2,1)}, u32[]{:S(2)}, u32[]{:S(2)}) collective-permute-start(bf16[2,2,4,64,512]{4,3,2,1,0:T(8,128)(2,1)S(1)} %bitcast.153), channel_id=1, source_target_pairs={{0,16},{1,9},{2,18},{3,11},{4,20},{5,13},{6,22},{7,15},{8,24},{9,1... | collective-permute-start | bytes 3145736 | tf_op jit(solution)/shard_map/ppermute | solution.py:818
  38.1 12.0 %collective-permute-start.8 = (bf16[8,64,512]{2,1,0:T(8,128)(2,1)S(1)}, bf16[8,64,512]{2,1,0:T(8,128)(2,1)}, u32[]{:S(2)}, u32[]{:S(2)}) collective-permute-start(bf16[8,64,512]{2,1,0:T(8,128)(2,1)S(1)} %get-tuple-element.335.refs_3_.w0), channel_id=1, source_target_pairs={{0,2},{1,3},{2,0},{3,1},{4,6},{5,7},{6,4},{7,5},{8,10},{9,11},{10,... | collective-permute-start | bytes 1572872 | tf_op jit(solution)/shard_map/ppermute | solution.py:36
  54.5 6.4 %collective-permute-start.11 = (bf16[8,64,512]{2,1,0:T(8,128)(2,1)}, bf16[8,64,512]{2,1,0:T(8,128)(2,1)S(1)}, u32[]{:S(2)}, u32[]{:S(2)}) collective-permute-start(bf16[8,64,512]{2,1,0:T(8,128)(2,1)} %collective-permute-done.8.refs_5_.w2), channel_id=1, source_target_pairs={{0,1},{1,0},{2,3},{3,2},{4,5},{5,4},{6,7},{7,6},{8,9},{9,8},{10,11... | collective-permute-start | bytes 1572872 | tf_op jit(solution)/shard_map/ppermute | solution.py:36
  54.6 26.1 %collective-permute-start.26 = (bf16[2,2,4,64,512]{4,3,2,1,0:T(8,128)(2,1)S(1)}, bf16[2,2,4,64,512]{4,3,2,1,0:T(8,128)(2,1)}, u32[]{:S(2)}, u32[]{:S(2)}) collective-permute-start(bf16[2,2,4,64,512]{4,3,2,1,0:T(8,128)(2,1)S(1)} %bitcast.154), channel_id=1, source_target_pairs={{0,8},{1,17},{2,10},{3,19},{4,12},{5,21},{6,14},{7,23},{8,0},{9,25... | collective-permute-start | bytes 3145736 | tf_op jit(solution)/shard_map/ppermute | solution.py:818
  56.8 14.2 %collective-permute-start.13 = (bf16[2,2,64,512]{3,2,0,1:T(8,128)(2,1)}, bf16[2,2,64,512]{3,2,0,1:T(8,128)(2,1)S(1)}, u32[]{:S(2)}, u32[]{:S(2)}) collective-permute-start(bf16[2,2,64,512]{3,2,0,1:T(8,128)(2,1)} %get-tuple-element.337), channel_id=1, source_target_pairs={{0,2},{1,3},{2,0},{3,1},{4,6},{5,7},{6,4},{7,5},{8,10},{9,11},{10,... | collective-permute-start | bytes 786440 | tf_op jit(solution)/shard_map/ppermute | solution.py:36
  57.6 13.3 %collective-permute-start.15 = (bf16[2,2,64,512]{3,2,0,1:T(8,128)(2,1)}, bf16[2,2,64,512]{3,2,0,1:T(8,128)(2,1)}, u32[]{:S(2)}, u32[]{:S(2)}) collective-permute-start(bf16[2,2,64,512]{3,2,0,1:T(8,128)(2,1)} %get-tuple-element.338), channel_id=1, source_target_pairs={{0,6},{1,7},{2,4},{3,5},{4,2},{5,3},{6,0},{7,1},{8,14},{9,15},{10,... | collective-permute-start | bytes 786440 | tf_op jit(solution)/shard_map/ppermute | solution.py:36
  59.1 13.1 %collective-permute-start.14 = (bf16[2,2,64,512]{3,2,0,1:T(8,128)(2,1)S(1)}, bf16[2,2,64,512]{3,2,0,1:T(8,128)(2,1)S(1)}, u32[]{:S(2)}, u32[]{:S(2)}) collective-permute-start(bf16[2,2,64,512]{3,2,0,1:T(8,128)(2,1)S(1)} %get-tuple-element.339), channel_id=1, source_target_pairs={{0,4},{1,5},{2,6},{3,7},{4,0},{5,1},{6,2},{7,3},{8,12},{9,13},{10,... | collective-permute-start | bytes 786440 | tf_op jit(solution)/shard_map/ppermute | solution.py:36
  60.9 42.3 %collective-permute-start.27 = (bf16[2,2,4,64,512]{4,3,2,1,0:T(8,128)(2,1)}, bf16[2,2,4,64,512]{4,3,2,1,0:T(8,128)(2,1)}, u32[]{:S(2)}, u32[]{:S(2)}) collective-permute-start(bf16[2,2,4,64,512]{4,3,2,1,0:T(8,128)(2,1)} %collective-permute-done.9.refs_14_.refs_16_), channel_id=1, source_target_pairs={{0,8},{1,17},{2,10},{3,19},{4,12},{5,21},{6,14},{7,23},{8,0},{9,25... | collective-permute-start | bytes 3145736 | tf_op jit(solution)/shard_map/ppermute | solution.py:818
  73.4 17.4 %collective-permute-start.24 = (bf16[8,64,512]{2,1,0:T(8,128)(2,1)S(1)}, bf16[8,64,512]{2,1,0:T(8,128)(2,1)S(1)}, u32[]{:S(2)}, u32[]{:S(2)}) collective-permute-start(bf16[8,64,512]{2,1,0:T(8,128)(2,1)S(1)} %get-tuple-element.189.refs_8_.w0), channel_id=1, source_target_pairs={{0,2},{1,3},{2,0},{3,1},{4,6},{5,7},{6,4},{7,5},{8,10},{9,11},{10,... | collective-permute-start | bytes 1572872 | tf_op jit(solution)/shard_map/ppermute | solution.py:36
  74.3 16.5 %collective-permute-start.21 = (bf16[1,200,512]{2,1,0:T(8,128)(2,1)S(1)}, bf16[1,200,512]{2,1,0:T(8,128)(2,1)S(1)}, u32[]{:S(2)}, u32[]{:S(2)}) collective-permute-start(bf16[1,200,512]{2,1,0:T(8,128)(2,1)S(1)} %copy-done.38), channel_id=1, source_target_pairs={{0,6},{1,7},{2,4},{3,5},{4,2},{5,3},{6,0},{7,1},{8,14},{9,15},{10,... | collective-permute-start | bytes 614408 | tf_op jit(solution)/shard_map/ppermute | solution.py:36
  75.8 16.0 %collective-permute-start.19 = (bf16[1,200,512]{2,1,0:T(8,128)(2,1)S(1)}, bf16[1,200,512]{2,1,0:T(8,128)(2,1)S(1)}, u32[]{:S(2)}, u32[]{:S(2)}) collective-permute-start(bf16[1,200,512]{2,1,0:T(8,128)(2,1)S(1)} %copy-done.38), channel_id=1, source_target_pairs={{0,4},{1,5},{2,6},{3,7},{4,0},{5,1},{6,2},{7,3},{8,12},{9,13},{10,... | collective-permute-start | bytes 614408 | tf_op jit(solution)/shard_map/ppermute | solution.py:36
  80.7 24.1 %collective-permute-start.23 = (bf16[8,64,512]{2,1,0:T(8,128)(2,1)S(1)}, bf16[8,64,512]{2,1,0:T(8,128)(2,1)S(1)}, u32[]{:S(2)}, u32[]{:S(2)}) collective-permute-start(bf16[8,64,512]{2,1,0:T(8,128)(2,1)S(1)} %get-tuple-element.189.refs_8_.w0), channel_id=1, source_target_pairs={{0,1},{1,0},{2,3},{3,2},{4,5},{5,4},{6,7},{7,6},{8,9},{9,8},{10,11... | collective-permute-start | bytes 1572872 | tf_op jit(solution)/shard_map/ppermute | solution.py:36
  90.9 14.0 %collective-permute-start.25 = (bf16[8,64,512]{2,1,0:T(8,128)(2,1)S(1)}, bf16[8,64,512]{2,1,0:T(8,128)(2,1)S(1)}, u32[]{:S(2)}, u32[]{:S(2)}) collective-permute-start(bf16[8,64,512]{2,1,0:T(8,128)(2,1)S(1)} %collective-permute-done.24.refs_10_.w2), channel_id=1, source_target_pairs={{0,1},{1,0},{2,3},{3,2},{4,5},{5,4},{6,7},{7,6},{8,9},{9,8},{10,11... | collective-permute-start | bytes 1572872 | tf_op jit(solution)/shard_map/ppermute | solution.py:36
  90.9 7.5 %collective-permute-start.17 = (bf16[1,200,512]{2,1,0:T(8,128)(2,1)S(1)}, bf16[1,200,512]{2,1,0:T(8,128)(2,1)S(1)}, u32[]{:S(2)}, u32[]{:S(2)}) collective-permute-start(bf16[1,200,512]{2,1,0:T(8,128)(2,1)S(1)} %copy-done.38), channel_id=1, source_target_pairs={{0,2},{1,3},{2,0},{3,1},{4,6},{5,7},{6,4},{7,5},{8,10},{9,11},{10,... | collective-permute-start | bytes 614408 | tf_op jit(solution)/shard_map/ppermute | solution.py:36
  91.8 6.6 %collective-permute-start.16 = (bf16[1,200,512]{2,1,0:T(8,128)(2,1)S(1)}, bf16[1,200,512]{2,1,0:T(8,128)(2,1)S(1)}, u32[]{:S(2)}, u32[]{:S(2)}) collective-permute-start(bf16[1,200,512]{2,1,0:T(8,128)(2,1)S(1)} %copy-done.38), channel_id=1, source_target_pairs={{0,1},{1,0},{2,3},{3,2},{4,5},{5,4},{6,7},{7,6},{8,9},{9,8},{10,11... | collective-permute-start | bytes 614408 | tf_op jit(solution)/shard_map/ppermute | solution.py:36
  98.4 6.4 %collective-permute-start.20 = (bf16[1,200,512]{2,1,0:T(8,128)(2,1)S(1)}, bf16[1,200,512]{2,1,0:T(8,128)(2,1)S(1)}, u32[]{:S(2)}, u32[]{:S(2)}) collective-permute-start(bf16[1,200,512]{2,1,0:T(8,128)(2,1)S(1)} %collective-permute-done.19.refs_9_), channel_id=1, source_target_pairs={{0,1},{1,0},{2,3},{3,2},{4,5},{5,4},{6,7},{7,6},{8,9},{9,8},{10,11... | collective-permute-start | bytes 614408 | tf_op jit(solution)/shard_map/ppermute | solution.py:36
  103.2 38.1 %collective-permute-start.32 = (bf16[2,2,4,64,512]{4,3,2,1,0:T(8,128)(2,1)S(1)}, bf16[2,2,4,64,512]{4,3,2,1,0:T(8,128)(2,1)}, u32[]{:S(2)}, u32[]{:S(2)}) collective-permute-start(bf16[2,2,4,64,512]{4,3,2,1,0:T(8,128)(2,1)S(1)} %bitcast.159), channel_id=1, source_target_pairs={{0,16},{1,9},{2,18},{3,11},{4,20},{5,13},{6,22},{7,15},{8,24},{9,1... | collective-permute-start | bytes 3145736 | tf_op jit(solution)/shard_map/ppermute | solution.py:818
  114.9 36.1 %collective-permute-start.35 = (bf16[2,2,4,64,512]{4,3,2,1,0:T(8,128)(2,1)S(1)}, bf16[2,2,4,64,512]{4,3,2,1,0:T(8,128)(2,1)S(1)}, u32[]{:S(2)}, u32[]{:S(2)}) collective-permute-start(bf16[2,2,4,64,512]{4,3,2,1,0:T(8,128)(2,1)S(1)} %bitcast.160), channel_id=1, source_target_pairs={{0,8},{1,17},{2,10},{3,19},{4,12},{5,21},{6,14},{7,23},{8,0},{9,25... | collective-permute-start | bytes 3145736 | tf_op jit(solution)/shard_map/ppermute | solution.py:818
  120.6 7.3 %collective-permute-start.29 = (bf16[200,512]{1,0:T(8,128)(2,1)}, bf16[200,512]{1,0:T(8,128)(2,1)S(1)}, u32[]{:S(2)}, u32[]{:S(2)}) collective-permute-start(bf16[200,512]{1,0:T(8,128)(2,1)} %get-tuple-element.186), channel_id=1, source_target_pairs={{0,2},{1,3},{2,0},{3,1},{4,6},{5,7},{6,4},{7,5},{8,10},{9,11},{10,... | collective-permute-start | bytes 614408 | tf_op jit(solution)/shard_map/ppermute | solution.py:36
  122.1 8.2 %collective-permute-start.30 = (bf16[200,512]{1,0:T(8,128)(2,1)}, bf16[200,512]{1,0:T(8,128)(2,1)S(1)}, u32[]{:S(2)}, u32[]{:S(2)}) collective-permute-start(bf16[200,512]{1,0:T(8,128)(2,1)} %get-tuple-element.187), channel_id=1, source_target_pairs={{0,4},{1,5},{2,6},{3,7},{4,0},{5,1},{6,2},{7,3},{8,12},{9,13},{10,... | collective-permute-start | bytes 614408 | tf_op jit(solution)/shard_map/ppermute | solution.py:36
  122.7 10.9 %collective-permute-start.31 = (bf16[200,512]{1,0:T(8,128)(2,1)}, bf16[200,512]{1,0:T(8,128)(2,1)S(1)}, u32[]{:S(2)}, u32[]{:S(2)}) collective-permute-start(bf16[200,512]{1,0:T(8,128)(2,1)} %get-tuple-element.188), channel_id=1, source_target_pairs={{0,6},{1,7},{2,4},{3,5},{4,2},{5,3},{6,0},{7,1},{8,14},{9,15},{10,... | collective-permute-start | bytes 614408 | tf_op jit(solution)/shard_map/ppermute | solution.py:36
  141.3 30.9 %collective-permute-start.41 = (bf16[2,2,4,64,512]{4,3,2,1,0:T(8,128)(2,1)}, bf16[2,2,4,64,512]{4,3,2,1,0:T(8,128)(2,1)}, u32[]{:S(2)}, u32[]{:S(2)}) collective-permute-start(bf16[2,2,4,64,512]{4,3,2,1,0:T(8,128)(2,1)} %collective-permute-done.32.refs_14_), channel_id=1, source_target_pairs={{0,8},{1,17},{2,10},{3,19},{4,12},{5,21},{6,14},{7,23},{8,0},{9,25... | collective-permute-start | bytes 3145736 | tf_op jit(solution)/shard_map/ppermute | solution.py:818
  144.5 13.5 %collective-permute-start.39 = (bf16[2,200,512]{2,1,0:T(8,128)(2,1)}, bf16[2,200,512]{2,1,0:T(8,128)(2,1)S(1)}, u32[]{:S(2)}, u32[]{:S(2)}) collective-permute-start(bf16[2,200,512]{2,1,0:T(8,128)(2,1)} %get-tuple-element.196.refs_5_), channel_id=1, source_target_pairs={{0,6},{1,7},{2,4},{3,5},{4,2},{5,3},{6,0},{7,1},{8,14},{9,15},{10,... | collective-permute-start | bytes 1228808 | tf_op jit(solution)/shard_map/ppermute | solution.py:36
  146.0 17.7 %collective-permute-start.37 = (bf16[2,200,512]{2,1,0:T(8,128)(2,1)}, bf16[2,200,512]{2,1,0:T(8,128)(2,1)S(1)}, u32[]{:S(2)}, u32[]{:S(2)}) collective-permute-start(bf16[2,200,512]{2,1,0:T(8,128)(2,1)} %get-tuple-element.196.refs_5_), channel_id=1, source_target_pairs={{0,4},{1,5},{2,6},{3,7},{4,0},{5,1},{6,2},{7,3},{8,12},{9,13},{10,... | collective-permute-start | bytes 1228808 | tf_op jit(solution)/shard_map/ppermute | solution.py:36
  147.5 16.2 %collective-permute-start.34 = (bf16[2,200,512]{2,1,0:T(8,128)(2,1)}, bf16[2,200,512]{2,1,0:T(8,128)(2,1)S(1)}, u32[]{:S(2)}, u32[]{:S(2)}) collective-permute-start(bf16[2,200,512]{2,1,0:T(8,128)(2,1)} %get-tuple-element.196.refs_5_), channel_id=1, source_target_pairs={{0,2},{1,3},{2,0},{3,1},{4,6},{5,7},{6,4},{7,5},{8,10},{9,11},{10,... | collective-permute-start | bytes 1228808 | tf_op jit(solution)/shard_map/ppermute | solution.py:36
  150.9 13.3 %collective-permute-start.33 = (bf16[2,200,512]{2,1,0:T(8,128)(2,1)}, bf16[2,200,512]{2,1,0:T(8,128)(2,1)S(1)}, u32[]{:S(2)}, u32[]{:S(2)}) collective-permute-start(bf16[2,200,512]{2,1,0:T(8,128)(2,1)} %get-tuple-element.196.refs_5_), channel_id=1, source_target_pairs={{0,1},{1,0},{2,3},{3,2},{4,5},{5,4},{6,7},{7,6},{8,9},{9,8},{10,11... | collective-permute-start | bytes 1228808 | tf_op jit(solution)/shard_map/ppermute | solution.py:36
  188.2 48.6 %collective-permute-start.53 = (bf16[2,2,2,4,64,512]{5,4,3,2,1,0:T(8,128)(2,1)}, bf16[2,2,2,4,64,512]{5,4,3,2,1,0:T(8,128)(2,1)S(1)}, u32[]{:S(2)}, u32[]{:S(2)}) collective-permute-start(bf16[2,2,2,4,64,512]{5,4,3,2,1,0:T(8,128)(2,1)} %get-tuple-element.212), channel_id=1, source_target_pairs={{0,8},{1,17},{2,10},{3,19},{4,12},{5,21},{6,14},{7,23},{8,0},{9,25... | collective-permute-start | bytes 6291464 | tf_op jit(solution)/shard_map/ppermute | solution.py:818
  196.6 7.6 %collective-permute-start.43 = (bf16[200,512]{1,0:T(8,128)(2,1)}, bf16[200,512]{1,0:T(8,128)(2,1)S(1)}, u32[]{:S(2)}, u32[]{:S(2)}) collective-permute-start(bf16[200,512]{1,0:T(8,128)(2,1)} %get-tuple-element.203), channel_id=1, source_target_pairs={{0,2},{1,3},{2,0},{3,1},{4,6},{5,7},{6,4},{7,5},{8,10},{9,11},{10,... | collective-permute-start | bytes 614408 | tf_op jit(solution)/shard_map/ppermute | solution.py:36
  197.9 8.2 %collective-permute-start.44 = (bf16[200,512]{1,0:T(8,128)(2,1)}, bf16[200,512]{1,0:T(8,128)(2,1)S(1)}, u32[]{:S(2)}, u32[]{:S(2)}) collective-permute-start(bf16[200,512]{1,0:T(8,128)(2,1)} %get-tuple-element.204), channel_id=1, source_target_pairs={{0,4},{1,5},{2,6},{3,7},{4,0},{5,1},{6,2},{7,3},{8,12},{9,13},{10,... | collective-permute-start | bytes 614408 | tf_op jit(solution)/shard_map/ppermute | solution.py:36
  199.0 10.8 %collective-permute-start.45 = (bf16[200,512]{1,0:T(8,128)(2,1)}, bf16[200,512]{1,0:T(8,128)(2,1)S(1)}, u32[]{:S(2)}, u32[]{:S(2)}) collective-permute-start(bf16[200,512]{1,0:T(8,128)(2,1)} %get-tuple-element.205), channel_id=1, source_target_pairs={{0,6},{1,7},{2,4},{3,5},{4,2},{5,3},{6,0},{7,1},{8,14},{9,15},{10,... | collective-permute-start | bytes 614408 | tf_op jit(solution)/shard_map/ppermute | solution.py:36
  221.2 13.2 %collective-permute-start.54 = (bf16[8,64,512]{2,1,0:T(8,128)(2,1)}, bf16[8,64,512]{2,1,0:T(8,128)(2,1)S(1)}, u32[]{:S(2)}, u32[]{:S(2)}) collective-permute-start(bf16[8,64,512]{2,1,0:T(8,128)(2,1)} %get-tuple-element.214), channel_id=1, source_target_pairs={{0,1},{1,0},{2,3},{3,2},{4,5},{5,4},{6,7},{7,6},{8,9},{9,8},{10,11... | collective-permute-start | bytes 1572872 | tf_op jit(solution)/shard_map/ppermute | solution.py:36
  221.3 9.1 %collective-permute-start.51 = (bf16[1,200,512]{2,1,0:T(8,128)(2,1)}, bf16[1,200,512]{2,1,0:T(8,128)(2,1)S(1)}, u32[]{:S(2)}, u32[]{:S(2)}) collective-permute-start(bf16[1,200,512]{2,1,0:T(8,128)(2,1)} %bitcast.190), channel_id=1, source_target_pairs={{0,6},{1,7},{2,4},{3,5},{4,2},{5,3},{6,0},{7,1},{8,14},{9,15},{10,... | collective-permute-start | bytes 614408 | tf_op jit(solution)/shard_map/ppermute | solution.py:36
  223.1 10.8 %collective-permute-start.49 = (bf16[1,200,512]{2,1,0:T(8,128)(2,1)}, bf16[1,200,512]{2,1,0:T(8,128)(2,1)S(1)}, u32[]{:S(2)}, u32[]{:S(2)}) collective-permute-start(bf16[1,200,512]{2,1,0:T(8,128)(2,1)} %bitcast.191), channel_id=1, source_target_pairs={{0,4},{1,5},{2,6},{3,7},{4,0},{5,1},{6,2},{7,3},{8,12},{9,13},{10,... | collective-permute-start | bytes 614408 | tf_op jit(solution)/shard_map/ppermute | solution.py:36
  223.8 10.4 %collective-permute-start.47 = (bf16[1,200,512]{2,1,0:T(8,128)(2,1)}, bf16[1,200,512]{2,1,0:T(8,128)(2,1)S(1)}, u32[]{:S(2)}, u32[]{:S(2)}) collective-permute-start(bf16[1,200,512]{2,1,0:T(8,128)(2,1)} %bitcast.192), channel_id=1, source_target_pairs={{0,2},{1,3},{2,0},{3,1},{4,6},{5,7},{6,4},{7,5},{8,10},{9,11},{10,... | collective-permute-start | bytes 614408 | tf_op jit(solution)/shard_map/ppermute | solution.py:36
  236.9 20.6 %collective-permute-start.55 = (bf16[8,64,512]{2,1,0:T(8,128)(2,1)S(1)}, bf16[8,64,512]{2,1,0:T(8,128)(2,1)}, u32[]{:S(2)}, u32[]{:S(2)}) collective-permute-start(bf16[8,64,512]{2,1,0:T(8,128)(2,1)S(1)} %add.109), channel_id=1, source_target_pairs={{0,2},{1,3},{2,0},{3,1},{4,6},{5,7},{6,4},{7,5},{8,10},{9,11},{10,... | collective-permute-start | bytes 1572872 | tf_op jit(solution)/shard_map/ppermute | solution.py:36
  239.7 35.3 %collective-permute-start.60 = (bf16[2,2,4,64,512]{4,3,2,1,0:T(8,128)(2,1)}, bf16[2,2,4,64,512]{4,3,2,1,0:T(8,128)(2,1)S(1)}, u32[]{:S(2)}, u32[]{:S(2)}) collective-permute-start(bf16[2,2,4,64,512]{4,3,2,1,0:T(8,128)(2,1)} %bitcast_add_fusion.3), channel_id=1, source_target_pairs={{0,16},{1,9},{2,18},{3,11},{4,20},{5,13},{6,22},{7,15},{8,24},{9,1... | collective-permute-start | bytes 3145736 | tf_op jit(solution)/shard_map/ppermute | solution.py:818
  257.5 53.1 %collective-permute-start.71 = (bf16[2,2,2,4,64,512]{5,4,3,2,1,0:T(8,128)(2,1)}, bf16[2,2,2,4,64,512]{5,4,3,2,1,0:T(8,128)(2,1)S(1)}, u32[]{:S(2)}, u32[]{:S(2)}) collective-permute-start(bf16[2,2,2,4,64,512]{5,4,3,2,1,0:T(8,128)(2,1)} %get-tuple-element.262), channel_id=1, source_target_pairs={{0,8},{1,17},{2,10},{3,19},{4,12},{5,21},{6,14},{7,23},{8,0},{9,25... | collective-permute-start | bytes 6291464 | tf_op jit(solution)/shard_map/ppermute | solution.py:818
  262.5 12.5 %collective-permute-start.59 = (bf16[200,512]{1,0:T(8,128)(2,1)}, bf16[200,512]{1,0:T(8,128)(2,1)S(1)}, u32[]{:S(2)}, u32[]{:S(2)}) collective-permute-start(bf16[200,512]{1,0:T(8,128)(2,1)} %get-tuple-element.233), channel_id=1, source_target_pairs={{0,6},{1,7},{2,4},{3,5},{4,2},{5,3},{6,0},{7,1},{8,14},{9,15},{10,... | collective-permute-start | bytes 614408 | tf_op jit(solution)/shard_map/ppermute | solution.py:36
  263.0 12.1 %collective-permute-start.57 = (bf16[200,512]{1,0:T(8,128)(2,1)}, bf16[200,512]{1,0:T(8,128)(2,1)S(1)}, u32[]{:S(2)}, u32[]{:S(2)}) collective-permute-start(bf16[200,512]{1,0:T(8,128)(2,1)} %get-tuple-element.231), channel_id=1, source_target_pairs={{0,2},{1,3},{2,0},{3,1},{4,6},{5,7},{6,4},{7,5},{8,10},{9,11},{10,... | collective-permute-start | bytes 614408 | tf_op jit(solution)/shard_map/ppermute | solution.py:36
  264.5 10.6 %collective-permute-start.58 = (bf16[200,512]{1,0:T(8,128)(2,1)}, bf16[200,512]{1,0:T(8,128)(2,1)S(1)}, u32[]{:S(2)}, u32[]{:S(2)}) collective-permute-start(bf16[200,512]{1,0:T(8,128)(2,1)} %get-tuple-element.232), channel_id=1, source_target_pairs={{0,4},{1,5},{2,6},{3,7},{4,0},{5,1},{6,2},{7,3},{8,12},{9,13},{10,... | collective-permute-start | bytes 614408 | tf_op jit(solution)/shard_map/ppermute | solution.py:36
  275.0 14.5 %collective-permute-start.63 = (bf16[8,64,512]{2,1,0:T(8,128)(2,1)}, bf16[8,64,512]{2,1,0:T(8,128)(2,1)S(1)}, u32[]{:S(2)}, u32[]{:S(2)}) collective-permute-start(bf16[8,64,512]{2,1,0:T(8,128)(2,1)} %get-tuple-element.242), channel_id=1, source_target_pairs={{0,1},{1,0},{2,3},{3,2},{4,5},{5,4},{6,7},{7,6},{8,9},{9,8},{10,11... | collective-permute-start | bytes 1572872 | tf_op jit(solution)/shard_map/ppermute | solution.py:36
  293.9 16.7 %collective-permute-start.70 = (bf16[2,2,64,512]{3,2,1,0:T(8,128)(2,1)}, bf16[2,2,64,512]{3,2,1,0:T(8,128)(2,1)S(1)}, u32[]{:S(2)}, u32[]{:S(2)}) collective-permute-start(bf16[2,2,64,512]{3,2,1,0:T(8,128)(2,1)} %get-tuple-element.328), channel_id=1, source_target_pairs={{0,6},{1,7},{2,4},{3,5},{4,2},{5,3},{6,0},{7,1},{8,14},{9,15},{10,... | collective-permute-start | bytes 786440 | tf_op jit(solution)/shard_map/ppermute | solution.py:36
  294.1 16.5 %collective-permute-start.68 = (bf16[2,2,64,512]{3,2,1,0:T(8,128)(2,1)}, bf16[2,2,64,512]{3,2,1,0:T(8,128)(2,1)}, u32[]{:S(2)}, u32[]{:S(2)}) collective-permute-start(bf16[2,2,64,512]{3,2,1,0:T(8,128)(2,1)} %get-tuple-element.330), channel_id=1, source_target_pairs={{0,2},{1,3},{2,0},{3,1},{4,6},{5,7},{6,4},{7,5},{8,10},{9,11},{10,... | collective-permute-start | bytes 786440 | tf_op jit(solution)/shard_map/ppermute | solution.py:36
  295.6 15.0 %collective-permute-start.69 = (bf16[2,2,64,512]{3,2,1,0:T(8,128)(2,1)}, bf16[2,2,64,512]{3,2,1,0:T(8,128)(2,1)}, u32[]{:S(2)}, u32[]{:S(2)}) collective-permute-start(bf16[2,2,64,512]{3,2,1,0:T(8,128)(2,1)} %get-tuple-element.331), channel_id=1, source_target_pairs={{0,4},{1,5},{2,6},{3,7},{4,0},{5,1},{6,2},{7,3},{8,12},{9,13},{10,... | collective-permute-start | bytes 786440 | tf_op jit(solution)/shard_map/ppermute | solution.py:36
  302.0 17.4 %collective-permute-start.64 = (bf16[8,64,512]{2,1,0:T(8,128)(2,1)S(1)}, bf16[8,64,512]{2,1,0:T(8,128)(2,1)S(1)}, u32[]{:S(2)}, u32[]{:S(2)}) collective-permute-start(bf16[8,64,512]{2,1,0:T(8,128)(2,1)S(1)} %add.114), channel_id=1, source_target_pairs={{0,2},{1,3},{2,0},{3,1},{4,6},{5,7},{6,4},{7,5},{8,10},{9,11},{10,... | collective-permute-start | bytes 1572872 | tf_op jit(solution)/shard_map/ppermute | solution.py:36
  310.7 14.9 %collective-permute-start.76 = (bf16[4,200,512]{2,1,0:T(8,128)(2,1)}, bf16[4,200,512]{2,1,0:T(8,128)(2,1)}, u32[]{:S(2)}, u32[]{:S(2)}) collective-permute-start(bf16[4,200,512]{2,1,0:T(8,128)(2,1)} %get-tuple-element.281), channel_id=1, source_target_pairs={{0,1},{1,0},{2,3},{3,2},{4,5},{5,4},{6,7},{7,6},{8,9},{9,8},{10,11... | collective-permute-start | bytes 2457608 | tf_op jit(solution)/shard_map/ppermute | solution.py:36
  313.5 27.2 %collective-permute-start.75 = (bf16[2,2,4,64,512]{4,3,2,1,0:T(8,128)(2,1)}, bf16[2,2,4,64,512]{4,3,2,1,0:T(8,128)(2,1)}, u32[]{:S(2)}, u32[]{:S(2)}) collective-permute-start(bf16[2,2,4,64,512]{4,3,2,1,0:T(8,128)(2,1)} %bitcast_add_fusion.1), channel_id=1, source_target_pairs={{0,16},{1,9},{2,18},{3,11},{4,20},{5,13},{6,22},{7,15},{8,24},{9,1... | collective-permute-start | bytes 3145736 | tf_op jit(solution)/shard_map/ppermute | solution.py:818
  314.8 9.2 %collective-permute-start.66 = (bf16[4,64,512]{2,1,0:T(8,128)(2,1)S(1)}, bf16[4,64,512]{2,1,0:T(8,128)(2,1)S(1)}, u32[]{:S(2)}, u32[]{:S(2)}) collective-permute-start(bf16[4,64,512]{2,1,0:T(8,128)(2,1)S(1)} %slice.271), channel_id=1, source_target_pairs={{0,4},{1,5},{2,6},{3,7},{4,0},{5,1},{6,2},{7,3},{8,12},{9,13},{10,... | collective-permute-start | bytes 786440 | tf_op jit(solution)/shard_map/ppermute | solution.py:36
  319.5 10.1 %collective-permute-start.65 = (bf16[4,64,512]{2,1,0:T(8,128)(2,1)S(1)}, bf16[4,64,512]{2,1,0:T(8,128)(2,1)S(1)}, u32[]{:S(2)}, u32[]{:S(2)}) collective-permute-start(bf16[4,64,512]{2,1,0:T(8,128)(2,1)S(1)} %slice.269), channel_id=1, source_target_pairs={{0,4},{1,5},{2,6},{3,7},{4,0},{5,1},{6,2},{7,3},{8,12},{9,13},{10,... | collective-permute-start | bytes 786440 | tf_op jit(solution)/shard_map/ppermute | solution.py:36
  324.1 7.3 %collective-permute-start.73 = (f32[24,512]{1,0:T(8,128)S(1)}, f32[24,512]{1,0:T(8,128)S(1)}, u32[]{:S(2)}, u32[]{:S(2)}) collective-permute-start(f32[24,512]{1,0:T(8,128)S(1)} %add.120), channel_id=1, source_target_pairs={{0,4},{1,5},{2,6},{3,7},{4,0},{5,1},{6,2},{7,3},{8,12},{9,13},{10,... | collective-permute-start | bytes 147464 | tf_op jit(solution)/shard_map/ppermute | solution.py:36
  327.9 8.7 %collective-permute-start.77 = (bf16[200,512]{1,0:T(8,128)(2,1)}, bf16[200,512]{1,0:T(8,128)(2,1)}, u32[]{:S(2)}, u32[]{:S(2)}) collective-permute-start(bf16[200,512]{1,0:T(8,128)(2,1)} %get-tuple-element.283), channel_id=1, source_target_pairs={{0,2},{1,3},{2,0},{3,1},{4,6},{5,7},{6,4},{7,5},{8,10},{9,11},{10,... | collective-permute-start | bytes 614408 | tf_op jit(solution)/shard_map/ppermute | solution.py:36
  328.7 8.3 %collective-permute-start.78 = (bf16[200,512]{1,0:T(8,128)(2,1)}, bf16[200,512]{1,0:T(8,128)(2,1)}, u32[]{:S(2)}, u32[]{:S(2)}) collective-permute-start(bf16[200,512]{1,0:T(8,128)(2,1)} %get-tuple-element.284), channel_id=1, source_target_pairs={{0,4},{1,5},{2,6},{3,7},{4,0},{5,1},{6,2},{7,3},{8,12},{9,13},{10,... | collective-permute-start | bytes 614408 | tf_op jit(solution)/shard_map/ppermute | solution.py:36
  329.7 10.1 %collective-permute-start.79 = (bf16[200,512]{1,0:T(8,128)(2,1)}, bf16[200,512]{1,0:T(8,128)(2,1)S(1)}, u32[]{:S(2)}, u32[]{:S(2)}) collective-permute-start(bf16[200,512]{1,0:T(8,128)(2,1)} %get-tuple-element.285), channel_id=1, source_target_pairs={{0,6},{1,7},{2,4},{3,5},{4,2},{5,3},{6,0},{7,1},{8,14},{9,15},{10,... | collective-permute-start | bytes 614408 | tf_op jit(solution)/shard_map/ppermute | solution.py:36
  344.9 9.5 %collective-permute-start.81 = (bf16[304,512]{1,0:T(8,128)(2,1)S(1)}, bf16[304,512]{1,0:T(8,128)(2,1)S(1)}, u32[]{:S(2)}, u32[]{:S(2)}) collective-permute-start(bf16[304,512]{1,0:T(8,128)(2,1)S(1)} %pad_maximum_fusion.8), channel_id=1, source_target_pairs={{0,8},{1,9},{2,10},{3,11},{4,12},{5,13},{6,14},{7,15},{8,0},{9,1},... | collective-permute-start | bytes 933896 | tf_op jit(solution)/shard_map/ppermute | solution.py:36
  345.8 10.7 %collective-permute-start.85 = (bf16[2,2,64,512]{3,2,1,0:T(8,128)(2,1)S(1)}, bf16[2,2,64,512]{3,2,1,0:T(8,128)(2,1)S(1)}, u32[]{:S(2)}, u32[]{:S(2)}) collective-permute-start(bf16[2,2,64,512]{3,2,1,0:T(8,128)(2,1)S(1)} %get-tuple-element.322), channel_id=1, source_target_pairs={{0,6},{1,7},{2,4},{3,5},{4,2},{5,3},{6,0},{7,1},{8,14},{9,15},{10,... | collective-permute-start | bytes 786440 | tf_op jit(solution)/shard_map/ppermute | solution.py:36
  346.8 13.1 %collective-permute-start.84 = (bf16[2,2,64,512]{3,2,1,0:T(8,128)(2,1)S(1)}, bf16[2,2,64,512]{3,2,1,0:T(8,128)(2,1)S(1)}, u32[]{:S(2)}, u32[]{:S(2)}) collective-permute-start(bf16[2,2,64,512]{3,2,1,0:T(8,128)(2,1)S(1)} %get-tuple-element.323), channel_id=1, source_target_pairs={{0,4},{1,5},{2,6},{3,7},{4,0},{5,1},{6,2},{7,3},{8,12},{9,13},{10,... | collective-permute-start | bytes 786440 | tf_op jit(solution)/shard_map/ppermute | solution.py:36
  348.1 12.5 %collective-permute-start.83 = (bf16[2,2,64,512]{3,2,1,0:T(8,128)(2,1)S(1)}, bf16[2,2,64,512]{3,2,1,0:T(8,128)(2,1)S(1)}, u32[]{:S(2)}, u32[]{:S(2)}) collective-permute-start(bf16[2,2,64,512]{3,2,1,0:T(8,128)(2,1)S(1)} %get-tuple-element.324), channel_id=1, source_target_pairs={{0,2},{1,3},{2,0},{3,1},{4,6},{5,7},{6,4},{7,5},{8,10},{9,11},{10,... | collective-permute-start | bytes 786440 | tf_op jit(solution)/shard_map/ppermute | solution.py:36
  354.5 10.6 %collective-permute-start.82 = (bf16[176,512]{1,0:T(8,128)(2,1)S(1)}, bf16[176,512]{1,0:T(8,128)(2,1)S(1)}, u32[]{:S(2)}, u32[]{:S(2)}) collective-permute-start(bf16[176,512]{1,0:T(8,128)(2,1)S(1)} %pad_maximum_fusion.12), channel_id=1, source_target_pairs={{0,16},{1,17},{2,18},{3,19},{4,20},{5,21},{6,22},{7,23},{8,24},{9,... | collective-permute-start | bytes 540680 | tf_op jit(solution)/shard_map/ppermute | solution.py:36
  (95 other events, 621.8 us)
